TPU v7x, 32 devices: a whole 2x2x4 slice. The times are simulated.
32 devices in a mesh: fsdp: 16 (over z, x, core), ctx: 2 (over y).
Axes of the slice: x: 2, y: 2, z: 4, core: 2. Of those that a mesh axis runs over, the one named last changes fastest.
Arguments:
- tokens: bfloat16 [16, 1024, 768], P('fsdp', 'ctx'), may hold values from -6 to 6
- cotangent: bfloat16 [16, 1024, 768], P('fsdp', 'ctx'), may hold values from -6 to 6
- kept_blocks: int32 [16, 12, 8], P('fsdp'), may hold values from 0 to 7, as said below
- picture_starts: int32 [16, 2], P('fsdp'), may hold values from 0 to 768, as said below
- qkv_weight: bfloat16 [2, 768, 2304], P(None, 'fsdp', 'ctx'), may hold values from -0.21875 to 0.21875
- score_weight: bfloat16 [2, 768, 12], P(None, 'fsdp'), may hold values from -0.21875 to 0.21875
- out_weight: bfloat16 [2, 768, 768], P(None, 'fsdp', 'ctx'), may hold values from -1.5 to 1.5
- up_weight: bfloat16 [2, 768, 3072], P(None, 'fsdp', 'ctx'), may hold values from -0.21875 to 0.21875
- down_weight: bfloat16 [2, 3072, 768], P(None, 'fsdp', 'ctx'), may hold values from -0.109375 to 0.109375
- norm_gain: bfloat16 [2, 2, 768], P(None, None, 'fsdp'), may hold values from 0.5 to 1.5
- norm_bias: bfloat16 [2, 2, 768], P(None, None, 'fsdp'), may hold values from -4 to 4
Outputs:
- block_output: float32 [16, 1024, 768], P('fsdp', 'ctx')
- token_grad: float32 [16, 1024, 768], P('fsdp', 'ctx')
- qkv_grad: float32 [2, 768, 2304], P(None, 'fsdp', 'ctx')
- score_grad: float32 [2, 768, 12], P(None, 'fsdp')
- out_grad: float32 [2, 768, 768], P(None, 'fsdp', 'ctx')
- up_grad: float32 [2, 768, 3072], P(None, 'fsdp', 'ctx')
- down_grad: float32 [2, 3072, 768], P(None, 'fsdp', 'ctx')
- gain_grad: float32 [2, 2, 768], P(None, None, 'fsdp')
- bias_grad: float32 [2, 2, 768], P(None, None, 'fsdp')
Inputs may be any that keep to these rules, and one draw needn't show every extreme that they name: `kept_blocks`: the key block of 128 keys kept by a query block is never later than that query block. `picture_starts`: each start is a multiple of 128; a piece of 256 tokens lies inside its sequence; pieces may intersect.
All inputs are finite; a program needn't handle non-finite values.
Results may differ from a plain program's by a relative error of at most 0.018.
Values may be sent and summed in bfloat16 or wider, within the bound.
No kernel may reach another device: no remote copies, remote signals or barrier semaphores. Data moves between devices by JAX's collectives and lax.ppermute only.
A program may use at most 256 MiB of HBM per device.

v0:
```python
from functools import partial

import jax
import jax.numpy as jnp
from jax import lax
from jax.sharding import PartitionSpec as P

HEADS = 12
HEAD_DIM = 64
LAYERS = 2
BLK = 128
WINDOW = 64
PIC_LEN = 256


def normalize(residual, gain, bias):
    mean_value = jnp.mean(residual, axis=-1, keepdims=True)
    centered = residual - mean_value
    variance = jnp.mean(centered * centered, axis=-1, keepdims=True)
    return centered * lax.rsqrt(variance + 1e-05) * gain + bias


def gelu_tanh(value):
    return jax.nn.gelu(value, approximate=True)


def log_sigmoid(value):
    return -(jnp.maximum(-value, 0.0) + jnp.log1p(jnp.exp(-jnp.abs(value))))


def split_heads(tensor):
    return jnp.moveaxis(tensor.reshape(tensor.shape[:-1] + (HEADS, HEAD_DIM)), 2, 0)


def join_heads(tensor):
    moved = jnp.moveaxis(tensor, 0, 2)
    return moved.reshape(moved.shape[:2] + (HEADS * HEAD_DIM,))


def masked_logits(queries, keys, scores, kept, base, causal, key_block):
    logits = jnp.einsum(
        "sqd,skd->sqk", queries, keys, preferred_element_type=jnp.float32
    ) * HEAD_DIM ** (-0.5)
    logits = logits + log_sigmoid(scores.astype(jnp.float32))[:, None, :]
    allowed = base | causal[None] & (key_block[None, None, :] == kept[:, :, None])
    return (logits, allowed)


def attend_head(items, base, causal, key_block):
    queries, keys, values, scores, kept = items
    logits, allowed = masked_logits(queries, keys, scores, kept, base, causal, key_block)
    logits = jnp.where(allowed, logits, -1e30)
    largest = jnp.max(logits, axis=-1, keepdims=True)
    weights = jnp.exp(logits - largest)
    totals = jnp.sum(weights, axis=-1, keepdims=True)
    probs_low = (weights / totals).astype(jnp.bfloat16)
    outputs = jnp.einsum("sqk,skd->sqd", probs_low, values, preferred_element_type=jnp.float32)
    return (outputs, (largest + jnp.log(totals))[..., 0])


def query_side_grads(items, base, causal, key_block):
    queries, keys, values, scores, kept, grad_out, log_totals = items
    logits, allowed = masked_logits(queries, keys, scores, kept, base, causal, key_block)
    probs = jnp.where(allowed, jnp.exp(logits - log_totals[..., None]), 0.0)
    grad_probs = jnp.einsum("sqd,skd->sqk", grad_out, values, preferred_element_type=jnp.float32)
    inner = jnp.sum(probs * grad_probs, axis=-1, keepdims=True)
    grad_logits = (probs * (grad_probs - inner)).astype(jnp.bfloat16)
    grad_queries = jnp.einsum(
        "sqk,skd->sqd", grad_logits, keys, preferred_element_type=jnp.float32
    ) * HEAD_DIM ** (-0.5)
    return (grad_queries, inner[..., 0])


def key_side_grads(items, base, causal, key_block):
    queries, keys, values, scores, kept, grad_out, log_totals, inner = items
    logits, allowed = masked_logits(queries, keys, scores, kept, base, causal, key_block)
    probs = jnp.where(allowed, jnp.exp(logits - log_totals[..., None]), 0.0)
    grad_probs = jnp.einsum("sqd,skd->sqk", grad_out, values, preferred_element_type=jnp.float32)
    grad_logits = (probs * (grad_probs - inner[..., None])).astype(jnp.bfloat16)
    grad_values = jnp.einsum(
        "sqk,sqd->skd", probs.astype(jnp.bfloat16), grad_out, preferred_element_type=jnp.float32
    )
    grad_keys = jnp.einsum(
        "sqk,sqd->skd", grad_logits, queries, preferred_element_type=jnp.float32
    ) * HEAD_DIM ** (-0.5)
    grad_scores = jnp.sum(grad_logits.astype(jnp.float32), axis=1) * jax.nn.sigmoid(
        -scores.astype(jnp.float32)
    )
    return (grad_keys, grad_values, grad_scores)


def build_masks(kept_blocks, picture_starts, query_start, query_len, key_start, key_len):
    query_pos = query_start + jnp.arange(query_len, dtype=jnp.int32)
    key_pos = key_start + jnp.arange(key_len, dtype=jnp.int32)
    causal = key_pos[None, :] <= query_pos[:, None]
    local = causal & (query_pos[:, None] - key_pos[None, :] < WINDOW)
    starts = picture_starts[:, :, None]
    inside_query = (query_pos[None, None, :] >= starts) & (
        query_pos[None, None, :] < starts + PIC_LEN
    )
    inside_key = (key_pos[None, None, :] >= starts) & (key_pos[None, None, :] < starts + PIC_LEN)
    picture = jnp.any(inside_query[:, :, :, None] & inside_key[:, :, None, :], axis=1)
    base = local[None] | picture
    kept_all = jnp.repeat(kept_blocks, BLK, axis=2)
    kept_rows = jnp.moveaxis(lax.dynamic_slice_in_dim(kept_all, query_start, query_len, 2), 1, 0)
    return (base, causal, key_pos // BLK, kept_rows)


def forward_layer(residual, weights, masks):
    qkv_w, score_w, out_w, up_w, down_w, gain, bias = weights
    base, causal, key_block, kept_rows = masks
    gains = gain.astype(jnp.float32)
    biases = bias.astype(jnp.float32)
    hidden = normalize(residual, gains[0], biases[0]).astype(jnp.bfloat16)
    qkv = jnp.dot(hidden, qkv_w, preferred_element_type=jnp.float32).astype(jnp.bfloat16)
    scores = jnp.dot(hidden, score_w, preferred_element_type=jnp.float32).astype(jnp.bfloat16)
    queries, keys, values = jnp.split(qkv, 3, axis=-1)
    all_keys, all_values, all_scores = (
        lax.all_gather(keys, "ctx", axis=1, tiled=True),
        lax.all_gather(values, "ctx", axis=1, tiled=True),
        lax.all_gather(scores, "ctx", axis=1, tiled=True),
    )
    head_items = (
        split_heads(queries),
        split_heads(all_keys),
        split_heads(all_values),
        jnp.moveaxis(all_scores, 2, 0),
        kept_rows,
    )
    heads, log_totals = lax.map(
        partial(attend_head, base=base, causal=causal, key_block=key_block), head_items
    )
    mixed = join_heads(heads).astype(jnp.bfloat16)
    after_attn = residual + jnp.dot(mixed, out_w, preferred_element_type=jnp.float32)
    hidden2 = normalize(after_attn, gains[1], biases[1]).astype(jnp.bfloat16)
    up_part = jnp.dot(hidden2, up_w, preferred_element_type=jnp.float32)
    active = gelu_tanh(up_part).astype(jnp.bfloat16)
    result = after_attn + jnp.dot(active, down_w, preferred_element_type=jnp.float32)
    own_side = (queries, keys, values, scores)
    saved = (
        residual,
        hidden,
        head_items,
        log_totals,
        mixed,
        after_attn,
        hidden2,
        up_part,
        active,
        own_side,
    )
    return (result, saved)


def backward_layer(grad, saved, weights, masks, key_masks):
    qkv_w, score_w, out_w, up_w, down_w, gain, bias = weights
    base, causal, key_block, kept_rows = masks
    (
        residual,
        hidden,
        head_items,
        log_totals,
        mixed,
        after_attn,
        hidden2,
        up_part,
        active,
        own_side,
    ) = saved
    gains = gain.astype(jnp.float32)
    biases = bias.astype(jnp.float32)
    grad_down = grad.astype(jnp.bfloat16)
    grad_active = jnp.einsum("sto,io->sti", grad_down, down_w, preferred_element_type=jnp.float32)
    grad_up = jax.vjp(gelu_tanh, up_part)[1](grad_active)[0].astype(jnp.bfloat16)
    grad_hidden2 = jnp.einsum("stf,df->std", grad_up, up_w, preferred_element_type=jnp.float32)
    late_back = jax.vjp(normalize, after_attn, gains[1], biases[1])[1]
    grad_norm_late, gain_late, bias_late = late_back(grad_hidden2)
    grad_after = grad + grad_norm_late
    grad_attn = grad_after.astype(jnp.bfloat16)
    grad_mixed = jnp.einsum(
        "ste,de->std", grad_attn, out_w, preferred_element_type=jnp.float32
    ).astype(jnp.bfloat16)
    grad_items = head_items + (split_heads(grad_mixed), log_totals)
    grad_queries, inner = lax.map(
        partial(query_side_grads, base=base, causal=causal, key_block=key_block), grad_items
    )
    own_queries, own_keys, own_values, own_scores = own_side
    all_queries, all_grad_mixed = (
        lax.all_gather(own_queries, "ctx", axis=1, tiled=True),
        lax.all_gather(grad_mixed, "ctx", axis=1, tiled=True),
    )
    all_totals, all_inner = (
        lax.all_gather(log_totals, "ctx", axis=2, tiled=True),
        lax.all_gather(inner, "ctx", axis=2, tiled=True),
    )
    key_base, key_causal, key_block_own, kept_all_rows = key_masks
    key_items = (
        split_heads(all_queries),
        split_heads(own_keys),
        split_heads(own_values),
        jnp.moveaxis(own_scores, 2, 0),
        kept_all_rows,
        split_heads(all_grad_mixed),
        all_totals,
        all_inner,
    )
    grad_keys, grad_values, grad_scores = lax.map(
        partial(key_side_grads, base=key_base, causal=key_causal, key_block=key_block_own),
        key_items,
    )
    key_part = join_heads(grad_keys)
    value_part = join_heads(grad_values)
    score_part = jnp.moveaxis(grad_scores, 0, 2)
    grad_qkv = jnp.concatenate([join_heads(grad_queries), key_part, value_part], axis=-1).astype(
        jnp.bfloat16
    )
    grad_score_low = score_part.astype(jnp.bfloat16)
    grad_hidden = jnp.einsum("ste,de->std", grad_qkv, qkv_w, preferred_element_type=jnp.float32)
    grad_hidden = grad_hidden + jnp.einsum(
        "sth,dh->std", grad_score_low, score_w, preferred_element_type=jnp.float32
    )
    early_back = jax.vjp(normalize, residual, gains[0], biases[0])[1]
    grad_norm_early, gain_early, bias_early = early_back(grad_hidden)
    grad_residual = grad_after + grad_norm_early
    inputs = (hidden, mixed, hidden2, active, grad_score_low)
    outputs = (grad_qkv, grad_attn, grad_up, grad_down)
    norms = (jnp.stack([gain_early, gain_late]), jnp.stack([bias_early, bias_late]))
    return (grad_residual, inputs, outputs, norms)


def weight_terms(inputs, outputs, norms):
    all_hidden, all_mixed, all_hidden2, all_active, all_score = (
        lax.all_gather(inputs[0], "ctx", axis=1, tiled=True),
        lax.all_gather(inputs[1], "ctx", axis=1, tiled=True),
        lax.all_gather(inputs[2], "ctx", axis=1, tiled=True),
        lax.all_gather(inputs[3], "ctx", axis=1, tiled=True),
        lax.all_gather(inputs[4], "ctx", axis=1, tiled=True),
    )
    col_qkv, col_attn, col_up, col_down = (
        lax.all_to_all(outputs[0], "ctx", split_axis=2, concat_axis=1, tiled=True),
        lax.all_to_all(outputs[1], "ctx", split_axis=2, concat_axis=1, tiled=True),
        lax.all_to_all(outputs[2], "ctx", split_axis=2, concat_axis=1, tiled=True),
        lax.all_to_all(outputs[3], "ctx", split_axis=2, concat_axis=1, tiled=True),
    )
    gain_total, bias_total = lax.psum((norms[0], norms[1]), "ctx")
    qkv_term = jnp.einsum("std,ste->de", all_hidden, col_qkv, preferred_element_type=jnp.float32)
    score_term = jnp.einsum(
        "std,sth->dh", all_hidden, all_score, preferred_element_type=jnp.float32
    )
    out_term = jnp.einsum("std,ste->de", all_mixed, col_attn, preferred_element_type=jnp.float32)
    up_term = jnp.einsum("std,stf->df", all_hidden2, col_up, preferred_element_type=jnp.float32)
    down_term = jnp.einsum("sti,sto->io", all_active, col_down, preferred_element_type=jnp.float32)
    return (qkv_term, score_term, out_term, up_term, down_term, gain_total, bias_total)


def per_device(
    tokens,
    cotangent,
    kept_blocks,
    picture_starts,
    qkv_weight,
    score_weight,
    out_weight,
    up_weight,
    down_weight,
    norm_gain,
    norm_bias,
):
    local_len = tokens.shape[1]
    whole_len = local_len * lax.axis_size("ctx")
    own_start = lax.axis_index("ctx") * local_len
    masks = build_masks(kept_blocks, picture_starts, own_start, local_len, 0, whole_len)
    key_masks = build_masks(kept_blocks, picture_starts, 0, whole_len, own_start, local_len)
    residual = tokens.astype(jnp.float32)
    kept_weights = []
    saved_all = []
    for layer_index in range(LAYERS):
        rows = (
            lax.all_gather(qkv_weight[layer_index], "fsdp", axis=0, tiled=True),
            lax.all_gather(score_weight[layer_index], "fsdp", axis=0, tiled=True),
            lax.all_gather(out_weight[layer_index], "fsdp", axis=0, tiled=True),
            lax.all_gather(up_weight[layer_index], "fsdp", axis=0, tiled=True),
            lax.all_gather(down_weight[layer_index], "fsdp", axis=0, tiled=True),
            lax.all_gather(norm_gain[layer_index], "fsdp", axis=1, tiled=True),
            lax.all_gather(norm_bias[layer_index], "fsdp", axis=1, tiled=True),
        )
        full_qkv, full_out, full_up, full_down = (
            lax.all_gather(rows[0], "ctx", axis=1, tiled=True),
            lax.all_gather(rows[2], "ctx", axis=1, tiled=True),
            lax.all_gather(rows[3], "ctx", axis=1, tiled=True),
            lax.all_gather(rows[4], "ctx", axis=1, tiled=True),
        )
        weights = (full_qkv, rows[1], full_out, full_up, full_down, rows[5], rows[6])
        kept_weights.append(weights)
        residual, saved = forward_layer(residual, weights, masks)
        saved_all.append(saved)
    grad = cotangent.astype(jnp.float32)
    layer_terms = []
    for layer_index in reversed(range(LAYERS)):
        rows = (
            lax.all_gather(qkv_weight[layer_index], "fsdp", axis=0, tiled=True),
            lax.all_gather(score_weight[layer_index], "fsdp", axis=0, tiled=True),
            lax.all_gather(out_weight[layer_index], "fsdp", axis=0, tiled=True),
            lax.all_gather(up_weight[layer_index], "fsdp", axis=0, tiled=True),
            lax.all_gather(down_weight[layer_index], "fsdp", axis=0, tiled=True),
            lax.all_gather(norm_gain[layer_index], "fsdp", axis=1, tiled=True),
            lax.all_gather(norm_bias[layer_index], "fsdp", axis=1, tiled=True),
        )
        full_qkv, full_out, full_up, full_down = (
            lax.all_gather(rows[0], "ctx", axis=1, tiled=True),
            lax.all_gather(rows[2], "ctx", axis=1, tiled=True),
            lax.all_gather(rows[3], "ctx", axis=1, tiled=True),
            lax.all_gather(rows[4], "ctx", axis=1, tiled=True),
        )
        weights = (full_qkv, rows[1], full_out, full_up, full_down, rows[5], rows[6])
        grad, inputs, outputs, norms = backward_layer(
            grad, saved_all[layer_index], weights, masks, key_masks
        )
        terms = weight_terms(inputs, outputs, norms)
        layer_terms.insert(0, terms)
    stacked = [jnp.stack([entry[number] for entry in layer_terms]) for number in range(7)]
    summed = (
        lax.psum_scatter(
            stacked[0].astype(jnp.bfloat16), "fsdp", scatter_dimension=1, tiled=True
        ).astype(jnp.float32),
        lax.psum_scatter(
            stacked[1].astype(jnp.bfloat16), "fsdp", scatter_dimension=1, tiled=True
        ).astype(jnp.float32),
        lax.psum_scatter(
            stacked[2].astype(jnp.bfloat16), "fsdp", scatter_dimension=1, tiled=True
        ).astype(jnp.float32),
        lax.psum_scatter(
            stacked[3].astype(jnp.bfloat16), "fsdp", scatter_dimension=1, tiled=True
        ).astype(jnp.float32),
        lax.psum_scatter(
            stacked[4].astype(jnp.bfloat16), "fsdp", scatter_dimension=1, tiled=True
        ).astype(jnp.float32),
        lax.psum_scatter(
            stacked[5].astype(jnp.bfloat16), "fsdp", scatter_dimension=2, tiled=True
        ).astype(jnp.float32),
        lax.psum_scatter(
            stacked[6].astype(jnp.bfloat16), "fsdp", scatter_dimension=2, tiled=True
        ).astype(jnp.float32),
    )
    return (
        residual,
        grad,
        summed[0],
        summed[1],
        summed[2],
        summed[3],
        summed[4],
        summed[5],
        summed[6],
    )


def solution(mesh):
    in_specs = (
        P("fsdp", "ctx", None),
        P("fsdp", "ctx", None),
        P("fsdp", None, None),
        P("fsdp", None),
        P(None, "fsdp", "ctx"),
        P(None, "fsdp", None),
        P(None, "fsdp", "ctx"),
        P(None, "fsdp", "ctx"),
        P(None, "fsdp", "ctx"),
        P(None, None, "fsdp"),
        P(None, None, "fsdp"),
    )
    out_specs = (
        P("fsdp", "ctx", None),
        P("fsdp", "ctx", None),
        P(None, "fsdp", "ctx"),
        P(None, "fsdp", None),
        P(None, "fsdp", "ctx"),
        P(None, "fsdp", "ctx"),
        P(None, "fsdp", "ctx"),
        P(None, None, "fsdp"),
        P(None, None, "fsdp"),
    )
    return jax.shard_map(
        per_device, mesh=mesh, in_specs=in_specs, out_specs=out_specs, check_vma=False
    )
```

profile of v0, /device:TPU:0, one launch (start us, length us, event | category | flops | bytes accessed | tf_op | source)
XLA Modules:
  0.0 1856.5 jit_solution(17737955625194765399)
XLA Ops:
  9.0 44.8 %all-gather.83.cloned.1.call-done = bf16[1,768,1152]{2,1,0:T(8,128)(2,1)} async-done(((bf16[1,48,1152]{2,1,0:T(8,128)(2,1)}), bf16[1,768,1152]{2,1,0:T(8,128)(2,1)}) %all-gather.83.cloned.1.call-update) | async-done | bytes 1769488 | tf_op jit(solution)/shard_map/all_gather | solution.py:279
  56.3 20.1 %all-gather = bf16[1,2,768]{1,0,2:T(2,128)(2,1)S(1)} all-gather(bf16[1,2,48]{1,0,2:T(2,128)(2,1)S(1)} %copy.409), channel_id=2, replica_groups=mesh['fsdp'=16,'ctx'=2] {'fsdp'}, dimensions={2}, use_global_device_ids=true | all-gather | bytes 3264 | tf_op jit(solution)/shard_map/all_gather | solution.py:284
  77.0 18.5 all-gather.1
  113.1 22.8 %all-gather.6 = bf16[1,768,384]{2,1,0:T(8,128)(2,1)} all-gather(bf16[1,48,384]{2,1,0:T(8,128)(2,1)S(1)} %get-tuple-element.1310), channel_id=8, replica_groups=mesh['fsdp'=16,'ctx'=2] {'fsdp'}, dimensions={1}, use_global_device_ids=true | all-gather | bytes 626688 | tf_op jit(solution)/shard_map/all_gather | solution.py:281
  136.0 13.9 all-gather.89.cloned.1.call-done
  149.9 43.8 %all-gather.93.cloned.1.call-done = bf16[1,3072,384]{2,1,0:T(8,128)(2,1)} async-done(((bf16[1,192,384]{2,1,0:T(8,128)(2,1)}), bf16[1,3072,384]{2,1,0:T(8,128)(2,1)}) %all-gather.93.cloned.1.call-update) | async-done | bytes 2359312 | tf_op jit(solution)/shard_map/all_gather | solution.py:283
  193.8 41.7 %all-gather.97.cloned.1.call-done = bf16[1,768,1152]{2,1,0:T(8,128)(2,1)} async-done(((bf16[1,48,1152]{2,1,0:T(8,128)(2,1)}), bf16[1,768,1152]{2,1,0:T(8,128)(2,1)}) %all-gather.97.cloned.1.call-update) | async-done | bytes 1769488 | tf_op jit(solution)/shard_map/all_gather | solution.py:279
  238.3 20.2 %all-gather.4 = bf16[1,768,12]{2,0,1:T(2,128)(2,1)S(1)} all-gather(bf16[1,48,12]{2,0,1:T(2,128)(2,1)S(1)} %copy.411), channel_id=6, replica_groups=mesh['fsdp'=16,'ctx'=2] {'fsdp'}, dimensions={1}, use_global_device_ids=true | all-gather | bytes 19584 | tf_op jit(solution)/shard_map/all_gather | solution.py:280
  264.0 18.5 all-gather.12
  287.6 19.9 %all-gather.13 = bf16[1,2,768]{1,0,2:T(2,128)(2,1)S(1)} all-gather(bf16[1,2,48]{1,0,2:T(2,128)(2,1)S(1)} %copy.413), channel_id=15, replica_groups=mesh['fsdp'=16,'ctx'=2] {'fsdp'}, dimensions={2}, use_global_device_ids=true | all-gather | bytes 3264 | tf_op jit(solution)/shard_map/all_gather | solution.py:285
  323.6 51.2 %while.82 = (s32[]{:T(128)}, bf16[12,1,512,64]{2,3,1,0:T(8,128)(2,1)S(1)}, f32[12,1,512]{2,1,0:T(1,128)S(1)}, pred[1,512,1024]{2,1,0:T(32,128)(4,1)S(1)}, s32[12...) while((s32[]{:T(128)}, ...), condition=%wide.region_6.7_spmd.clone, body=%wide.region_3.6_spmd.clone.sunk | while | flops 141048320 | bytes 7651449 | solution.py:130
  380.5 8.5 multiply_convert_fusion.7
  389.0 55.6 %all-gather.95.cloned.1.call-done = bf16[1,3072,768]{2,1,0:T(8,128)(2,1)} async-done(((bf16[1,3072,384]{2,1,0:T(8,128)(2,1)}), bf16[1,3072,768]{2,1,0:T(8,128)(2,1)}) %all-gather.95.cloned.1.call-update) | async-done | bytes 4718608 | tf_op jit(solution)/shard_map/all_gather | solution.py:291
  444.6 6.0 fusion.322
  451.2 44.3 %all-gather.99.cloned.1.call-done = bf16[1,768,2304]{2,1,0:T(8,128)(2,1)} async-done(((bf16[1,768,1152]{2,1,0:T(8,128)(2,1)}), bf16[1,768,2304]{2,1,0:T(8,128)(2,1)}) %all-gather.99.cloned.1.call-update) | async-done | bytes 3538960 | tf_op jit(solution)/shard_map/all_gather | solution.py:288
  501.5 25.2 %all-gather.18 = bf16[1,768,384]{2,1,0:T(8,128)(2,1)} all-gather(bf16[1,48,384]{2,1,0:T(8,128)(2,1)S(1)} %get-tuple-element.1309), channel_id=20, replica_groups=mesh['fsdp'=16,'ctx'=2] {'fsdp'}, dimensions={1}, use_global_device_ids=true | all-gather | bytes 626688 | tf_op jit(solution)/shard_map/all_gather | solution.py:281
  526.8 14.9 all-gather.103.cloned.1.call-done
  541.7 43.9 %all-gather.107.cloned.1.call-done = bf16[1,3072,384]{2,1,0:T(8,128)(2,1)} async-done(((bf16[1,192,384]{2,1,0:T(8,128)(2,1)}), bf16[1,3072,384]{2,1,0:T(8,128)(2,1)}) %all-gather.107.cloned.1.call-update) | async-done | bytes 2359312 | tf_op jit(solution)/shard_map/all_gather | solution.py:283
  586.4 20.5 %all-gather.16 = bf16[1,768,12]{2,0,1:T(2,128)(2,1)S(1)} all-gather(bf16[1,48,12]{2,0,1:T(2,128)(2,1)} %copy.414), channel_id=18, replica_groups=mesh['fsdp'=16,'ctx'=2] {'fsdp'}, dimensions={1}, use_global_device_ids=true | all-gather | bytes 19584 | tf_op jit(solution)/shard_map/all_gather | solution.py:280
  621.2 20.9 %all-gather.65.cloned.1.call-done = bf16[1,1024,768]{2,1,0:T(8,128)(2,1)} async-done(((bf16[1,512,768]{2,1,0:T(8,128)(2,1)}), bf16[1,1024,768]{2,1,0:T(8,128)(2,1)}) %all-gather.65.cloned.1.call-update) | async-done | bytes 1572880 | tf_op jit(solution)/shard_map/all_gather | solution.py:120
  646.7 61.0 %while.83 = (s32[]{:T(128)}, bf16[12,1,512,64]{2,3,1,0:T(8,128)(2,1)S(1)}, f32[12,1,512]{2,1,0:T(1,128)S(1)}, pred[1,512,1024]{2,1,0:T(32,128)(4,1)}, s32[12,1,5...) while((s32[]{:T(128)}, ...), condition=%wide.region_14.15_spmd.clone, body=%wide.region_11.14_spmd.clone.sunk | while | flops 141048320 | bytes 7651449 | solution.py:130
  711.7 18.7 %all-gather.105.cloned.1.call-done = bf16[1,768,3072]{2,1,0:T(8,128)(2,1)} async-done(((bf16[1,768,1536]{2,1,0:T(8,128)(2,1)}), bf16[1,768,3072]{2,1,0:T(8,128)(2,1)}) %all-gather.105.cloned.1.call-update) | async-done | bytes 4718608 | tf_op jit(solution)/shard_map/all_gather | solution.py:290
  730.4 8.5 multiply_convert_fusion.6
  738.9 55.6 %all-gather.109.cloned.1.call-done = bf16[1,3072,768]{2,1,0:T(8,128)(2,1)} async-done(((bf16[1,3072,384]{2,1,0:T(8,128)(2,1)}), bf16[1,3072,768]{2,1,0:T(8,128)(2,1)}) %all-gather.109.cloned.1.call-update) | async-done | bytes 4718608 | tf_op jit(solution)/shard_map/all_gather | solution.py:291
  794.5 8.9 fusion.167
  823.7 73.0 %while.84 = (s32[]{:T(128)}, bf16[12,1,512,64]{2,3,1,0:T(8,128)(2,1)S(1)}, f32[12,1,512]{2,1,0:T(1,128)S(1)}, pred[1,512,1024]{2,1,0:T(32,128)(4,1)S(1)}, s32[12...) while((s32[]{:T(128)}, ...), condition=%wide.region_21.22_spmd.clone, body=%wide.region_19.21_spmd.clone.sunk | while | flops 208189952 | bytes 12168333 | solution.py:184
  896.7 5.0 all_gather.189
  908.1 98.1 %while.85 = (s32[]{:T(128)}, bf16[12,1,512,64]{2,3,1,0:T(8,128)(2,1)S(1)}, bf16[12,1,512,64]{2,3,1,0:T(8,128)(2,1)}, bf16[12,1,512]{2,0,1:T(8,128)(2,1)S(1)}, pr...) while((s32[]{:T(128)}, ...), condition=%wide.region_25.26_spmd.clone, body=%wide.region_23.25_spmd.clone.sunk | while | flops 275822080 | bytes 9890997 | solution.py:207
  1006.2 5.0 fusion.188
  1014.2 10.2 fusion.160
  1039.1 6.3 reduce.64
  1057.4 11.1 all_gather.191
  1079.9 89.5 %while.86 = (s32[]{:T(128)}, bf16[12,1,512,64]{2,3,1,0:T(8,128)(2,1)}, f32[12,1,512]{2,1,0:T(1,128)S(1)}, pred[1,512,1024]{2,1,0:T(32,128)(4,1)}, s32[12,1,512]{...) while((s32[]{:T(128)}, ...), condition=%wide.region_32.33_spmd.clone, body=%wide.region_30.32_spmd.clone.sunk | while | flops 208189952 | bytes 14265513 | solution.py:184
  1176.1 5.4 reduce.65
  1187.2 20.6 %all_gather.197 = bf16[1,1024,12]{1,2,0:T(8,128)(2,1)S(1)} all-gather(bf16[1,512,12]{1,2,0:T(8,128)(2,1)S(1)} %bitcast.890), channel_id=1, replica_groups=mesh['fsdp'=16,'ctx'=2] {'ctx'}, dimensions={1}, use_global_device_ids=true | all-gather | bytes 36864 | tf_op jit(solution)/shard_map/all_gather | solution.py:237
  1207.9 21.0 %copy.442 = bf16[1,512,2304]{1,0,2:T(2,128)(2,1)} copy(bf16[1,512,2304]{1,2,0:T(8,128)(2,1)S(1)} %pad_maximum_fusion.4) | data formatting | bytes 4718592 | tf_op jit(solution)/shard_map/concatenate | solution.py:214
  1228.9 15.6 reduce.62
  1253.1 5.1 all-to-all-start.1
  1267.7 106.8 %while.87 = (s32[]{:T(128)}, bf16[12,1,512,64]{2,3,1,0:T(8,128)(2,1)S(1)}, bf16[12,1,512,64]{2,3,1,0:T(8,128)(2,1)}, bf16[12,1,512]{2,0,1:T(8,128)(2,1)S(1)}, pr...) while((s32[]{:T(128)}, ...), condition=%wide.region_35.36_spmd.clone, body=%wide.region_33.35_spmd.clone.sunk | while | flops 275822080 | bytes 9890997 | solution.py:207
  1381.7 8.8 all-reduce
  1396.7 20.7 %copy.443 = bf16[1,512,2304]{1,0,2:T(2,128)(2,1)} copy(bf16[1,512,2304]{1,2,0:T(8,128)(2,1)S(1)} %pad_maximum_fusion.3) | data formatting | bytes 4718592 | tf_op jit(solution)/shard_map/concatenate | solution.py:214
  1417.4 15.6 reduce.63
  1464.9 5.6 fusion.197
  1486.2 14.0 copy.372
  1500.1 21.9 %reduce.66 = bf16[3072,512]{1,0:T(8,128)(2,1)} reduce(bf16[3072,1,512]{2,1,0:T(2,128)(2,1)} %bitcast.809, bf16[]{:T(256)} %broadcast.841), dimensions={1}, to_apply=%bitcast.586.reduce_sub_computation | reduce | bytes 6291458
  1522.0 5.2 reshape.1725
  1527.2 5.2 all-to-all-start.5
  1532.4 14.0 copy.370
  1546.4 21.9 %reduce.67 = bf16[3072,512]{1,0:T(8,128)(2,1)} reduce(bf16[3072,1,512]{2,1,0:T(2,128)(2,1)} %bitcast.810, bf16[]{:T(256)} %broadcast.841), dimensions={1}, to_apply=%bitcast.588.reduce_sub_computation | reduce | bytes 6291458
  1573.1 5.2 all-to-all-start.4
  1578.4 5.7 reshape.1726
  1584.1 5.4 copy.406
  1594.1 5.0 fusion.195
  1599.1 10.4 all-to-all-done.4
  1609.5 5.7 reshape.1728
  1615.2 5.4 copy.405
  1625.2 5.1 fusion.194
  1635.5 5.4 reduce.68
  1648.0 5.4 reduce.69
  1668.3 6.5 fusion.186
  1674.9 6.6 fusion.187
  1685.7 7.2 bitcast_add_fusion
  1702.6 66.7 %reduce-scatter.18.cloned.1.call-done = bf16[2,48,1536]{2,1,0:T(8,128)(2,1)} async-done(((bf16[2,768,1536]{2,1,0:T(8,128)(2,1)}), bf16[2,48,1536]{2,1,0:T(8,128)(2,1)}) %reduce-scatter.18.cloned.1.call-update) | async-done | bytes 294928 | tf_op jit(solution)/shard_map/reduce_scatter | solution.py:332
  1771.1 76.5 %reduce-scatter.20.cloned.1.call-done = bf16[2,192,384]{2,1,0:T(8,128)(2,1)} async-done(((bf16[2,3072,384]{2,1,0:T(8,128)(2,1)}), bf16[2,192,384]{2,1,0:T(8,128)(2,1)}) %reduce-scatter.20.cloned.1.call-update) | async-done | bytes 294928 | tf_op jit(solution)/shard_map/reduce_scatter | solution.py:335
  (1188 shorter events, 781.0 us)
Async XLA Ops:
  7.2 46.8 %copy-start.56 = (bf16[2,48,1536]{2,1,0:T(8,128)(2,1)S(1)}, bf16[2,48,1536]{2,1,0:T(8,128)(2,1)}, u32[]{:S(2)}) copy-start(bf16[2,48,1536]{2,1,0:T(8,128)(2,1)} %param.30) | copy-start | bytes 884740
  7.2 47.6 %copy-start.57 = (bf16[2,192,384]{2,1,0:T(8,128)(2,1)S(1)}, bf16[2,192,384]{2,1,0:T(8,128)(2,1)}, u32[]{:S(2)}) copy-start(bf16[2,192,384]{2,1,0:T(8,128)(2,1)} %param.31) | copy-start | bytes 884740
  7.2 49.0 %copy-start.106 = (bf16[2,2,48]{2,1,0:T(2,128)(2,1)S(1)}, bf16[2,2,48]{2,1,0:T(2,128)(2,1)}, u32[]{:S(2)}) copy-start(bf16[2,2,48]{2,1,0:T(2,128)(2,1)} %param.32) | copy-start | bytes 1156
  7.2 46.7 %all-gather.83.cloned.1.call-start = ((), (), s32[]{:S(2)}) async-start(), calls=%async_computation.31 | async-start | bytes 1880064 | tf_op jit(solution)/shard_map/all_gather | solution.py:279
  9.0 97.6 %all-gather.85.cloned.1.call-start = ((), (), s32[]{:S(2)}) async-start(), calls=%async_computation.32 | async-start | bytes 5308416 | tf_op jit(solution)/shard_map/all_gather | solution.py:288
  53.9 42.0 %copy-start.2 = (bf16[1,512,768]{2,1,0:T(8,128)(2,1)S(1)}, bf16[1,512,768]{2,1,0:T(8,128)(2,1)}, u32[]{:S(2)}) copy-start(bf16[1,512,768]{2,1,0:T(8,128)(2,1)} %param.23) | copy-start | bytes 2359300
  53.9 95.9 %all-gather.89.cloned.1.call-start = ((), (), s32[]{:S(2)}) async-start(), calls=%async_computation.34 | async-start | bytes 2506752 | tf_op jit(solution)/shard_map/all_gather | solution.py:282
  54.7 139.0 %all-gather.93.cloned.1.call-start = ((), (), s32[]{:S(2)}) async-start(), calls=%async_computation.36 | async-start | bytes 2506752 | tf_op jit(solution)/shard_map/all_gather | solution.py:283
  55.5 179.9 %all-gather.97.cloned.1.call-start = ((), (), s32[]{:S(2)}) async-start(), calls=%async_computation.38 | async-start | bytes 1880064 | tf_op jit(solution)/shard_map/all_gather | solution.py:279
  56.1 258.4 %all-gather.59.cloned.1.call-start = ((), (), s32[]{:S(2)}) async-start(), calls=%async_computation.15 | async-start | bytes 2359296 | tf_op jit(solution)/shard_map/all_gather | solution.py:119
  106.5 152.3 %copy-start.16 = (bf16[1,512,768]{2,1,0:T(8,128)(2,1)}, bf16[1,512,768]{2,1,0:T(8,128)(2,1)S(1)}, u32[]{:S(2)}) copy-start(bf16[1,512,768]{2,1,0:T(8,128)(2,1)S(1)} %fusion.223) | copy-start | bytes 2359300
  112.2 200.3 %copy-start.18 = (bf16[1,512,768]{2,1,0:T(8,128)(2,1)}, bf16[1,512,768]{2,1,0:T(8,128)(2,1)S(1)}, u32[]{:S(2)}) copy-start(bf16[1,512,768]{2,1,0:T(8,128)(2,1)S(1)} %get-tuple-element.1302) | copy-start | bytes 2359300
  112.2 206.8 %all-gather.61.cloned.1.call-start = ((), (), s32[]{:S(2)}) async-start(), calls=%async_computation.16 | async-start | bytes 2359296 | tf_op jit(solution)/shard_map/all_gather | solution.py:120
  113.0 262.0 %all-gather.87.cloned.1.call-start = ((), (), s32[]{:S(2)}) async-start(), calls=%async_computation.33 | async-start | bytes 1769472 | tf_op jit(solution)/shard_map/all_gather | solution.py:289
  135.9 244.6 %all-gather.91.cloned.1.call-start = ((), (), s32[]{:S(2)}) async-start(), calls=%async_computation.35 | async-start | bytes 7077888 | tf_op jit(solution)/shard_map/all_gather | solution.py:290
  149.9 294.7 %all-gather.95.cloned.1.call-start = ((), (), s32[]{:S(2)}) async-start(), calls=%async_computation.37 | async-start | bytes 7077888 | tf_op jit(solution)/shard_map/all_gather | solution.py:291
  193.7 43.2 %copy-start.105 = (s32[1,2]{1,0:T(1,128)S(1)}, s32[1,2]{1,0:T(1,128)}, u32[]{:S(2)}) copy-start(s32[1,2]{1,0:T(1,128)} %param.26) | copy-start | bytes 28
  193.7 44.5 %copy-start.84 = (bf16[2,48,12]{1,0,2:T(2,128)(2,1)S(1)}, bf16[2,48,12]{1,0,2:T(2,128)(2,1)}, u32[]{:S(2)}) copy-start(bf16[2,48,12]{1,0,2:T(2,128)(2,1)} %param.28) | copy-start | bytes 6916
  193.7 301.8 %all-gather.99.cloned.1.call-start = ((), (), s32[]{:S(2)}) async-start(), calls=%async_computation.39 | async-start | bytes 5308416 | tf_op jit(solution)/shard_map/all_gather | solution.py:288
  235.5 28.2 %copy-start.103 = (s32[1,12,8]{1,2,0:T(8,128)S(1)}, s32[1,12,8]{1,2,0:T(8,128)}, u32[]{:S(2)}) copy-start(s32[1,12,8]{1,2,0:T(8,128)} %param.25) | copy-start | bytes 1156
  235.5 306.2 %all-gather.103.cloned.1.call-start = ((), (), s32[]{:S(2)}) async-start(), calls=%async_computation.41 | async-start | bytes 2506752 | tf_op jit(solution)/shard_map/all_gather | solution.py:282
  236.1 349.6 %all-gather.107.cloned.1.call-start = ((), (), s32[]{:S(2)}) async-start(), calls=%async_computation.43 | async-start | bytes 2506752 | tf_op jit(solution)/shard_map/all_gather | solution.py:283
  236.8 379.9 %all-gather.63.cloned.1.call-start = ((), (), s32[]{:S(2)}) async-start(), calls=%async_computation.17 | async-start | bytes 2359296 | tf_op jit(solution)/shard_map/all_gather | solution.py:119
  258.9 49.1 %copy-start.58 = (bf16[1,768,12]{1,2,0:T(8,128)(2,1)}, bf16[1,768,12]{1,2,0:T(8,128)(2,1)S(1)}, u32[]{:S(2)}) copy-start(bf16[1,768,12]{1,2,0:T(8,128)(2,1)S(1)} %copy.307) | copy-start | bytes 55300
  263.8 48.7 %copy-start.55 = (s32[12,8,128]{2,1,0:T(8,128)}, s32[12,8,128]{2,1,0:T(8,128)S(1)}, u32[]{:S(2)}) copy-start(s32[12,8,128]{2,1,0:T(8,128)S(1)} %broadcast_in_dim.102) | copy-start | bytes 147460
  377.9 66.7 %copy-start.12 = (f32[1,512,768]{2,1,0:T(8,128)}, f32[1,512,768]{2,1,0:T(8,128)S(1)}, u32[]{:S(2)}) copy-start(f32[1,512,768]{2,1,0:T(8,128)S(1)} %get-tuple-element.1318) | copy-start | bytes 4718596
  450.5 258.0 %copy-start = (f32[1,512,768]{2,1,0:T(8,128)}, f32[1,512,768]{2,1,0:T(8,128)S(1)}, u32[]{:S(2)}) copy-start(f32[1,512,768]{2,1,0:T(8,128)S(1)} %get-tuple-element.1322) | copy-start | bytes 4718596
  450.9 48.7 %copy-start.95 = (f32[512]{0:T(512)}, f32[512]{0:T(512)S(1)}, u32[]{:S(2)}) copy-start(f32[512]{0:T(512)S(1)} %multiply_reduce_fusion.3) | copy-start | bytes 6148
  450.9 48.7 %copy-start.78 = (f32[512]{0:T(512)}, f32[512]{0:T(512)S(1)}, u32[]{:S(2)}) copy-start(f32[512]{0:T(512)S(1)} %fusion.301) | copy-start | bytes 6148
  451.2 160.7 %copy-start.24 = (bf16[1,512,768]{2,1,0:T(8,128)(2,1)}, bf16[1,512,768]{2,1,0:T(8,128)(2,1)S(1)}, u32[]{:S(2)}) copy-start(bf16[1,512,768]{2,1,0:T(8,128)(2,1)S(1)} %add_convert_fusion.1) | copy-start | bytes 2359300
  500.9 107.3 %copy-start.20 = (bf16[1,512,768]{2,1,0:T(8,128)(2,1)}, bf16[1,512,768]{2,1,0:T(8,128)(2,1)S(1)}, u32[]{:S(2)}) copy-start(bf16[1,512,768]{2,1,0:T(8,128)(2,1)S(1)} %get-tuple-element.1299) | copy-start | bytes 2359300
  500.9 141.2 %all-gather.65.cloned.1.call-start = ((), (), s32[]{:S(2)}) async-start(), calls=%async_computation.18 | async-start | bytes 2359296 | tf_op jit(solution)/shard_map/all_gather | solution.py:120
  501.5 206.2 %all-gather.101.cloned.1.call-start = ((), (), s32[]{:S(2)}) async-start(), calls=%async_computation.40 | async-start | bytes 1769472 | tf_op jit(solution)/shard_map/all_gather | solution.py:289
  526.8 203.6 %all-gather.105.cloned.1.call-start = ((), (), s32[]{:S(2)}) async-start(), calls=%async_computation.42 | async-start | bytes 7077888 | tf_op jit(solution)/shard_map/all_gather | solution.py:290
  541.7 252.8 %all-gather.109.cloned.1.call-start = ((), (), s32[]{:S(2)}) async-start(), calls=%async_computation.44 | async-start | bytes 7077888 | tf_op jit(solution)/shard_map/all_gather | solution.py:291
  585.7 316.0 %all-gather.67.cloned.1.call-start = ((), (), s32[]{:S(2)}) async-start(), calls=%async_computation.19 | async-start | bytes 2359296 | tf_op jit(solution)/shard_map/all_gather | solution.py:189
  616.6 287.8 %all-gather.111.cloned.1.call-start = ((), (), s32[]{:S(2)}) async-start(), calls=%async_computation.45 | async-start | bytes 2359296 | tf_op jit(solution)/shard_map/all_gather | solution.py:190
  711.0 95.8 %copy-start.4 = (f32[1,512,768]{2,1,0:T(8,128)}, f32[1,512,768]{2,1,0:T(8,128)S(1)}, u32[]{:S(2)}) copy-start(f32[1,512,768]{2,1,0:T(8,128)S(1)} %get-tuple-element.1324) | copy-start | bytes 4718596
  711.7 82.8 %copy-start.25 = (bf16[1,512,768]{2,1,0:T(8,128)(2,1)S(1)}, bf16[1,512,768]{2,1,0:T(8,128)(2,1)}, u32[]{:S(2)}) copy-start(bf16[1,512,768]{2,1,0:T(8,128)(2,1)} %param.24) | copy-start | bytes 2359300
  812.2 242.5 %all-gather.69.cloned.1.call-start = ((), (), s32[]{:S(2)}) async-start(), calls=%async_computation.20 | async-start | bytes 2359296 | tf_op jit(solution)/shard_map/all_gather | solution.py:189
  812.9 434.4 %all-gather.73.cloned.1.call-start = ((), (), s32[]{:S(2)}) async-start(), calls=%async_computation.22 | async-start | bytes 2359296 | tf_op jit(solution)/shard_map/all_gather | solution.py:233
  813.7 436.0 %all-gather.77.cloned.1.call-start = ((), (), s32[]{:S(2)}) async-start(), calls=%async_computation.25 | async-start | bytes 2359296 | tf_op jit(solution)/shard_map/all_gather | solution.py:234
  814.4 446.4 %all-gather.75.cloned.1.call-start = ((), (), s32[]{:S(2)}) async-start(), calls=%async_computation.24 | async-start | bytes 2359296 | tf_op jit(solution)/shard_map/all_gather | solution.py:234
  816.1 448.0 %all-gather.113.cloned.1.call-start = ((), (), s32[]{:S(2)}) async-start(), calls=%async_computation.46 | async-start | bytes 2359296 | tf_op jit(solution)/shard_map/all_gather | solution.py:190
  1032.4 411.9 %all-gather.71.cloned.1.call-start = ((), (), s32[]{:S(2)}) async-start(), calls=%async_computation.21 | async-start | bytes 2359296 | tf_op jit(solution)/shard_map/all_gather | solution.py:233
  1033.0 561.1 %all-gather.81.cloned.1.call-start = ((), (), s32[]{:S(2)}) async-start(), calls=%async_computation.28 | async-start | bytes 2359296 | tf_op jit(solution)/shard_map/all_gather | solution.py:235
  1033.6 591.7 %all-gather.79.cloned.1.call-start = ((), (), s32[]{:S(2)}) async-start(), calls=%async_computation.27 | async-start | bytes 2359296 | tf_op jit(solution)/shard_map/all_gather | solution.py:235
  1034.3 634.0 %all-gather.115.cloned.1.call-start = ((), (), s32[]{:S(2)}) async-start(), calls=%async_computation.47 | async-start | bytes 9437184 | tf_op jit(solution)/shard_map/all_gather | solution.py:236
  1047.9 20.8 %all-to-all-start.3 = ((bf16[2,2,98304]{2,1,0:T(2,128)(2,1)}), bf16[2,2,98304]{2,1,0:T(2,128)(2,1)}, u32[]{:S(2)}, u32[]{:S(2)}) async-start(bf16[2,2,98304]{2,1,0:T(2,128)(2,1)} %reshape.1721), calls=%async_computation.4 | async-start | bytes 1572864 | tf_op jit(solution)/shard_map/all_to_all | solution.py:241
  1052.2 622.7 %all-gather.117.cloned.1.call-start = ((), (), s32[]{:S(2)}) async-start(), calls=%async_computation.48 | async-start | bytes 9437184 | tf_op jit(solution)/shard_map/all_gather | solution.py:236
  1182.9 70.2 %all-to-all-start.2 = ((bf16[2,2,98304]{2,1,0:T(2,128)(2,1)}), bf16[2,2,98304]{2,1,0:T(2,128)(2,1)}, u32[]{:S(2)}, u32[]{:S(2)}) async-start(bf16[2,2,98304]{2,1,0:T(2,128)(2,1)} %reshape.1723), calls=%async_computation.3 | async-start | bytes 1572864 | tf_op jit(solution)/shard_map/all_to_all | solution.py:241
  1253.1 187.1 %all-to-all-start.1 = ((bf16[2,2,294912]{2,1,0:T(2,128)(2,1)}), bf16[2,2,294912]{2,1,0:T(2,128)(2,1)}, u32[]{:S(2)}, u32[]{:S(2)}) async-start(bf16[2,2,294912]{2,1,0:T(2,128)(2,1)} %reshape.1717), calls=%async_computation.1 | async-start | bytes 4718592 | tf_op jit(solution)/shard_map/all_to_all | solution.py:240
  1258.2 436.6 %reduce-scatter.26.cloned.1.call-start = ((), (), s32[]{:S(2)}) async-start(), calls=%async_computation.51 | async-start | bytes 208896
  1391.9 304.4 %reduce-scatter.24.cloned.1.call-start = ((), (), s32[]{:S(2)}) async-start(), calls=%async_computation.50 | async-start | bytes 208896
  1440.3 30.3 %all-to-all-start = ((bf16[2,2,294912]{2,1,0:T(2,128)(2,1)}), bf16[2,2,294912]{2,1,0:T(2,128)(2,1)S(1)}, u32[]{:S(2)}, u32[]{:S(2)}) async-start(bf16[2,2,294912]{2,1,0:T(2,128)(2,1)} %reshape.1719), calls=%async_computation | async-start | bytes 4718592 | tf_op jit(solution)/shard_map/all_to_all | solution.py:240
  1444.2 253.5 %reduce-scatter.22.cloned.1.call-start = ((), (), s32[]{:S(2)}) async-start(), calls=%async_computation.49 | async-start | bytes 208896
  1448.7 250.6 %reduce-scatter.16.cloned.1.call-start = ((), (), s32[]{:S(2)}) async-start(), calls=%async_computation.26 | async-start | bytes 1253376 | tf_op jit(solution)/shard_map/reduce_scatter | solution.py:329
  1451.2 249.7 %reduce-scatter.14.cloned.1.call-start = ((), (), s32[]{:S(2)}) async-start(), calls=%async_computation.23 | async-start | bytes 3760128 | tf_op jit(solution)/shard_map/reduce_scatter | solution.py:323
  1527.2 45.8 %all-to-all-start.5 = ((bf16[2,2,393216]{2,1,0:T(2,128)(2,1)}), bf16[2,2,393216]{2,1,0:T(2,128)(2,1)}, u32[]{:S(2)}, u32[]{:S(2)}) async-start(bf16[2,2,393216]{2,1,0:T(2,128)(2,1)} %reshape.1725), calls=%async_computation.7 | async-start | bytes 6291456 | tf_op jit(solution)/shard_map/all_to_all | solution.py:242
  1573.1 36.4 %all-to-all-start.4 = ((bf16[2,2,393216]{2,1,0:T(2,128)(2,1)}), bf16[2,2,393216]{2,1,0:T(2,128)(2,1)}, u32[]{:S(2)}, u32[]{:S(2)}) async-start(bf16[2,2,393216]{2,1,0:T(2,128)(2,1)} %reshape.1727), calls=%async_computation.6 | async-start | bytes 6291456 | tf_op jit(solution)/shard_map/all_to_all | solution.py:242
  1578.3 190.9 %reduce-scatter.18.cloned.1.call-start = ((), (), s32[]{:S(2)}) async-start(), calls=%async_computation.29 | async-start | bytes 5013504 | tf_op jit(solution)/shard_map/reduce_scatter | solution.py:332
  1642.3 12.4 all-to-all-start.7
  1654.8 11.5 all-to-all-start.6
  1658.3 189.3 %reduce-scatter.20.cloned.1.call-start = ((), (), s32[]{:S(2)}) async-start(), calls=%async_computation.30 | async-start | bytes 5013504 | tf_op jit(solution)/shard_map/reduce_scatter | solution.py:335
  (104 other events, 613.3 us)
Sparse Core Ops, SparseCore 0:
  10.8 43.0 all-gather.82
  55.4 48.0 all-gather.84
  106.3 43.4 all-gather.88
  152.5 41.0 all-gather.92
  196.3 39.1 all-gather.96
  236.8 25.8 all-gather.58
  264.3 27.5 all-gather.60
  293.4 22.7 all-gather.86
  317.8 62.6 all-gather.90
  381.9 62.6 all-gather.94
  446.1 49.3 all-gather.98
  498.2 43.3 all-gather.102
  544.5 41.0 all-gather.106
  587.0 25.9 all-gather.62
  614.5 27.5 all-gather.64
  643.5 22.7 all-gather.100
  667.7 62.6 all-gather.104
  731.8 62.6 all-gather.108
  796.0 27.7 all-gather.66
  825.2 27.1 all-gather.110
  854.0 27.1 all-gather.68
  882.7 27.7 all-gather.72
  912.1 27.2 all-gather.76
  940.8 27.1 all-gather.74
  1032.5 32.7 all-gather.112
  1066.7 27.5 all-gather.70
  1095.7 27.2 all-gather.80
  1124.5 27.2 all-gather.78
  1153.3 89.6 all-gather.114
  1244.4 105.6 all-gather.116
  1392.0 53.6 reduce-scatter.25
  1449.2 52.6 reduce-scatter.23
  1505.8 52.6 reduce-scatter.21
  1562.2 56.3 reduce-scatter.15
  1622.9 67.6 reduce-scatter.13
  1694.8 74.4 reduce-scatter.17
  1773.0 74.5 reduce-scatter.19
where the time goes:
time: 1880 us; the launch traced here: 1860 us
  waiting for transfers between devices  564 us (30%)
  matrix products  514 us (27%)
  local copies, waits for them, and re-layouts  313 us (17%)
  blocking collectives  234 us (12%)
  other arithmetic  174 us (9%)
  starting transfers between devices  37.4 us (2%)
    dot_general x72, matrix products, masked_logits(): jnp.einsum('sqd,skd->sqk', queries, keys, preferred_element_type=jnp.floa...  162 us
    all_gather x2, waiting for transfers between devices, per_device(): lax.all_gather(rows[4], 'ctx', axis=1, tiled=True)  111 us
    unnamed x277, local copies, waits for them, and re-layouts  108 us
    unnamed x9, other arithmetic  97.5 us
    all_gather x2, waiting for transfers between devices, per_device(): lax.all_gather(down_weight[layer_index], 'fsdp', axis=0, tiled=True)  87.7 us
    all_gather x2, waiting for transfers between devices, per_device(): lax.all_gather(qkv_weight[layer_index], 'fsdp', axis=0, tiled=True)  86.5 us
    reduce_scatter x1, waiting for transfers between devices, per_device(): lax.psum_scatter(stacked[4].astype(jnp.bfloat16), 'fsdp', scatter_dimensi...  76.5 us
    reduce_scatter x1, waiting for transfers between devices, per_device(): lax.psum_scatter(stacked[3].astype(jnp.bfloat16), 'fsdp', scatter_dimensi...  66.7 us
  transfers between devices with their start and end apart: 45, of which 16 were waited for; matrix products, arithmetic and copies ran while one was open for 53% of the time, Pallas kernels for 0%

commit v1 on v0

--- a/solution.py
+++ b/solution.py
@@ -1,8 +1,11 @@
+import math
 from functools import partial
 
 import jax
 import jax.numpy as jnp
 from jax import lax
+from jax.experimental import pallas as pl
+from jax.experimental.pallas import tpu as pltpu
 from jax.sharding import PartitionSpec as P
 
 HEADS = 12
@@ -355,6 +358,962 @@
     )
 
 
+D = 768
+FF = 3072
+HALF = 384
+TOK = 512
+SEQ = 1024
+ROWS = 48
+DROWS = 192
+NEG = -1e30
+F32 = jnp.float32
+BF16 = jnp.bfloat16
+VM = pl.BlockSpec(memory_space=pltpu.VMEM)
+HB = pl.BlockSpec(memory_space=pl.ANY)
+SM = pl.BlockSpec(memory_space=pltpu.SMEM)
+
+
+def nn(a, b):
+    return lax.dot_general(a, b, (((1,), (0,)), ((), ())), preferred_element_type=F32)
+
+
+def nt(a, b):
+    return lax.dot_general(a, b, (((1,), (1,)), ((), ())), preferred_element_type=F32)
+
+
+def tn(a, b):
+    return lax.dot_general(a, b, (((0,), (0,)), ((), ())), preferred_element_type=F32)
+
+
+def sds(shape, dtype):
+    return jax.ShapeDtypeStruct(shape, dtype)
+
+
+def kernel_call(body, ins, in_specs, outs, out_specs, scratch, flops, limit_mib, name):
+    moved = sum(v.size * v.dtype.itemsize for v in ins)
+    moved += sum(math.prod(o.shape) * jnp.dtype(o.dtype).itemsize for o in outs)
+    return pl.pallas_call(
+        body,
+        out_shape=tuple(outs),
+        in_specs=in_specs,
+        out_specs=tuple(out_specs),
+        scratch_shapes=scratch,
+        compiler_params=pltpu.CompilerParams(vmem_limit_bytes=limit_mib << 20),
+        cost_estimate=pl.CostEstimate(flops=flops, bytes_accessed=moved, transcendentals=0),
+        name=name,
+    )(*ins)
+
+
+def aligned(v, m):
+    return pl.multiple_of(v, m)
+
+
+def layer_norm_parts(x):
+    centered = x - jnp.mean(x, axis=-1, keepdims=True)
+    variance = jnp.mean(centered * centered, axis=-1, keepdims=True)
+    scale = lax.rsqrt(variance + 1e-05)
+    return centered * scale, scale
+
+
+def split_blocks(src, keep, send, c, rows):
+    for b in range(8):
+        keep[b] = src[pl.ds(aligned((2 * b + c) * rows, 16), rows), :]
+        send[b] = src[pl.ds(aligned((2 * b + 1 - c) * rows, 16), rows), :]
+
+
+def device_of(f, q, pz):
+    return f ^ (pz * 4 + (q & 1) * 2 + (q >> 2))
+
+
+def qkv_kernel(idx, res, gb, sw0, sw1, *refs):
+    wa, wb = refs[:8], refs[8:16]
+    keep, send, htk, hts, wout, w, h, ht, sem, osem = refs[16:]
+    f, y, c = idx[0], idx[1], idx[2]
+
+    def fetch(pz, carry):
+        for q in range(8):
+            row = aligned(device_of(f, q, pz) * ROWS, 16)
+            y2 = y ^ ((q >> 1) & 1)
+            for g in range(3):
+                src = wa[q].at[pz, :, pl.ds(g * HALF, HALF)] if g < 2 else wb[q].at[pz, :, pl.ds(0, HALF)]
+                pltpu.make_async_copy(src, w.at[y2 * 3 + g, pl.ds(row, ROWS), :], sem).start()
+        return carry
+
+    lax.fori_loop(0, 4, fetch, 0)
+    gain, bias = gb[0:1, :], gb[2:3, :]
+    for t in range(4):
+        rows = pl.ds(t * 128, 128)
+        n, _ = layer_norm_parts(res[rows, :])
+        v = n * gain + bias
+        h[rows, :] = v.astype(BF16)
+        ht[:, rows] = v.T.astype(BF16)
+    split_blocks(ht, htk, hts, c, ROWS)
+    pltpu.make_async_copy(w, w, sem).wait()
+    out = pltpu.make_async_copy(w, wout, osem)
+    out.start()
+
+    def tile(t, carry):
+        rows = pl.ds(aligned(t * 256, 256), 256)
+        hv = h[rows, :]
+        for j in range(3):
+            cols = pl.ds(j * HALF, HALF)
+            keep[rows, cols] = nn(hv, w[2 * j + c]).astype(BF16)
+            send[rows, cols] = nn(hv, w[2 * j + 1 - c]).astype(BF16)
+        keep[rows, pl.ds(1152, 128)] = nt(hv, sw0[...]).astype(BF16)
+        send[rows, pl.ds(1152, 128)] = nt(hv, sw1[...]).astype(BF16)
+        return carry
+
+    lax.fori_loop(0, 2, tile, 0)
+    out.wait()
+
+
+def qkv_call(idx, res, gb, sw0, sw1, wa, wb):
+    return kernel_call(
+        qkv_kernel,
+        [idx, res, gb, sw0, sw1, *wa, *wb],
+        [SM, VM, VM, VM, VM] + [HB] * 16,
+        [
+            sds((TOK, 1280), BF16),
+            sds((TOK, 1280), BF16),
+            sds((8, ROWS, TOK), BF16),
+            sds((8, ROWS, TOK), BF16),
+            sds((6, D, HALF), BF16),
+        ],
+        [VM, VM, VM, VM, HB],
+        [
+            pltpu.VMEM((6, D, HALF), BF16),
+            pltpu.VMEM((TOK, D), BF16),
+            pltpu.VMEM((D, TOK), BF16),
+            pltpu.SemaphoreType.DMA,
+            pltpu.SemaphoreType.DMA,
+        ],
+        2 * TOK * D * 2304,
+        32,
+        "qkv",
+    )
+
+
+def load_halves(pairs, c, pad, sem):
+    copies = []
+    for number, (own, other, dst) in enumerate(pairs):
+        for k, (src, half) in enumerate(((own, c), (other, 1 - c))):
+            rows = pl.ds(aligned(pad + half * TOK, 128), TOK)
+            copy = pltpu.make_async_copy(src, dst.at[rows, :], sem.at[2 * number + k])
+            copy.start()
+            copies.append(copy)
+    return copies
+
+
+def mask_tiles(tab):
+    key = lax.broadcasted_iota(jnp.int32, (BLK, BLK), 0)
+    query = lax.broadcasted_iota(jnp.int32, (BLK, BLK), 1)
+    gap = query - key
+    tab[0] = jnp.where((gap >= 0) & (gap < WINDOW), 0.0, NEG)
+    tab[1] = jnp.where(gap >= 0, 0.0, NEG)
+    tab[2] = jnp.zeros((BLK, BLK), F32)
+    tab[3] = jnp.where(gap + BLK < WINDOW, 0.0, NEG)
+    tab[4] = jnp.full((BLK, BLK), NEG, F32)
+
+
+def log_sigmoid_of(v):
+    return -(jnp.maximum(-v, 0.0) + jnp.log1p(jnp.exp(-jnp.abs(v))))
+
+
+def picture_flags(pics, i):
+    p0, p1 = pics[0] // BLK, pics[1] // BLK
+    starts = (p0 == i) | (p1 == i)
+    follows = (p0 == i - 1) | (p1 == i - 1)
+    return starts, follows
+
+
+def block_probs(s, ls, tab, kept, i, h, blocks, starts, follows):
+    pair, odd = h // 2, h % 2
+    lane = lax.broadcasted_iota(jnp.int32, (BLK, BLK), 1)
+    mine = (lane >= 64) if odd else (lane < 64)
+    base = aligned(i * BLK, BLK)
+    cols = pair * BLK
+    q = s[pl.ds(base + BLK, BLK), pl.ds(cols, BLK)] * jnp.asarray(HEAD_DIM**-0.5, BF16)
+    q = jnp.where(mine, q, jnp.zeros_like(q))
+    near, chosen = pl.ds(base, blocks * BLK), kept[h, i]
+    far = pl.ds(aligned((chosen + 1) * BLK, BLK), BLK)
+    kcols, vcols = pl.ds(HALF + cols, BLK), pl.ds(2 * HALF + cols, BLK)
+    k = jnp.concatenate([s[near, kcols], s[far, kcols]], axis=0)
+    v = jnp.concatenate([s[near, vcols], s[far, vcols]], axis=0)
+    before = jnp.where(i == 0, 4, jnp.where(follows | (chosen == i - 1), 2, 3))
+    here = jnp.where(starts | follows, 2, jnp.where(chosen == i, 1, 0))
+    beyond = jnp.where(chosen < i - 1, 0.0, NEG).astype(F32)
+    logits = nt(k, q)
+    parts = [
+        logits[0:BLK] + (tab[before] + ls[pl.ds(base, BLK), h : h + 1]),
+        logits[BLK : 2 * BLK] + (tab[here] + ls[pl.ds(base + BLK, BLK), h : h + 1]),
+    ]
+    if blocks == 3:
+        parts.append(logits[2 * BLK : 3 * BLK] + ls[pl.ds(base + 2 * BLK, BLK), h : h + 1])
+    parts.append(logits[blocks * BLK :] + (ls[far, h : h + 1] + beyond))
+    logits = jnp.concatenate(parts, axis=0)
+    largest = jnp.max(logits, axis=0, keepdims=True)
+    weights = jnp.exp(logits - largest)
+    probs = weights * (1.0 / jnp.sum(weights, axis=0, keepdims=True))
+    return q, k, v, probs, near, far, mine
+
+
+def attend_kernel(idx, kept, pics, own, other, okeep, osend, s, ls, o, tab, sem):
+    c = idx[2]
+    copies = load_halves([(own, other, s)], c, BLK, sem)
+    s[0:BLK, :] = jnp.zeros((BLK, 1280), BF16)
+    mask_tiles(tab)
+    for copy in copies:
+        copy.wait()
+    ls[...] = log_sigmoid_of(s[:, 1152:1280].astype(F32))
+
+    def step(i, carry):
+        starts, follows = picture_flags(pics, i)
+
+        def run(blocks):
+            rows = pl.ds(aligned(i * BLK, BLK), BLK)
+            for pair in range(3):
+                halves = []
+                for odd in range(2):
+                    _, _, v, probs, _, _, mine = block_probs(
+                        s, ls, tab, kept, i, 2 * pair + odd, blocks, starts, follows
+                    )
+                    halves.append(tn(probs.astype(BF16), v))
+                o[rows, pl.ds(pair * BLK, BLK)] = jnp.where(mine, halves[1], halves[0]).astype(BF16)
+
+        @pl.when(starts)
+        def _():
+            run(3)
+
+        @pl.when(jnp.logical_not(starts))
+        def _():
+            run(2)
+
+        return carry
+
+    lax.fori_loop(0, 8, step, 0)
+    okeep[...] = o[pl.ds(aligned(c * TOK, TOK), TOK), :]
+    osend[...] = o[pl.ds(aligned((1 - c) * TOK, TOK), TOK), :]
+
+
+def attend_call(idx, kept, pics, own, other):
+    return kernel_call(
+        attend_kernel,
+        [idx, kept, pics, own, other],
+        [SM, SM, SM, HB, HB],
+        [sds((TOK, HALF), BF16), sds((TOK, HALF), BF16)],
+        [VM, VM],
+        [
+            pltpu.VMEM((SEQ + BLK, 1280), BF16),
+            pltpu.VMEM((SEQ + BLK, BLK), F32),
+            pltpu.VMEM((SEQ, HALF), BF16),
+            pltpu.VMEM((5, BLK, BLK), F32),
+            pltpu.SemaphoreType.DMA((2,)),
+        ],
+        6 * 8 * 4 * BLK * BLK * BLK * 4,
+        32,
+        "attend",
+    )
+
+
+def up_kernel(idx, res, mk, mr, gb, *refs):
+    wo_in, wa, wb = refs[:8], refs[8:16], refs[16:24]
+    aa, act, slope, mtk, mts, htk, hts, atk, ats, woo, wuo = refs[24:35]
+    wo, wu, h, ht, at, sem, osem = refs[35:]
+    f, y, c = idx[0], idx[1], idx[2]
+
+    def fetch_out(pz, carry):
+        for q in range(8):
+            row = aligned(device_of(f, q, pz) * ROWS, 16)
+            y2 = y ^ ((q >> 1) & 1)
+            src = wo_in[q].at[pz, :, pl.ds(HALF, HALF)]
+            pltpu.make_async_copy(src, wo.at[y2, pl.ds(row, ROWS), :], sem.at[0]).start()
+        return carry
+
+    def fetch_up(pz, carry):
+        for q in range(8):
+            row = aligned(device_of(f, q, pz) * ROWS, 16)
+            y2 = y ^ ((q >> 1) & 1)
+            for part, w in enumerate((wa, wb)):
+                dst = wu.at[y2 * 2 + part, pl.ds(row, ROWS), :]
+                pltpu.make_async_copy(w[q].at[pz], dst, sem.at[1]).start()
+        return carry
+
+    lax.fori_loop(0, 4, fetch_out, 0)
+    lax.fori_loop(0, 4, fetch_up, 0)
+    for t in range(4):
+        rows = pl.ds(t * 128, 128)
+        ht[pl.ds(aligned(c * HALF, HALF), HALF), rows] = mk[rows, :].astype(F32).T.astype(BF16)
+        ht[pl.ds(aligned((1 - c) * HALF, HALF), HALF), rows] = mr[rows, :].astype(F32).T.astype(BF16)
+    split_blocks(ht, mtk, mts, c, ROWS)
+    pltpu.make_async_copy(wo, wo, sem.at[0]).wait()
+    out0 = pltpu.make_async_copy(wo, woo, osem.at[0])
+    out0.start()
+    gain, bias = gb[1:2, :], gb[3:4, :]
+    mine, theirs = pl.ds(aligned(c * HALF, HALF), HALF), pl.ds(aligned((1 - c) * HALF, HALF), HALF)
+    for t in range(4):
+        rows = pl.ds(t * 128, 128)
+        for half in range(2):
+            cols = pl.ds(half * HALF, HALF)
+            part = nn(mk[rows, :], wo[half, mine, :]) + nn(mr[rows, :], wo[half, theirs, :])
+            aa[rows, cols] = res[rows, cols] + part
+        n, _ = layer_norm_parts(aa[rows, :])
+        v = n * gain + bias
+        h[rows, :] = v.astype(BF16)
+        ht[:, rows] = v.T.astype(BF16)
+    split_blocks(ht, htk, hts, c, ROWS)
+    pltpu.make_async_copy(wu, wu, sem.at[1]).wait()
+    out1 = pltpu.make_async_copy(wu, wuo, osem.at[1])
+    out1.start()
+    for g in range(4):
+
+        def tile(t, carry):
+            rows = pl.ds(aligned(t * 128, 128), 128)
+            u = nn(h[rows, :], wu[g])
+            inner = 0.7978845608 * (u + 0.044715 * (u * u * u))
+            th = jnp.tanh(inner)
+            a = 0.5 * u * (1.0 + th)
+            d = 0.5 * (1.0 + th) + (0.5 * u) * (1.0 - th * th) * (
+                0.7978845608 * (1.0 + (3 * 0.044715) * (u * u))
+            )
+            cols = pl.ds(g * D, D)
+            act[rows, cols] = a.astype(BF16)
+            slope[rows, cols] = d.astype(BF16)
+            at[cols, rows] = a.T.astype(BF16)
+            return carry
+
+        lax.fori_loop(0, 4, tile, 0)
+    split_blocks(at, atk, ats, c, DROWS)
+    out0.wait()
+    out1.wait()
+
+
+def up_call(idx, res, mk, mr, gb, wo, wa, wb):
+    return kernel_call(
+        up_kernel,
+        [idx, res, mk, mr, gb, *wo, *wa, *wb],
+        [SM, VM, VM, VM, VM] + [HB] * 24,
+        [
+            sds((TOK, D), F32),
+            sds((TOK, FF), BF16),
+            sds((TOK, FF), BF16),
+            sds((8, ROWS, TOK), BF16),
+            sds((8, ROWS, TOK), BF16),
+            sds((8, ROWS, TOK), BF16),
+            sds((8, ROWS, TOK), BF16),
+            sds((8, DROWS, TOK), BF16),
+            sds((8, DROWS, TOK), BF16),
+            sds((2, D, HALF), BF16),
+            sds((4, D, D), BF16),
+        ],
+        [VM] * 9 + [HB, HB],
+        [
+            pltpu.VMEM((2, D, HALF), BF16),
+            pltpu.VMEM((4, D, D), BF16),
+            pltpu.VMEM((TOK, D), BF16),
+            pltpu.VMEM((D, TOK), BF16),
+            pltpu.VMEM((FF, TOK), BF16),
+            pltpu.SemaphoreType.DMA((2,)),
+            pltpu.SemaphoreType.DMA((2,)),
+        ],
+        2 * TOK * D * (D + FF),
+        48,
+        "up",
+    )
+
+
+def down_kernel(idx, act, aa, *refs):
+    wa, wb = refs[:8], refs[8:16]
+    res, wdo, wd, sem, osem = refs[16:]
+    f, y = idx[0], idx[1]
+
+    def fetch(pz, carry):
+        for q in range(8):
+            row = device_of(f, q, pz) * DROWS
+            y2 = y ^ ((q >> 1) & 1)
+            for part, w in enumerate((wa, wb)):
+                dst = wd.at[y2, pl.ds(aligned(row + part * 96, 16), 96), :]
+                pltpu.make_async_copy(w[q].at[pz], dst, sem).start()
+        return carry
+
+    lax.fori_loop(0, 4, fetch, 0)
+    pltpu.make_async_copy(wd, wd, sem).wait()
+    out = pltpu.make_async_copy(wd, wdo, osem)
+    out.start()
+
+    def tile(t, carry):
+        rows = pl.ds(aligned(t * 256, 256), 256)
+        for half in range(2):
+            cols = pl.ds(half * HALF, HALF)
+            res[rows, cols] = aa[rows, cols] + nn(act[rows, :], wd[half])
+        return carry
+
+    lax.fori_loop(0, 2, tile, 0)
+    out.wait()
+
+
+def down_call(idx, act, aa, wa, wb):
+    return kernel_call(
+        down_kernel,
+        [idx, act, aa, *wa, *wb],
+        [SM, VM, VM] + [HB] * 16,
+        [sds((TOK, D), F32), sds((2, FF, HALF), BF16)],
+        [VM, HB],
+        [
+            pltpu.VMEM((2, FF, HALF), BF16),
+            pltpu.SemaphoreType.DMA,
+            pltpu.SemaphoreType.DMA,
+        ],
+        2 * TOK * D * FF,
+        32,
+        "down",
+    )
+
+
+def down_back_kernel(grad, slope, wd_in, gu, wd, sem):
+    copy = pltpu.make_async_copy(wd_in, wd, sem)
+    copy.start()
+    copy.wait()
+    for g in range(4):
+
+        def tile(t, carry):
+            rows = pl.ds(aligned(t * 256, 256), 256)
+            cols = pl.ds(g * D, D)
+            part = nt(grad[rows, 0:HALF], wd[0, cols, :]) + nt(grad[rows, HALF:D], wd[1, cols, :])
+            gu[rows, cols] = (part * slope[rows, cols].astype(F32)).astype(BF16)
+            return carry
+
+        lax.fori_loop(0, 2, tile, 0)
+
+
+def down_back_call(grad, slope, wd):
+    return kernel_call(
+        down_back_kernel,
+        [grad, slope, wd],
+        [VM, VM, HB],
+        [sds((TOK, FF), BF16)],
+        [VM],
+        [pltpu.VMEM((2, FF, HALF), BF16), pltpu.SemaphoreType.DMA],
+        2 * TOK * D * FF,
+        32,
+        "down_back",
+    )[0]
+
+
+def norm_back(x, grad_out, gain):
+    n, scale = layer_norm_parts(x)
+    e = grad_out * gain
+    back = scale * (
+        e - jnp.mean(e, axis=-1, keepdims=True) - n * jnp.mean(e * n, axis=-1, keepdims=True)
+    )
+    gain_part = jnp.sum(grad_out * n, axis=0, keepdims=True)
+    bias_part = jnp.sum(grad_out, axis=0, keepdims=True)
+    return back, gain_part, bias_part
+
+
+def up_back_kernel(idx, grad, gu, aa, gb, wu_in, wo_in, ga, gat, gmk, gms, nrm, wu, wo, sem):
+    c = idx[2]
+    c0 = pltpu.make_async_copy(wu_in, wu, sem.at[0])
+    c1 = pltpu.make_async_copy(wo_in, wo, sem.at[1])
+    c0.start()
+    c1.start()
+    nrm[...] = jnp.zeros_like(nrm)
+    gain = gb[1:2, :]
+    mine, theirs = pl.ds(aligned(c * HALF, HALF), HALF), pl.ds(aligned((1 - c) * HALF, HALF), HALF)
+    c0.wait()
+    c1.wait()
+
+    def tile(t, carry):
+        rows = pl.ds(aligned(t * 128, 128), 128)
+        gh = nt(gu[rows, 0:D], wu[0])
+        for g in range(1, 4):
+            gh += nt(gu[rows, pl.ds(g * D, D)], wu[g])
+        back, gain_part, bias_part = norm_back(aa[rows, :], gh, gain)
+        total = grad[rows, :] + back
+        ga[rows, :] = total
+        low = total.astype(BF16)
+        gat[rows, :] = low
+        nrm[0:1, :] += gain_part
+        nrm[1:2, :] += bias_part
+        for dst, part in ((gmk, mine), (gms, theirs)):
+            dst[rows, :] = (
+                nt(low[:, 0:HALF], wo[0, part, :]) + nt(low[:, HALF:D], wo[1, part, :])
+            ).astype(BF16)
+        return carry
+
+    lax.fori_loop(0, 4, tile, 0)
+
+
+def up_back_call(idx, grad, gu, aa, gb, wu, wo):
+    return kernel_call(
+        up_back_kernel,
+        [idx, grad, gu, aa, gb, wu, wo],
+        [SM, VM, VM, VM, VM, HB, HB],
+        [
+            sds((TOK, D), F32),
+            sds((TOK, D), BF16),
+            sds((TOK, HALF), BF16),
+            sds((TOK, HALF), BF16),
+            sds((8, D), F32),
+        ],
+        [VM] * 5,
+        [
+            pltpu.VMEM((4, D, D), BF16),
+            pltpu.VMEM((2, D, HALF), BF16),
+            pltpu.SemaphoreType.DMA((2,)),
+        ],
+        2 * TOK * D * (D + FF),
+        40,
+        "up_back",
+    )
+
+
+def attend_back_kernel(
+    idx, kept, pics, own, other, gown, gother, down_, doth, s, g, ls, d, dk, dv, ds, tab, sem
+):
+    c = idx[2]
+    copies = load_halves([(own, other, s)], c, BLK, sem)
+    copies += load_halves([(gown, gother, g)], c, 0, sem.at[pl.ds(2, 2)])
+    s[0:BLK, :] = jnp.zeros((BLK, 1280), BF16)
+    mask_tiles(tab)
+    dk[...] = jnp.zeros_like(dk)
+    dv[...] = jnp.zeros_like(dv)
+    ds[...] = jnp.zeros_like(ds)
+    for copy in copies:
+        copy.wait()
+    ls[...] = log_sigmoid_of(s[:, 1152:1280].astype(F32))
+    lane = lax.broadcasted_iota(jnp.int32, (BLK, BLK), 1)
+
+    def step(i, carry):
+        starts, follows = picture_flags(pics, i)
+
+        def run(blocks):
+            rows = pl.ds(aligned(i * BLK, BLK), BLK)
+            for pair in range(3):
+                cols = pl.ds(pair * BLK, BLK)
+                gp = g[rows, cols]
+                halves = []
+                for odd in range(2):
+                    h = 2 * pair + odd
+                    q, k, v, probs, near, far, mine = block_probs(
+                        s, ls, tab, kept, i, h, blocks, starts, follows
+                    )
+                    gm = jnp.where(mine, gp, jnp.zeros_like(gp))
+                    gprob = nt(v, gm)
+                    inner = jnp.sum(probs * gprob, axis=0, keepdims=True)
+                    gl = (probs * (gprob - inner)).astype(BF16)
+                    gv = nn(probs.astype(BF16), gm)
+                    ind = jnp.where(lane == h, 1.0, 0.0).astype(BF16)
+                    gk = nn(gl, jnp.concatenate([q, ind], axis=1))
+                    cut = blocks * BLK
+                    dv[near, cols] += gv[:cut]
+                    dv[far, cols] += gv[cut:]
+                    dk[near, cols] += gk[:cut, :BLK]
+                    dk[far, cols] += gk[cut:, :BLK]
+                    ds[near, :] += gk[:cut, BLK:]
+                    ds[far, :] += gk[cut:, BLK:]
+                    halves.append(tn(gl, k))
+                d[rows, cols] = (
+                    jnp.where(mine, halves[1], halves[0]) * (HEAD_DIM**-0.5)
+                ).astype(BF16)
+
+        @pl.when(starts)
+        def _():
+            run(3)
+
+        @pl.when(jnp.logical_not(starts))
+        def _():
+            run(2)
+
+        return carry
+
+    lax.fori_loop(0, 8, step, 0)
+    keys = pl.ds(BLK, SEQ)
+    d[:, HALF : 2 * HALF] = dk[keys, :].astype(BF16)
+    d[:, 2 * HALF : 3 * HALF] = dv[keys, :].astype(BF16)
+    back = ds[keys, :] * jax.nn.sigmoid(-s[keys, 1152:1280].astype(F32))
+    d[:, 1152:1280] = back.astype(BF16)
+    down_[...] = d[pl.ds(aligned(c * TOK, TOK), TOK), :]
+    doth[...] = d[pl.ds(aligned((1 - c) * TOK, TOK), TOK), :]
+
+
+def attend_back_call(idx, kept, pics, own, other, gown, gother):
+    return kernel_call(
+        attend_back_kernel,
+        [idx, kept, pics, own, other, gown, gother],
+        [SM, SM, SM, HB, HB, HB, HB],
+        [sds((TOK, 1280), BF16), sds((TOK, 1280), BF16)],
+        [VM, VM],
+        [
+            pltpu.VMEM((SEQ + BLK, 1280), BF16),
+            pltpu.VMEM((SEQ, HALF), BF16),
+            pltpu.VMEM((SEQ + BLK, BLK), F32),
+            pltpu.VMEM((SEQ, 1280), BF16),
+            pltpu.VMEM((SEQ + BLK, HALF), F32),
+            pltpu.VMEM((SEQ + BLK, HALF), F32),
+            pltpu.VMEM((SEQ + BLK, BLK), F32),
+            pltpu.VMEM((5, BLK, BLK), F32),
+            pltpu.SemaphoreType.DMA((4,)),
+        ],
+        6 * 8 * 4 * BLK * BLK * BLK * 10,
+        40,
+        "attend_back",
+    )
+
+
+def qkv_back_kernel(idx, ga, down_, dr, res, gb, sw0, sw1, w_in, gout, glow, nrm, w, sem):
+    c = idx[2]
+    copy = pltpu.make_async_copy(w_in, w, sem)
+    copy.start()
+    nrm[...] = jnp.zeros_like(nrm)
+    gain = gb[0:1, :]
+    copy.wait()
+
+    def tile(t, carry):
+        rows = pl.ds(aligned(t * 128, 128), 128)
+        gh = nn(down_[rows, 1152:1280], sw0[...]) + nn(dr[rows, 1152:1280], sw1[...])
+        for j in range(3):
+            cols = pl.ds(j * HALF, HALF)
+            gh += nt(down_[rows, cols], w[2 * j + c]) + nt(dr[rows, cols], w[2 * j + 1 - c])
+        back, gain_part, bias_part = norm_back(res[rows, :], gh, gain)
+        total = ga[rows, :] + back
+        gout[rows, :] = total
+        glow[rows, :] = total.astype(BF16)
+        nrm[0:1, :] += gain_part
+        nrm[1:2, :] += bias_part
+        return carry
+
+    lax.fori_loop(0, 4, tile, 0)
+
+
+def qkv_back_call(idx, ga, down_, dr, res, gb, sw0, sw1, w):
+    return kernel_call(
+        qkv_back_kernel,
+        [idx, ga, down_, dr, res, gb, sw0, sw1, w],
+        [SM, VM, VM, VM, VM, VM, VM, VM, HB],
+        [sds((TOK, D), F32), sds((TOK, D), BF16), sds((8, D), F32)],
+        [VM, VM, VM],
+        [pltpu.VMEM((6, D, HALF), BF16), pltpu.SemaphoreType.DMA],
+        2 * TOK * D * 2304,
+        32,
+        "qkv_back",
+    )
+
+
+def scatter_rows(src, f, rows, offset, count, pyy, portion, ka, sa, kb, sb):
+    for pxx in range(2):
+        for pz in range(4):
+            block = (f >> 1) ^ (pz * 2 + pxx)
+            value = src[pl.ds(aligned(block * rows + offset, 16), count), :]
+            if portion == 0:
+                (sa if pxx else ka)[pyy, pz] = value
+            else:
+                (sb if pyy else kb)[pxx, pz] = value
+
+
+def up_grad_kernel(idx, xk, xr, gk, gr, ka, sa, kb, sb, tmp):
+    f, y = idx[0], idx[1]
+    for portion in range(2):
+        for pyy in range(2):
+            cols = pl.ds(aligned((y ^ pyy) * 1536 + portion * D, 128), D)
+            tmp[portion * 2 + pyy] = (nn(xk[...], gk[:, cols]) + nn(xr[...], gr[:, cols])).astype(
+                BF16
+            )
+            scatter_rows(
+                tmp.at[portion * 2 + pyy], f, ROWS, 0, ROWS, pyy, portion, ka, sa, kb, sb
+            )
+
+
+def up_grad_call(idx, xk, xr, gk, gr):
+    piece = sds((2, 4, ROWS, D), BF16)
+    return kernel_call(
+        up_grad_kernel,
+        [idx, xk.reshape(HALF, TOK), xr.reshape(HALF, TOK), gk, gr],
+        [SM, VM, VM, VM, VM],
+        [piece] * 4,
+        [VM] * 4,
+        [pltpu.VMEM((4, HALF, D), BF16)],
+        2 * SEQ * HALF * FF,
+        32,
+        "up_grad",
+    )
+
+
+def down_grad_kernel(idx, xk, xr, gk, gr, ka, sa, kb, sb, tmp):
+    f, y = idx[0], idx[1]
+    for pyy in range(2):
+        cols = pl.ds(aligned((y ^ pyy) * HALF, 128), HALF)
+
+        def tile(t, carry):
+            rows = pl.ds(aligned(t * HALF, HALF), HALF)
+            tmp[pyy, rows, :] = (nn(xk[rows, :], gk[:, cols]) + nn(xr[rows, :], gr[:, cols])).astype(
+                BF16
+            )
+            return carry
+
+        lax.fori_loop(0, 4, tile, 0)
+        for portion in range(2):
+            scatter_rows(
+                tmp.at[pyy], f, DROWS, portion * 96, 96, pyy, portion, ka, sa, kb, sb
+            )
+
+
+def down_grad_call(idx, xk, xr, gk, gr):
+    piece = sds((2, 4, 96, HALF), BF16)
+    return kernel_call(
+        down_grad_kernel,
+        [idx, xk.reshape(4 * HALF, TOK), xr.reshape(4 * HALF, TOK), gk, gr],
+        [SM, VM, VM, VM, VM],
+        [piece] * 4,
+        [VM] * 4,
+        [pltpu.VMEM((2, 4 * HALF, HALF), BF16)],
+        2 * SEQ * HALF * FF,
+        32,
+        "down_grad",
+    )
+
+
+def qkv_grad_kernel(
+    idx, xk, xr, mk, mr, d00, d01, d10, d11, gk, gr, ka, sa, kb, sb, sc, dy, tmp, tsc, sem
+):
+    f, y, c = idx[0], idx[1], idx[2]
+    copies = []
+    for tok, pair in enumerate(((d00, d01), (d10, d11))):
+        for k, src in enumerate(pair):
+            for j in range(3):
+                copy = pltpu.make_async_copy(
+                    src.at[:, pl.ds(j * HALF, HALF)],
+                    dy.at[tok, 2 * j + (c ^ k)],
+                    sem.at[tok * 6 + k * 3 + j],
+                )
+                copy.start()
+                copies.append(copy)
+    for tok, pair in enumerate(((d00, d01), (d10, d11))):
+        for k, src in enumerate(pair):
+            copy = pltpu.make_async_copy(
+                src.at[:, pl.ds(1152, 128)], tsc.at[tok * 2 + k], sem.at[12 + tok * 2 + k]
+            )
+            copy.start()
+            copies.append(copy)
+    for copy in copies:
+        copy.wait()
+    for pyy in range(2):
+        y2 = y ^ pyy
+        for part in range(4):
+            portion, side = part // 2, part % 2
+            cols = pl.ds(side * HALF, HALF)
+            if part < 3:
+                g = y2 * 3 + part
+                value = nn(xk[...], dy[0, g]) + nn(xr[...], dy[1, g])
+            else:
+                oc = pl.ds(aligned(y2 * HALF, 128), HALF)
+                value = nn(mk[...], gk[:, oc]) + nn(mr[...], gr[:, oc])
+            tmp[portion * 2 + pyy, :, cols] = value.astype(BF16)
+        for portion in range(2):
+            scatter_rows(
+                tmp.at[portion * 2 + pyy], f, ROWS, 0, ROWS, pyy, portion, ka, sa, kb, sb
+            )
+    own = nn(xk[...], tsc[0]) + nn(xr[...], tsc[2])
+    theirs = nn(xk[...], tsc[1]) + nn(xr[...], tsc[3])
+    first = jnp.where(c == 0, own, theirs)
+    second = jnp.where(c == 0, theirs, own)
+    both = first + pltpu.roll(second, 64, 1)
+    for pxx in range(2):
+        for pz in range(4):
+            target = (f >> 1) ^ (pz * 2 + pxx)
+            for b in range(8):
+
+                @pl.when(target == b)
+                def _():
+                    sc[pxx, pz] = both[b * ROWS : (b + 1) * ROWS, :]
+
+
+def qkv_grad_call(idx, xk, xr, mk, mr, d00, d01, d10, d11, gk, gr):
+    piece = sds((2, 4, ROWS, D), BF16)
+    flat = [v.reshape(HALF, TOK) for v in (xk, xr, mk, mr)]
+    return kernel_call(
+        qkv_grad_kernel,
+        [idx, *flat, d00, d01, d10, d11, gk, gr],
+        [SM, VM, VM, VM, VM, HB, HB, HB, HB, VM, VM],
+        [piece] * 4 + [sds((2, 4, ROWS, 128), F32)],
+        [VM] * 5,
+        [
+            pltpu.VMEM((2, 6, TOK, HALF), BF16),
+            pltpu.VMEM((4, HALF, D), BF16),
+            pltpu.VMEM((4, TOK, 128), BF16),
+            pltpu.SemaphoreType.DMA((16,)),
+        ],
+        2 * SEQ * HALF * FF,
+        40,
+        "qkv_grad",
+    )
+
+
+def pairwise(v, bits):
+    return lax.ppermute(v, "fsdp", [(i, i ^ bits) for i in range(16)])
+
+
+def over_ctx(v):
+    return lax.ppermute(v, "ctx", [(0, 1), (1, 0)])
+
+
+def over_core(v):
+    return pairwise(v, 1)
+
+
+def over_x(v):
+    return pairwise(v, 2)
+
+
+def turn(v):
+    perm = [
+        ((g * 2 + a) * 2 + b, (g * 2 + b) * 2 + a) for g in range(8) for a in range(2) for b in range(2)
+    ]
+    return lax.ppermute(v, ("fsdp", "ctx"), perm)
+
+
+def gather_piece(part_a, part_b):
+    both = jnp.stack([part_a, part_b])
+    near = [both] + [pairwise(both, k << 2) for k in range(1, 4)]
+    a0, b0 = (jnp.stack([v[part] for v in near]) for part in range(2))
+    a1 = over_x(a0)
+    b2 = over_ctx(b0)
+    a = [a0, a1, over_ctx(a0), over_ctx(a1)]
+    b = [b0, over_x(b0), b2, over_x(b2)]
+    return (a + [over_core(v) for v in a], b + [over_core(v) for v in b])
+
+
+def reduce_piece(ka, sa, kb, sb):
+    def add(mine, received):
+        return mine.astype(F32) + received.astype(F32)
+
+    def last(total, received):
+        low = total.astype(BF16)
+        return total[0] + sum(pairwise(low[k], k << 2).astype(F32) for k in range(1, 4))
+
+    ta = add(ka, over_x(sa))
+    tb = add(kb, over_ctx(sb))
+    ta = add(ta[0], over_ctx(ta[1].astype(BF16)))
+    tb = add(tb[0], over_x(tb[1].astype(BF16)))
+    return last(ta, None), last(tb, None)
+
+
+def pair_device(
+    tokens,
+    cotangent,
+    kept_blocks,
+    picture_starts,
+    qkv_weight,
+    score_weight,
+    out_weight,
+    up_weight,
+    down_weight,
+    norm_gain,
+    norm_bias,
+):
+    f = lax.axis_index("fsdp").astype(jnp.int32)
+    y = lax.axis_index("ctx").astype(jnp.int32)
+    c = f & 1
+    idx = jnp.stack([f, y, c])
+    start = turn(tokens[0])
+    cot = turn(cotangent[0])
+    kept = jnp.where(c == y, kept_blocks[0], over_core(kept_blocks[0]))
+    pics = jnp.where(c == y, picture_starts[0], over_core(picture_starts[0]))
+    kept = lax.dynamic_slice_in_dim(kept, c * 6, 6, 0)
+    small = jnp.concatenate(
+        [jnp.swapaxes(score_weight, 1, 2), norm_gain, norm_bias], axis=1
+    ).reshape(LAYERS * 16, ROWS)
+    small = jnp.pad(small, ((0, 0), (0, 128 - ROWS)))
+    small = jnp.stack([small] + [pairwise(small, k << 2) for k in range(1, 4)])
+    small = jnp.concatenate([small, over_x(small)])
+    small = jnp.concatenate([small, over_core(small)])
+    away = jnp.arange(16, dtype=jnp.int32) ^ f
+    small = jnp.take(small, (away & 1) * 8 + ((away >> 1) & 1) * 4 + (away >> 2), axis=0)
+    small = jnp.moveaxis(small[:, :, :ROWS], 0, 1).reshape(LAYERS, 16, D)
+    pieces = []
+    for l in range(LAYERS):
+        qo = gather_piece(
+            qkv_weight[l][:, :D], jnp.concatenate([qkv_weight[l][:, D:], out_weight[l]], axis=1)
+        )
+        up = gather_piece(up_weight[l][:, :D], up_weight[l][:, D:])
+        dn = gather_piece(down_weight[l][:96], down_weight[l][96:])
+        pieces.append((qo, up, dn))
+    residual = start.astype(F32)
+    saved = []
+    for l in range(LAYERS):
+        (qa, qb), (ua, ub), (da, db) = pieces[l]
+        gb = jnp.pad(small[l, 12:16].astype(F32), ((0, 4), (0, 0)))
+        own_rows = lax.dynamic_slice_in_dim(small[l], c * 6, 6, 0)
+        other_rows = lax.dynamic_slice_in_dim(small[l], (1 - c) * 6, 6, 0)
+        sw0 = jnp.pad(own_rows, ((0, 122), (0, 0)))
+        sw1 = jnp.pad(other_rows, ((0, 122), (0, 0)))
+        own, send, xk, xs, w_qkv = qkv_call(idx, residual, gb, sw0, sw1, qa, qb)
+        other = over_core(send)
+        mixed, msend = attend_call(idx, kept, pics, own, other)
+        after, act, slope, mk, ms, hk, hs, ak, as_, w_out, w_up = up_call(
+            idx, residual, mixed, over_core(msend), gb, qb, ua, ub
+        )
+        new, w_down = down_call(idx, act, after, da, db)
+        received = tuple(over_core(v) for v in (xs, ms, hs, as_))
+        saved.append(
+            (residual, gb, sw0, sw1, own, other, after, slope, (xk, mk, hk, ak), received)
+            + (w_qkv, w_out, w_up, w_down)
+        )
+        residual = new
+    block_output = turn(residual.astype(BF16)).astype(F32)
+    grad = cot.astype(F32)
+    grad_low = cot
+    grads = [None] * LAYERS
+    norms = [None] * LAYERS
+    for l in reversed(range(LAYERS)):
+        res, gb, sw0, sw1, own, other, after, slope, kept_t, recv_t, w_qkv, w_out, w_up, w_down = saved[l]
+        xk, mk, hk, ak = kept_t
+        xr, mr, hr, ar = recv_t
+        gu = down_back_call(grad_low, slope, w_down)
+        gd_r = over_core(grad_low)
+        gu_r = over_core(gu)
+        down_pieces = reduce_piece(*down_grad_call(idx, ak, ar, grad_low, gd_r))
+        ga, gat, gmk, gms, nrm2 = up_back_call(idx, grad, gu, after, gb, w_up, w_out)
+        gm_r = over_core(gms)
+        gat_r = over_core(gat)
+        up_pieces = reduce_piece(*up_grad_call(idx, hk, hr, gu, gu_r))
+        d_own, d_oth = attend_back_call(idx, kept, pics, own, other, gmk, gm_r)
+        r1 = over_core(d_oth)
+        r2 = over_core(d_own)
+        *qo, sc = qkv_grad_call(idx, xk, xr, mk, mr, d_own, r1, d_oth, r2, gat, gat_r)
+        qo_pieces = reduce_piece(*qo)
+        grad, grad_low, nrm1 = qkv_back_call(idx, ga, d_own, r1, res, gb, sw0, sw1, w_qkv)
+        sc = sc + over_ctx(sc)
+        sc = sc[0] + over_x(sc[1])
+        sc = sc[0] + sum(pairwise(sc[k], k << 2) for k in range(1, 4))
+        grads[l] = (qo_pieces, up_pieces, down_pieces, sc)
+        norms[l] = jnp.concatenate([nrm1[0:1], nrm2[0:1], nrm1[1:2], nrm2[1:2]])
+    token_grad = turn(grad_low).astype(F32)
+    nrm = jnp.concatenate(norms)
+    nrm = nrm + over_core(nrm)
+    nrm = nrm + over_ctx(nrm)
+    nrm = nrm + over_x(nrm)
+    nrm = nrm + sum(pairwise(nrm, k << 2) for k in range(1, 4))
+    nrm = lax.dynamic_slice_in_dim(nrm, f * ROWS, ROWS, 1).reshape(LAYERS, 2, 2, ROWS)
+    qkv_grad = jnp.stack([jnp.concatenate([a, b[:, :HALF]], 1) for (a, b), _, _, _ in grads])
+    out_grad = jnp.stack([b[:, HALF:] for (_, b), _, _, _ in grads])
+    up_grad = jnp.stack([jnp.concatenate([a, b], 1) for _, (a, b), _, _ in grads])
+    down_grad = jnp.stack([jnp.concatenate([a, b], 0) for _, _, (a, b), _ in grads])
+    score_grad = jnp.stack(
+        [jnp.concatenate([s[:, 0:6], s[:, 64:70]], 1) for _, _, _, s in grads]
+    )
+    return (
+        block_output[None],
+        token_grad[None],
+        qkv_grad,
+        score_grad,
+        out_grad,
+        up_grad,
+        down_grad,
+        nrm[:, 0],
+        nrm[:, 1],
+    )
+
+
 def solution(mesh):
     in_specs = (
         P("fsdp", "ctx", None),
@@ -380,6 +1339,7 @@
         P(None, None, "fsdp"),
         P(None, None, "fsdp"),
     )
+    pairs = mesh.shape["fsdp"] == 16 and mesh.shape["ctx"] == 2
     return jax.shard_map(
-        per_device, mesh=mesh, in_specs=in_specs, out_specs=out_specs, check_vma=False
-    )
+        pair_device if pairs else per_device, mesh=mesh, in_specs=in_specs, out_specs=out_specs, check_vma=False
+    )

time: 1880 us -> 801 us (0.43)
  matrix products: 514 us -> 0 us
  waiting for transfers between devices: 564 us -> 207 us
  Pallas kernels: 0 us -> 257 us
  local copies, waits for them, and re-layouts: 313 us -> 71.4 us
  blocking collectives: 234 us -> 0 us
  starting transfers between devices: 37.4 us -> 227 us
  other arithmetic: 174 us -> 28.1 us
    dot_general x246 -> x0, matrix products: 514 us -> none  [the longest x72 162 us: masked_logits(): jnp.einsum('sqd,skd->sqk', queries, keys, preferred_element_type=jnp.floa...]
    all_gather x30 -> x0, waiting for transfers between devices: 400 us -> none  [the longest x2 111 us: per_device(): lax.all_gather(rows[4], 'ctx', axis=1, tiled=True)]
    pallas_call x0 -> x22, Pallas kernels: none -> 257 us  [kernel_call(): pl.pallas_call(body, out_shape=tuple(outs), in_specs=in_specs, out_specs=...]
    ppermute x0 -> x213, starting transfers between devices: none -> 227 us  [the longest x176 176 us: pairwise(): return lax.ppermute(v, 'fsdp', [(i, i ^ bits) for i in range(16)])]
    all_gather x16 -> x0, blocking collectives: 226 us -> none  [the longest x2 48 us: per_device(): lax.all_gather(out_weight[layer_index], 'fsdp', axis=0, tiled=True)]
    ppermute x0 -> x213, waiting for transfers between devices: none -> 207 us  [the longest x33 115 us: over_ctx(): return lax.ppermute(v, 'ctx', [(0, 1), (1, 0)])]
    reduce_scatter x4 -> x0, waiting for transfers between devices: 143 us -> none  [the longest x1 76.5 us: per_device(): lax.psum_scatter(stacked[4].astype(jnp.bfloat16), 'fsdp', scatter_dimensi...]
    unnamed x9 -> x1, other arithmetic: 97.5 us -> 0.01 us
  transfers between devices with their start and end apart: 45 -> 213, of which waited for: 16 -> 67; matrix products, arithmetic and copies ran while one was open for 53% -> 6% of each run, Pallas kernels for 0% -> 32%
where the time goes in v1:
time: 801 us; the launch traced here: 794 us
  Pallas kernels  257 us (32%)
  starting transfers between devices  227 us (28%)
  waiting for transfers between devices  207 us (26%)
  local copies, waits for them, and re-layouts  71.4 us (9%)
  other arithmetic  28.1 us (4%)
    pallas_call x22, Pallas kernels, kernel_call(): pl.pallas_call(body, out_shape=tuple(outs), in_specs=in_specs, out_specs=...  257 us
    ppermute x176, starting transfers between devices, pairwise(): return lax.ppermute(v, 'fsdp', [(i, i ^ bits) for i in range(16)])  176 us
    ppermute x33, waiting for transfers between devices, over_ctx(): return lax.ppermute(v, 'ctx', [(0, 1), (1, 0)])  115 us
    ppermute x176, waiting for transfers between devices, pairwise(): return lax.ppermute(v, 'fsdp', [(i, i ^ bits) for i in range(16)])  91.4 us
    unnamed x409, local copies, waits for them, and re-layouts  52.5 us
    ppermute x33, starting transfers between devices, over_ctx(): return lax.ppermute(v, 'ctx', [(0, 1), (1, 0)])  40.2 us
  transfers between devices with their start and end apart: 213, of which 67 were waited for; matrix products, arithmetic and copies ran while one was open for 6% of the time, Pallas kernels for 32%

profile of v1, /device:TPU:0, one launch (start us, length us, event | category | flops | bytes accessed | tf_op | source)
XLA Modules:
  0.0 794.2 jit_solution(14546661409665385089)
XLA Ops:
  2.1 3.1 collective-permute-start.3
  10.6 3.5 collective-permute-start.9
  21.0 3.8 collective-permute-start.28
  27.0 7.4 collective-permute-start.45
  38.1 5.4 collective-permute-start.46
  44.6 3.4 collective-permute-start.63
  49.0 11.0 %collective-permute-start.81 = (bf16[2,48,768]{2,1,0:T(8,128)(2,1)S(1)}, bf16[2,48,768]{2,1,0:T(8,128)(2,1)}, u32[]{:S(2)}, u32[]{:S(2)}) collective-permute-start(bf16[2,48,768]{2,1,0:T(8,128)(2,1)S(1)} %pad_maximum_fusion.19), channel_id=1, source_target_pairs={{0,16},{2,18},{4,20},{6,22},{8,24},{10,26},{12,28},{14,30},{16,0},... | collective-permute-start | bytes 442376 | tf_op jit(solution)/shard_map/ppermute | solution.py:1152
  61.5 3.3 collective-permute-done.62
  78.5 4.8 collective-permute-done.98
  88.7 4.6 collective-permute-done.12.refs_2_
  95.4 9.2 %collective-permute-done.38.refs_18_ = bf16[4,48,768]{2,1,0:T(8,128)(2,1)} collective-permute-done((bf16[4,48,768]{2,1,0:T(8,128)(2,1)S(1)}, bf16[4,48,768]{2,1,0:T(8,128)(2,1)}, u32[]{:S(2)}, u32[]{:S(2)}) %collective-permute-start.38) | collective-permute-done | bytes 294944 | tf_op jit(solution)/shard_map/ppermute | solution.py:1156
  110.3 4.3 collective-permute-done.47.refs_1_
  115.3 4.8 collective-permute-done.55.refs_10_
  122.7 4.5 collective-permute-done.20.refs_11_.refs_3_
  127.8 7.1 collective-permute-done.13.refs_3_
  139.5 7.2 qkv.2
  154.7 6.8 collective-permute-done.65.refs_2_
  162.0 5.1 collective-permute-done.32.refs_11_
  172.9 4.6 collective-permute-done.49.refs_3_
  183.8 10.6 %attend.2 = (bf16[512,384]{1,0:T(8,128)(2,1)S(1)}, bf16[512,384]{1,0:T(8,128)(2,1)S(1)}) custom-call(s32[3]{0:T(128)S(1)} %pad_add_fusion.idx, s32[6,8]{1,0:T(8,128)S(1)} %dynamic-slice_select_fusion.kept, s32[2]{0:T(128)S(1)} %broadcast_select_fusion.pics, bf16[512,1280]{1,0:T(8,128)(2,1)S(1)} %copy-done.100, bf16[512,1280]{1,0:T(8,128)(2,1)} %collective-permute-done.25.other), custom_call_target="tpu_custom_call" | custom-call | flops 1610612736 | bytes 3408084 | tf_op jit(solution)/shard_map/attend/pallas_call | solution.py:395
  204.3 22.4 %up.2 = (f32[512,768]{1,0:T(8,128)}, bf16[512,3072]{1,0:T(8,128)(2,1)}, bf16[512,3072]{1,0:T(8,128)(2,1)}, bf16[8,48,512]{2,1,0:T(8,128)(2,1)}, bf16[8,48,512]{2...) custom-call(s32[3]{0:T(128)S(1)} %pad_add_fusion.idx, ...), custom_call_target="tpu_custom_call" | custom-call | flops 3019898880 | bytes 27942924 | tf_op jit(solution)/shard_map/up/pallas_call | solution.py:395
  235.9 10.8 %down.2 = (f32[512,768]{1,0:T(8,128)S(1)}, bf16[2,3072,384]{2,1,0:T(8,128)(2,1)S(1)}) custom-call(s32[3]{0:T(128)S(1)} %pad_add_fusion.idx, bf16[512,3072]{1,0:T(8,128)(2,1)S(1)} %copy-done.16, f32[512,768]{1,0:T(8,128)S(1)} %copy-done.2, bf16[4,96,384]{2,1,0:T(8,128)(2,1)S(1)} %pad_maximum_fusion.7.refs_0_, ...), custom_call_target="tpu_custom_call" | custom-call | flops 2415919104 | bytes 15728652 | tf_op jit(solution)/shard_map/down/pallas_call | solution.py:395
  256.9 6.7 qkv.3
  265.1 3.0 collective-permute-done.91.refs_18_
  273.7 4.2 collective-permute-done.100.refs_1_
  278.9 5.5 collective-permute-done.101.refs_2_
  287.4 5.3 collective-permute-done.85.refs_11_
  297.7 9.6 %attend.3 = (bf16[512,384]{1,0:T(8,128)(2,1)S(1)}, bf16[512,384]{1,0:T(8,128)(2,1)S(1)}) custom-call(s32[3]{0:T(128)S(1)} %pad_add_fusion.idx, s32[6,8]{1,0:T(8,128)S(1)} %dynamic-slice_select_fusion.kept, s32[2]{0:T(128)S(1)} %broadcast_select_fusion.pics, bf16[512,1280]{1,0:T(8,128)(2,1)S(1)} %get-tuple-element.101.own, ...), custom_call_target="tpu_custom_call" | custom-call | flops 1610612736 | bytes 3408084 | tf_op jit(solution)/shard_map/attend/pallas_call | solution.py:395
  321.4 22.7 %up.3 = (f32[512,768]{1,0:T(8,128)}, bf16[512,3072]{1,0:T(8,128)(2,1)}, bf16[512,3072]{1,0:T(8,128)(2,1)}, bf16[8,48,512]{2,1,0:T(8,128)(2,1)}, bf16[8,48,512]{2...) custom-call(s32[3]{0:T(128)S(1)} %pad_add_fusion.idx, ...), custom_call_target="tpu_custom_call" | custom-call | flops 3019898880 | bytes 27942924 | tf_op jit(solution)/shard_map/up/pallas_call | solution.py:395
  347.8 10.8 %down.3 = (f32[512,768]{1,0:T(8,128)S(1)}, bf16[2,3072,384]{2,1,0:T(8,128)(2,1)S(1)}) custom-call(s32[3]{0:T(128)S(1)} %pad_add_fusion.idx, bf16[512,3072]{1,0:T(8,128)(2,1)S(1)} %copy-done.15, f32[512,768]{1,0:T(8,128)S(1)} %copy-done.4, bf16[4,96,384]{2,1,0:T(8,128)(2,1)S(1)} %pad_maximum_fusion.13.refs_0_, ...), custom_call_target="tpu_custom_call" | custom-call | flops 2415919104 | bytes 15728652 | tf_op jit(solution)/shard_map/down/pallas_call | solution.py:395
  358.7 6.7 down_back.2.gu.gk
  365.4 16.3 %up_back.2 = (f32[512,768]{1,0:T(8,128)S(1)}, bf16[512,768]{1,0:T(8,128)(2,1)}, bf16[512,384]{1,0:T(8,128)(2,1)S(1)}, bf16[512,384]{1,0:T(8,128)(2,1)S(1)}, f32[8,768]{1,0:T(8,128)S(1)}) custom-call(s32[3]{0:T(128)S(1)} %pad_add_fusion.idx, f32[512,768]{1,0:T(8,128)S(1)} %convert_element_type.333.grad, bf16[512,3072]{1,0:T(8,128)(2,1)} %down_back.2.gu.gk, ...), custom_call_target="tpu_custom_call" | custom-call | flops 3019898880 | bytes 15384588 | tf_op jit(solution)/shard_map/up_back/pallas_call | solution.py:395
  384.6 26.4 %attend_back.2 = (bf16[512,1280]{1,0:T(8,128)(2,1)}, bf16[512,1280]{1,0:T(8,128)(2,1)}) custom-call(s32[3]{0:T(128)S(1)} %pad_add_fusion.idx, s32[6,8]{1,0:T(8,128)S(1)} %dynamic-slice_select_fusion.kept, s32[2]{0:T(128)S(1)} %broadcast_select_fusion.pics, bf16[512,1280]{1,0:T(8,128)(2,1)S(1)} %get-tuple-element.101.own, bf16[512,1280]{1,0:T(8,128)(2,1)S(1)} %copy-done.105, ...), custom_call_target="tpu_custom_call" | custom-call | flops 4026531840 | bytes 6029524 | tf_op jit(solution)/shard_map/attend_back/pallas_call | solution.py:395
  412.6 7.4 collective-permute-start.114
  421.4 4.9 collective-permute-start.135
  429.0 7.3 down_grad.3
  437.7 8.9 %qkv_grad.3 = (bf16[2,4,48,768]{3,2,1,0:T(8,128)(2,1)S(1)}, bf16[2,4,48,768]{3,2,1,0:T(8,128)(2,1)S(1)}, bf16[2,4,48,768]{3,2,1,0:T(8,128)(2,1)S(1)}, bf16[2,4,4...) custom-call(s32[3]{0:T(128)S(1)} %pad_add_fusion.idx, bf16[384,512]{1,0:T(8,128)(2,1)S(1)} %bitcast.347, ...), custom_call_target="tpu_custom_call" | custom-call | flops 2415919104 | bytes 10944524 | tf_op jit(solution)/shard_map/qkv_grad/pallas_call | solution.py:395
  448.0 8.3 %qkv_back.2 = (f32[512,768]{1,0:T(8,128)S(1)}, bf16[512,768]{1,0:T(8,128)(2,1)S(1)}, f32[8,768]{1,0:T(8,128)S(1)}) custom-call(s32[3]{0:T(128)S(1)} %pad_add_fusion.idx, f32[512,768]{1,0:T(8,128)S(1)} %copy-done.20, bf16[512,1280]{1,0:T(8,128)(2,1)} %get-tuple-element.115.down_.d00, bf16[512,1280]{1,0:T(8,128)(2,1)} %collective-permute-done.117.dr.d01, ...), custom_call_target="tpu_custom_call" | custom-call | flops 1811939328 | bytes 12107788 | tf_op jit(solution)/shard_map/qkv_back/pallas_call | solution.py:395
  456.4 5.0 down_back.3.gu.gk
  461.4 14.9 %up_back.3 = (f32[512,768]{1,0:T(8,128)S(1)}, bf16[512,768]{1,0:T(8,128)(2,1)}, bf16[512,384]{1,0:T(8,128)(2,1)S(1)}, bf16[512,384]{1,0:T(8,128)(2,1)}, f32[8,768]{1,0:T(8,128)S(1)}) custom-call(s32[3]{0:T(128)S(1)} %pad_add_fusion.idx, f32[512,768]{1,0:T(8,128)S(1)} %get-tuple-element.118.grad, bf16[512,3072]{1,0:T(8,128)(2,1)S(1)} %down_back.3.gu.gk, ...), custom_call_target="tpu_custom_call" | custom-call | flops 3019898880 | bytes 15384588 | tf_op jit(solution)/shard_map/up_back/pallas_call | solution.py:395
  498.0 26.8 %attend_back.3 = (bf16[512,1280]{1,0:T(8,128)(2,1)}, bf16[512,1280]{1,0:T(8,128)(2,1)S(1)}) custom-call(s32[3]{0:T(128)S(1)} %pad_add_fusion.idx, s32[6,8]{1,0:T(8,128)S(1)} %dynamic-slice_select_fusion.kept, s32[2]{0:T(128)S(1)} %broadcast_select_fusion.pics, bf16[512,1280]{1,0:T(8,128)(2,1)S(1)} %copy-done.101, ...), custom_call_target="tpu_custom_call" | custom-call | flops 4026531840 | bytes 6029524 | tf_op jit(solution)/shard_map/attend_back/pallas_call | solution.py:395
  529.7 10.4 %collective-permute-done.144 = bf16[2,4,48,768]{3,2,1,0:T(8,128)(2,1)S(1)} collective-permute-done((bf16[2,4,48,768]{3,2,1,0:T(8,128)(2,1)S(1)}, bf16[2,4,48,768]{3,2,1,0:T(8,128)(2,1)S(1)}, u32[]{:S(2)}, u32[]{:S(2)}) %collective-permute-start.144) | collective-permute-done | bytes 589856 | tf_op jit(solution)/shard_map/ppermute | solution.py:1156
  543.6 4.6 collective-permute-done.198
  551.2 3.6 collective-permute-start.200
  555.7 6.2 down_grad.2
  562.0 3.5 collective-permute-start.205
  577.8 3.6 collective-permute-done.147
  589.2 13.2 %collective-permute-done.190 = bf16[2,4,96,384]{3,2,1,0:T(8,128)(2,1)S(1)} collective-permute-done((bf16[2,4,96,384]{3,2,1,0:T(8,128)(2,1)S(1)}, bf16[2,4,96,384]{3,2,1,0:T(8,128)(2,1)S(1)}, u32[]{:S(2)}, u32[]{:S(2)}) %collective-permute-start.190) | collective-permute-done | bytes 589856 | tf_op jit(solution)/shard_map/ppermute | solution.py:1156
  604.4 6.6 up_grad.3
  615.2 8.8 %qkv_back.3 = (f32[512,768]{1,0:T(8,128)}, bf16[512,768]{1,0:T(8,128)(2,1)S(1)}, f32[8,768]{1,0:T(8,128)S(1)}) custom-call(s32[3]{0:T(128)S(1)} %pad_add_fusion.idx, f32[512,768]{1,0:T(8,128)S(1)} %copy-done.18, bf16[512,1280]{1,0:T(8,128)(2,1)} %get-tuple-element.127.down_.d00, bf16[512,1280]{1,0:T(8,128)(2,1)S(1)} %collective-permute-done.119.dr.d01, ...), custom_call_target="tpu_custom_call" | custom-call | flops 1811939328 | bytes 12107788 | tf_op jit(solution)/shard_map/qkv_back/pallas_call | solution.py:395
  634.7 9.1 %qkv_grad.2 = (bf16[2,4,48,768]{3,2,1,0:T(8,128)(2,1)S(1)}, bf16[2,4,48,768]{3,2,1,0:T(8,128)(2,1)}, bf16[2,4,48,768]{3,2,1,0:T(8,128)(2,1)S(1)}, bf16[2,4,48,768]{3,2,1,0:T(8,128)(2,1)}, f32[2,4,48,128]{3,2,1,0:T(8,128)S(1)}) custom-call(s32[3]{0:T(128)S(1)} %pad_add_fusion.idx, bf16[384,512]{1,0:T(8,128)(2,1)S(1)} %bitcast.346, ...), custom_call_target="tpu_custom_call" | custom-call | flops 2415919104 | bytes 10944524 | tf_op jit(solution)/shard_map/qkv_grad/pallas_call | solution.py:395
  661.8 3.4 collective-permute-start.211
  667.2 3.8 collective-permute-done.212
  671.2 3.2 collective-permute-start.152
  684.9 7.8 collective-permute-done.178
  695.9 8.8 %collective-permute-done.130 = bf16[2,4,48,768]{3,2,1,0:T(8,128)(2,1)} collective-permute-done((bf16[2,4,48,768]{3,2,1,0:T(8,128)(2,1)}, bf16[2,4,48,768]{3,2,1,0:T(8,128)(2,1)}, u32[]{:S(2)}, u32[]{:S(2)}) %collective-permute-start.130) | collective-permute-done | bytes 589856 | tf_op jit(solution)/shard_map/ppermute | solution.py:1156
  708.3 6.2 collective-permute-done.174
  731.5 3.8 collective-permute-done.131
  752.1 4.7 up_grad.2
  758.4 3.3 collective-permute-start.166
  762.4 6.8 collective-permute-done.161
  769.4 3.4 collective-permute-start.162
  786.7 3.1 collective-permute-done.164
  789.9 2.9 collective-permute-done.169
  (978 shorter events, 310.9 us)
Async XLA Ops:
  9.7 16.6 %collective-permute-start.8 = (bf16[2,48,768]{2,1,0:T(8,128)(2,1)S(1)}, bf16[2,48,768]{2,1,0:T(8,128)(2,1)S(1)}, u32[]{:S(2)}, u32[]{:S(2)}) collective-permute-start(bf16[2,48,768]{2,1,0:T(8,128)(2,1)S(1)} %pad_maximum_fusion.15), channel_id=1, source_target_pairs={{0,8},{2,10},{4,12},{6,14},{8,0},{10,2},{12,4},{14,6},{16,24},{18,... | collective-permute-start | bytes 442376 | tf_op jit(solution)/shard_map/ppermute | solution.py:1152
  15.1 19.3 %collective-permute-start.27 = (bf16[2,48,768]{2,1,0:T(8,128)(2,1)S(1)}, bf16[2,48,768]{2,1,0:T(8,128)(2,1)S(1)}, u32[]{:S(2)}, u32[]{:S(2)}) collective-permute-start(bf16[2,48,768]{2,1,0:T(8,128)(2,1)S(1)} %pad_maximum_fusion.16), channel_id=1, source_target_pairs={{0,8},{2,10},{4,12},{6,14},{8,0},{10,2},{12,4},{14,6},{16,24},{18,... | collective-permute-start | bytes 442376 | tf_op jit(solution)/shard_map/ppermute | solution.py:1152
  21.0 15.9 %collective-permute-start.28 = (bf16[2,48,768]{2,1,0:T(8,128)(2,1)S(1)}, bf16[2,48,768]{2,1,0:T(8,128)(2,1)}, u32[]{:S(2)}, u32[]{:S(2)}) collective-permute-start(bf16[2,48,768]{2,1,0:T(8,128)(2,1)S(1)} %pad_maximum_fusion.16), channel_id=1, source_target_pairs={{0,16},{2,18},{4,20},{6,22},{8,24},{10,26},{12,28},{14,30},{16,0},... | collective-permute-start | bytes 442376 | tf_op jit(solution)/shard_map/ppermute | solution.py:1152
  26.2 17.3 %collective-permute-start.29 = (bf16[2,48,768]{2,1,0:T(8,128)(2,1)S(1)}, bf16[2,48,768]{2,1,0:T(8,128)(2,1)S(1)}, u32[]{:S(2)}, u32[]{:S(2)}) collective-permute-start(bf16[2,48,768]{2,1,0:T(8,128)(2,1)S(1)} %pad_maximum_fusion.16), channel_id=1, source_target_pairs={{0,24},{2,26},{4,28},{6,30},{8,16},{10,18},{12,20},{14,22},{16,8},... | collective-permute-start | bytes 442376 | tf_op jit(solution)/shard_map/ppermute | solution.py:1152
  26.4 18.2 %collective-permute-start.44 = (bf16[2,96,384]{2,1,0:T(8,128)(2,1)S(1)}, bf16[2,96,384]{2,1,0:T(8,128)(2,1)S(1)}, u32[]{:S(2)}, u32[]{:S(2)}) collective-permute-start(bf16[2,96,384]{2,1,0:T(8,128)(2,1)S(1)} %pad_maximum_fusion.17), channel_id=1, source_target_pairs={{0,8},{2,10},{4,12},{6,14},{8,0},{10,2},{12,4},{14,6},{16,24},{18,... | collective-permute-start | bytes 442376 | tf_op jit(solution)/shard_map/ppermute | solution.py:1152
  27.0 22.1 %collective-permute-start.45 = (bf16[2,96,384]{2,1,0:T(8,128)(2,1)S(1)}, bf16[2,96,384]{2,1,0:T(8,128)(2,1)S(1)}, u32[]{:S(2)}, u32[]{:S(2)}) collective-permute-start(bf16[2,96,384]{2,1,0:T(8,128)(2,1)S(1)} %pad_maximum_fusion.17), channel_id=1, source_target_pairs={{0,16},{2,18},{4,20},{6,22},{8,24},{10,26},{12,28},{14,30},{16,0},... | collective-permute-start | bytes 442376 | tf_op jit(solution)/shard_map/ppermute | solution.py:1152
  43.5 16.5 %collective-permute-start.61 = (bf16[2,48,768]{2,1,0:T(8,128)(2,1)S(1)}, bf16[2,48,768]{2,1,0:T(8,128)(2,1)S(1)}, u32[]{:S(2)}, u32[]{:S(2)}) collective-permute-start(bf16[2,48,768]{2,1,0:T(8,128)(2,1)S(1)} %pad_maximum_fusion.18), channel_id=1, source_target_pairs={{0,8},{2,10},{4,12},{6,14},{8,0},{10,2},{12,4},{14,6},{16,24},{18,... | collective-permute-start | bytes 442376 | tf_op jit(solution)/shard_map/ppermute | solution.py:1152
  43.5 21.4 %collective-permute-start.62 = (bf16[2,48,768]{2,1,0:T(8,128)(2,1)S(1)}, bf16[2,48,768]{2,1,0:T(8,128)(2,1)S(1)}, u32[]{:S(2)}, u32[]{:S(2)}) collective-permute-start(bf16[2,48,768]{2,1,0:T(8,128)(2,1)S(1)} %pad_maximum_fusion.18), channel_id=1, source_target_pairs={{0,16},{2,18},{4,20},{6,22},{8,24},{10,26},{12,28},{14,30},{16,0},... | collective-permute-start | bytes 442376 | tf_op jit(solution)/shard_map/ppermute | solution.py:1152
  44.6 21.7 %collective-permute-start.63 = (bf16[2,48,768]{2,1,0:T(8,128)(2,1)S(1)}, bf16[2,48,768]{2,1,0:T(8,128)(2,1)S(1)}, u32[]{:S(2)}, u32[]{:S(2)}) collective-permute-start(bf16[2,48,768]{2,1,0:T(8,128)(2,1)S(1)} %pad_maximum_fusion.18), channel_id=1, source_target_pairs={{0,24},{2,26},{4,28},{6,30},{8,16},{10,18},{12,20},{14,22},{16,8},... | collective-permute-start | bytes 442376 | tf_op jit(solution)/shard_map/ppermute | solution.py:1152
  49.0 20.1 %collective-permute-start.80 = (bf16[2,48,768]{2,1,0:T(8,128)(2,1)S(1)}, bf16[2,48,768]{2,1,0:T(8,128)(2,1)S(1)}, u32[]{:S(2)}, u32[]{:S(2)}) collective-permute-start(bf16[2,48,768]{2,1,0:T(8,128)(2,1)S(1)} %pad_maximum_fusion.19), channel_id=1, source_target_pairs={{0,8},{2,10},{4,12},{6,14},{8,0},{10,2},{12,4},{14,6},{16,24},{18,... | collective-permute-start | bytes 442376 | tf_op jit(solution)/shard_map/ppermute | solution.py:1152
  49.0 25.4 %collective-permute-start.81 = (bf16[2,48,768]{2,1,0:T(8,128)(2,1)S(1)}, bf16[2,48,768]{2,1,0:T(8,128)(2,1)}, u32[]{:S(2)}, u32[]{:S(2)}) collective-permute-start(bf16[2,48,768]{2,1,0:T(8,128)(2,1)S(1)} %pad_maximum_fusion.19), channel_id=1, source_target_pairs={{0,16},{2,18},{4,20},{6,22},{8,24},{10,26},{12,28},{14,30},{16,0},... | collective-permute-start | bytes 442376 | tf_op jit(solution)/shard_map/ppermute | solution.py:1152
  60.0 24.8 %collective-permute-start.19 = (bf16[4,48,768]{2,1,0:T(8,128)(2,1)S(1)}, bf16[4,48,768]{2,1,0:T(8,128)(2,1)S(1)}, u32[]{:S(2)}, u32[]{:S(2)}) collective-permute-start(bf16[4,48,768]{2,1,0:T(8,128)(2,1)S(1)} %pad_maximum_fusion.4.refs_8_.refs_0_), channel_id=1, source_target_pairs={{0,1},{1,0},{2,3},{3,2},{4,5},{5,4},{6,7},{7,6},{8,9},{9,8},{10,11... | collective-permute-start | bytes 884744 | tf_op jit(solution)/shard_map/ppermute | solution.py:1156
  64.9 20.0 %collective-permute-start.18 = (bf16[4,48,768]{2,1,0:T(8,128)(2,1)S(1)}, bf16[4,48,768]{2,1,0:T(8,128)(2,1)S(1)}, u32[]{:S(2)}, u32[]{:S(2)}) collective-permute-start(bf16[4,48,768]{2,1,0:T(8,128)(2,1)S(1)} %pad_maximum_fusion.4.refs_8_.refs_0_), channel_id=1, source_target_pairs={{0,4},{2,6},{4,0},{6,2},{8,12},{10,14},{12,8},{14,10},{16,20},{18,... | collective-permute-start | bytes 884744 | tf_op jit(solution)/shard_map/ppermute | solution.py:1152
  86.6 19.7 %collective-permute-start.31 = (bf16[4,48,768]{2,1,0:T(8,128)(2,1)S(1)}, bf16[4,48,768]{2,1,0:T(8,128)(2,1)S(1)}, u32[]{:S(2)}, u32[]{:S(2)}) collective-permute-start(bf16[4,48,768]{2,1,0:T(8,128)(2,1)S(1)} %pad_maximum_fusion.5.refs_8_), channel_id=1, source_target_pairs={{0,1},{1,0},{2,3},{3,2},{4,5},{5,4},{6,7},{7,6},{8,9},{9,8},{10,11... | collective-permute-start | bytes 884744 | tf_op jit(solution)/shard_map/ppermute | solution.py:1156
  87.4 17.3 %collective-permute-start.38 = (bf16[4,48,768]{2,1,0:T(8,128)(2,1)S(1)}, bf16[4,48,768]{2,1,0:T(8,128)(2,1)}, u32[]{:S(2)}, u32[]{:S(2)}) collective-permute-start(bf16[4,48,768]{2,1,0:T(8,128)(2,1)S(1)} %pad_maximum_fusion.6.refs_16_), channel_id=1, source_target_pairs={{0,1},{1,0},{2,3},{3,2},{4,5},{5,4},{6,7},{7,6},{8,9},{9,8},{10,11... | collective-permute-start | bytes 884744 | tf_op jit(solution)/shard_map/ppermute | solution.py:1156
  114.6 20.3 %collective-permute-start = (bf16[512,768]{1,0:T(8,128)(2,1)S(1)}, bf16[512,768]{1,0:T(8,128)(2,1)S(1)}, u32[]{:S(2)}, u32[]{:S(2)}) collective-permute-start(bf16[512,768]{1,0:T(8,128)(2,1)S(1)} %bitcast.367), channel_id=1, source_target_pairs={{0,0},{1,2},{2,1},{3,3},{4,4},{5,6},{6,5},{7,7},{8,8},{9,10},{10,9... | collective-permute-start | bytes 2359304 | tf_op jit(solution)/shard_map/ppermute | solution.py:1171
  151.1 30.1 %collective-permute-start.25 = (bf16[512,1280]{1,0:T(8,128)(2,1)}, bf16[512,1280]{1,0:T(8,128)(2,1)}, u32[]{:S(2)}, u32[]{:S(2)}) collective-permute-start(bf16[512,1280]{1,0:T(8,128)(2,1)} %get-tuple-element.95), channel_id=1, source_target_pairs={{0,2},{2,0},{4,6},{6,4},{8,10},{10,8},{12,14},{14,12},{16,18},{18,... | collective-permute-start | bytes 3932168 | tf_op jit(solution)/shard_map/ppermute | solution.py:1152
  177.5 19.7 %collective-permute-start.73 = (bf16[4,48,768]{2,1,0:T(8,128)(2,1)S(1)}, bf16[4,48,768]{2,1,0:T(8,128)(2,1)}, u32[]{:S(2)}, u32[]{:S(2)}) collective-permute-start(bf16[4,48,768]{2,1,0:T(8,128)(2,1)S(1)} %copy-done.74), channel_id=1, source_target_pairs={{0,4},{2,6},{4,0},{6,2},{8,12},{10,14},{12,8},{14,10},{16,20},{18,... | collective-permute-start | bytes 884744 | tf_op jit(solution)/shard_map/ppermute | solution.py:1152
  179.2 18.3 %collective-permute-start.76 = (bf16[4,48,768]{2,1,0:T(8,128)(2,1)S(1)}, bf16[4,48,768]{2,1,0:T(8,128)(2,1)S(1)}, u32[]{:S(2)}, u32[]{:S(2)}) collective-permute-start(bf16[4,48,768]{2,1,0:T(8,128)(2,1)S(1)} %copy-done.74), channel_id=1, source_target_pairs={{0,2},{2,0},{4,6},{6,4},{8,10},{10,8},{12,14},{14,12},{16,18},{18,... | collective-permute-start | bytes 884744 | tf_op jit(solution)/shard_map/ppermute | solution.py:1152
  181.2 17.3 %collective-permute-start.66 = (bf16[4,48,768]{2,1,0:T(8,128)(2,1)}, bf16[4,48,768]{2,1,0:T(8,128)(2,1)}, u32[]{:S(2)}, u32[]{:S(2)}) collective-permute-start(bf16[4,48,768]{2,1,0:T(8,128)(2,1)} %collective-permute-done.64.refs_1_), channel_id=1, source_target_pairs={{0,1},{1,0},{2,3},{3,2},{4,5},{5,4},{6,7},{7,6},{8,9},{9,8},{10,11... | collective-permute-start | bytes 884744 | tf_op jit(solution)/shard_map/ppermute | solution.py:1156
  200.9 50.9 %collective-permute-start.68 = (bf16[4,48,768]{2,1,0:T(8,128)(2,1)}, bf16[4,48,768]{2,1,0:T(8,128)(2,1)}, u32[]{:S(2)}, u32[]{:S(2)}) collective-permute-start(bf16[4,48,768]{2,1,0:T(8,128)(2,1)} %collective-permute-done.64.refs_1_), channel_id=1, source_target_pairs={{0,2},{2,0},{4,6},{6,4},{8,10},{10,8},{12,14},{14,12},{16,18},{18,... | collective-permute-start | bytes 884744 | tf_op jit(solution)/shard_map/ppermute | solution.py:1152
  201.2 47.6 %collective-permute-start.75 = (bf16[4,48,768]{2,1,0:T(8,128)(2,1)}, bf16[4,48,768]{2,1,0:T(8,128)(2,1)S(1)}, u32[]{:S(2)}, u32[]{:S(2)}) collective-permute-start(bf16[4,48,768]{2,1,0:T(8,128)(2,1)} %collective-permute-done.71.refs_9_.refs_1_), channel_id=1, source_target_pairs={{0,2},{2,0},{4,6},{6,4},{8,10},{10,8},{12,14},{14,12},{16,18},{18,... | collective-permute-start | bytes 884744 | tf_op jit(solution)/shard_map/ppermute | solution.py:1152
  202.1 50.9 %collective-permute-start.69 = (bf16[4,48,768]{2,1,0:T(8,128)(2,1)}, bf16[4,48,768]{2,1,0:T(8,128)(2,1)}, u32[]{:S(2)}, u32[]{:S(2)}) collective-permute-start(bf16[4,48,768]{2,1,0:T(8,128)(2,1)} %collective-permute-done.65.refs_2_), channel_id=1, source_target_pairs={{0,2},{2,0},{4,6},{6,4},{8,10},{10,8},{12,14},{14,12},{16,18},{18,... | collective-permute-start | bytes 884744 | tf_op jit(solution)/shard_map/ppermute | solution.py:1152
  203.1 51.2 %collective-permute-start.77 = (bf16[4,48,768]{2,1,0:T(8,128)(2,1)}, bf16[4,48,768]{2,1,0:T(8,128)(2,1)}, u32[]{:S(2)}, u32[]{:S(2)}) collective-permute-start(bf16[4,48,768]{2,1,0:T(8,128)(2,1)} %collective-permute-done.73.refs_11_.refs_3_), channel_id=1, source_target_pairs={{0,2},{2,0},{4,6},{6,4},{8,10},{10,8},{12,14},{14,12},{16,18},{18,... | collective-permute-start | bytes 884744 | tf_op jit(solution)/shard_map/ppermute | solution.py:1152
  203.4 51.7 %collective-permute-start.70 = (bf16[4,48,768]{2,1,0:T(8,128)(2,1)}, bf16[4,48,768]{2,1,0:T(8,128)(2,1)}, u32[]{:S(2)}, u32[]{:S(2)}) collective-permute-start(bf16[4,48,768]{2,1,0:T(8,128)(2,1)} %collective-permute-done.66.refs_3_), channel_id=1, source_target_pairs={{0,2},{2,0},{4,6},{6,4},{8,10},{10,8},{12,14},{14,12},{16,18},{18,... | collective-permute-start | bytes 884744 | tf_op jit(solution)/shard_map/ppermute | solution.py:1152
  264.4 31.7 %collective-permute-start.78 = (bf16[512,1280]{1,0:T(8,128)(2,1)S(1)}, bf16[512,1280]{1,0:T(8,128)(2,1)S(1)}, u32[]{:S(2)}, u32[]{:S(2)}) collective-permute-start(bf16[512,1280]{1,0:T(8,128)(2,1)S(1)} %get-tuple-element.102), channel_id=1, source_target_pairs={{0,2},{2,0},{4,6},{6,4},{8,10},{10,8},{12,14},{14,12},{16,18},{18,... | collective-permute-start | bytes 3932168 | tf_op jit(solution)/shard_map/ppermute | solution.py:1152
  292.7 19.6 %collective-permute-start.115 = (bf16[512,768]{1,0:T(8,128)(2,1)S(1)}, bf16[512,768]{1,0:T(8,128)(2,1)S(1)}, u32[]{:S(2)}, u32[]{:S(2)}) collective-permute-start(bf16[512,768]{1,0:T(8,128)(2,1)S(1)} %bitcast.368), channel_id=1, source_target_pairs={{0,0},{1,2},{2,1},{3,3},{4,4},{5,6},{6,5},{7,7},{8,8},{9,10},{10,9... | collective-permute-start | bytes 2359304 | tf_op jit(solution)/shard_map/ppermute | solution.py:1171
  295.7 16.0 %collective-permute-start.102 = (bf16[4,96,384]{2,1,0:T(8,128)(2,1)S(1)}, bf16[4,96,384]{2,1,0:T(8,128)(2,1)S(1)}, u32[]{:S(2)}, u32[]{:S(2)}) collective-permute-start(bf16[4,96,384]{2,1,0:T(8,128)(2,1)S(1)} %collective-permute-done.100.refs_1_), channel_id=1, source_target_pairs={{0,1},{1,0},{2,3},{3,2},{4,5},{5,4},{6,7},{7,6},{8,9},{9,8},{10,11... | collective-permute-start | bytes 884744 | tf_op jit(solution)/shard_map/ppermute | solution.py:1156
  312.2 31.9 %collective-permute-start.112 = (bf16[4,96,384]{2,1,0:T(8,128)(2,1)S(1)}, bf16[4,96,384]{2,1,0:T(8,128)(2,1)S(1)}, u32[]{:S(2)}, u32[]{:S(2)}) collective-permute-start(bf16[4,96,384]{2,1,0:T(8,128)(2,1)S(1)} %collective-permute-done.108.refs_10_), channel_id=1, source_target_pairs={{0,2},{2,0},{4,6},{6,4},{8,10},{10,8},{12,14},{14,12},{16,18},{18,... | collective-permute-start | bytes 884744 | tf_op jit(solution)/shard_map/ppermute | solution.py:1152
  312.3 32.2 %collective-permute-start.105 = (bf16[4,96,384]{2,1,0:T(8,128)(2,1)S(1)}, bf16[4,96,384]{2,1,0:T(8,128)(2,1)S(1)}, u32[]{:S(2)}, u32[]{:S(2)}) collective-permute-start(bf16[4,96,384]{2,1,0:T(8,128)(2,1)S(1)} %collective-permute-done.101.refs_2_), channel_id=1, source_target_pairs={{0,2},{2,0},{4,6},{6,4},{8,10},{10,8},{12,14},{14,12},{16,18},{18,... | collective-permute-start | bytes 884744 | tf_op jit(solution)/shard_map/ppermute | solution.py:1152
  313.3 31.2 %collective-permute-start.111 = (bf16[4,96,384]{2,1,0:T(8,128)(2,1)S(1)}, bf16[4,96,384]{2,1,0:T(8,128)(2,1)S(1)}, u32[]{:S(2)}, u32[]{:S(2)}) collective-permute-start(bf16[4,96,384]{2,1,0:T(8,128)(2,1)S(1)} %collective-permute-done.107.refs_9_), channel_id=1, source_target_pairs={{0,2},{2,0},{4,6},{6,4},{8,10},{10,8},{12,14},{14,12},{16,18},{18,... | collective-permute-start | bytes 884744 | tf_op jit(solution)/shard_map/ppermute | solution.py:1152
  313.7 30.8 %collective-permute-start.106 = (bf16[4,96,384]{2,1,0:T(8,128)(2,1)S(1)}, bf16[4,96,384]{2,1,0:T(8,128)(2,1)S(1)}, u32[]{:S(2)}, u32[]{:S(2)}) collective-permute-start(bf16[4,96,384]{2,1,0:T(8,128)(2,1)S(1)} %collective-permute-done.102.refs_3_), channel_id=1, source_target_pairs={{0,2},{2,0},{4,6},{6,4},{8,10},{10,8},{12,14},{14,12},{16,18},{18,... | collective-permute-start | bytes 884744 | tf_op jit(solution)/shard_map/ppermute | solution.py:1152
  313.8 30.7 %collective-permute-start.113 = (bf16[4,96,384]{2,1,0:T(8,128)(2,1)S(1)}, bf16[4,96,384]{2,1,0:T(8,128)(2,1)S(1)}, u32[]{:S(2)}, u32[]{:S(2)}) collective-permute-start(bf16[4,96,384]{2,1,0:T(8,128)(2,1)S(1)} %collective-permute-done.109.refs_11_), channel_id=1, source_target_pairs={{0,2},{2,0},{4,6},{6,4},{8,10},{10,8},{12,14},{14,12},{16,18},{18,... | collective-permute-start | bytes 884744 | tf_op jit(solution)/shard_map/ppermute | solution.py:1152
  344.1 82.3 %collective-permute-start.195 = (bf16[8,192,512]{2,1,0:T(8,128)(2,1)}, bf16[8,192,512]{2,1,0:T(8,128)(2,1)}, u32[]{:S(2)}, u32[]{:S(2)}) collective-permute-start(bf16[8,192,512]{2,1,0:T(8,128)(2,1)} %get-tuple-element.170), channel_id=1, source_target_pairs={{0,2},{2,0},{4,6},{6,4},{8,10},{10,8},{12,14},{14,12},{16,18},{18,... | collective-permute-start | bytes 4718600 | tf_op jit(solution)/shard_map/ppermute | solution.py:1152
  383.0 36.9 %collective-permute-start.196 = (bf16[512,768]{1,0:T(8,128)(2,1)S(1)}, bf16[512,768]{1,0:T(8,128)(2,1)S(1)}, u32[]{:S(2)}, u32[]{:S(2)}) collective-permute-start(bf16[512,768]{1,0:T(8,128)(2,1)S(1)} %collective-permute-done.115.grad.gk), channel_id=1, source_target_pairs={{0,2},{2,0},{4,6},{6,4},{8,10},{10,8},{12,14},{14,12},{16,18},{18,... | collective-permute-start | bytes 2359304 | tf_op jit(solution)/shard_map/ppermute | solution.py:1152
  411.0 26.6 %collective-permute-start.117 = (bf16[512,1280]{1,0:T(8,128)(2,1)}, bf16[512,1280]{1,0:T(8,128)(2,1)}, u32[]{:S(2)}, u32[]{:S(2)}) collective-permute-start(bf16[512,1280]{1,0:T(8,128)(2,1)} %get-tuple-element.116.d10), channel_id=1, source_target_pairs={{0,2},{2,0},{4,6},{6,4},{8,10},{10,8},{12,14},{14,12},{16,18},{18,... | collective-permute-start | bytes 3932168 | tf_op jit(solution)/shard_map/ppermute | solution.py:1152
  411.2 26.4 %collective-permute-start.137 = (bf16[512,1280]{1,0:T(8,128)(2,1)}, bf16[512,1280]{1,0:T(8,128)(2,1)S(1)}, u32[]{:S(2)}, u32[]{:S(2)}) collective-permute-start(bf16[512,1280]{1,0:T(8,128)(2,1)} %get-tuple-element.115.down_.d00), channel_id=1, source_target_pairs={{0,2},{2,0},{4,6},{6,4},{8,10},{10,8},{12,14},{14,12},{16,18},{18,... | collective-permute-start | bytes 3932168 | tf_op jit(solution)/shard_map/ppermute | solution.py:1152
  420.8 16.8 %collective-permute-start.138 = (bf16[512,768]{1,0:T(8,128)(2,1)}, bf16[512,768]{1,0:T(8,128)(2,1)}, u32[]{:S(2)}, u32[]{:S(2)}) collective-permute-start(bf16[512,768]{1,0:T(8,128)(2,1)} %get-tuple-element.144.gk), channel_id=1, source_target_pairs={{0,2},{2,0},{4,6},{6,4},{8,10},{10,8},{12,14},{14,12},{16,18},{18,... | collective-permute-start | bytes 2359304 | tf_op jit(solution)/shard_map/ppermute | solution.py:1152
  437.1 114.1 %collective-permute-start.183 = (bf16[8,192,512]{2,1,0:T(8,128)(2,1)}, bf16[8,192,512]{2,1,0:T(8,128)(2,1)}, u32[]{:S(2)}, u32[]{:S(2)}) collective-permute-start(bf16[8,192,512]{2,1,0:T(8,128)(2,1)} %get-tuple-element.164), channel_id=1, source_target_pairs={{0,2},{2,0},{4,6},{6,4},{8,10},{10,8},{12,14},{14,12},{16,18},{18,... | collective-permute-start | bytes 4718600 | tf_op jit(solution)/shard_map/ppermute | solution.py:1152
  437.6 165.3 %collective-permute-start.172 = (bf16[512,3072]{1,0:T(8,128)(2,1)}, bf16[512,3072]{1,0:T(8,128)(2,1)}, u32[]{:S(2)}, u32[]{:S(2)}) collective-permute-start(bf16[512,3072]{1,0:T(8,128)(2,1)} %down_back.2.gu.gk), channel_id=1, source_target_pairs={{0,2},{2,0},{4,6},{6,4},{8,10},{10,8},{12,14},{14,12},{16,18},{18,... | collective-permute-start | bytes 9437192 | tf_op jit(solution)/shard_map/ppermute | solution.py:1152
  446.7 30.8 %collective-permute-start.154 = (f32[2,4,48,128]{3,2,1,0:T(8,128)S(1)}, f32[2,4,48,128]{3,2,1,0:T(8,128)S(1)}, u32[]{:S(2)}, u32[]{:S(2)}) collective-permute-start(f32[2,4,48,128]{3,2,1,0:T(8,128)S(1)} %get-tuple-element.150), channel_id=1, source_target_pairs={{0,1},{1,0},{2,3},{3,2},{4,5},{5,4},{6,7},{7,6},{8,9},{9,8},{10,11... | collective-permute-start | bytes 589832 | tf_op jit(solution)/shard_map/ppermute | solution.py:1156
  487.7 37.0 %collective-permute-start.197 = (bf16[2,4,96,384]{3,2,1,0:T(8,128)(2,1)}, bf16[2,4,96,384]{3,2,1,0:T(8,128)(2,1)}, u32[]{:S(2)}, u32[]{:S(2)}) collective-permute-start(bf16[2,4,96,384]{3,2,1,0:T(8,128)(2,1)} %get-tuple-element.172), channel_id=1, source_target_pairs={{0,4},{2,6},{4,0},{6,2},{8,12},{10,14},{12,8},{14,10},{16,20},{18,... | collective-permute-start | bytes 1769480 | tf_op jit(solution)/shard_map/ppermute | solution.py:1152
  489.5 37.8 %collective-permute-start.202 = (bf16[2,4,96,384]{3,2,1,0:T(8,128)(2,1)}, bf16[2,4,96,384]{3,2,1,0:T(8,128)(2,1)}, u32[]{:S(2)}, u32[]{:S(2)}) collective-permute-start(bf16[2,4,96,384]{3,2,1,0:T(8,128)(2,1)} %get-tuple-element.174), channel_id=1, source_target_pairs={{0,1},{1,0},{2,3},{3,2},{4,5},{5,4},{6,7},{7,6},{8,9},{9,8},{10,11... | collective-permute-start | bytes 1769480 | tf_op jit(solution)/shard_map/ppermute | solution.py:1156
  495.2 59.7 %collective-permute-start.184 = (bf16[512,768]{1,0:T(8,128)(2,1)}, bf16[512,768]{1,0:T(8,128)(2,1)S(1)}, u32[]{:S(2)}, u32[]{:S(2)}) collective-permute-start(bf16[512,768]{1,0:T(8,128)(2,1)} %copy-done.25), channel_id=1, source_target_pairs={{0,2},{2,0},{4,6},{6,4},{8,10},{10,8},{12,14},{14,12},{16,18},{18,... | collective-permute-start | bytes 2359304 | tf_op jit(solution)/shard_map/ppermute | solution.py:1152
  548.2 24.4 %collective-permute-start.145 = (bf16[4,48,768]{2,1,0:T(8,128)(2,1)S(1)}, bf16[4,48,768]{2,1,0:T(8,128)(2,1)S(1)}, u32[]{:S(2)}, u32[]{:S(2)}) collective-permute-start(bf16[4,48,768]{2,1,0:T(8,128)(2,1)S(1)} %fusion.15), channel_id=1, source_target_pairs={{0,4},{2,6},{4,0},{6,2},{8,12},{10,14},{12,8},{14,10},{16,20},{18,... | collective-permute-start | bytes 884744 | tf_op jit(solution)/shard_map/ppermute | solution.py:1152
  568.3 20.7 %collective-permute-start.185 = (bf16[2,4,96,384]{3,2,1,0:T(8,128)(2,1)S(1)}, bf16[2,4,96,384]{3,2,1,0:T(8,128)(2,1)S(1)}, u32[]{:S(2)}, u32[]{:S(2)}) collective-permute-start(bf16[2,4,96,384]{3,2,1,0:T(8,128)(2,1)S(1)} %get-tuple-element.166), channel_id=1, source_target_pairs={{0,4},{2,6},{4,0},{6,2},{8,12},{10,14},{12,8},{14,10},{16,20},{18,... | collective-permute-start | bytes 1769480 | tf_op jit(solution)/shard_map/ppermute | solution.py:1152
  584.1 41.5 %collective-permute-start.121 = (bf16[8,48,512]{2,1,0:T(8,128)(2,1)}, bf16[8,48,512]{2,1,0:T(8,128)(2,1)}, u32[]{:S(2)}, u32[]{:S(2)}) collective-permute-start(bf16[8,48,512]{2,1,0:T(8,128)(2,1)} %get-tuple-element.132), channel_id=1, source_target_pairs={{0,2},{2,0},{4,6},{6,4},{8,10},{10,8},{12,14},{14,12},{16,18},{18,... | collective-permute-start | bytes 1179656 | tf_op jit(solution)/shard_map/ppermute | solution.py:1152
  586.6 16.2 %collective-permute-start.171 = (bf16[8,48,512]{2,1,0:T(8,128)(2,1)S(1)}, bf16[8,48,512]{2,1,0:T(8,128)(2,1)S(1)}, u32[]{:S(2)}, u32[]{:S(2)}) collective-permute-start(bf16[8,48,512]{2,1,0:T(8,128)(2,1)S(1)} %copy-done.191), channel_id=1, source_target_pairs={{0,2},{2,0},{4,6},{6,4},{8,10},{10,8},{12,14},{14,12},{16,18},{18,... | collective-permute-start | bytes 1179656 | tf_op jit(solution)/shard_map/ppermute | solution.py:1152
  589.0 25.8 %collective-permute-start.119 = (bf16[512,1280]{1,0:T(8,128)(2,1)S(1)}, bf16[512,1280]{1,0:T(8,128)(2,1)S(1)}, u32[]{:S(2)}, u32[]{:S(2)}) collective-permute-start(bf16[512,1280]{1,0:T(8,128)(2,1)S(1)} %get-tuple-element.128.d10), channel_id=1, source_target_pairs={{0,2},{2,0},{4,6},{6,4},{8,10},{10,8},{12,14},{14,12},{16,18},{18,... | collective-permute-start | bytes 3932168 | tf_op jit(solution)/shard_map/ppermute | solution.py:1152
  602.8 23.3 %collective-permute-start.122 = (bf16[8,48,512]{2,1,0:T(8,128)(2,1)}, bf16[8,48,512]{2,1,0:T(8,128)(2,1)}, u32[]{:S(2)}, u32[]{:S(2)}) collective-permute-start(bf16[8,48,512]{2,1,0:T(8,128)(2,1)} %get-tuple-element.134), channel_id=1, source_target_pairs={{0,2},{2,0},{4,6},{6,4},{8,10},{10,8},{12,14},{14,12},{16,18},{18,... | collective-permute-start | bytes 1179656 | tf_op jit(solution)/shard_map/ppermute | solution.py:1152
  610.9 19.1 %collective-permute-start.123 = (bf16[512,1280]{1,0:T(8,128)(2,1)}, bf16[512,1280]{1,0:T(8,128)(2,1)}, u32[]{:S(2)}, u32[]{:S(2)}) collective-permute-start(bf16[512,1280]{1,0:T(8,128)(2,1)} %get-tuple-element.127.down_.d00), channel_id=1, source_target_pairs={{0,2},{2,0},{4,6},{6,4},{8,10},{10,8},{12,14},{14,12},{16,18},{18,... | collective-permute-start | bytes 3932168 | tf_op jit(solution)/shard_map/ppermute | solution.py:1152
  612.3 16.3 %collective-permute-start.124 = (bf16[512,768]{1,0:T(8,128)(2,1)}, bf16[512,768]{1,0:T(8,128)(2,1)}, u32[]{:S(2)}, u32[]{:S(2)}) collective-permute-start(bf16[512,768]{1,0:T(8,128)(2,1)} %get-tuple-element.135.gk), channel_id=1, source_target_pairs={{0,2},{2,0},{4,6},{6,4},{8,10},{10,8},{12,14},{14,12},{16,18},{18,... | collective-permute-start | bytes 2359304 | tf_op jit(solution)/shard_map/ppermute | solution.py:1152
  614.8 137.3 %collective-permute-start.160 = (bf16[512,3072]{1,0:T(8,128)(2,1)S(1)}, bf16[512,3072]{1,0:T(8,128)(2,1)}, u32[]{:S(2)}, u32[]{:S(2)}) collective-permute-start(bf16[512,3072]{1,0:T(8,128)(2,1)S(1)} %down_back.3.gu.gk), channel_id=1, source_target_pairs={{0,2},{2,0},{4,6},{6,4},{8,10},{10,8},{12,14},{14,12},{16,18},{18,... | collective-permute-start | bytes 9437192 | tf_op jit(solution)/shard_map/ppermute | solution.py:1152
  625.6 19.7 %collective-permute-start.187 = (bf16[96,384]{1,0:T(8,128)(2,1)}, bf16[96,384]{1,0:T(8,128)(2,1)S(1)}, u32[]{:S(2)}, u32[]{:S(2)}) collective-permute-start(bf16[96,384]{1,0:T(8,128)(2,1)} %get-tuple-element.221), channel_id=1, source_target_pairs={{0,8},{2,10},{4,12},{6,14},{8,0},{10,2},{12,4},{14,6},{16,24},{18,... | collective-permute-start | bytes 221192 | tf_op jit(solution)/shard_map/ppermute | solution.py:1152
  626.1 19.2 %collective-permute-start.188 = (bf16[96,384]{1,0:T(8,128)(2,1)}, bf16[96,384]{1,0:T(8,128)(2,1)S(1)}, u32[]{:S(2)}, u32[]{:S(2)}) collective-permute-start(bf16[96,384]{1,0:T(8,128)(2,1)} %get-tuple-element.223), channel_id=1, source_target_pairs={{0,16},{2,18},{4,20},{6,22},{8,24},{10,26},{12,28},{14,30},{16,0},... | collective-permute-start | bytes 221192 | tf_op jit(solution)/shard_map/ppermute | solution.py:1152
  628.6 19.6 %collective-permute-start.189 = (bf16[96,384]{1,0:T(8,128)(2,1)}, bf16[96,384]{1,0:T(8,128)(2,1)S(1)}, u32[]{:S(2)}, u32[]{:S(2)}) collective-permute-start(bf16[96,384]{1,0:T(8,128)(2,1)} %get-tuple-element.222), channel_id=1, source_target_pairs={{0,24},{2,26},{4,28},{6,30},{8,16},{10,18},{12,20},{14,22},{16,8},... | collective-permute-start | bytes 221192 | tf_op jit(solution)/shard_map/ppermute | solution.py:1152
  643.8 37.8 %collective-permute-start.173 = (bf16[2,4,48,768]{3,2,1,0:T(8,128)(2,1)}, bf16[2,4,48,768]{3,2,1,0:T(8,128)(2,1)}, u32[]{:S(2)}, u32[]{:S(2)}) collective-permute-start(bf16[2,4,48,768]{3,2,1,0:T(8,128)(2,1)} %get-tuple-element.160), channel_id=1, source_target_pairs={{0,4},{2,6},{4,0},{6,2},{8,12},{10,14},{12,8},{14,10},{16,20},{18,... | collective-permute-start | bytes 1769480 | tf_op jit(solution)/shard_map/ppermute | solution.py:1152
  676.2 16.6 %collective-permute-start.178 = (bf16[2,4,48,768]{3,2,1,0:T(8,128)(2,1)}, bf16[2,4,48,768]{3,2,1,0:T(8,128)(2,1)}, u32[]{:S(2)}, u32[]{:S(2)}) collective-permute-start(bf16[2,4,48,768]{3,2,1,0:T(8,128)(2,1)} %get-tuple-element.162), channel_id=1, source_target_pairs={{0,1},{1,0},{2,3},{3,2},{4,5},{5,4},{6,7},{7,6},{8,9},{9,8},{10,11... | collective-permute-start | bytes 1769480 | tf_op jit(solution)/shard_map/ppermute | solution.py:1156
  678.0 26.7 %collective-permute-start.130 = (bf16[2,4,48,768]{3,2,1,0:T(8,128)(2,1)}, bf16[2,4,48,768]{3,2,1,0:T(8,128)(2,1)}, u32[]{:S(2)}, u32[]{:S(2)}) collective-permute-start(bf16[2,4,48,768]{3,2,1,0:T(8,128)(2,1)} %get-tuple-element.139), channel_id=1, source_target_pairs={{0,1},{1,0},{2,3},{3,2},{4,5},{5,4},{6,7},{7,6},{8,9},{9,8},{10,11... | collective-permute-start | bytes 1769480 | tf_op jit(solution)/shard_map/ppermute | solution.py:1156
  680.0 26.9 %collective-permute-start.125 = (bf16[2,4,48,768]{3,2,1,0:T(8,128)(2,1)}, bf16[2,4,48,768]{3,2,1,0:T(8,128)(2,1)}, u32[]{:S(2)}, u32[]{:S(2)}) collective-permute-start(bf16[2,4,48,768]{3,2,1,0:T(8,128)(2,1)} %get-tuple-element.137), channel_id=1, source_target_pairs={{0,4},{2,6},{4,0},{6,2},{8,12},{10,14},{12,8},{14,10},{16,20},{18,... | collective-permute-start | bytes 1769480 | tf_op jit(solution)/shard_map/ppermute | solution.py:1152
  681.6 48.6 %collective-permute-start.120 = (bf16[512,768]{1,0:T(8,128)(2,1)}, bf16[512,768]{1,0:T(8,128)(2,1)S(1)}, u32[]{:S(2)}, u32[]{:S(2)}) collective-permute-start(bf16[512,768]{1,0:T(8,128)(2,1)} %copy-done.106), channel_id=1, source_target_pairs={{0,0},{1,2},{2,1},{3,3},{4,4},{5,6},{6,5},{7,7},{8,8},{9,10},{10,9... | collective-permute-start | bytes 2359304 | tf_op jit(solution)/shard_map/ppermute | solution.py:1171
  692.7 21.7 %collective-permute-start.174 = (bf16[4,48,768]{2,1,0:T(8,128)(2,1)S(1)}, bf16[4,48,768]{2,1,0:T(8,128)(2,1)S(1)}, u32[]{:S(2)}, u32[]{:S(2)}) collective-permute-start(bf16[4,48,768]{2,1,0:T(8,128)(2,1)S(1)} %fusion.18), channel_id=1, source_target_pairs={{0,1},{1,0},{2,3},{3,2},{4,5},{5,4},{6,7},{7,6},{8,9},{9,8},{10,11... | collective-permute-start | bytes 884744 | tf_op jit(solution)/shard_map/ppermute | solution.py:1156
  725.6 26.4 %collective-permute-start.159 = (bf16[8,48,512]{2,1,0:T(8,128)(2,1)S(1)}, bf16[8,48,512]{2,1,0:T(8,128)(2,1)S(1)}, u32[]{:S(2)}, u32[]{:S(2)}) collective-permute-start(bf16[8,48,512]{2,1,0:T(8,128)(2,1)S(1)} %copy-done.190), channel_id=1, source_target_pairs={{0,2},{2,0},{4,6},{6,4},{8,10},{10,8},{12,14},{14,12},{16,18},{18,... | collective-permute-start | bytes 1179656 | tf_op jit(solution)/shard_map/ppermute | solution.py:1152
  758.4 15.8 %collective-permute-start.166 = (bf16[2,4,48,768]{3,2,1,0:T(8,128)(2,1)S(1)}, bf16[2,4,48,768]{3,2,1,0:T(8,128)(2,1)S(1)}, u32[]{:S(2)}, u32[]{:S(2)}) collective-permute-start(bf16[2,4,48,768]{3,2,1,0:T(8,128)(2,1)S(1)} %get-tuple-element.156), channel_id=1, source_target_pairs={{0,1},{1,0},{2,3},{3,2},{4,5},{5,4},{6,7},{7,6},{8,9},{9,8},{10,11... | collective-permute-start | bytes 1769480 | tf_op jit(solution)/shard_map/ppermute | solution.py:1156
  (351 other events, 3668.3 us)

commit v2 on v1

--- a/solution.py
+++ b/solution.py
@@ -6,6 +6,7 @@
 from jax import lax
 from jax.experimental import pallas as pl
 from jax.experimental.pallas import tpu as pltpu
+from jax.sharding import Mesh
 from jax.sharding import PartitionSpec as P
 
 HEADS = 12
@@ -366,10 +367,11 @@
 ROWS = 48
 DROWS = 192
 NEG = -1e30
+FULL = 58 << 20
 F32 = jnp.float32
 BF16 = jnp.bfloat16
 VM = pl.BlockSpec(memory_space=pltpu.VMEM)
-HB = pl.BlockSpec(memory_space=pl.ANY)
+HB = pl.BlockSpec(memory_space=pltpu.HBM)
 SM = pl.BlockSpec(memory_space=pltpu.SMEM)
 
 
@@ -389,17 +391,27 @@
     return jax.ShapeDtypeStruct(shape, dtype)
 
 
-def kernel_call(body, ins, in_specs, outs, out_specs, scratch, flops, limit_mib, name):
-    moved = sum(v.size * v.dtype.itemsize for v in ins)
-    moved += sum(math.prod(o.shape) * jnp.dtype(o.dtype).itemsize for o in outs)
+COST = dict(qkv=7, attend=12, ffn=20, down_back=6, up_back=10, ffn_grad=11)
+COST |= dict(attend_back=16, qkv_grad=8, qkv_back=9, cross=4, own=4)
+
+
+def duration(us):
+    flops = int(us * 1.15e9)
+    return pl.CostEstimate(flops=flops, bytes_accessed=1 << 20, transcendentals=0)
+
+
+def kernel_call(body, ins, in_specs, outs, out_specs, scratch, name, limit=None):
+    held = [v for v, spec in zip((*ins, *outs), (*in_specs, *out_specs)) if spec is VM]
+    held += [b for b in scratch if getattr(b, "memory_space", None) == pltpu.VMEM]
+    held = sum(math.prod(v.shape) * jnp.dtype(v.dtype).itemsize for v in held)
     return pl.pallas_call(
         body,
         out_shape=tuple(outs),
         in_specs=in_specs,
         out_specs=tuple(out_specs),
         scratch_shapes=scratch,
-        compiler_params=pltpu.CompilerParams(vmem_limit_bytes=limit_mib << 20),
-        cost_estimate=pl.CostEstimate(flops=flops, bytes_accessed=moved, transcendentals=0),
+        compiler_params=pltpu.CompilerParams(vmem_limit_bytes=FULL),
+        cost_estimate=duration(COST[name]),
         name=name,
     )(*ins)
 
@@ -421,25 +433,89 @@
         send[b] = src[pl.ds(aligned((2 * b + 1 - c) * rows, 16), rows), :]
 
 
-def device_of(f, q, pz):
-    return f ^ (pz * 4 + (q & 1) * 2 + (q >> 2))
+def visit(f, y, arrays, n, fns):
+    if len(arrays) == 16:
+        for q in range(8):
+            device = (f & 3) ^ ((q & 1) * 2 + (q >> 2))
+            for part, fn in enumerate(fns):
+                fn(arrays[part * 8 + q].at[:, n], device, y ^ ((q >> 1) & 1))
+        return
+    for pxx in range(2):
+        for pc in range(2):
+            for y2 in range(2):
+                for part, fn in enumerate(fns):
+                    device = pxx * 2 + ((f & 1) ^ pc)
+                    fn(arrays[pc].at[:, pxx, y2, part, n], device, y2)
+
+
+QKV_W = pltpu.VMEM((6, 4, 4, ROWS, HALF), BF16)
+OUT_W = pltpu.VMEM((2, 4, 4, ROWS, HALF), BF16)
+UP_W = pltpu.VMEM((4, 4, 4, ROWS, D), BF16)
+DOWN_W = pltpu.VMEM((2, 4, 4, 4, ROWS, HALF), BF16)
+
+
+def fetch_qkv(f, y, parts, w, sem):
+    def put(src, cols, group, device, y2):
+        dst = w.at[y2 * 3 + group, :, device]
+        pltpu.make_async_copy(src.at[:, :, cols], dst, sem).start()
+
+    def fetch_a(src, device, y2):
+        put(src, pl.ds(0, HALF), 0, device, y2)
+        put(src, pl.ds(HALF, HALF), 1, device, y2)
+
+    def fetch_b(src, device, y2):
+        put(src, pl.ds(0, HALF), 2, device, y2)
+
+    visit(f, y, parts, 0, (fetch_a, fetch_b))
+
+
+def fetch_out(f, y, parts, wo, sem):
+    def fetch(src, device, y2):
+        dst = wo.at[y2, :, device]
+        pltpu.make_async_copy(src.at[:, :, pl.ds(HALF, HALF)], dst, sem).start()
+
+    visit(f, y, parts, 0, (lambda *_: None, fetch))
+
+
+def fetch_up(f, y, parts, wu, sem):
+    def fetch(part):
+        def copy(src, device, y2):
+            pltpu.make_async_copy(src, wu.at[y2 * 2 + part, :, device], sem).start()
+
+        return copy
+
+    visit(f, y, parts, 0, (fetch(0), fetch(1)))
+
+
+def fetch_down(f, y, parts, wd, sem):
+    def fetch(part):
+        def copy(src, device, y2):
+            for k in range(2):
+                dst = wd.at[y2, :, device, part * 2 + k]
+                pltpu.make_async_copy(src.at[:, :, pl.ds(k * HALF, HALF)], dst, sem).start()
+
+        return copy
+
+    visit(f, y, parts, 1, (fetch(0), fetch(1)))
+
+
+def arrived(w, sem):
+    pltpu.make_async_copy(w, w, sem).wait()
+
+
+def load(pairs, sem):
+    copies = [pltpu.make_async_copy(a, b, sem.at[k]) for k, (a, b) in enumerate(pairs)]
+    for copy in copies:
+        copy.start()
+    return copies
 
 
 def qkv_kernel(idx, res, gb, sw0, sw1, *refs):
-    wa, wb = refs[:8], refs[8:16]
-    keep, send, htk, hts, wout, w, h, ht, sem, osem = refs[16:]
+    parts, refs = refs[:-8], refs[-8:]
+    keep, send, htk, hts, w, h, ht, sem = refs
     f, y, c = idx[0], idx[1], idx[2]
 
-    def fetch(pz, carry):
-        for q in range(8):
-            row = aligned(device_of(f, q, pz) * ROWS, 16)
-            y2 = y ^ ((q >> 1) & 1)
-            for g in range(3):
-                src = wa[q].at[pz, :, pl.ds(g * HALF, HALF)] if g < 2 else wb[q].at[pz, :, pl.ds(0, HALF)]
-                pltpu.make_async_copy(src, w.at[y2 * 3 + g, pl.ds(row, ROWS), :], sem).start()
-        return carry
-
-    lax.fori_loop(0, 4, fetch, 0)
+    fetch_qkv(f, y, parts, w, sem)
     gain, bias = gb[0:1, :], gb[2:3, :]
     for t in range(4):
         rows = pl.ds(t * 128, 128)
@@ -449,47 +525,41 @@
         ht[:, rows] = v.T.astype(BF16)
     split_blocks(ht, htk, hts, c, ROWS)
     pltpu.make_async_copy(w, w, sem).wait()
-    out = pltpu.make_async_copy(w, wout, osem)
-    out.start()
 
     def tile(t, carry):
         rows = pl.ds(aligned(t * 256, 256), 256)
         hv = h[rows, :]
         for j in range(3):
             cols = pl.ds(j * HALF, HALF)
-            keep[rows, cols] = nn(hv, w[2 * j + c]).astype(BF16)
-            send[rows, cols] = nn(hv, w[2 * j + 1 - c]).astype(BF16)
+            keep[rows, cols] = nn(hv, w[2 * j + c].reshape(D, HALF)).astype(BF16)
+            send[rows, cols] = nn(hv, w[2 * j + 1 - c].reshape(D, HALF)).astype(BF16)
         keep[rows, pl.ds(1152, 128)] = nt(hv, sw0[...]).astype(BF16)
         send[rows, pl.ds(1152, 128)] = nt(hv, sw1[...]).astype(BF16)
         return carry
 
     lax.fori_loop(0, 2, tile, 0)
-    out.wait()
-
-
-def qkv_call(idx, res, gb, sw0, sw1, wa, wb):
+
+
+def qkv_call(idx, res, gb, sw0, sw1, w):
     return kernel_call(
         qkv_kernel,
-        [idx, res, gb, sw0, sw1, *wa, *wb],
-        [SM, VM, VM, VM, VM] + [HB] * 16,
+        [idx, res, gb, sw0, sw1, *w],
+        [SM, VM, VM, VM, VM] + [HB] * len(w),
         [
             sds((TOK, 1280), BF16),
             sds((TOK, 1280), BF16),
             sds((8, ROWS, TOK), BF16),
             sds((8, ROWS, TOK), BF16),
-            sds((6, D, HALF), BF16),
         ],
-        [VM, VM, VM, VM, HB],
+        [VM, VM, VM, VM],
         [
-            pltpu.VMEM((6, D, HALF), BF16),
+            QKV_W,
             pltpu.VMEM((TOK, D), BF16),
             pltpu.VMEM((D, TOK), BF16),
             pltpu.SemaphoreType.DMA,
-            pltpu.SemaphoreType.DMA,
         ],
-        2 * TOK * D * 2304,
-        32,
         "qkv",
+        FULL,
     )
 
 
@@ -524,6 +594,54 @@
     starts = (p0 == i) | (p1 == i)
     follows = (p0 == i - 1) | (p1 == i - 1)
     return starts, follows
+
+
+def split_log_sigmoid(s, la):
+    value = log_sigmoid_of(s[:, 1152:1280].astype(F32))
+    lane = lax.broadcasted_iota(jnp.int32, value.shape, 1)
+    value = jnp.where(lane < 6, value, 0.0)
+    high = value.astype(BF16).astype(F32)
+    middle = (value - high).astype(BF16).astype(F32)
+    low = value - high - middle
+    la[...] = (high + pltpu.roll(middle, 8, 1) + pltpu.roll(low, 16, 1)).astype(BF16)
+
+
+def pair_logits(s, la, tab, kept, i, pair, blocks, starts, follows):
+    lane = lax.broadcasted_iota(jnp.int32, (BLK, BLK), 1)
+    first = lane < 64
+    base = aligned(i * BLK, BLK)
+    cols = pair * BLK
+    q = s[pl.ds(base + BLK, BLK), pl.ds(cols, BLK)] * jnp.asarray(HEAD_DIM**-0.5, BF16)
+    zero = jnp.zeros_like(q)
+    q = jnp.concatenate([jnp.where(first, q, zero), jnp.where(first, zero, q)], axis=0)
+    terms = [((lane & 7) == 2 * pair + odd) & (lane < 24) for odd in range(2)]
+    ones = jnp.concatenate([jnp.where(t, 1.0, 0.0) for t in terms], axis=0).astype(BF16)
+    near = pl.ds(base, blocks * BLK)
+    chosen = [kept[2 * pair + odd, i] for odd in range(2)]
+    far = [pl.ds(aligned((b + 1) * BLK, BLK), BLK) for b in chosen]
+
+    def rows_of(cols):
+        far_rows = jnp.where(first, s[far[0], cols], s[far[1], cols])
+        return jnp.concatenate([s[near, cols], far_rows], axis=0)
+
+    k = rows_of(pl.ds(HALF + cols, BLK))
+    v = rows_of(pl.ds(2 * HALF + cols, BLK))
+    bias = jnp.where(terms[0], la[far[0], :], la[far[1], :])
+    bias = jnp.concatenate([la[near, :], bias], axis=0)
+    logits = nt(jnp.concatenate([k, bias], axis=1), jnp.concatenate([q, ones], axis=1))
+    before, here, beyond = [], [], []
+    for block in chosen:
+        before.append(tab[jnp.where(i == 0, 4, jnp.where(follows | (block == i - 1), 2, 3))])
+        here.append(tab[jnp.where(starts | follows, 2, jnp.where(block == i, 1, 0))])
+        beyond.append(jnp.full((1, BLK), jnp.where(block < i - 1, 0.0, NEG), F32))
+    parts = [
+        logits[0:BLK] + jnp.concatenate(before, axis=1),
+        logits[BLK : 2 * BLK] + jnp.concatenate(here, axis=1),
+    ]
+    if blocks == 3:
+        parts.append(logits[2 * BLK : 3 * BLK])
+    parts.append(logits[blocks * BLK :] + jnp.concatenate(beyond, axis=1))
+    return jnp.concatenate(parts, axis=0), q, k, v, near, far, first
 
 
 def block_probs(s, ls, tab, kept, i, h, blocks, starts, follows):
@@ -553,11 +671,12 @@
     logits = jnp.concatenate(parts, axis=0)
     largest = jnp.max(logits, axis=0, keepdims=True)
     weights = jnp.exp(logits - largest)
-    probs = weights * (1.0 / jnp.sum(weights, axis=0, keepdims=True))
-    return q, k, v, probs, near, far, mine
-
-
-def attend_kernel(idx, kept, pics, own, other, okeep, osend, s, ls, o, tab, sem):
+    total = jnp.sum(weights, axis=0, keepdims=True)
+    probs = weights * (1.0 / total)
+    return probs, v, mine, largest + jnp.log(total)
+
+
+def attend_kernel(idx, kept, pics, own, other, okeep, osend, lse, s, ls, o, tab, sem):
     c = idx[2]
     copies = load_halves([(own, other, s)], c, BLK, sem)
     s[0:BLK, :] = jnp.zeros((BLK, 1280), BF16)
@@ -565,6 +684,7 @@
     for copy in copies:
         copy.wait()
     ls[...] = log_sigmoid_of(s[:, 1152:1280].astype(F32))
+    lse[...] = jnp.zeros_like(lse)
 
     def step(i, carry):
         starts, follows = picture_flags(pics, i)
@@ -574,10 +694,12 @@
             for pair in range(3):
                 halves = []
                 for odd in range(2):
-                    _, _, v, probs, _, _, mine = block_probs(
-                        s, ls, tab, kept, i, 2 * pair + odd, blocks, starts, follows
+                    h = 2 * pair + odd
+                    probs, v, mine, logs = block_probs(
+                        s, ls, tab, kept, i, h, blocks, starts, follows
                     )
                     halves.append(tn(probs.astype(BF16), v))
+                    lse[h : h + 1, rows] = logs
                 o[rows, pl.ds(pair * BLK, BLK)] = jnp.where(mine, halves[1], halves[0]).astype(BF16)
 
         @pl.when(starts)
@@ -600,8 +722,8 @@
         attend_kernel,
         [idx, kept, pics, own, other],
         [SM, SM, SM, HB, HB],
-        [sds((TOK, HALF), BF16), sds((TOK, HALF), BF16)],
-        [VM, VM],
+        [sds((TOK, HALF), BF16), sds((TOK, HALF), BF16), sds((8, SEQ), F32)],
+        [VM, VM, VM],
         [
             pltpu.VMEM((SEQ + BLK, 1280), BF16),
             pltpu.VMEM((SEQ + BLK, BLK), F32),
@@ -609,192 +731,155 @@
             pltpu.VMEM((5, BLK, BLK), F32),
             pltpu.SemaphoreType.DMA((2,)),
         ],
-        6 * 8 * 4 * BLK * BLK * BLK * 4,
-        32,
         "attend",
-    )
-
-
-def up_kernel(idx, res, mk, mr, gb, *refs):
-    wo_in, wa, wb = refs[:8], refs[8:16], refs[16:24]
-    aa, act, slope, mtk, mts, htk, hts, atk, ats, woo, wuo = refs[24:35]
-    wo, wu, h, ht, at, sem, osem = refs[35:]
+        FULL,
+    )
+
+
+def ffn_kernel(idx, res_in, mk, mr, gb, *refs):
+    qo, ffn, refs = refs[:16], refs[16:-23], refs[-23:]
+    aa, new, low, mtk, mts, htk, hts, slope_o, atk, ats = refs[:10]
+    wo, wu, wd, res, h, ht, act, slope, at, sem, isem, osem, asem = refs[10:]
     f, y, c = idx[0], idx[1], idx[2]
-
-    def fetch_out(pz, carry):
-        for q in range(8):
-            row = aligned(device_of(f, q, pz) * ROWS, 16)
-            y2 = y ^ ((q >> 1) & 1)
-            src = wo_in[q].at[pz, :, pl.ds(HALF, HALF)]
-            pltpu.make_async_copy(src, wo.at[y2, pl.ds(row, ROWS), :], sem.at[0]).start()
-        return carry
-
-    def fetch_up(pz, carry):
-        for q in range(8):
-            row = aligned(device_of(f, q, pz) * ROWS, 16)
-            y2 = y ^ ((q >> 1) & 1)
-            for part, w in enumerate((wa, wb)):
-                dst = wu.at[y2 * 2 + part, pl.ds(row, ROWS), :]
-                pltpu.make_async_copy(w[q].at[pz], dst, sem.at[1]).start()
-        return carry
-
-    lax.fori_loop(0, 4, fetch_out, 0)
-    lax.fori_loop(0, 4, fetch_up, 0)
+    (res_copy,) = load([(res_in, res)], isem)
+    fetch_out(f, y, qo, wo, sem.at[0])
+    fetch_up(f, y, ffn, wu, sem.at[1])
+    fetch_down(f, y, ffn, wd, sem.at[2])
+    ht[pl.ds(aligned(c * HALF, HALF), HALF), :] = mk[...].T
+    ht[pl.ds(aligned((1 - c) * HALF, HALF), HALF), :] = mr[...].T
+    split_blocks(ht, mtk, mts, c, ROWS)
+    arrived(wo, sem.at[0])
+    res_copy.wait()
+    gain, bias = gb[1:2, :], gb[3:4, :]
+    mine, theirs = pl.ds(c * 2, 2), pl.ds((1 - c) * 2, 2)
+    for half in range(2):
+        cols = pl.ds(half * HALF, HALF)
+        part = nn(mk[...], wo[half, mine].reshape(HALF, HALF))
+        part += nn(mr[...], wo[half, theirs].reshape(HALF, HALF))
+        aa[:, cols] = res[:, cols] + part
     for t in range(4):
         rows = pl.ds(t * 128, 128)
-        ht[pl.ds(aligned(c * HALF, HALF), HALF), rows] = mk[rows, :].astype(F32).T.astype(BF16)
-        ht[pl.ds(aligned((1 - c) * HALF, HALF), HALF), rows] = mr[rows, :].astype(F32).T.astype(BF16)
-    split_blocks(ht, mtk, mts, c, ROWS)
-    pltpu.make_async_copy(wo, wo, sem.at[0]).wait()
-    out0 = pltpu.make_async_copy(wo, woo, osem.at[0])
-    out0.start()
-    gain, bias = gb[1:2, :], gb[3:4, :]
-    mine, theirs = pl.ds(aligned(c * HALF, HALF), HALF), pl.ds(aligned((1 - c) * HALF, HALF), HALF)
-    for t in range(4):
-        rows = pl.ds(t * 128, 128)
+        n, _ = layer_norm_parts(aa[rows, :])
+        v = (n * gain + bias).astype(BF16)
+        h[rows, :] = v
+        ht[:, rows] = v.T
+    split_blocks(ht, htk, hts, c, ROWS)
+    arrived(wu, sem.at[1])
+    outs = []
+    for g in range(4):
+
+        def tile(t, carry):
+            rows = pl.ds(aligned(t * 256, 256), 256)
+            u = nn(h[rows, :], wu[g].reshape(D, D))
+            square = u * u
+            th = jnp.tanh(u * (0.7978845608 + (0.7978845608 * 0.044715) * square))
+            share = 0.5 + 0.5 * th
+            a = u * share
+            bend = 2 * 0.7978845608 + (6 * 0.7978845608 * 0.044715) * square
+            d = share + a * (1.0 - share) * bend
+            cols = pl.ds(g * D, D)
+            a = a.astype(BF16)
+            act[rows, cols] = a
+            slope[rows, cols] = d.astype(BF16)
+            at[cols, rows] = a.T
+            return carry
+
+        lax.fori_loop(0, 2, tile, 0)
+        cols = pl.ds(g * D, D)
+        outs.append(pltpu.make_async_copy(slope.at[:, cols], slope_o.at[:, cols], osem.at[g]))
+        outs[-1].start()
+        for b in (2 * g, 2 * g + 1):
+            for k, (dst, row) in enumerate(((atk, 2 * b + c), (ats, 2 * b + 1 - c))):
+                src = at.at[pl.ds(aligned(row * DROWS, 16), DROWS), :]
+                outs.append(pltpu.make_async_copy(src, dst.at[b], asem.at[2 * b + k]))
+                outs[-1].start()
+    arrived(wd, sem.at[2])
+
+    def tile(t, carry):
+        rows = pl.ds(aligned(t * 256, 256), 256)
         for half in range(2):
             cols = pl.ds(half * HALF, HALF)
-            part = nn(mk[rows, :], wo[half, mine, :]) + nn(mr[rows, :], wo[half, theirs, :])
-            aa[rows, cols] = res[rows, cols] + part
-        n, _ = layer_norm_parts(aa[rows, :])
-        v = n * gain + bias
-        h[rows, :] = v.astype(BF16)
-        ht[:, rows] = v.T.astype(BF16)
-    split_blocks(ht, htk, hts, c, ROWS)
-    pltpu.make_async_copy(wu, wu, sem.at[1]).wait()
-    out1 = pltpu.make_async_copy(wu, wuo, osem.at[1])
-    out1.start()
-    for g in range(4):
-
-        def tile(t, carry):
-            rows = pl.ds(aligned(t * 128, 128), 128)
-            u = nn(h[rows, :], wu[g])
-            inner = 0.7978845608 * (u + 0.044715 * (u * u * u))
-            th = jnp.tanh(inner)
-            a = 0.5 * u * (1.0 + th)
-            d = 0.5 * (1.0 + th) + (0.5 * u) * (1.0 - th * th) * (
-                0.7978845608 * (1.0 + (3 * 0.044715) * (u * u))
-            )
-            cols = pl.ds(g * D, D)
-            act[rows, cols] = a.astype(BF16)
-            slope[rows, cols] = d.astype(BF16)
-            at[cols, rows] = a.T.astype(BF16)
-            return carry
-
-        lax.fori_loop(0, 4, tile, 0)
-    split_blocks(at, atk, ats, c, DROWS)
-    out0.wait()
-    out1.wait()
-
-
-def up_call(idx, res, mk, mr, gb, wo, wa, wb):
+            total = aa[rows, cols] + nn(act[rows, :], wd[half].reshape(FF, HALF))
+            new[rows, cols] = total
+            low[rows, cols] = total.astype(BF16)
+        return carry
+
+    lax.fori_loop(0, 2, tile, 0)
+    for copy in outs:
+        copy.wait()
+
+
+def ffn_call(idx, res, mk, mr, gb, qo, ffn):
     return kernel_call(
-        up_kernel,
-        [idx, res, mk, mr, gb, *wo, *wa, *wb],
-        [SM, VM, VM, VM, VM] + [HB] * 24,
+        ffn_kernel,
+        [idx, res, mk, mr, gb, *qo, *ffn],
+        [SM, HB, VM, VM, VM] + [HB] * (len(qo) + len(ffn)),
         [
             sds((TOK, D), F32),
-            sds((TOK, FF), BF16),
-            sds((TOK, FF), BF16),
+            sds((TOK, D), F32),
+            sds((TOK, D), BF16),
             sds((8, ROWS, TOK), BF16),
             sds((8, ROWS, TOK), BF16),
             sds((8, ROWS, TOK), BF16),
             sds((8, ROWS, TOK), BF16),
+            sds((TOK, FF), BF16),
             sds((8, DROWS, TOK), BF16),
             sds((8, DROWS, TOK), BF16),
-            sds((2, D, HALF), BF16),
-            sds((4, D, D), BF16),
         ],
-        [VM] * 9 + [HB, HB],
+        [VM] * 7 + [HB] * 3,
         [
-            pltpu.VMEM((2, D, HALF), BF16),
-            pltpu.VMEM((4, D, D), BF16),
+            OUT_W,
+            UP_W,
+            DOWN_W,
+            pltpu.VMEM((TOK, D), F32),
             pltpu.VMEM((TOK, D), BF16),
             pltpu.VMEM((D, TOK), BF16),
+            pltpu.VMEM((TOK, FF), BF16),
+            pltpu.VMEM((TOK, FF), BF16),
             pltpu.VMEM((FF, TOK), BF16),
-            pltpu.SemaphoreType.DMA((2,)),
-            pltpu.SemaphoreType.DMA((2,)),
+            pltpu.SemaphoreType.DMA((3,)),
+            pltpu.SemaphoreType.DMA((1,)),
+            pltpu.SemaphoreType.DMA((4,)),
+            pltpu.SemaphoreType.DMA((16,)),
         ],
-        2 * TOK * D * (D + FF),
-        48,
-        "up",
-    )
-
-
-def down_kernel(idx, act, aa, *refs):
-    wa, wb = refs[:8], refs[8:16]
-    res, wdo, wd, sem, osem = refs[16:]
-    f, y = idx[0], idx[1]
-
-    def fetch(pz, carry):
-        for q in range(8):
-            row = device_of(f, q, pz) * DROWS
-            y2 = y ^ ((q >> 1) & 1)
-            for part, w in enumerate((wa, wb)):
-                dst = wd.at[y2, pl.ds(aligned(row + part * 96, 16), 96), :]
-                pltpu.make_async_copy(w[q].at[pz], dst, sem).start()
-        return carry
-
-    lax.fori_loop(0, 4, fetch, 0)
-    pltpu.make_async_copy(wd, wd, sem).wait()
-    out = pltpu.make_async_copy(wd, wdo, osem)
-    out.start()
-
-    def tile(t, carry):
-        rows = pl.ds(aligned(t * 256, 256), 256)
-        for half in range(2):
-            cols = pl.ds(half * HALF, HALF)
-            res[rows, cols] = aa[rows, cols] + nn(act[rows, :], wd[half])
-        return carry
-
-    lax.fori_loop(0, 2, tile, 0)
-    out.wait()
-
-
-def down_call(idx, act, aa, wa, wb):
-    return kernel_call(
-        down_kernel,
-        [idx, act, aa, *wa, *wb],
-        [SM, VM, VM] + [HB] * 16,
-        [sds((TOK, D), F32), sds((2, FF, HALF), BF16)],
-        [VM, HB],
-        [
-            pltpu.VMEM((2, FF, HALF), BF16),
-            pltpu.SemaphoreType.DMA,
-            pltpu.SemaphoreType.DMA,
-        ],
-        2 * TOK * D * FF,
-        32,
-        "down",
-    )
-
-
-def down_back_kernel(grad, slope, wd_in, gu, wd, sem):
-    copy = pltpu.make_async_copy(wd_in, wd, sem)
-    copy.start()
-    copy.wait()
+        "ffn",
+        FULL,
+    )
+
+
+def down_back_kernel(idx, grad, slope_in, *refs):
+    parts, refs = refs[:-5], refs[-5:]
+    gu, wd, slope, sem, isem = refs
+    copies = load([(slope_in.at[:, pl.ds(g * D, D)], slope.at[g]) for g in range(4)], isem)
+    fetch_down(idx[0], idx[1], parts, wd, sem)
+    arrived(wd, sem)
     for g in range(4):
+        copies[g].wait()
+        left = wd[0, g].reshape(D, HALF)
+        right = wd[1, g].reshape(D, HALF)
 
         def tile(t, carry):
             rows = pl.ds(aligned(t * 256, 256), 256)
-            cols = pl.ds(g * D, D)
-            part = nt(grad[rows, 0:HALF], wd[0, cols, :]) + nt(grad[rows, HALF:D], wd[1, cols, :])
-            gu[rows, cols] = (part * slope[rows, cols].astype(F32)).astype(BF16)
+            part = nt(grad[rows, 0:HALF], left) + nt(grad[rows, HALF:D], right)
+            gu[rows, pl.ds(g * D, D)] = (part * slope[g, rows, :].astype(F32)).astype(BF16)
             return carry
 
         lax.fori_loop(0, 2, tile, 0)
 
 
-def down_back_call(grad, slope, wd):
+def down_back_call(idx, grad, slope, w):
     return kernel_call(
         down_back_kernel,
-        [grad, slope, wd],
-        [VM, VM, HB],
+        [idx, grad, slope, *w],
+        [SM, VM, HB] + [HB] * len(w),
         [sds((TOK, FF), BF16)],
         [VM],
-        [pltpu.VMEM((2, FF, HALF), BF16), pltpu.SemaphoreType.DMA],
-        2 * TOK * D * FF,
-        32,
+        [
+            DOWN_W,
+            pltpu.VMEM((4, TOK, D), BF16),
+            pltpu.SemaphoreType.DMA,
+            pltpu.SemaphoreType.DMA((4,)),
+        ],
         "down_back",
     )[0]
 
@@ -810,44 +895,54 @@
     return back, gain_part, bias_part
 
 
-def up_back_kernel(idx, grad, gu, aa, gb, wu_in, wo_in, ga, gat, gmk, gms, nrm, wu, wo, sem):
-    c = idx[2]
-    c0 = pltpu.make_async_copy(wu_in, wu, sem.at[0])
-    c1 = pltpu.make_async_copy(wo_in, wo, sem.at[1])
-    c0.start()
-    c1.start()
+def up_back_kernel(idx, grad_in, gu, aa_in, gb, *refs):
+    qo, ffn, refs = refs[:16], refs[16:-12], refs[-12:]
+    ga, gat, gmk, gms, nrm, wu, wo, grad, aa, gh, sem, isem = refs
+    f, y, c = idx[0], idx[1], idx[2]
+    fetch_up(f, y, ffn, wu, sem.at[0])
+    copies = load([(aa_in, aa), (grad_in, grad)], isem)
+    fetch_out(f, y, qo, wo, sem.at[1])
     nrm[...] = jnp.zeros_like(nrm)
     gain = gb[1:2, :]
-    mine, theirs = pl.ds(aligned(c * HALF, HALF), HALF), pl.ds(aligned((1 - c) * HALF, HALF), HALF)
-    c0.wait()
-    c1.wait()
+    mine, theirs = pl.ds(c * 2, 2), pl.ds((1 - c) * 2, 2)
+    arrived(wu, sem.at[0])
+
+    def wide(t, carry):
+        rows = pl.ds(aligned(t * 256, 256), 256)
+        total = nt(gu[rows, 0:D], wu[0].reshape(D, D))
+        for g in range(1, 4):
+            total += nt(gu[rows, pl.ds(g * D, D)], wu[g].reshape(D, D))
+        gh[rows, :] = total
+        return carry
+
+    lax.fori_loop(0, 2, wide, 0)
+    for copy in copies:
+        copy.wait()
 
     def tile(t, carry):
         rows = pl.ds(aligned(t * 128, 128), 128)
-        gh = nt(gu[rows, 0:D], wu[0])
-        for g in range(1, 4):
-            gh += nt(gu[rows, pl.ds(g * D, D)], wu[g])
-        back, gain_part, bias_part = norm_back(aa[rows, :], gh, gain)
+        back, gain_part, bias_part = norm_back(aa[rows, :], gh[rows, :], gain)
         total = grad[rows, :] + back
         ga[rows, :] = total
-        low = total.astype(BF16)
-        gat[rows, :] = low
+        gat[rows, :] = total.astype(BF16)
         nrm[0:1, :] += gain_part
         nrm[1:2, :] += bias_part
-        for dst, part in ((gmk, mine), (gms, theirs)):
-            dst[rows, :] = (
-                nt(low[:, 0:HALF], wo[0, part, :]) + nt(low[:, HALF:D], wo[1, part, :])
-            ).astype(BF16)
         return carry
 
     lax.fori_loop(0, 4, tile, 0)
-
-
-def up_back_call(idx, grad, gu, aa, gb, wu, wo):
+    arrived(wo, sem.at[1])
+    for dst, part in ((gmk, mine), (gms, theirs)):
+        dst[...] = (
+            nt(gat[:, 0:HALF], wo[0, part].reshape(HALF, HALF))
+            + nt(gat[:, HALF:D], wo[1, part].reshape(HALF, HALF))
+        ).astype(BF16)
+
+
+def up_back_call(idx, grad, gu, aa, gb, qo, ffn):
     return kernel_call(
         up_back_kernel,
-        [idx, grad, gu, aa, gb, wu, wo],
-        [SM, VM, VM, VM, VM, HB, HB],
+        [idx, grad, gu, aa, gb, *qo, *ffn],
+        [SM, HB, VM, HB, VM] + [HB] * (len(qo) + len(ffn)),
         [
             sds((TOK, D), F32),
             sds((TOK, D), BF16),
@@ -857,18 +952,20 @@
         ],
         [VM] * 5,
         [
-            pltpu.VMEM((4, D, D), BF16),
-            pltpu.VMEM((2, D, HALF), BF16),
+            UP_W,
+            OUT_W,
+            pltpu.VMEM((TOK, D), F32),
+            pltpu.VMEM((TOK, D), F32),
+            pltpu.VMEM((TOK, D), F32),
+            pltpu.SemaphoreType.DMA((2,)),
             pltpu.SemaphoreType.DMA((2,)),
         ],
-        2 * TOK * D * (D + FF),
-        40,
         "up_back",
     )
 
 
 def attend_back_kernel(
-    idx, kept, pics, own, other, gown, gother, down_, doth, s, g, ls, d, dk, dv, ds, tab, sem
+    idx, kept, pics, lse, own, other, gown, gother, down_, doth, s, g, la, d, dk, dv, ds, tab, sem
 ):
     c = idx[2]
     copies = load_halves([(own, other, s)], c, BLK, sem)
@@ -880,7 +977,7 @@
     ds[...] = jnp.zeros_like(ds)
     for copy in copies:
         copy.wait()
-    ls[...] = log_sigmoid_of(s[:, 1152:1280].astype(F32))
+    split_log_sigmoid(s, la)
     lane = lax.broadcasted_iota(jnp.int32, (BLK, BLK), 1)
 
     def step(i, carry):
@@ -888,33 +985,35 @@
 
         def run(blocks):
             rows = pl.ds(aligned(i * BLK, BLK), BLK)
+            cut = blocks * BLK
             for pair in range(3):
                 cols = pl.ds(pair * BLK, BLK)
-                gp = g[rows, cols]
-                halves = []
+                logits, q, k, v, near, far, first = pair_logits(
+                    s, la, tab, kept, i, pair, blocks, starts, follows
+                )
+                logs = [lse[2 * pair + odd : 2 * pair + odd + 1, rows] for odd in range(2)]
+                probs = jnp.exp(logits - jnp.concatenate(logs, axis=1))
+                gm = g[rows, cols]
+                zero = jnp.zeros_like(gm)
+                gm = jnp.concatenate([jnp.where(first, gm, zero), jnp.where(first, zero, gm)], axis=0)
+                gprob = nt(v, gm)
+                inner = jnp.sum(probs * gprob, axis=0, keepdims=True)
+                gl = (probs * (gprob - inner)).astype(BF16)
+                gv = nn(probs.astype(BF16), gm)
+                heads = [jnp.where(lane == 2 * pair + odd, 1.0, 0.0) for odd in range(2)]
+                heads = jnp.concatenate(heads, axis=0).astype(BF16)
+                gk = nn(gl, jnp.concatenate([q, heads], axis=1))
+                dv[near, cols] += gv[:cut]
+                dk[near, cols] += gk[:cut, :BLK]
+                ds[near, :] += gk[:cut, BLK:]
                 for odd in range(2):
-                    h = 2 * pair + odd
-                    q, k, v, probs, near, far, mine = block_probs(
-                        s, ls, tab, kept, i, h, blocks, starts, follows
-                    )
-                    gm = jnp.where(mine, gp, jnp.zeros_like(gp))
-                    gprob = nt(v, gm)
-                    inner = jnp.sum(probs * gprob, axis=0, keepdims=True)
-                    gl = (probs * (gprob - inner)).astype(BF16)
-                    gv = nn(probs.astype(BF16), gm)
-                    ind = jnp.where(lane == h, 1.0, 0.0).astype(BF16)
-                    gk = nn(gl, jnp.concatenate([q, ind], axis=1))
-                    cut = blocks * BLK
-                    dv[near, cols] += gv[:cut]
-                    dv[far, cols] += gv[cut:]
-                    dk[near, cols] += gk[:cut, :BLK]
-                    dk[far, cols] += gk[cut:, :BLK]
-                    ds[near, :] += gk[:cut, BLK:]
-                    ds[far, :] += gk[cut:, BLK:]
-                    halves.append(tn(gl, k))
-                d[rows, cols] = (
-                    jnp.where(mine, halves[1], halves[0]) * (HEAD_DIM**-0.5)
-                ).astype(BF16)
+                    mine = jnp.logical_not(first) if odd else first
+                    dv[far[odd], cols] += jnp.where(mine, gv[cut:], 0.0)
+                    dk[far[odd], cols] += jnp.where(mine, gk[cut:, :BLK], 0.0)
+                    ds[far[odd], :] += jnp.where(lane == 2 * pair + odd, gk[cut:, BLK:], 0.0)
+                dq = tn(gl, k)
+                dq = jnp.where(first, dq[:BLK], dq[BLK:]) * (HEAD_DIM**-0.5)
+                d[rows, cols] = dq.astype(BF16)
 
         @pl.when(starts)
         def _():
@@ -936,17 +1035,17 @@
     doth[...] = d[pl.ds(aligned((1 - c) * TOK, TOK), TOK), :]
 
 
-def attend_back_call(idx, kept, pics, own, other, gown, gother):
+def attend_back_call(idx, kept, pics, lse, own, other, gown, gother):
     return kernel_call(
         attend_back_kernel,
-        [idx, kept, pics, own, other, gown, gother],
-        [SM, SM, SM, HB, HB, HB, HB],
+        [idx, kept, pics, lse, own, other, gown, gother],
+        [SM, SM, SM, VM, HB, HB, HB, HB],
         [sds((TOK, 1280), BF16), sds((TOK, 1280), BF16)],
         [VM, VM],
         [
             pltpu.VMEM((SEQ + BLK, 1280), BF16),
             pltpu.VMEM((SEQ, HALF), BF16),
-            pltpu.VMEM((SEQ + BLK, BLK), F32),
+            pltpu.VMEM((SEQ + BLK, BLK), BF16),
             pltpu.VMEM((SEQ, 1280), BF16),
             pltpu.VMEM((SEQ + BLK, HALF), F32),
             pltpu.VMEM((SEQ + BLK, HALF), F32),
@@ -954,27 +1053,37 @@
             pltpu.VMEM((5, BLK, BLK), F32),
             pltpu.SemaphoreType.DMA((4,)),
         ],
-        6 * 8 * 4 * BLK * BLK * BLK * 10,
-        40,
         "attend_back",
     )
 
 
-def qkv_back_kernel(idx, ga, down_, dr, res, gb, sw0, sw1, w_in, gout, glow, nrm, w, sem):
+def qkv_back_kernel(idx, ga_in, down_, dr, res_in, gb, sw0, sw1, *refs):
+    parts, refs = refs[:-9], refs[-9:]
+    gout, glow, nrm, w, ga, res, gh, sem, isem = refs
     c = idx[2]
-    copy = pltpu.make_async_copy(w_in, w, sem)
-    copy.start()
+    fetch_qkv(idx[0], idx[1], parts, w, sem)
+    copies = load([(res_in, res), (ga_in, ga)], isem)
     nrm[...] = jnp.zeros_like(nrm)
     gain = gb[0:1, :]
-    copy.wait()
+    arrived(w, sem)
+
+    def wide(t, carry):
+        rows = pl.ds(aligned(t * 256, 256), 256)
+        total = nn(down_[rows, 1152:1280], sw0[...]) + nn(dr[rows, 1152:1280], sw1[...])
+        for j in range(3):
+            cols = pl.ds(j * HALF, HALF)
+            total += nt(down_[rows, cols], w[2 * j + c].reshape(D, HALF))
+            total += nt(dr[rows, cols], w[2 * j + 1 - c].reshape(D, HALF))
+        gh[rows, :] = total
+        return carry
+
+    lax.fori_loop(0, 2, wide, 0)
+    for copy in copies:
+        copy.wait()
 
     def tile(t, carry):
         rows = pl.ds(aligned(t * 128, 128), 128)
-        gh = nn(down_[rows, 1152:1280], sw0[...]) + nn(dr[rows, 1152:1280], sw1[...])
-        for j in range(3):
-            cols = pl.ds(j * HALF, HALF)
-            gh += nt(down_[rows, cols], w[2 * j + c]) + nt(dr[rows, cols], w[2 * j + 1 - c])
-        back, gain_part, bias_part = norm_back(res[rows, :], gh, gain)
+        back, gain_part, bias_part = norm_back(res[rows, :], gh[rows, :], gain)
         total = ga[rows, :] + back
         gout[rows, :] = total
         glow[rows, :] = total.astype(BF16)
@@ -988,93 +1097,93 @@
 def qkv_back_call(idx, ga, down_, dr, res, gb, sw0, sw1, w):
     return kernel_call(
         qkv_back_kernel,
-        [idx, ga, down_, dr, res, gb, sw0, sw1, w],
-        [SM, VM, VM, VM, VM, VM, VM, VM, HB],
+        [idx, ga, down_, dr, res, gb, sw0, sw1, *w],
+        [SM, HB, VM, VM, HB, VM, VM, VM] + [HB] * len(w),
         [sds((TOK, D), F32), sds((TOK, D), BF16), sds((8, D), F32)],
         [VM, VM, VM],
-        [pltpu.VMEM((6, D, HALF), BF16), pltpu.SemaphoreType.DMA],
-        2 * TOK * D * 2304,
-        32,
+        [
+            QKV_W,
+            pltpu.VMEM((TOK, D), F32),
+            pltpu.VMEM((TOK, D), F32),
+            pltpu.VMEM((TOK, D), F32),
+            pltpu.SemaphoreType.DMA,
+            pltpu.SemaphoreType.DMA((2,)),
+        ],
         "qkv_back",
     )
 
 
-def scatter_rows(src, f, rows, offset, count, pyy, portion, ka, sa, kb, sb):
+def scatter_rows(src, f, rows, offset, pyy, portion, outs, n, cols):
+    if len(outs) == 1:
+        for block in range(8):
+            value = src[pl.ds(block * rows + offset, ROWS), :]
+            outs[0][2 * block + pyy, portion, n, :, cols] = value
+        return
+    ka, sa, kb, sb = outs
     for pxx in range(2):
         for pz in range(4):
             block = (f >> 1) ^ (pz * 2 + pxx)
-            value = src[pl.ds(aligned(block * rows + offset, 16), count), :]
+            value = src[pl.ds(aligned(block * rows + offset, 16), ROWS), :]
             if portion == 0:
-                (sa if pxx else ka)[pyy, pz] = value
+                (sa if pxx else ka)[pyy, pz, n, :, cols] = value
             else:
-                (sb if pyy else kb)[pxx, pz] = value
-
-
-def up_grad_kernel(idx, xk, xr, gk, gr, ka, sa, kb, sb, tmp):
-    f, y = idx[0], idx[1]
+                (sb if pyy else kb)[pxx, pz, n, :, cols] = value
+
+
+def up_grads_into(f, y, xk, xr, gk, gr, outs, tmp):
     for portion in range(2):
         for pyy in range(2):
             cols = pl.ds(aligned((y ^ pyy) * 1536 + portion * D, 128), D)
-            tmp[portion * 2 + pyy] = (nn(xk[...], gk[:, cols]) + nn(xr[...], gr[:, cols])).astype(
-                BF16
-            )
-            scatter_rows(
-                tmp.at[portion * 2 + pyy], f, ROWS, 0, ROWS, pyy, portion, ka, sa, kb, sb
-            )
-
-
-def up_grad_call(idx, xk, xr, gk, gr):
-    piece = sds((2, 4, ROWS, D), BF16)
-    return kernel_call(
-        up_grad_kernel,
-        [idx, xk.reshape(HALF, TOK), xr.reshape(HALF, TOK), gk, gr],
-        [SM, VM, VM, VM, VM],
-        [piece] * 4,
-        [VM] * 4,
-        [pltpu.VMEM((4, HALF, D), BF16)],
-        2 * SEQ * HALF * FF,
-        32,
-        "up_grad",
-    )
-
-
-def down_grad_kernel(idx, xk, xr, gk, gr, ka, sa, kb, sb, tmp):
-    f, y = idx[0], idx[1]
+            slot = portion * 2 + pyy
+            tmp[slot] = (nn(xk[...], gk[:, cols]) + nn(xr[...], gr[:, cols])).astype(BF16)
+            scatter_rows(tmp.at[slot], f, ROWS, 0, pyy, portion, outs, 0, pl.ds(0, D))
+
+
+def down_grads_into(f, y, ak, ar, dk, dr, outs, tmp):
     for pyy in range(2):
         cols = pl.ds(aligned((y ^ pyy) * HALF, 128), HALF)
 
         def tile(t, carry):
             rows = pl.ds(aligned(t * HALF, HALF), HALF)
-            tmp[pyy, rows, :] = (nn(xk[rows, :], gk[:, cols]) + nn(xr[rows, :], gr[:, cols])).astype(
-                BF16
-            )
+            value = nn(ak[rows, :], dk[:, cols]) + nn(ar[rows, :], dr[:, cols])
+            tmp[pyy, rows, :] = value.astype(BF16)
             return carry
 
         lax.fori_loop(0, 4, tile, 0)
         for portion in range(2):
-            scatter_rows(
-                tmp.at[pyy], f, DROWS, portion * 96, 96, pyy, portion, ka, sa, kb, sb
-            )
-
-
-def down_grad_call(idx, xk, xr, gk, gr):
-    piece = sds((2, 4, 96, HALF), BF16)
+            for k in range(2):
+                offset, half = (portion * 2 + k) * ROWS, pl.ds(k * HALF, HALF)
+                scatter_rows(tmp.at[pyy], f, DROWS, offset, pyy, portion, outs, 1, half)
+
+
+def ffn_grad_kernel(count, idx, xk, xr, gk, gr, ak, ar, dk, dr, *refs):
+    outs, tmp, tmp2 = refs[:count], refs[count], refs[count + 1]
+    f, y = (idx[0], idx[1]) if count == 4 else (0, 0)
+    up_grads_into(f, y, xk, xr, gk, gr, outs, tmp)
+    down_grads_into(f, y, ak, ar, dk, dr, outs, tmp2)
+
+
+def ffn_grad_call(idx, xk, xr, gk, gr, ak, ar, dk, dr, by_position):
+    ins = [idx] + [v.reshape(HALF, TOK) for v in (xk, xr)] + [gk, gr]
+    ins += [v.reshape(4 * HALF, TOK) for v in (ak, ar)] + [dk, dr]
+    outs = [sds((16, 2, 2, ROWS, D), BF16)]
+    if by_position:
+        outs = [sds((2, 4, 2, ROWS, D), BF16)] * 4
     return kernel_call(
-        down_grad_kernel,
-        [idx, xk.reshape(4 * HALF, TOK), xr.reshape(4 * HALF, TOK), gk, gr],
-        [SM, VM, VM, VM, VM],
-        [piece] * 4,
-        [VM] * 4,
-        [pltpu.VMEM((2, 4 * HALF, HALF), BF16)],
-        2 * SEQ * HALF * FF,
-        32,
-        "down_grad",
+        partial(ffn_grad_kernel, len(outs)),
+        ins,
+        [SM] + [VM] * 8,
+        outs,
+        [VM] * len(outs),
+        [pltpu.VMEM((4, HALF, D), BF16), pltpu.VMEM((2, 4 * HALF, HALF), BF16)],
+        "ffn_grad",
     )
 
 
 def qkv_grad_kernel(
     idx, xk, xr, mk, mr, d00, d01, d10, d11, gk, gr, ka, sa, kb, sb, sc, dy, tmp, tsc, sem
 ):
+    outs = (ka, sa, kb, sb)
     f, y, c = idx[0], idx[1], idx[2]
     copies = []
     for tok, pair in enumerate(((d00, d01), (d10, d11))):
@@ -1110,7 +1219,7 @@
             tmp[portion * 2 + pyy, :, cols] = value.astype(BF16)
         for portion in range(2):
             scatter_rows(
-                tmp.at[portion * 2 + pyy], f, ROWS, 0, ROWS, pyy, portion, ka, sa, kb, sb
+                tmp.at[portion * 2 + pyy], f, ROWS, 0, pyy, portion, outs, 0, pl.ds(0, D)
             )
     own = nn(xk[...], tsc[0]) + nn(xr[...], tsc[2])
     theirs = nn(xk[...], tsc[1]) + nn(xr[...], tsc[3])
@@ -1128,13 +1237,12 @@
 
 
 def qkv_grad_call(idx, xk, xr, mk, mr, d00, d01, d10, d11, gk, gr):
-    piece = sds((2, 4, ROWS, D), BF16)
     flat = [v.reshape(HALF, TOK) for v in (xk, xr, mk, mr)]
     return kernel_call(
         qkv_grad_kernel,
         [idx, *flat, d00, d01, d10, d11, gk, gr],
         [SM, VM, VM, VM, VM, HB, HB, HB, HB, VM, VM],
-        [piece] * 4 + [sds((2, 4, ROWS, 128), F32)],
+        [sds((2, 4, 1, ROWS, D), BF16)] * 4 + [sds((2, 4, ROWS, 128), F32)],
         [VM] * 5,
         [
             pltpu.VMEM((2, 6, TOK, HALF), BF16),
@@ -1142,14 +1250,59 @@
             pltpu.VMEM((4, TOK, 128), BF16),
             pltpu.SemaphoreType.DMA((16,)),
         ],
-        2 * SEQ * HALF * FF,
-        40,
         "qkv_grad",
     )
 
 
+def cross_kernel(ka, ra, kb, rb, qa, qb):
+    for k, r, q in ((ka, ra, qa), (kb, rb, qb)):
+        q[...] = (k[...].astype(F32) + r[...].astype(F32)).astype(BF16)[0]
+
+
+def cross_call(ka, ra, kb, rb):
+    n = ka.shape[2]
+    block = pl.BlockSpec((1, 1, n, ROWS, D), lambda z: (1, z, 0, 0, 0))
+    out = pl.BlockSpec((1, n, ROWS, D), lambda z: (z, 0, 0, 0))
+    return pl.pallas_call(
+        cross_kernel,
+        out_shape=(sds((4, n, ROWS, D), BF16),) * 2,
+        grid=(4,),
+        in_specs=[block] * 4,
+        out_specs=(out,) * 2,
+        cost_estimate=duration(COST["cross"]),
+        name="cross",
+    )(ka, ra, kb, rb)
+
+
+def own_kernel(ka, ra, ca, kb, rb, cb, *outs):
+    z = pl.program_id(0)
+    for part, (k, r, q) in enumerate(((ka, ra, ca), (kb, rb, cb))):
+        total = k[0, 0].astype(F32) + r[0, 0].astype(F32) + q[0].astype(F32)
+        for t in range(4):
+
+            @pl.when(z == t)
+            def _():
+                outs[t][part] = total.astype(outs[t].dtype)
+
+
+def own_call(ka, ra, ca, kb, rb, cb):
+    n = ka.shape[2]
+    block = pl.BlockSpec((1, 1, n, ROWS, D), lambda z: (0, z, 0, 0, 0))
+    quarter = pl.BlockSpec((1, n, ROWS, D), lambda z: (z, 0, 0, 0))
+    out = pl.BlockSpec((2, n, ROWS, D), lambda z: (0, 0, 0, 0))
+    return pl.pallas_call(
+        own_kernel,
+        out_shape=tuple(sds((2, n, ROWS, D), F32 if t == 0 else BF16) for t in range(4)),
+        grid=(4,),
+        in_specs=[block, block, quarter] * 2,
+        out_specs=(out,) * 4,
+        cost_estimate=duration(COST["own"]),
+        name="own",
+    )(ka, ra, ca, kb, rb, cb)
+
+
 def pairwise(v, bits):
-    return lax.ppermute(v, "fsdp", [(i, i ^ bits) for i in range(16)])
+    return lax.ppermute(v, "zx", [(i, i ^ bits) for i in range(8)])
 
 
 def over_ctx(v):
@@ -1157,44 +1310,84 @@
 
 
 def over_core(v):
+    return lax.ppermute(v, "core", [(0, 1), (1, 0)])
+
+
+def over_x(v):
     return pairwise(v, 1)
 
 
-def over_x(v):
-    return pairwise(v, 2)
+def diagonal(v):
+    return lax.ppermute(v, ("zx", "ctx"), [(i, i ^ 3) for i in range(16)])
 
 
 def turn(v):
-    perm = [
-        ((g * 2 + a) * 2 + b, (g * 2 + b) * 2 + a) for g in range(8) for a in range(2) for b in range(2)
-    ]
-    return lax.ppermute(v, ("fsdp", "ctx"), perm)
-
-
-def gather_piece(part_a, part_b):
-    both = jnp.stack([part_a, part_b])
-    near = [both] + [pairwise(both, k << 2) for k in range(1, 4)]
-    a0, b0 = (jnp.stack([v[part] for v in near]) for part in range(2))
-    a1 = over_x(a0)
-    b2 = over_ctx(b0)
-    a = [a0, a1, over_ctx(a0), over_ctx(a1)]
-    b = [b0, over_x(b0), b2, over_x(b2)]
-    return (a + [over_core(v) for v in a], b + [over_core(v) for v in b])
-
-
-def reduce_piece(ka, sa, kb, sb):
-    def add(mine, received):
-        return mine.astype(F32) + received.astype(F32)
-
-    def last(total, received):
-        low = total.astype(BF16)
-        return total[0] + sum(pairwise(low[k], k << 2).astype(F32) for k in range(1, 4))
-
-    ta = add(ka, over_x(sa))
-    tb = add(kb, over_ctx(sb))
-    ta = add(ta[0], over_ctx(ta[1].astype(BF16)))
-    tb = add(tb[0], over_x(tb[1].astype(BF16)))
-    return last(ta, None), last(tb, None)
+    return lax.ppermute(v, ("core", "ctx"), [(0, 0), (1, 2), (2, 1), (3, 3)])
+
+
+class Chain:
+    def __init__(self, stages):
+        self.stages, self.result = stages, None
+        self.flying = next(stages)
+
+    def advance(self, arrived):
+        try:
+            self.flying = self.stages.send(arrived)
+        except StopIteration as stop:
+            self.flying, self.result = None, stop.value
+
+
+class Order:
+    def __init__(self, idx):
+        self.gate = idx
+
+    def after(self, value):
+        return lax.optimization_barrier((value, self.gate))[0]
+
+    def passed(self, value):
+        self.gate, value = lax.optimization_barrier((self.gate, value))
+        return value
+
+    def meet(self, *chains):
+        for chain, items in zip(chains, self.passed([c.flying for c in chains])):
+            chain.advance(items)
+
+
+def gather_stages(both, z):
+    near = yield [pairwise(both, k << 1) for k in range(1, 4)]
+    near = [both] + near
+    near = [lax.select_n(z, *(near[k ^ t] for t in range(4))) for k in range(4)]
+    a, b = (jnp.stack([v[part] for v in near]) for part in range(2))
+    xa, yb, ya, xb = yield [over_x(a), over_ctx(b), over_ctx(a), over_x(b)]
+    a, b = [a, xa, ya], [b, xb, yb]
+    da, db, *other = yield [over_ctx(xa), over_x(yb)] + [over_core(v) for v in a + b]
+    ca, cb = yield [over_core(da), over_core(db)]
+    return a + [da] + other[:3] + [ca] + b + [db] + other[3:] + [cb]
+
+
+def small_gather_stages(small, start):
+    *near, start = yield [pairwise(small, k << 1) for k in range(1, 4)] + [start]
+    small = jnp.stack([small] + near)
+    (r,) = yield [over_x(small)]
+    small = jnp.concatenate([small, r])
+    (r,) = yield [over_core(small)]
+    return jnp.concatenate([small, r]), start
+
+
+def reduce_stages(ka, sa, kb, sb):
+    ra, rb = yield [over_x(sa), over_ctx(sb)]
+    qa, qb = cross_call(ka, ra, kb, rb)
+    ca, cb = yield [over_ctx(qa), over_x(qb)]
+    total, *low = own_call(ka, ra, ca, kb, rb, cb)
+    rest = yield [pairwise(v, k << 1) for k, v in enumerate(low, 1)]
+    return total + sum(v.astype(F32) for v in rest)
+
+
+def small_stages(t):
+    ry, rx, rd = yield [over_ctx(t[0]), over_x(t[1]), diagonal(t[1])]
+    t = t[0] + ry + (rx + rd)
+    rest = yield [pairwise(t[k], k << 1) for k in range(1, 4)]
+    return t[0] + sum(rest)
 
 
 def pair_device(
@@ -1210,12 +1403,24 @@
     norm_gain,
     norm_bias,
 ):
-    f = lax.axis_index("fsdp").astype(jnp.int32)
+    zx = lax.axis_index("zx").astype(jnp.int32)
     y = lax.axis_index("ctx").astype(jnp.int32)
-    c = f & 1
+    c = lax.axis_index("core").astype(jnp.int32)
+    f = zx * 2 + c
     idx = jnp.stack([f, y, c])
-    start = turn(tokens[0])
-    cot = turn(cotangent[0])
+    order = Order(idx)
+
+    def shards(l):
+        joined = jnp.concatenate([qkv_weight[l], out_weight[l]], axis=1)
+        up = up_weight[l].reshape(ROWS, 2, D).swapaxes(0, 1)
+        down = down_weight[l].reshape(2, 2, ROWS, HALF).swapaxes(1, 2).reshape(2, ROWS, D)
+        return jnp.stack([joined[:, :D], joined[:, D:]]), up, down
+
+    def gather(v):
+        return Chain(gather_stages(order.after(v), zx >> 1))
+
+    w = [shards(l) for l in range(LAYERS)]
+    qo0 = gather(w[0][0][:, None])
     kept = jnp.where(c == y, kept_blocks[0], over_core(kept_blocks[0]))
     pics = jnp.where(c == y, picture_starts[0], over_core(picture_starts[0]))
     kept = lax.dynamic_slice_in_dim(kept, c * 6, 6, 0)
@@ -1223,83 +1428,134 @@
         [jnp.swapaxes(score_weight, 1, 2), norm_gain, norm_bias], axis=1
     ).reshape(LAYERS * 16, ROWS)
     small = jnp.pad(small, ((0, 0), (0, 128 - ROWS)))
-    small = jnp.stack([small] + [pairwise(small, k << 2) for k in range(1, 4)])
-    small = jnp.concatenate([small, over_x(small)])
-    small = jnp.concatenate([small, over_core(small)])
+    small = Chain(small_gather_stages(small, turn(tokens[0])))
+    ffn0 = lax.all_gather(jnp.stack(w[0][1:], axis=1), ("zx", "ctx"), axis=0, tiled=False)
+    order.meet(qo0, small)
+    order.meet(qo0, small)
+    order.meet(qo0, small)
+    order.meet(qo0)
+    qo0 = qo0.result
+    small, residual = small.result
+    residual = residual.astype(F32)
     away = jnp.arange(16, dtype=jnp.int32) ^ f
     small = jnp.take(small, (away & 1) * 8 + ((away >> 1) & 1) * 4 + (away >> 2), axis=0)
     small = jnp.moveaxis(small[:, :, :ROWS], 0, 1).reshape(LAYERS, 16, D)
-    pieces = []
+    scale = []
     for l in range(LAYERS):
-        qo = gather_piece(
-            qkv_weight[l][:, :D], jnp.concatenate([qkv_weight[l][:, D:], out_weight[l]], axis=1)
-        )
-        up = gather_piece(up_weight[l][:, :D], up_weight[l][:, D:])
-        dn = gather_piece(down_weight[l][:96], down_weight[l][96:])
-        pieces.append((qo, up, dn))
-    residual = start.astype(F32)
-    saved = []
-    for l in range(LAYERS):
-        (qa, qb), (ua, ub), (da, db) = pieces[l]
         gb = jnp.pad(small[l, 12:16].astype(F32), ((0, 4), (0, 0)))
         own_rows = lax.dynamic_slice_in_dim(small[l], c * 6, 6, 0)
         other_rows = lax.dynamic_slice_in_dim(small[l], (1 - c) * 6, 6, 0)
-        sw0 = jnp.pad(own_rows, ((0, 122), (0, 0)))
-        sw1 = jnp.pad(other_rows, ((0, 122), (0, 0)))
-        own, send, xk, xs, w_qkv = qkv_call(idx, residual, gb, sw0, sw1, qa, qb)
-        other = over_core(send)
-        mixed, msend = attend_call(idx, kept, pics, own, other)
-        after, act, slope, mk, ms, hk, hs, ak, as_, w_out, w_up = up_call(
-            idx, residual, mixed, over_core(msend), gb, qb, ua, ub
+        pad = ((0, 122), (0, 0))
+        scale.append((gb, jnp.pad(own_rows, pad), jnp.pad(other_rows, pad)))
+
+    def qkv(l, residual, w):
+        own, send, xk, xs = order.passed(qkv_call(order.gate, residual, *scale[l], w))
+        return own, over_core(send), xk, over_core(xs)
+
+    def attend(head):
+        mixed, send, lse = order.passed(attend_call(order.gate, kept, pics, head[0], head[1]))
+        return (mixed, over_core(send)), lse
+
+    def feed(l, residual, mixed, qo, ffn):
+        outs = ffn_call(order.gate, residual, *mixed, scale[l][0], qo, ffn)
+        after, new, low, mk, ms, hk, hs, slope, ak, as_ = order.passed(outs)
+        hr, ar, mr = over_core(hs), over_core(as_), over_core(ms)
+        return new, low, (after, slope, (hk, hr), (ak, ar), (mk, mr))
+
+    qo1 = gather(w[1][0][:, None])
+    head0 = qkv(0, residual, qo0)
+    order.meet(qo1)
+    ffn1 = gather(jnp.stack(w[1][1:], axis=1))
+    mixed, lse0 = attend(head0)
+    order.meet(qo1, ffn1)
+    order.meet(qo1)
+    ffn0 = order.passed(ffn0)
+    ffn0 = order.passed([v.reshape(4, 2, 2, 2, 2, ROWS, D) for v in (ffn0, over_core(ffn0))])
+    res1, _, out0 = feed(0, residual, mixed, qo0, ffn0)
+    order.meet(qo1, ffn1)
+    qo1 = qo1.result
+    head1 = qkv(1, res1, qo1)
+    order.meet(ffn1)
+    mixed, lse1 = attend(head1)
+    order.meet(ffn1)
+    ffn1 = ffn1.result
+    cot = turn(order.after(cotangent[0]))
+    _, low, out1 = feed(1, res1, mixed, qo1, ffn1)
+    block_output = turn(low).astype(F32)
+
+    weights = ((qo0, ffn0), (qo1, ffn1))
+
+    def down_back(l, low, out):
+        gu = order.passed(down_back_call(order.gate, low, out[1], weights[l][1]))
+        return gu, over_core(gu)
+
+    def up_back(l, grad, gu, out):
+        ga, gat, gmk, gms, nrm = order.passed(
+            up_back_call(order.gate, grad, gu, out[0], scale[l][0], *weights[l])
         )
-        new, w_down = down_call(idx, act, after, da, db)
-        received = tuple(over_core(v) for v in (xs, ms, hs, as_))
-        saved.append(
-            (residual, gb, sw0, sw1, own, other, after, slope, (xk, mk, hk, ak), received)
-            + (w_qkv, w_out, w_up, w_down)
+        return ga, nrm, (gmk, over_core(gms)), (gat, over_core(gat))
+
+    def attend_back(head, lse, gm):
+        d_own, d_oth = order.passed(
+            attend_back_call(order.gate, kept, pics, lse, head[0], head[1], *gm)
         )
-        residual = new
-    block_output = turn(residual.astype(BF16)).astype(F32)
-    grad = cot.astype(F32)
-    grad_low = cot
-    grads = [None] * LAYERS
-    norms = [None] * LAYERS
-    for l in reversed(range(LAYERS)):
-        res, gb, sw0, sw1, own, other, after, slope, kept_t, recv_t, w_qkv, w_out, w_up, w_down = saved[l]
-        xk, mk, hk, ak = kept_t
-        xr, mr, hr, ar = recv_t
-        gu = down_back_call(grad_low, slope, w_down)
-        gd_r = over_core(grad_low)
-        gu_r = over_core(gu)
-        down_pieces = reduce_piece(*down_grad_call(idx, ak, ar, grad_low, gd_r))
-        ga, gat, gmk, gms, nrm2 = up_back_call(idx, grad, gu, after, gb, w_up, w_out)
-        gm_r = over_core(gms)
-        gat_r = over_core(gat)
-        up_pieces = reduce_piece(*up_grad_call(idx, hk, hr, gu, gu_r))
-        d_own, d_oth = attend_back_call(idx, kept, pics, own, other, gmk, gm_r)
-        r1 = over_core(d_oth)
-        r2 = over_core(d_own)
-        *qo, sc = qkv_grad_call(idx, xk, xr, mk, mr, d_own, r1, d_oth, r2, gat, gat_r)
-        qo_pieces = reduce_piece(*qo)
-        grad, grad_low, nrm1 = qkv_back_call(idx, ga, d_own, r1, res, gb, sw0, sw1, w_qkv)
-        sc = sc + over_ctx(sc)
-        sc = sc[0] + over_x(sc[1])
-        sc = sc[0] + sum(pairwise(sc[k], k << 2) for k in range(1, 4))
-        grads[l] = (qo_pieces, up_pieces, down_pieces, sc)
-        norms[l] = jnp.concatenate([nrm1[0:1], nrm2[0:1], nrm1[1:2], nrm2[1:2]])
-    token_grad = turn(grad_low).astype(F32)
-    nrm = jnp.concatenate(norms)
-    nrm = nrm + over_core(nrm)
-    nrm = nrm + over_ctx(nrm)
-    nrm = nrm + over_x(nrm)
-    nrm = nrm + sum(pairwise(nrm, k << 2) for k in range(1, 4))
-    nrm = lax.dynamic_slice_in_dim(nrm, f * ROWS, ROWS, 1).reshape(LAYERS, 2, 2, ROWS)
-    qkv_grad = jnp.stack([jnp.concatenate([a, b[:, :HALF]], 1) for (a, b), _, _, _ in grads])
-    out_grad = jnp.stack([b[:, HALF:] for (_, b), _, _, _ in grads])
-    up_grad = jnp.stack([jnp.concatenate([a, b], 1) for _, (a, b), _, _ in grads])
-    down_grad = jnp.stack([jnp.concatenate([a, b], 0) for _, _, (a, b), _ in grads])
-    score_grad = jnp.stack(
-        [jnp.concatenate([s[:, 0:6], s[:, 64:70]], 1) for _, _, _, s in grads]
+        return d_own, over_core(d_oth), d_oth, over_core(d_own)
+
+    def qkv_grads(head, out, d, gat):
+        return order.passed(qkv_grad_call(order.gate, head[2], head[3], *out[4], *d, *gat))
+
+    def qkv_back(l, ga, d, res, head):
+        return order.passed(qkv_back_call(order.gate, ga, d[0], d[1], res, *scale[l], weights[l][0]))
+
+    scores, norms = [None] * LAYERS, [None] * LAYERS
+    low, low_r = cot, over_core(cot)
+    gu, gu_r = down_back(1, low, out1)
+    ga, nrm2, gm, gat = up_back(1, cot.astype(F32), gu, out1)
+    grads = ffn_grad_call(order.gate, *out1[2], gu, gu_r, *out1[3], low, low_r, False)
+    ffn1 = order.passed(grads[0])
+    ffn1 = lax.psum_scatter(ffn1, ("zx", "ctx"), scatter_dimension=0, tiled=False)
+    d = attend_back(head1, lse1, gm)
+    grad, low, nrm1 = qkv_back(1, ga, d, res1, head1)
+    low_r = over_core(low)
+    *g, scores[1] = qkv_grads(head1, out1, d, gat)
+    norms[1] = jnp.concatenate([nrm1[0:1], nrm2[0:1], nrm1[1:2], nrm2[1:2]])
+    qo1 = Chain(reduce_stages(*g))
+    gu, gu_r = down_back(0, low, out0)
+    ga, nrm2, gm, gat = up_back(0, grad, gu, out0)
+    order.meet(qo1)
+    grads = ffn_grad_call(order.gate, *out0[2], gu, gu_r, *out0[3], low, low_r, True)
+    ffn0 = Chain(reduce_stages(*order.passed(grads)))
+    order.meet(qo1)
+    d = attend_back(head0, lse0, gm)
+    order.meet(ffn0, qo1)
+    *g, scores[0] = qkv_grads(head0, out0, d, gat)
+    qo0 = Chain(reduce_stages(*g))
+    grad, low, nrm1 = qkv_back(0, ga, d, residual, head0)
+    norms[0] = jnp.concatenate([nrm1[0:1], nrm2[0:1], nrm1[1:2], nrm2[1:2]])
+    nrm = jnp.concatenate(norms).reshape(8, 8, 2, ROWS)
+    mine, theirs = (lax.dynamic_index_in_dim(nrm, b, 2, keepdims=False) for b in (c, 1 - c))
+    nrm = jnp.moveaxis(mine + over_core(theirs), 0, 2)
+    nrm = jnp.take(nrm, zx ^ jnp.array([0, 2, 4, 6, 1, 3, 5, 7], jnp.int32), axis=0)
+    nrm = nrm.reshape(2, 4, ROWS, 8)
+    lanes = [jnp.concatenate([s[..., :6], s[..., 64:70]], -1) for s in scores] + [nrm]
+    lanes = jnp.pad(jnp.concatenate(lanes, -1), ((0, 0), (0, 0), (0, 0), (0, 96)))
+    lanes = Chain(small_stages(lanes))
+    token_grad = turn(low)
+    order.meet(ffn0, qo0)
+    order.meet(qo0, lanes)
+    order.meet(ffn0, lanes)
+    order.meet(qo0)
+    token_grad = order.passed(token_grad).astype(F32)
+    lanes = order.after(lanes.result)
+    score_grad = jnp.stack([lanes[:, 0:12], lanes[:, 12:24]])
+    nrm = lanes[:, 24:32].T.reshape(LAYERS, 2, 2, ROWS)
+    qo = [qo0.result[:, 0], qo1.result[:, 0]]
+    qkv_grad = jnp.stack([jnp.concatenate([v[0], v[1, :, :HALF]], 1) for v in qo])
+    out_grad = jnp.stack([v[1, :, HALF:] for v in qo])
+    ffn = [ffn0.result, ffn1.astype(F32)]
+    up_grad = jnp.stack([jnp.concatenate([v[0, 0], v[1, 0]], 1) for v in ffn])
+    down_grad = jnp.stack(
+        [v[:, 1].reshape(2, ROWS, 2, HALF).swapaxes(1, 2).reshape(DROWS, HALF) for v in ffn]
     )
     return (
         block_output[None],
@@ -1339,7 +1595,14 @@
         P(None, None, "fsdp"),
         P(None, None, "fsdp"),
     )
-    pairs = mesh.shape["fsdp"] == 16 and mesh.shape["ctx"] == 2
+    step = per_device
+    if mesh.shape["fsdp"] == 16 and mesh.shape["ctx"] == 2:
+        step = pair_device
+        mesh = Mesh(mesh.devices.reshape(8, 2, 2), ("zx", "core", "ctx"))
+        in_specs, out_specs = (
+            tuple(P(*(("zx", "core") if a == "fsdp" else a for a in spec)) for spec in specs)
+            for specs in (in_specs, out_specs)
+        )
     return jax.shard_map(
-        pair_device if pairs else per_device, mesh=mesh, in_specs=in_specs, out_specs=out_specs, check_vma=False
-    )
+        step, mesh=mesh, in_specs=in_specs, out_specs=out_specs, check_vma=False
+    )

time: 801 us -> 593 us (0.74)
  starting transfers between devices: 227 us -> 119 us
  waiting for transfers between devices: 207 us -> 160 us
  local copies, waits for them, and re-layouts: 71.4 us -> 30.8 us
  Pallas kernels: 257 us -> 244 us
  other arithmetic: 28.1 us -> 15.8 us
  between operations: 4.23 us -> 16.2 us
    ppermute x180 -> x99, starting transfers between devices: 187 us -> 97.4 us  [the longest x41 76.7 us: pairwise(): return lax.ppermute(v, 'zx', [(i, i ^ bits) for i in range(8)])]
    ppermute x33 -> x16, waiting for transfers between devices: 115 us -> 43.9 us  [over_ctx(): return lax.ppermute(v, 'ctx', [(0, 1), (1, 0)])]
    unnamed x409 -> x173, local copies, waits for them, and re-layouts: 52.5 us -> 16.6 us
    pallas_call x22 -> x18, Pallas kernels: 257 us -> 222 us  [kernel_call(): pl.pallas_call(body, out_shape=tuple(outs), in_specs=in_specs, out_specs=...]
    ppermute x180 -> x99, waiting for transfers between devices: 91.4 us -> 116 us  [the longest x41 104 us: pairwise(): return lax.ppermute(v, 'zx', [(i, i ^ bits) for i in range(8)])]
    pallas_call x0 -> x6, Pallas kernels: none -> 21.6 us  [the longest x3 11 us: own_call(): pl.pallas_call(own_kernel, out_shape=tuple((sds((2, n, ROWS, D), F32 if t...]
    ppermute x33 -> x16, starting transfers between devices: 40.2 us -> 21.6 us  [over_ctx(): return lax.ppermute(v, 'ctx', [(0, 1), (1, 0)])]
    add x34 -> x5, other arithmetic: 10.9 us -> 0.33 us  [the longest x3 0.25 us: reduce_stages(): return total + sum((v.astype(F32) for v in rest))]
  transfers between devices with their start and end apart: 213 -> 117, of which waited for: 67 -> 36; matrix products, arithmetic and copies ran while one was open for 6% -> 5% of each run, Pallas kernels for 32% -> 35%
where the time goes in v2:
time: 593 us; the launch traced here: 587 us
  Pallas kernels  244 us (41%)
  waiting for transfers between devices  160 us (27%)
  starting transfers between devices  119 us (20%)
  local copies, waits for them, and re-layouts  30.8 us (5%)
  between operations  16.2 us (3%)
  other arithmetic  15.8 us (3%)
    pallas_call x18, Pallas kernels, kernel_call(): pl.pallas_call(body, out_shape=tuple(outs), in_specs=in_specs, out_specs=...  222 us
    ppermute x41, waiting for transfers between devices, pairwise(): return lax.ppermute(v, 'zx', [(i, i ^ bits) for i in range(8)])  104 us
    ppermute x41, starting transfers between devices, pairwise(): return lax.ppermute(v, 'zx', [(i, i ^ bits) for i in range(8)])  76.7 us
    ppermute x16, waiting for transfers between devices, over_ctx(): return lax.ppermute(v, 'ctx', [(0, 1), (1, 0)])  43.9 us
    ppermute x16, starting transfers between devices, over_ctx(): return lax.ppermute(v, 'ctx', [(0, 1), (1, 0)])  21.6 us
    unnamed x173, local copies, waits for them, and re-layouts  16.6 us
    ppermute x53, starting transfers between devices, over_core(): return lax.ppermute(v, 'core', [(0, 1), (1, 0)])  13.8 us
    ppermute x53, waiting for transfers between devices, over_core(): return lax.ppermute(v, 'core', [(0, 1), (1, 0)])  12.1 us
  transfers between devices with their start and end apart: 117, of which 36 were waited for; matrix products, arithmetic and copies ran while one was open for 5% of the time, Pallas kernels for 35%

profile of v2, /device:TPU:0, one launch (start us, length us, event | category | flops | bytes accessed | tf_op | source)
XLA Modules:
  0.0 586.5 jit_solution(8009034069151635765)
XLA Ops:
  8.6 3.1 collective-permute-start.3
  18.1 3.0 collective-permute-start.1
  24.1 15.7 %collective-permute-done.4 = bf16[32,128]{1,0:T(8,128)(2,1)S(1)} collective-permute-done((bf16[32,128]{1,0:T(8,128)(2,1)S(1)}, bf16[32,128]{1,0:T(8,128)(2,1)S(1)}, u32[]{:S(2)}, u32[]{:S(2)}) %collective-permute-start.4) | collective-permute-done | bytes 8224 | tf_op jit(solution)/shard_map/ppermute | solution.py:1305
  39.8 5.0 collective-permute-start.5
  46.7 2.0 collective-permute-start.10
  51.0 1.9 collective-permute-start.11
  52.9 18.5 %collective-permute-done.11 = bf16[4,32,128]{2,1,0:T(8,128)(2,1)S(1)} collective-permute-done((bf16[4,32,128]{2,1,0:T(8,128)(2,1)S(1)}, bf16[4,32,128]{2,1,0:T(8,128)(2,1)S(1)}, u32[]{:S(2)}, u32[]{:S(2)}) %collective-permute-start.11) | collective-permute-done | bytes 32800 | tf_op jit(solution)/shard_map/ppermute | solution.py:1305
  74.8 6.4 %collective-permute-done.12.refs_3_ = bf16[4,1,48,768]{3,2,1,0:T(8,128)(2,1)S(1)} collective-permute-done((bf16[4,1,48,768]{3,2,1,0:T(8,128)(2,1)S(1)}, bf16[4,1,48,768]{3,2,1,0:T(8,128)(2,1)S(1)}, u32[]{:S(2)}, u32[]{:S(2)}) %collective-permute-start.12) | collective-permute-done | bytes 294944 | tf_op jit(solution)/shard_map/ppermute | solution.py:1309
  90.2 4.5 collective-permute-start.24
  94.8 8.6 %qkv.2 = (bf16[512,1280]{1,0:T(8,128)(2,1)}, bf16[512,1280]{1,0:T(8,128)(2,1)}, bf16[8,48,512]{2,1,0:T(8,128)(2,1)}, bf16[8,48,512]{2,1,0:T(8,128)(2,1)}) custom-call(s32[3]{0:T(128)} %pad_add_fusion.idx, f32[512,768]{1,0:T(8,128)} %convert_element_type.61.res.res_in, f32[8,768]{1,0:T(8,128)} %pad_convert_fusion.1.gb, bf16[128,768]{1,0:T(8,128)(2,1)} %pad.35.sw0, ...), custom_call_target="tpu_custom_call" | custom-call | flops 8049999872 | bytes 1048576 | tf_op jit(solution)/shard_map/qkv/pallas_call | solution.py:407
  103.4 2.3 collective-permute-done.23
  106.9 7.3 %collective-permute-done.25 = bf16[2,1,48,768]{3,2,1,0:T(8,128)(2,1)S(1)} collective-permute-done((bf16[2,1,48,768]{3,2,1,0:T(8,128)(2,1)S(1)}, bf16[2,1,48,768]{3,2,1,0:T(8,128)(2,1)S(1)}, u32[]{:S(2)}, u32[]{:S(2)}) %collective-permute-start.25) | collective-permute-done | bytes 147488 | tf_op jit(solution)/shard_map/ppermute | solution.py:1305
  114.4 1.9 collective-permute-start.30
  119.8 4.6 collective-permute-done.30.refs_10_
  124.4 5.5 collective-permute-start.33
  129.9 2.3 collective-permute-start.34
  132.2 2.1 collective-permute-start.35
  134.3 11.8 %attend.2 = (bf16[512,384]{1,0:T(8,128)(2,1)}, bf16[512,384]{1,0:T(8,128)(2,1)}, f32[8,1024]{1,0:T(8,128)}) custom-call(s32[3]{0:T(128)} %pad_add_fusion.idx, s32[6,8]{1,0:T(8,128)} %dynamic-slice_select_fusion.kept, s32[2]{0:T(128)} %broadcast_select_fusion.1.pics, bf16[512,1280]{1,0:T(8,128)(2,1)} %get-tuple-element.318.own, bf16[512,1280]{1,0:T(8,128)(2,1)} %copy-done.21), custom_call_target="tpu_custom_call" | custom-call | flops 13799999488 | bytes 1048576 | tf_op jit(solution)/shard_map/attend/pallas_call | solution.py:407
  146.9 4.8 collective-permute-done.34
  153.2 2.1 collective-permute-start.37
  155.9 2.5 collective-permute-done.36.refs_3_
  158.4 4.6 collective-permute-done.37.refs_11_
  169.9 2.9 collective-permute-done.44
  173.5 7.6 %collective-permute-done.49.refs_26_.refs_10_ = bf16[4,2,48,768]{3,2,1,0:T(8,128)(2,1)S(1)} collective-permute-done((bf16[4,2,48,768]{3,2,1,0:T(8,128)(2,1)S(1)}, bf16[4,2,48,768]{3,2,1,0:T(8,128)(2,1)S(1)}, u32[]{:S(2)}, u32[]{:S(2)}) %collective-permute-start.49) | collective-permute-done | bytes 589856 | tf_op jit(solution)/shard_map/ppermute | solution.py:1309
  181.1 17.4 %ffn.2 = (f32[512,768]{1,0:T(8,128)}, f32[512,768]{1,0:T(8,128)}, bf16[512,768]{1,0:T(8,128)(2,1)}, bf16[8,48,512]{2,1,0:T(8,128)(2,1)}, bf16[8,48,512]{2,1,0:T(...) custom-call(s32[3]{0:T(128)} %pad_add_fusion.idx, ...), custom_call_target="tpu_custom_call" | custom-call | flops 23000000512 | bytes 1048576 | tf_op jit(solution)/shard_map/ffn/pallas_call | solution.py:407
  200.5 8.4 %qkv.3 = (bf16[512,1280]{1,0:T(8,128)(2,1)}, bf16[512,1280]{1,0:T(8,128)(2,1)}, bf16[8,48,512]{2,1,0:T(8,128)(2,1)}, bf16[8,48,512]{2,1,0:T(8,128)(2,1)}) custom-call(s32[3]{0:T(128)} %pad_add_fusion.idx, f32[512,768]{1,0:T(8,128)} %get-tuple-element.357.res.res_in, f32[8,768]{1,0:T(8,128)} %pad_convert_fusion.gb, bf16[128,768]{1,0:T(8,128)(2,1)} %pad.39.sw0, ...), custom_call_target="tpu_custom_call" | custom-call | flops 8049999872 | bytes 1048576 | tf_op jit(solution)/shard_map/qkv/pallas_call | solution.py:407
  214.0 11.3 %collective-permute-done.52.refs_19_.refs_3_ = bf16[4,2,48,768]{3,2,1,0:T(8,128)(2,1)} collective-permute-done((bf16[4,2,48,768]{3,2,1,0:T(8,128)(2,1)S(1)}, bf16[4,2,48,768]{3,2,1,0:T(8,128)(2,1)}, u32[]{:S(2)}, u32[]{:S(2)}) %collective-permute-start.52) | collective-permute-done | bytes 589856 | tf_op jit(solution)/shard_map/ppermute | solution.py:1309
  230.0 11.9 %attend.3 = (bf16[512,384]{1,0:T(8,128)(2,1)}, bf16[512,384]{1,0:T(8,128)(2,1)}, f32[8,1024]{1,0:T(8,128)}) custom-call(s32[3]{0:T(128)} %pad_add_fusion.idx, s32[6,8]{1,0:T(8,128)} %dynamic-slice_select_fusion.kept, s32[2]{0:T(128)} %broadcast_select_fusion.1.pics, bf16[512,1280]{1,0:T(8,128)(2,1)} %get-tuple-element.376.own, bf16[512,1280]{1,0:T(8,128)(2,1)} %copy-done.22), custom_call_target="tpu_custom_call" | custom-call | flops 13799999488 | bytes 1048576 | tf_op jit(solution)/shard_map/attend/pallas_call | solution.py:407
  244.7 17.4 %ffn.3 = (f32[512,768]{1,0:T(8,128)}, f32[512,768]{1,0:T(8,128)}, bf16[512,768]{1,0:T(8,128)(2,1)}, bf16[8,48,512]{2,1,0:T(8,128)(2,1)}, bf16[8,48,512]{2,1,0:T(...) custom-call(s32[3]{0:T(128)} %pad_add_fusion.idx, ...), custom_call_target="tpu_custom_call" | custom-call | flops 23000000512 | bytes 1048576 | tf_op jit(solution)/shard_map/ffn/pallas_call | solution.py:407
  263.0 11.2 %down_back.2.gu.gk = bf16[512,3072]{1,0:T(8,128)(2,1)} custom-call(s32[3]{0:T(128)} %pad_add_fusion.idx, bf16[512,768]{1,0:T(8,128)(2,1)} %copy-done.2, bf16[512,3072]{1,0:T(8,128)(2,1)} %get-tuple-element.407.slope_in, bf16[4,2,48,768]{3,2,1,0:T(8,128)(2,1)} %copy-done.5, bf16[4,2,48,768]{3,2,1,0:T(8,128)(2,1)} %copy-done.38, ...), custom_call_target="tpu_custom_call" | custom-call | flops 6899999744 | bytes 1048576 | tf_op jit(solution)/shard_map/down_back/pallas_call | solution.py:407
  276.0 2.4 convert_element_type.64.grad_in
  278.5 10.8 %up_back.2 = (f32[512,768]{1,0:T(8,128)}, bf16[512,768]{1,0:T(8,128)(2,1)}, bf16[512,384]{1,0:T(8,128)(2,1)}, bf16[512,384]{1,0:T(8,128)(2,1)}, f32[8,768]{1,0:T(8,128)}) custom-call(s32[3]{0:T(128)} %pad_add_fusion.idx, f32[512,768]{1,0:T(8,128)} %convert_element_type.64.grad_in, bf16[512,3072]{1,0:T(8,128)(2,1)} %down_back.2.gu.gk, ...), custom_call_target="tpu_custom_call" | custom-call | flops 11500000256 | bytes 1048576 | tf_op jit(solution)/shard_map/up_back/pallas_call | solution.py:407
  291.4 14.0 %ffn_grad.2 = bf16[16,2,2,48,768]{4,3,2,1,0:T(8,128)(2,1)} custom-call(s32[3]{0:T(128)} %pad_add_fusion.idx, bf16[384,512]{1,0:T(8,128)(2,1)} %bitcast.213, bf16[384,512]{1,0:T(8,128)(2,1)} %bitcast.40.xr, bf16[512,3072]{1,0:T(8,128)(2,1)} %down_back.2.gu.gk, bf16[512,3072]{1,0:T(8,128)(2,1)} %copy-done.18, bf16[1536,512]{1,0:T(8,128)(2,1)} %bitcast.207, ...), custom_call_target="tpu_custom_call" | custom-call | flops 12650000384 | bytes 1048576 | tf_op jit(solution)/shard_map/ffn_grad/pallas_call | solution.py:407
  305.5 17.2 %attend_back.2 = (bf16[512,1280]{1,0:T(8,128)(2,1)}, bf16[512,1280]{1,0:T(8,128)(2,1)}) custom-call(s32[3]{0:T(128)} %pad_add_fusion.idx, s32[6,8]{1,0:T(8,128)} %dynamic-slice_select_fusion.kept, s32[2]{0:T(128)} %broadcast_select_fusion.1.pics, f32[8,1024]{1,0:T(8,128)} %get-tuple-element.422.lse, bf16[512,1280]{1,0:T(8,128)(2,1)} %get-tuple-element.376.own, ...), custom_call_target="tpu_custom_call" | custom-call | flops 18400000000 | bytes 1048576 | tf_op jit(solution)/shard_map/attend_back/pallas_call | solution.py:407
  327.0 10.0 %qkv_back.2 = (f32[512,768]{1,0:T(8,128)}, bf16[512,768]{1,0:T(8,128)(2,1)}, f32[8,768]{1,0:T(8,128)}) custom-call(s32[3]{0:T(128)} %pad_add_fusion.idx, f32[512,768]{1,0:T(8,128)} %get-tuple-element.428.ga_in, bf16[512,1280]{1,0:T(8,128)(2,1)} %get-tuple-element.429.down_.d00, bf16[512,1280]{1,0:T(8,128)(2,1)} %copy-done.24, ...), custom_call_target="tpu_custom_call" | custom-call | flops 10350000128 | bytes 1048576 | tf_op jit(solution)/shard_map/qkv_back/pallas_call | solution.py:407
  338.4 10.2 %qkv_grad.2 = (bf16[2,4,1,48,768]{4,3,2,1,0:T(8,128)(2,1)}, bf16[2,4,1,48,768]{4,3,2,1,0:T(8,128)(2,1)}, bf16[2,4,1,48,768]{4,3,2,1,0:T(8,128)(2,1)}, bf16[2,4,1...) custom-call(s32[3]{0:T(128)} %pad_add_fusion.idx, bf16[384,512]{1,0:T(8,128)(2,1)} %bitcast.211, bf16[384,512]{1,0:T(8,128)(2,1)} %bitcast.44.xr, ...), custom_call_target="tpu_custom_call" | custom-call | flops 9200000000 | bytes 1048576 | tf_op jit(solution)/shard_map/qkv_grad/pallas_call | solution.py:407
  348.6 11.5 %down_back.3.gu.gk = bf16[512,3072]{1,0:T(8,128)(2,1)} custom-call(s32[3]{0:T(128)} %pad_add_fusion.idx, bf16[512,768]{1,0:T(8,128)(2,1)} %get-tuple-element.446.grad.dk, bf16[512,3072]{1,0:T(8,128)(2,1)} %get-tuple-element.447.slope_in, bf16[4,2,2,2,2,48,768]{6,5,4,3,2,1,0:T(8,128)(2,1)} %bitcast.198, ...), custom_call_target="tpu_custom_call" | custom-call | flops 6899999744 | bytes 1048576 | tf_op jit(solution)/shard_map/down_back/pallas_call | solution.py:407
  364.9 10.4 %up_back.3 = (f32[512,768]{1,0:T(8,128)}, bf16[512,768]{1,0:T(8,128)(2,1)}, bf16[512,384]{1,0:T(8,128)(2,1)}, bf16[512,384]{1,0:T(8,128)(2,1)}, f32[8,768]{1,0:T(8,128)}) custom-call(s32[3]{0:T(128)} %pad_add_fusion.idx, f32[512,768]{1,0:T(8,128)} %get-tuple-element.449.grad_in, bf16[512,3072]{1,0:T(8,128)(2,1)} %down_back.3.gu.gk, ...), custom_call_target="tpu_custom_call" | custom-call | flops 11500000256 | bytes 1048576 | tf_op jit(solution)/shard_map/up_back/pallas_call | solution.py:407
  375.3 1.8 collective-permute-start.76
  379.8 13.3 %collective-permute-done.76.ra = bf16[2,4,1,48,768]{4,3,2,1,0:T(8,128)(2,1)} collective-permute-done((bf16[2,4,1,48,768]{4,3,2,1,0:T(8,128)(2,1)}, bf16[2,4,1,48,768]{4,3,2,1,0:T(8,128)(2,1)}, u32[]{:S(2)}, u32[]{:S(2)}) %collective-permute-start.76) | collective-permute-done | bytes 589856 | tf_op jit(solution)/shard_map/ppermute | solution.py:1305
  394.6 3.4 cross.3
  399.9 14.1 %ffn_grad.3 = (bf16[2,4,2,48,768]{4,3,2,1,0:T(8,128)(2,1)}, bf16[2,4,2,48,768]{4,3,2,1,0:T(8,128)(2,1)}, bf16[2,4,2,48,768]{4,3,2,1,0:T(8,128)(2,1)}, bf16[2,4,2,48,768]{4,3,2,1,0:T(8,128)(2,1)}) custom-call(s32[3]{0:T(128)} %pad_add_fusion.idx, bf16[384,512]{1,0:T(8,128)(2,1)} %bitcast.210, bf16[384,512]{1,0:T(8,128)(2,1)} %bitcast.202, ...), custom_call_target="tpu_custom_call" | custom-call | flops 12650000384 | bytes 1048576 | tf_op jit(solution)/shard_map/ffn_grad/pallas_call | solution.py:407
  415.5 3.4 own.3
  418.9 4.3 collective-permute-start.87
  428.1 17.5 %attend_back.3 = (bf16[512,1280]{1,0:T(8,128)(2,1)}, bf16[512,1280]{1,0:T(8,128)(2,1)}) custom-call(s32[3]{0:T(128)} %pad_add_fusion.idx, s32[6,8]{1,0:T(8,128)} %dynamic-slice_select_fusion.kept, s32[2]{0:T(128)} %broadcast_select_fusion.1.pics, f32[8,1024]{1,0:T(8,128)} %get-tuple-element.477.lse, bf16[512,1280]{1,0:T(8,128)(2,1)} %get-tuple-element.318.own, ...), custom_call_target="tpu_custom_call" | custom-call | flops 18400000000 | bytes 1048576 | tf_op jit(solution)/shard_map/attend_back/pallas_call | solution.py:407
  446.3 12.3 %collective-permute-done.85.ra = bf16[2,4,2,48,768]{4,3,2,1,0:T(8,128)(2,1)S(1)} collective-permute-done((bf16[2,4,2,48,768]{4,3,2,1,0:T(8,128)(2,1)S(1)}, bf16[2,4,2,48,768]{4,3,2,1,0:T(8,128)(2,1)S(1)}, u32[]{:S(2)}, u32[]{:S(2)}) %collective-permute-start.85) | collective-permute-done | bytes 1179680 | tf_op jit(solution)/shard_map/ppermute | solution.py:1305
  459.8 3.7 cross.4
  467.6 10.2 %qkv_grad.3 = (bf16[2,4,1,48,768]{4,3,2,1,0:T(8,128)(2,1)}, bf16[2,4,1,48,768]{4,3,2,1,0:T(8,128)(2,1)}, bf16[2,4,1,48,768]{4,3,2,1,0:T(8,128)(2,1)}, bf16[2,4,1...) custom-call(s32[3]{0:T(128)} %pad_add_fusion.idx, bf16[384,512]{1,0:T(8,128)(2,1)} %bitcast.208, bf16[384,512]{1,0:T(8,128)(2,1)} %bitcast.55.xr, ...), custom_call_target="tpu_custom_call" | custom-call | flops 9200000000 | bytes 1048576 | tf_op jit(solution)/shard_map/qkv_grad/pallas_call | solution.py:407
  479.6 10.0 %qkv_back.3 = (f32[512,768]{1,0:T(8,128)}, bf16[512,768]{1,0:T(8,128)(2,1)}, f32[8,768]{1,0:T(8,128)}) custom-call(s32[3]{0:T(128)} %pad_add_fusion.idx, f32[512,768]{1,0:T(8,128)} %get-tuple-element.504.ga_in, bf16[512,1280]{1,0:T(8,128)(2,1)} %get-tuple-element.495.d00.down_, bf16[512,1280]{1,0:T(8,128)(2,1)} %copy-done.23, ...), custom_call_target="tpu_custom_call" | custom-call | flops 10350000128 | bytes 1048576 | tf_op jit(solution)/shard_map/qkv_back/pallas_call | solution.py:407
  495.4 3.1 collective-permute-start.105
  498.5 2.3 collective-permute-done.99.rb
  500.8 3.4 cross.5
  507.0 4.2 own.5
  511.3 9.6 %collective-permute-start.103 = (f32[4,48,128]{1,2,0:T(8,128)S(1)}, f32[4,48,128]{1,2,0:T(8,128)S(1)}, u32[]{:S(2)}, u32[]{:S(2)}) collective-permute-start(f32[4,48,128]{1,2,0:T(8,128)S(1)} %get-tuple-element.644), channel_id=1, source_target_pairs={{0,1},{1,0},{2,3},{3,2},{4,5},{5,4},{6,7},{7,6},{8,9},{9,8},{10,11... | collective-permute-start | bytes 294920 | tf_op jit(solution)/shard_map/ppermute | solution.py:1309
  522.2 6.6 %collective-permute-done.103 = f32[4,48,128]{1,2,0:T(8,128)S(1)} collective-permute-done((f32[4,48,128]{1,2,0:T(8,128)S(1)}, f32[4,48,128]{1,2,0:T(8,128)S(1)}, u32[]{:S(2)}, u32[]{:S(2)}) %collective-permute-start.103) | collective-permute-done | bytes 98336 | tf_op jit(solution)/shard_map/ppermute | solution.py:1309
  531.3 1.9 collective-permute-start.111
  533.3 2.5 collective-permute-start.113
  535.8 7.0 %collective-permute-done.109 = bf16[2,2,48,768]{3,2,1,0:T(8,128)(2,1)S(1)} collective-permute-done((bf16[2,2,48,768]{3,2,1,0:T(8,128)(2,1)S(1)}, bf16[2,2,48,768]{3,2,1,0:T(8,128)(2,1)S(1)}, u32[]{:S(2)}, u32[]{:S(2)}) %collective-permute-start.109) | collective-permute-done | bytes 294944 | tf_op jit(solution)/shard_map/ppermute | solution.py:1305
  542.8 2.1 collective-permute-start.114
  544.9 3.4 own.4
  548.2 7.9 %collective-permute-done.110 = bf16[2,2,48,768]{3,2,1,0:T(8,128)(2,1)S(1)} collective-permute-done((bf16[2,2,48,768]{3,2,1,0:T(8,128)(2,1)}, bf16[2,2,48,768]{3,2,1,0:T(8,128)(2,1)S(1)}, u32[]{:S(2)}, u32[]{:S(2)}) %collective-permute-start.110) | collective-permute-done | bytes 294944 | tf_op jit(solution)/shard_map/ppermute | solution.py:1305
  556.1 7.3 %collective-permute-start.107 = (bf16[2,1,48,768]{3,2,1,0:T(8,128)(2,1)}, bf16[2,1,48,768]{3,2,1,0:T(8,128)(2,1)S(1)}, u32[]{:S(2)}, u32[]{:S(2)}) collective-permute-start(bf16[2,1,48,768]{3,2,1,0:T(8,128)(2,1)} %get-tuple-element.532), channel_id=1, source_target_pairs={{0,16},{4,20},{8,24},{12,28},{16,0},{20,4},{24,8},{28,12},{1,17},{... | collective-permute-start | bytes 442376 | tf_op jit(solution)/shard_map/ppermute | solution.py:1305
  563.4 2.1 collective-permute-start.108
  568.8 5.8 collective-permute-done.107
  (494 shorter events, 112.1 us)
Async XLA Ops:
  7.2 157.3 %all-gather.3.cloned.1.call-start = ((), (), s32[]{:S(2)}) async-start(), calls=%async_computation.2 | async-start | bytes 5013504 | tf_op jit(solution)/shard_map/all_gather | solution.py:1432
  11.7 34.8 %collective-permute-start.6 = (bf16[512,768]{1,0:T(8,128)(2,1)}, bf16[512,768]{1,0:T(8,128)(2,1)S(1)}, u32[]{:S(2)}, u32[]{:S(2)}) collective-permute-start(bf16[512,768]{1,0:T(8,128)(2,1)} %bitcast.200), channel_id=1, source_target_pairs={{0,0},{1,2},{2,1},{3,3},{4,4},{5,6},{6,5},{7,7},{8,8},{9,10},{10,9... | collective-permute-start | bytes 2359304 | tf_op jit(solution)/shard_map/ppermute | solution.py:1325
  17.2 559.0 %reduce-scatter.2.cloned.1.call-start = ((), (), s32[]{:S(2)}) async-start(), calls=%async_computation.1 | async-start | bytes 5013504 | tf_op jit(solution)/shard_map/reduce_scatter | solution.py:1516
  18.0 28.5 %collective-permute-start = (bf16[2,1,48,768]{3,2,1,0:T(8,128)(2,1)S(1)}, bf16[2,1,48,768]{3,2,1,0:T(8,128)(2,1)S(1)}, u32[]{:S(2)}, u32[]{:S(2)}) collective-permute-start(bf16[2,1,48,768]{3,2,1,0:T(8,128)(2,1)S(1)} %maximum_bitcast_fusion.4), channel_id=1, source_target_pairs={{0,8},{4,12},{8,0},{12,4},{16,24},{20,28},{24,16},{28,20},{1,9},{5... | collective-permute-start | bytes 442376 | tf_op jit(solution)/shard_map/ppermute | solution.py:1305
  18.1 28.4 %collective-permute-start.1 = (bf16[2,1,48,768]{3,2,1,0:T(8,128)(2,1)S(1)}, bf16[2,1,48,768]{3,2,1,0:T(8,128)(2,1)S(1)}, u32[]{:S(2)}, u32[]{:S(2)}) collective-permute-start(bf16[2,1,48,768]{3,2,1,0:T(8,128)(2,1)S(1)} %maximum_bitcast_fusion.4), channel_id=1, source_target_pairs={{0,16},{4,20},{8,24},{12,28},{16,0},{20,4},{24,8},{28,12},{1,17},{... | collective-permute-start | bytes 442376 | tf_op jit(solution)/shard_map/ppermute | solution.py:1305
  21.1 25.4 %collective-permute-start.2 = (bf16[2,1,48,768]{3,2,1,0:T(8,128)(2,1)S(1)}, bf16[2,1,48,768]{3,2,1,0:T(8,128)(2,1)S(1)}, u32[]{:S(2)}, u32[]{:S(2)}) collective-permute-start(bf16[2,1,48,768]{3,2,1,0:T(8,128)(2,1)S(1)} %maximum_bitcast_fusion.4), channel_id=1, source_target_pairs={{0,24},{4,28},{8,16},{12,20},{16,8},{20,12},{24,0},{28,4},{1,25},{... | collective-permute-start | bytes 442376 | tf_op jit(solution)/shard_map/ppermute | solution.py:1305
  22.4 17.4 %collective-permute-start.4 = (bf16[32,128]{1,0:T(8,128)(2,1)S(1)}, bf16[32,128]{1,0:T(8,128)(2,1)S(1)}, u32[]{:S(2)}, u32[]{:S(2)}) collective-permute-start(bf16[32,128]{1,0:T(8,128)(2,1)S(1)} %get-tuple-element.682), channel_id=1, source_target_pairs={{0,16},{4,20},{8,24},{12,28},{16,0},{20,4},{24,8},{28,12},{1,17},{... | collective-permute-start | bytes 24584 | tf_op jit(solution)/shard_map/ppermute | solution.py:1305
  46.7 24.7 %collective-permute-start.10 = (bf16[4,1,48,768]{3,2,1,0:T(8,128)(2,1)S(1)}, bf16[4,1,48,768]{3,2,1,0:T(8,128)(2,1)S(1)}, u32[]{:S(2)}, u32[]{:S(2)}) collective-permute-start(bf16[4,1,48,768]{3,2,1,0:T(8,128)(2,1)S(1)} %pad_maximum_fusion.6.refs_8_), channel_id=1, source_target_pairs={{0,4},{4,0},{8,12},{12,8},{16,20},{20,16},{24,28},{28,24},{1,5},{5... | collective-permute-start | bytes 884744 | tf_op jit(solution)/shard_map/ppermute | solution.py:1305
  48.7 23.3 %collective-permute-start.8 = (bf16[4,1,48,768]{3,2,1,0:T(8,128)(2,1)S(1)}, bf16[4,1,48,768]{3,2,1,0:T(8,128)(2,1)S(1)}, u32[]{:S(2)}, u32[]{:S(2)}) collective-permute-start(bf16[4,1,48,768]{3,2,1,0:T(8,128)(2,1)S(1)} %pad_maximum_fusion.6.refs_8_), channel_id=1, source_target_pairs={{0,1},{1,0},{2,3},{3,2},{4,5},{5,4},{6,7},{7,6},{8,9},{9,8},{10,11... | collective-permute-start | bytes 884744 | tf_op jit(solution)/shard_map/ppermute | solution.py:1309
  49.1 22.8 %collective-permute-start.7 = (bf16[4,1,48,768]{3,2,1,0:T(8,128)(2,1)S(1)}, bf16[4,1,48,768]{3,2,1,0:T(8,128)(2,1)S(1)}, u32[]{:S(2)}, u32[]{:S(2)}) collective-permute-start(bf16[4,1,48,768]{3,2,1,0:T(8,128)(2,1)S(1)} %pad_maximum_fusion.5.refs_0_), channel_id=1, source_target_pairs={{0,4},{4,0},{8,12},{12,8},{16,20},{20,16},{24,28},{28,24},{1,5},{5... | collective-permute-start | bytes 884744 | tf_op jit(solution)/shard_map/ppermute | solution.py:1305
  49.7 22.2 %collective-permute-start.9 = (bf16[4,1,48,768]{3,2,1,0:T(8,128)(2,1)S(1)}, bf16[4,1,48,768]{3,2,1,0:T(8,128)(2,1)S(1)}, u32[]{:S(2)}, u32[]{:S(2)}) collective-permute-start(bf16[4,1,48,768]{3,2,1,0:T(8,128)(2,1)S(1)} %pad_maximum_fusion.5.refs_0_), channel_id=1, source_target_pairs={{0,1},{1,0},{2,3},{3,2},{4,5},{5,4},{6,7},{7,6},{8,9},{9,8},{10,11... | collective-permute-start | bytes 884744 | tf_op jit(solution)/shard_map/ppermute | solution.py:1309
  51.0 20.5 %collective-permute-start.11 = (bf16[4,32,128]{2,1,0:T(8,128)(2,1)S(1)}, bf16[4,32,128]{2,1,0:T(8,128)(2,1)S(1)}, u32[]{:S(2)}, u32[]{:S(2)}) collective-permute-start(bf16[4,32,128]{2,1,0:T(8,128)(2,1)S(1)} %pad_maximum_fusion.14), channel_id=1, source_target_pairs={{0,4},{4,0},{8,12},{12,8},{16,20},{20,16},{24,28},{28,24},{1,5},{5... | collective-permute-start | bytes 98312 | tf_op jit(solution)/shard_map/ppermute | solution.py:1305
  84.1 33.9 %collective-permute-start.26 = (s32[12,8]{1,0:T(8,128)S(1)}, s32[12,8]{1,0:T(8,128)S(1)}, u32[]{:S(2)}, u32[]{:S(2)}) collective-permute-start(s32[12,8]{1,0:T(8,128)S(1)} %copy.91), channel_id=1, source_target_pairs={{0,2},{2,0},{1,3},{3,1},{4,6},{6,4},{5,7},{7,5},{8,10},{10,8},{9,1... | collective-permute-start | bytes 1160 | tf_op jit(solution)/shard_map/ppermute | solution.py:1313
  84.1 33.3 %collective-permute-start.27 = (s32[2]{0:T(128)S(1)}, s32[2]{0:T(128)S(1)}, u32[]{:S(2)}, u32[]{:S(2)}) collective-permute-start(s32[2]{0:T(128)S(1)} %bitcast.195), channel_id=1, source_target_pairs={{0,2},{2,0},{1,3},{3,1},{4,6},{6,4},{5,7},{7,5},{8,10},{10,8},{9,1... | collective-permute-start | bytes 32 | tf_op jit(solution)/shard_map/ppermute | solution.py:1313
  90.2 16.7 %collective-permute-start.24 = (bf16[2,1,48,768]{3,2,1,0:T(8,128)(2,1)S(1)}, bf16[2,1,48,768]{3,2,1,0:T(8,128)(2,1)S(1)}, u32[]{:S(2)}, u32[]{:S(2)}) collective-permute-start(bf16[2,1,48,768]{3,2,1,0:T(8,128)(2,1)S(1)} %maximum_bitcast_fusion.5), channel_id=1, source_target_pairs={{0,16},{4,20},{8,24},{12,28},{16,0},{20,4},{24,8},{28,12},{1,17},{... | collective-permute-start | bytes 442376 | tf_op jit(solution)/shard_map/ppermute | solution.py:1305
  94.8 19.5 %collective-permute-start.25 = (bf16[2,1,48,768]{3,2,1,0:T(8,128)(2,1)S(1)}, bf16[2,1,48,768]{3,2,1,0:T(8,128)(2,1)S(1)}, u32[]{:S(2)}, u32[]{:S(2)}) collective-permute-start(bf16[2,1,48,768]{3,2,1,0:T(8,128)(2,1)S(1)} %maximum_bitcast_fusion.5), channel_id=1, source_target_pairs={{0,24},{4,28},{8,16},{12,20},{16,8},{20,12},{24,0},{28,4},{1,25},{... | collective-permute-start | bytes 442376 | tf_op jit(solution)/shard_map/ppermute | solution.py:1305
  105.7 26.6 %collective-permute-start.28 = (bf16[512,1280]{1,0:T(8,128)(2,1)}, bf16[512,1280]{1,0:T(8,128)(2,1)S(1)}, u32[]{:S(2)}, u32[]{:S(2)}) collective-permute-start(bf16[512,1280]{1,0:T(8,128)(2,1)} %get-tuple-element.319), channel_id=1, source_target_pairs={{0,2},{2,0},{1,3},{3,1},{4,6},{6,4},{5,7},{7,5},{8,10},{10,8},{9,1... | collective-permute-start | bytes 3932168 | tf_op jit(solution)/shard_map/ppermute | solution.py:1313
  118.6 27.6 %collective-permute-start.29 = (bf16[4,1,48,768]{3,2,1,0:T(8,128)(2,1)S(1)}, bf16[4,1,48,768]{3,2,1,0:T(8,128)(2,1)S(1)}, u32[]{:S(2)}, u32[]{:S(2)}) collective-permute-start(bf16[4,1,48,768]{3,2,1,0:T(8,128)(2,1)S(1)} %pad_maximum_fusion.7.refs_0_), channel_id=1, source_target_pairs={{0,4},{4,0},{8,12},{12,8},{16,20},{20,16},{24,28},{28,24},{1,5},{5... | collective-permute-start | bytes 884744 | tf_op jit(solution)/shard_map/ppermute | solution.py:1305
  119.6 26.7 %collective-permute-start.31 = (bf16[4,1,48,768]{3,2,1,0:T(8,128)(2,1)S(1)}, bf16[4,1,48,768]{3,2,1,0:T(8,128)(2,1)S(1)}, u32[]{:S(2)}, u32[]{:S(2)}) collective-permute-start(bf16[4,1,48,768]{3,2,1,0:T(8,128)(2,1)S(1)} %pad_maximum_fusion.7.refs_0_), channel_id=1, source_target_pairs={{0,1},{1,0},{2,3},{3,2},{4,5},{5,4},{6,7},{7,6},{8,9},{9,8},{10,11... | collective-permute-start | bytes 884744 | tf_op jit(solution)/shard_map/ppermute | solution.py:1309
  124.4 22.4 %collective-permute-start.33 = (bf16[2,2,48,768]{3,2,1,0:T(8,128)(2,1)S(1)}, bf16[2,2,48,768]{3,2,1,0:T(8,128)(2,1)S(1)}, u32[]{:S(2)}, u32[]{:S(2)}) collective-permute-start(bf16[2,2,48,768]{3,2,1,0:T(8,128)(2,1)S(1)} %pad_maximum_fusion.9), channel_id=1, source_target_pairs={{0,8},{4,12},{8,0},{12,4},{16,24},{20,28},{24,16},{28,20},{1,9},{5... | collective-permute-start | bytes 884744 | tf_op jit(solution)/shard_map/ppermute | solution.py:1305
  129.9 21.7 %collective-permute-start.34 = (bf16[2,2,48,768]{3,2,1,0:T(8,128)(2,1)S(1)}, bf16[2,2,48,768]{3,2,1,0:T(8,128)(2,1)S(1)}, u32[]{:S(2)}, u32[]{:S(2)}) collective-permute-start(bf16[2,2,48,768]{3,2,1,0:T(8,128)(2,1)S(1)} %pad_maximum_fusion.9), channel_id=1, source_target_pairs={{0,16},{4,20},{8,24},{12,28},{16,0},{20,4},{24,8},{28,12},{1,17},{... | collective-permute-start | bytes 884744 | tf_op jit(solution)/shard_map/ppermute | solution.py:1305
  132.2 19.4 %collective-permute-start.35 = (bf16[2,2,48,768]{3,2,1,0:T(8,128)(2,1)S(1)}, bf16[2,2,48,768]{3,2,1,0:T(8,128)(2,1)S(1)}, u32[]{:S(2)}, u32[]{:S(2)}) collective-permute-start(bf16[2,2,48,768]{3,2,1,0:T(8,128)(2,1)S(1)} %pad_maximum_fusion.9), channel_id=1, source_target_pairs={{0,24},{4,28},{8,16},{12,20},{16,8},{20,12},{24,0},{28,4},{1,25},{... | collective-permute-start | bytes 884744 | tf_op jit(solution)/shard_map/ppermute | solution.py:1305
  164.9 16.2 %collective-permute-start.49 = (bf16[4,2,48,768]{3,2,1,0:T(8,128)(2,1)S(1)}, bf16[4,2,48,768]{3,2,1,0:T(8,128)(2,1)S(1)}, u32[]{:S(2)}, u32[]{:S(2)}) collective-permute-start(bf16[4,2,48,768]{3,2,1,0:T(8,128)(2,1)S(1)} %pad_maximum_fusion.1.refs_24_.refs_8_), channel_id=1, source_target_pairs={{0,1},{1,0},{2,3},{3,2},{4,5},{5,4},{6,7},{7,6},{8,9},{9,8},{10,11... | collective-permute-start | bytes 1769480 | tf_op jit(solution)/shard_map/ppermute | solution.py:1309
  167.7 30.8 %collective-permute-start.51 = (bf16[4,2,48,768]{3,2,1,0:T(8,128)(2,1)S(1)}, bf16[4,2,48,768]{3,2,1,0:T(8,128)(2,1)S(1)}, u32[]{:S(2)}, u32[]{:S(2)}) collective-permute-start(bf16[4,2,48,768]{3,2,1,0:T(8,128)(2,1)S(1)} %pad_maximum_fusion.1.refs_24_.refs_8_), channel_id=1, source_target_pairs={{0,4},{4,0},{8,12},{12,8},{16,20},{20,16},{24,28},{28,24},{1,5},{5... | collective-permute-start | bytes 1769480 | tf_op jit(solution)/shard_map/ppermute | solution.py:1305
  169.6 29.0 %collective-permute-start.48 = (bf16[4,2,48,768]{3,2,1,0:T(8,128)(2,1)S(1)}, bf16[4,2,48,768]{3,2,1,0:T(8,128)(2,1)S(1)}, u32[]{:S(2)}, u32[]{:S(2)}) collective-permute-start(bf16[4,2,48,768]{3,2,1,0:T(8,128)(2,1)S(1)} %pad_maximum_fusion.refs_16_.refs_0_), channel_id=1, source_target_pairs={{0,4},{4,0},{8,12},{12,8},{16,20},{20,16},{24,28},{28,24},{1,5},{5... | collective-permute-start | bytes 1769480 | tf_op jit(solution)/shard_map/ppermute | solution.py:1305
  172.8 25.8 %collective-permute-start.50 = (bf16[4,2,48,768]{3,2,1,0:T(8,128)(2,1)S(1)}, bf16[4,2,48,768]{3,2,1,0:T(8,128)(2,1)S(1)}, u32[]{:S(2)}, u32[]{:S(2)}) collective-permute-start(bf16[4,2,48,768]{3,2,1,0:T(8,128)(2,1)S(1)} %pad_maximum_fusion.refs_16_.refs_0_), channel_id=1, source_target_pairs={{0,1},{1,0},{2,3},{3,2},{4,5},{5,4},{6,7},{7,6},{8,9},{9,8},{10,11... | collective-permute-start | bytes 1769480 | tf_op jit(solution)/shard_map/ppermute | solution.py:1309
  173.4 25.3 %collective-permute-start.46 = (bf16[4,1,48,768]{3,2,1,0:T(8,128)(2,1)}, bf16[4,1,48,768]{3,2,1,0:T(8,128)(2,1)S(1)}, u32[]{:S(2)}, u32[]{:S(2)}) collective-permute-start(bf16[4,1,48,768]{3,2,1,0:T(8,128)(2,1)} %copy-done.73), channel_id=1, source_target_pairs={{0,2},{2,0},{1,3},{3,1},{4,6},{6,4},{5,7},{7,5},{8,10},{10,8},{9,1... | collective-permute-start | bytes 884744 | tf_op jit(solution)/shard_map/ppermute | solution.py:1313
  181.1 17.5 %collective-permute-start.47 = (bf16[4,1,48,768]{3,2,1,0:T(8,128)(2,1)}, bf16[4,1,48,768]{3,2,1,0:T(8,128)(2,1)S(1)}, u32[]{:S(2)}, u32[]{:S(2)}) collective-permute-start(bf16[4,1,48,768]{3,2,1,0:T(8,128)(2,1)} %copy-done.75), channel_id=1, source_target_pairs={{0,2},{2,0},{1,3},{3,1},{4,6},{6,4},{5,7},{7,5},{8,10},{10,8},{9,1... | collective-permute-start | bytes 884744 | tf_op jit(solution)/shard_map/ppermute | solution.py:1313
  208.9 20.1 %collective-permute-start.60 = (bf16[512,1280]{1,0:T(8,128)(2,1)}, bf16[512,1280]{1,0:T(8,128)(2,1)S(1)}, u32[]{:S(2)}, u32[]{:S(2)}) collective-permute-start(bf16[512,1280]{1,0:T(8,128)(2,1)} %get-tuple-element.377), channel_id=1, source_target_pairs={{0,2},{2,0},{1,3},{3,1},{4,6},{6,4},{5,7},{7,5},{8,10},{10,8},{9,1... | collective-permute-start | bytes 3932168 | tf_op jit(solution)/shard_map/ppermute | solution.py:1313
  242.2 20.0 %collective-permute-start.65 = (bf16[512,768]{1,0:T(8,128)(2,1)S(1)}, bf16[512,768]{1,0:T(8,128)(2,1)S(1)}, u32[]{:S(2)}, u32[]{:S(2)}) collective-permute-start(bf16[512,768]{1,0:T(8,128)(2,1)S(1)} %bitcast.201), channel_id=1, source_target_pairs={{0,0},{1,2},{2,1},{3,3},{4,4},{5,6},{6,5},{7,7},{8,8},{9,10},{10,9... | collective-permute-start | bytes 2359304 | tf_op jit(solution)/shard_map/ppermute | solution.py:1325
  274.2 15.6 %collective-permute-start.67 = (bf16[512,3072]{1,0:T(8,128)(2,1)}, bf16[512,3072]{1,0:T(8,128)(2,1)S(1)}, u32[]{:S(2)}, u32[]{:S(2)}) collective-permute-start(bf16[512,3072]{1,0:T(8,128)(2,1)} %down_back.2.gu.gk), channel_id=1, source_target_pairs={{0,2},{2,0},{1,3},{3,1},{4,6},{6,4},{5,7},{7,5},{8,10},{10,8},{9,1... | collective-permute-start | bytes 9437192 | tf_op jit(solution)/shard_map/ppermute | solution.py:1313
  289.3 16.2 %collective-permute-start.70 = (bf16[512,384]{1,0:T(8,128)(2,1)}, bf16[512,384]{1,0:T(8,128)(2,1)}, u32[]{:S(2)}, u32[]{:S(2)}) collective-permute-start(bf16[512,384]{1,0:T(8,128)(2,1)} %get-tuple-element.424), channel_id=1, source_target_pairs={{0,2},{2,0},{1,3},{3,1},{4,6},{6,4},{5,7},{7,5},{8,10},{10,8},{9,1... | collective-permute-start | bytes 1179656 | tf_op jit(solution)/shard_map/ppermute | solution.py:1313
  323.8 38.3 %collective-permute-start.64 = (bf16[512,768]{1,0:T(8,128)(2,1)S(1)}, bf16[512,768]{1,0:T(8,128)(2,1)S(1)}, u32[]{:S(2)}, u32[]{:S(2)}) collective-permute-start(bf16[512,768]{1,0:T(8,128)(2,1)S(1)} %copy-done.31), channel_id=1, source_target_pairs={{0,0},{1,2},{2,1},{3,3},{4,4},{5,6},{6,5},{7,7},{8,8},{9,10},{10,9... | collective-permute-start | bytes 2359304 | tf_op jit(solution)/shard_map/ppermute | solution.py:1325
  360.1 39.8 %collective-permute-start.79 = (bf16[512,3072]{1,0:T(8,128)(2,1)}, bf16[512,3072]{1,0:T(8,128)(2,1)}, u32[]{:S(2)}, u32[]{:S(2)}) collective-permute-start(bf16[512,3072]{1,0:T(8,128)(2,1)} %down_back.3.gu.gk), channel_id=1, source_target_pairs={{0,2},{2,0},{1,3},{3,1},{4,6},{6,4},{5,7},{7,5},{8,10},{10,8},{9,1... | collective-permute-start | bytes 9437192 | tf_op jit(solution)/shard_map/ppermute | solution.py:1313
  361.1 37.9 %collective-permute-start.80 = (bf16[8,192,512]{2,1,0:T(8,128)(2,1)S(1)}, bf16[8,192,512]{2,1,0:T(8,128)(2,1)}, u32[]{:S(2)}, u32[]{:S(2)}) collective-permute-start(bf16[8,192,512]{2,1,0:T(8,128)(2,1)S(1)} %copy-done.19), channel_id=1, source_target_pairs={{0,2},{2,0},{1,3},{3,1},{4,6},{6,4},{5,7},{7,5},{8,10},{10,8},{9,1... | collective-permute-start | bytes 4718600 | tf_op jit(solution)/shard_map/ppermute | solution.py:1313
  364.4 35.4 %collective-permute-start.81 = (bf16[512,768]{1,0:T(8,128)(2,1)S(1)}, bf16[512,768]{1,0:T(8,128)(2,1)}, u32[]{:S(2)}, u32[]{:S(2)}) collective-permute-start(bf16[512,768]{1,0:T(8,128)(2,1)S(1)} %copy-done.32), channel_id=1, source_target_pairs={{0,2},{2,0},{1,3},{3,1},{4,6},{6,4},{5,7},{7,5},{8,10},{10,8},{9,1... | collective-permute-start | bytes 2359304 | tf_op jit(solution)/shard_map/ppermute | solution.py:1313
  375.3 17.8 %collective-permute-start.76 = (bf16[2,4,1,48,768]{4,3,2,1,0:T(8,128)(2,1)}, bf16[2,4,1,48,768]{4,3,2,1,0:T(8,128)(2,1)}, u32[]{:S(2)}, u32[]{:S(2)}) collective-permute-start(bf16[2,4,1,48,768]{4,3,2,1,0:T(8,128)(2,1)} %get-tuple-element.458), channel_id=1, source_target_pairs={{0,4},{4,0},{8,12},{12,8},{16,20},{20,16},{24,28},{28,24},{1,5},{5... | collective-permute-start | bytes 1769480 | tf_op jit(solution)/shard_map/ppermute | solution.py:1305
  377.1 17.5 %collective-permute-start.77 = (bf16[2,4,1,48,768]{4,3,2,1,0:T(8,128)(2,1)}, bf16[2,4,1,48,768]{4,3,2,1,0:T(8,128)(2,1)}, u32[]{:S(2)}, u32[]{:S(2)}) collective-permute-start(bf16[2,4,1,48,768]{4,3,2,1,0:T(8,128)(2,1)} %get-tuple-element.459), channel_id=1, source_target_pairs={{0,1},{1,0},{2,3},{3,2},{4,5},{5,4},{6,7},{7,6},{8,9},{9,8},{10,11... | collective-permute-start | bytes 1769480 | tf_op jit(solution)/shard_map/ppermute | solution.py:1309
  394.6 32.6 %collective-permute-start.84 = (bf16[512,384]{1,0:T(8,128)(2,1)}, bf16[512,384]{1,0:T(8,128)(2,1)}, u32[]{:S(2)}, u32[]{:S(2)}) collective-permute-start(bf16[512,384]{1,0:T(8,128)(2,1)} %get-tuple-element.479), channel_id=1, source_target_pairs={{0,2},{2,0},{1,3},{3,1},{4,6},{6,4},{5,7},{7,5},{8,10},{10,8},{9,1... | collective-permute-start | bytes 1179656 | tf_op jit(solution)/shard_map/ppermute | solution.py:1313
  398.0 16.0 %collective-permute-start.82 = (bf16[4,1,48,768]{3,2,1,0:T(8,128)(2,1)}, bf16[4,1,48,768]{3,2,1,0:T(8,128)(2,1)S(1)}, u32[]{:S(2)}, u32[]{:S(2)}) collective-permute-start(bf16[4,1,48,768]{3,2,1,0:T(8,128)(2,1)} %get-tuple-element.474), channel_id=1, source_target_pairs={{0,1},{1,0},{2,3},{3,2},{4,5},{5,4},{6,7},{7,6},{8,9},{9,8},{10,11... | collective-permute-start | bytes 884744 | tf_op jit(solution)/shard_map/ppermute | solution.py:1309
  418.9 26.8 %collective-permute-start.87 = (bf16[2,1,48,768]{3,2,0,1:T(8,128)(2,1)}, bf16[2,1,48,768]{3,2,0,1:T(8,128)(2,1)S(1)}, u32[]{:S(2)}, u32[]{:S(2)}) collective-permute-start(bf16[2,1,48,768]{3,2,0,1:T(8,128)(2,1)} %bitcast.205), channel_id=1, source_target_pairs={{0,8},{4,12},{8,0},{12,4},{16,24},{20,28},{24,16},{28,20},{1,9},{5... | collective-permute-start | bytes 442376 | tf_op jit(solution)/shard_map/ppermute | solution.py:1305
  423.2 22.5 %collective-permute-start.88 = (bf16[2,1,48,768]{3,2,0,1:T(8,128)(2,1)}, bf16[2,1,48,768]{3,2,0,1:T(8,128)(2,1)S(1)}, u32[]{:S(2)}, u32[]{:S(2)}) collective-permute-start(bf16[2,1,48,768]{3,2,0,1:T(8,128)(2,1)} %bitcast.204), channel_id=1, source_target_pairs={{0,16},{4,20},{8,24},{12,28},{16,0},{20,4},{24,8},{28,12},{1,17},{... | collective-permute-start | bytes 442376 | tf_op jit(solution)/shard_map/ppermute | solution.py:1305
  423.9 22.3 %collective-permute-start.89 = (bf16[2,1,48,768]{3,2,0,1:T(8,128)(2,1)}, bf16[2,1,48,768]{3,2,0,1:T(8,128)(2,1)S(1)}, u32[]{:S(2)}, u32[]{:S(2)}) collective-permute-start(bf16[2,1,48,768]{3,2,0,1:T(8,128)(2,1)} %bitcast.203), channel_id=1, source_target_pairs={{0,24},{4,28},{8,16},{12,20},{16,8},{20,12},{24,0},{28,4},{1,25},{... | collective-permute-start | bytes 442376 | tf_op jit(solution)/shard_map/ppermute | solution.py:1305
  425.6 33.0 %collective-permute-start.85 = (bf16[2,4,2,48,768]{4,3,2,1,0:T(8,128)(2,1)S(1)}, bf16[2,4,2,48,768]{4,3,2,1,0:T(8,128)(2,1)S(1)}, u32[]{:S(2)}, u32[]{:S(2)}) collective-permute-start(bf16[2,4,2,48,768]{4,3,2,1,0:T(8,128)(2,1)S(1)} %copy-done.29), channel_id=1, source_target_pairs={{0,4},{4,0},{8,12},{12,8},{16,20},{20,16},{24,28},{28,24},{1,5},{5... | collective-permute-start | bytes 3538952 | tf_op jit(solution)/shard_map/ppermute | solution.py:1305
  427.2 32.5 %collective-permute-start.86 = (bf16[2,4,2,48,768]{4,3,2,1,0:T(8,128)(2,1)S(1)}, bf16[2,4,2,48,768]{4,3,2,1,0:T(8,128)(2,1)}, u32[]{:S(2)}, u32[]{:S(2)}) collective-permute-start(bf16[2,4,2,48,768]{4,3,2,1,0:T(8,128)(2,1)S(1)} %copy-done.28), channel_id=1, source_target_pairs={{0,1},{1,0},{2,3},{3,2},{4,5},{5,4},{6,7},{7,6},{8,9},{9,8},{10,11... | collective-permute-start | bytes 3538952 | tf_op jit(solution)/shard_map/ppermute | solution.py:1309
  445.6 18.0 %collective-permute-start.90 = (bf16[8,48,512]{2,1,0:T(8,128)(2,1)}, bf16[8,48,512]{2,1,0:T(8,128)(2,1)}, u32[]{:S(2)}, u32[]{:S(2)}) collective-permute-start(bf16[8,48,512]{2,1,0:T(8,128)(2,1)} %get-tuple-element.492), channel_id=1, source_target_pairs={{0,2},{2,0},{1,3},{3,1},{4,6},{6,4},{5,7},{7,5},{8,10},{10,8},{9,1... | collective-permute-start | bytes 1179656 | tf_op jit(solution)/shard_map/ppermute | solution.py:1313
  445.7 18.8 %collective-permute-start.91 = (bf16[8,48,512]{2,1,0:T(8,128)(2,1)}, bf16[8,48,512]{2,1,0:T(8,128)(2,1)}, u32[]{:S(2)}, u32[]{:S(2)}) collective-permute-start(bf16[8,48,512]{2,1,0:T(8,128)(2,1)} %get-tuple-element.494), channel_id=1, source_target_pairs={{0,2},{2,0},{1,3},{3,1},{4,6},{6,4},{5,7},{7,5},{8,10},{10,8},{9,1... | collective-permute-start | bytes 1179656 | tf_op jit(solution)/shard_map/ppermute | solution.py:1313
  446.2 19.8 %collective-permute-start.94 = (bf16[512,768]{1,0:T(8,128)(2,1)}, bf16[512,768]{1,0:T(8,128)(2,1)}, u32[]{:S(2)}, u32[]{:S(2)}) collective-permute-start(bf16[512,768]{1,0:T(8,128)(2,1)} %get-tuple-element.497.gk), channel_id=1, source_target_pairs={{0,2},{2,0},{1,3},{3,1},{4,6},{6,4},{5,7},{7,5},{8,10},{10,8},{9,1... | collective-permute-start | bytes 2359304 | tf_op jit(solution)/shard_map/ppermute | solution.py:1313
  463.6 30.4 %collective-permute-start.96 = (bf16[4,2,48,768]{3,2,1,0:T(8,128)(2,1)}, bf16[4,2,48,768]{3,2,1,0:T(8,128)(2,1)}, u32[]{:S(2)}, u32[]{:S(2)}) collective-permute-start(bf16[4,2,48,768]{3,2,1,0:T(8,128)(2,1)} %get-tuple-element.513), channel_id=1, source_target_pairs={{0,1},{1,0},{2,3},{3,2},{4,5},{5,4},{6,7},{7,6},{8,9},{9,8},{10,11... | collective-permute-start | bytes 1769480 | tf_op jit(solution)/shard_map/ppermute | solution.py:1309
  464.6 30.8 %collective-permute-start.97 = (bf16[4,2,48,768]{3,2,1,0:T(8,128)(2,1)}, bf16[4,2,48,768]{3,2,1,0:T(8,128)(2,1)}, u32[]{:S(2)}, u32[]{:S(2)}) collective-permute-start(bf16[4,2,48,768]{3,2,1,0:T(8,128)(2,1)} %get-tuple-element.514), channel_id=1, source_target_pairs={{0,4},{4,0},{8,12},{12,8},{16,20},{20,16},{24,28},{28,24},{1,5},{5... | collective-permute-start | bytes 1769480 | tf_op jit(solution)/shard_map/ppermute | solution.py:1305
  477.8 20.7 %collective-permute-start.98 = (bf16[2,4,1,48,768]{4,3,2,1,0:T(8,128)(2,1)}, bf16[2,4,1,48,768]{4,3,2,1,0:T(8,128)(2,1)}, u32[]{:S(2)}, u32[]{:S(2)}) collective-permute-start(bf16[2,4,1,48,768]{4,3,2,1,0:T(8,128)(2,1)} %get-tuple-element.515), channel_id=1, source_target_pairs={{0,4},{4,0},{8,12},{12,8},{16,20},{20,16},{24,28},{28,24},{1,5},{5... | collective-permute-start | bytes 1769480 | tf_op jit(solution)/shard_map/ppermute | solution.py:1305
  478.4 22.3 %collective-permute-start.99 = (bf16[2,4,1,48,768]{4,3,2,1,0:T(8,128)(2,1)}, bf16[2,4,1,48,768]{4,3,2,1,0:T(8,128)(2,1)}, u32[]{:S(2)}, u32[]{:S(2)}) collective-permute-start(bf16[2,4,1,48,768]{4,3,2,1,0:T(8,128)(2,1)} %get-tuple-element.516), channel_id=1, source_target_pairs={{0,1},{1,0},{2,3},{3,2},{4,5},{5,4},{6,7},{7,6},{8,9},{9,8},{10,11... | collective-permute-start | bytes 1769480 | tf_op jit(solution)/shard_map/ppermute | solution.py:1309
  492.0 19.2 %collective-permute-start.95 = (bf16[512,768]{1,0:T(8,128)(2,1)S(1)}, bf16[512,768]{1,0:T(8,128)(2,1)S(1)}, u32[]{:S(2)}, u32[]{:S(2)}) collective-permute-start(bf16[512,768]{1,0:T(8,128)(2,1)S(1)} %copy-done.33), channel_id=1, source_target_pairs={{0,0},{1,2},{2,1},{3,3},{4,4},{5,6},{6,5},{7,7},{8,8},{9,10},{10,9... | collective-permute-start | bytes 2359304 | tf_op jit(solution)/shard_map/ppermute | solution.py:1325
  494.0 35.7 %collective-permute-start.104 = (f32[4,48,128]{1,2,0:T(8,128)S(1)}, f32[4,48,128]{1,2,0:T(8,128)S(1)}, u32[]{:S(2)}, u32[]{:S(2)}) collective-permute-start(f32[4,48,128]{1,2,0:T(8,128)S(1)} %get-tuple-element.643), channel_id=1, source_target_pairs={{0,4},{4,0},{8,12},{12,8},{16,20},{20,16},{24,28},{28,24},{1,5},{5... | collective-permute-start | bytes 294920 | tf_op jit(solution)/shard_map/ppermute | solution.py:1305
  495.4 35.9 %collective-permute-start.105 = (f32[4,48,128]{1,2,0:T(8,128)S(1)}, f32[4,48,128]{1,2,0:T(8,128)S(1)}, u32[]{:S(2)}, u32[]{:S(2)}) collective-permute-start(f32[4,48,128]{1,2,0:T(8,128)S(1)} %get-tuple-element.643), channel_id=1, source_target_pairs={{0,5},{1,4},{4,1},{5,0},{8,13},{9,12},{12,9},{13,8},{16,21},{17,20... | collective-permute-start | bytes 294920 | tf_op jit(solution)/shard_map/ppermute | solution.py:1321
  504.1 29.0 %collective-permute-start.100 = (bf16[4,1,48,768]{3,2,1,0:T(8,128)(2,1)}, bf16[4,1,48,768]{3,2,1,0:T(8,128)(2,1)}, u32[]{:S(2)}, u32[]{:S(2)}) collective-permute-start(bf16[4,1,48,768]{3,2,1,0:T(8,128)(2,1)} %get-tuple-element.520), channel_id=1, source_target_pairs={{0,1},{1,0},{2,3},{3,2},{4,5},{5,4},{6,7},{7,6},{8,9},{9,8},{10,11... | collective-permute-start | bytes 884744 | tf_op jit(solution)/shard_map/ppermute | solution.py:1309
  505.5 27.7 %collective-permute-start.101 = (bf16[4,1,48,768]{3,2,1,0:T(8,128)(2,1)}, bf16[4,1,48,768]{3,2,1,0:T(8,128)(2,1)}, u32[]{:S(2)}, u32[]{:S(2)}) collective-permute-start(bf16[4,1,48,768]{3,2,1,0:T(8,128)(2,1)} %get-tuple-element.521), channel_id=1, source_target_pairs={{0,4},{4,0},{8,12},{12,8},{16,20},{20,16},{24,28},{28,24},{1,5},{5... | collective-permute-start | bytes 884744 | tf_op jit(solution)/shard_map/ppermute | solution.py:1305
  511.3 17.5 %collective-permute-start.103 = (f32[4,48,128]{1,2,0:T(8,128)S(1)}, f32[4,48,128]{1,2,0:T(8,128)S(1)}, u32[]{:S(2)}, u32[]{:S(2)}) collective-permute-start(f32[4,48,128]{1,2,0:T(8,128)S(1)} %get-tuple-element.644), channel_id=1, source_target_pairs={{0,1},{1,0},{2,3},{3,2},{4,5},{5,4},{6,7},{7,6},{8,9},{9,8},{10,11... | collective-permute-start | bytes 294920 | tf_op jit(solution)/shard_map/ppermute | solution.py:1309
  529.7 26.4 %collective-permute-start.110 = (bf16[2,2,48,768]{3,2,1,0:T(8,128)(2,1)}, bf16[2,2,48,768]{3,2,1,0:T(8,128)(2,1)S(1)}, u32[]{:S(2)}, u32[]{:S(2)}) collective-permute-start(bf16[2,2,48,768]{3,2,1,0:T(8,128)(2,1)} %get-tuple-element.547), channel_id=1, source_target_pairs={{0,16},{4,20},{8,24},{12,28},{16,0},{20,4},{24,8},{28,12},{1,17},{... | collective-permute-start | bytes 884744 | tf_op jit(solution)/shard_map/ppermute | solution.py:1305
  531.3 24.9 %collective-permute-start.111 = (bf16[2,2,48,768]{3,2,1,0:T(8,128)(2,1)}, bf16[2,2,48,768]{3,2,1,0:T(8,128)(2,1)S(1)}, u32[]{:S(2)}, u32[]{:S(2)}) collective-permute-start(bf16[2,2,48,768]{3,2,1,0:T(8,128)(2,1)} %get-tuple-element.548), channel_id=1, source_target_pairs={{0,24},{4,28},{8,16},{12,20},{16,8},{20,12},{24,0},{28,4},{1,25},{... | collective-permute-start | bytes 884744 | tf_op jit(solution)/shard_map/ppermute | solution.py:1305
  533.2 30.2 %collective-permute-start.112 = (f32[48,128]{0,1:T(8,128)S(1)}, f32[48,128]{0,1:T(8,128)S(1)}, u32[]{:S(2)}, u32[]{:S(2)}) collective-permute-start(f32[48,128]{0,1:T(8,128)S(1)} %get-tuple-element.620), channel_id=1, source_target_pairs={{0,8},{4,12},{8,0},{12,4},{16,24},{20,28},{24,16},{28,20},{1,9},{5... | collective-permute-start | bytes 73736 | tf_op jit(solution)/shard_map/ppermute | solution.py:1305
  533.3 33.7 %collective-permute-start.113 = (f32[48,128]{0,1:T(8,128)S(1)}, f32[48,128]{0,1:T(8,128)S(1)}, u32[]{:S(2)}, u32[]{:S(2)}) collective-permute-start(f32[48,128]{0,1:T(8,128)S(1)} %get-tuple-element.619), channel_id=1, source_target_pairs={{0,16},{4,20},{8,24},{12,28},{16,0},{20,4},{24,8},{28,12},{1,17},{... | collective-permute-start | bytes 73736 | tf_op jit(solution)/shard_map/ppermute | solution.py:1305
  542.8 24.3 %collective-permute-start.114 = (f32[48,128]{0,1:T(8,128)S(1)}, f32[48,128]{0,1:T(8,128)S(1)}, u32[]{:S(2)}, u32[]{:S(2)}) collective-permute-start(f32[48,128]{0,1:T(8,128)S(1)} %get-tuple-element.618), channel_id=1, source_target_pairs={{0,24},{4,28},{8,16},{12,20},{16,8},{20,12},{24,0},{28,4},{1,25},{... | collective-permute-start | bytes 73736 | tf_op jit(solution)/shard_map/ppermute | solution.py:1305
  556.1 18.4 %collective-permute-start.107 = (bf16[2,1,48,768]{3,2,1,0:T(8,128)(2,1)}, bf16[2,1,48,768]{3,2,1,0:T(8,128)(2,1)S(1)}, u32[]{:S(2)}, u32[]{:S(2)}) collective-permute-start(bf16[2,1,48,768]{3,2,1,0:T(8,128)(2,1)} %get-tuple-element.532), channel_id=1, source_target_pairs={{0,16},{4,20},{8,24},{12,28},{16,0},{20,4},{24,8},{28,12},{1,17},{... | collective-permute-start | bytes 442376 | tf_op jit(solution)/shard_map/ppermute | solution.py:1305
  (136 other events, 1372.5 us)
Sparse Core Ops, SparseCore 0:
  17.3 102.9 all-gather.2
  363.4 152.2 reduce-scatter.1

commit v3 on v2

--- a/solution.py
+++ b/solution.py
@@ -391,12 +391,12 @@
     return jax.ShapeDtypeStruct(shape, dtype)
 
 
-COST = dict(qkv=7, attend=12, ffn=20, down_back=6, up_back=10, ffn_grad=11)
+COST = dict(layer_grad=20, qkv=7, attend=12, ffn=20, down_back=6, up_back=10, ffn_grad=11)
 COST |= dict(attend_back=16, qkv_grad=8, qkv_back=9, cross=4, own=4)
 
 
 def duration(us):
-    flops = int(us * 1.15e9)
+    flops = int(us * 0.4e9)
     return pl.CostEstimate(flops=flops, bytes_accessed=1 << 20, transcendentals=0)
 
 
@@ -1130,16 +1130,16 @@
                 (sb if pyy else kb)[pxx, pz, n, :, cols] = value
 
 
-def up_grads_into(f, y, xk, xr, gk, gr, outs, tmp):
+def up_grads_into(f, y, xk, xr, gk, gr, outs, tmp, n):
     for portion in range(2):
         for pyy in range(2):
             cols = pl.ds(aligned((y ^ pyy) * 1536 + portion * D, 128), D)
             slot = portion * 2 + pyy
             tmp[slot] = (nn(xk[...], gk[:, cols]) + nn(xr[...], gr[:, cols])).astype(BF16)
-            scatter_rows(tmp.at[slot], f, ROWS, 0, pyy, portion, outs, 0, pl.ds(0, D))
-
-
-def down_grads_into(f, y, ak, ar, dk, dr, outs, tmp):
+            scatter_rows(tmp.at[slot], f, ROWS, 0, pyy, portion, outs, n, pl.ds(0, D))
+
+
+def down_grads_into(f, y, ak, ar, dk, dr, outs, tmp, n):
     for pyy in range(2):
         cols = pl.ds(aligned((y ^ pyy) * HALF, 128), HALF)
 
@@ -1153,74 +1153,27 @@
         for portion in range(2):
             for k in range(2):
                 offset, half = (portion * 2 + k) * ROWS, pl.ds(k * HALF, HALF)
-                scatter_rows(tmp.at[pyy], f, DROWS, offset, pyy, portion, outs, 1, half)
-
-
-def ffn_grad_kernel(count, idx, xk, xr, gk, gr, ak, ar, dk, dr, *refs):
-    outs, tmp, tmp2 = refs[:count], refs[count], refs[count + 1]
-    f, y = (idx[0], idx[1]) if count == 4 else (0, 0)
-    up_grads_into(f, y, xk, xr, gk, gr, outs, tmp)
-    down_grads_into(f, y, ak, ar, dk, dr, outs, tmp2)
-
-
-def ffn_grad_call(idx, xk, xr, gk, gr, ak, ar, dk, dr, by_position):
-    ins = [idx] + [v.reshape(HALF, TOK) for v in (xk, xr)] + [gk, gr]
-    ins += [v.reshape(4 * HALF, TOK) for v in (ak, ar)] + [dk, dr]
-    outs = [sds((16, 2, 2, ROWS, D), BF16)]
-    if by_position:
-        outs = [sds((2, 4, 2, ROWS, D), BF16)] * 4
-    return kernel_call(
-        partial(ffn_grad_kernel, len(outs)),
-        ins,
-        [SM] + [VM] * 8,
-        outs,
-        [VM] * len(outs),
-        [pltpu.VMEM((4, HALF, D), BF16), pltpu.VMEM((2, 4 * HALF, HALF), BF16)],
-        "ffn_grad",
-    )
-
-
-def qkv_grad_kernel(
-    idx, xk, xr, mk, mr, d00, d01, d10, d11, gk, gr, ka, sa, kb, sb, sc, dy, tmp, tsc, sem
-):
-    outs = (ka, sa, kb, sb)
-    f, y, c = idx[0], idx[1], idx[2]
-    copies = []
-    for tok, pair in enumerate(((d00, d01), (d10, d11))):
-        for k, src in enumerate(pair):
-            for j in range(3):
-                copy = pltpu.make_async_copy(
-                    src.at[:, pl.ds(j * HALF, HALF)],
-                    dy.at[tok, 2 * j + (c ^ k)],
-                    sem.at[tok * 6 + k * 3 + j],
-                )
-                copy.start()
-                copies.append(copy)
-    for tok, pair in enumerate(((d00, d01), (d10, d11))):
-        for k, src in enumerate(pair):
-            copy = pltpu.make_async_copy(
-                src.at[:, pl.ds(1152, 128)], tsc.at[tok * 2 + k], sem.at[12 + tok * 2 + k]
-            )
-            copy.start()
-            copies.append(copy)
-    for copy in copies:
-        copy.wait()
+                scatter_rows(tmp.at[pyy], f, DROWS, offset, pyy, portion, outs, n, half)
+
+
+def qkv_grads_into(y, xk, xr, mk, mr, dy, gk, gr, outs, tmp, f):
     for pyy in range(2):
         y2 = y ^ pyy
         for part in range(4):
             portion, side = part // 2, part % 2
-            cols = pl.ds(side * HALF, HALF)
             if part < 3:
                 g = y2 * 3 + part
                 value = nn(xk[...], dy[0, g]) + nn(xr[...], dy[1, g])
             else:
                 oc = pl.ds(aligned(y2 * HALF, 128), HALF)
                 value = nn(mk[...], gk[:, oc]) + nn(mr[...], gr[:, oc])
-            tmp[portion * 2 + pyy, :, cols] = value.astype(BF16)
+            tmp[portion * 2 + pyy, :, pl.ds(side * HALF, HALF)] = value.astype(BF16)
         for portion in range(2):
-            scatter_rows(
-                tmp.at[portion * 2 + pyy], f, ROWS, 0, pyy, portion, outs, 0, pl.ds(0, D)
-            )
+            slot = portion * 2 + pyy
+            scatter_rows(tmp.at[slot], f, ROWS, 0, pyy, portion, outs, 0, pl.ds(0, D))
+
+
+def score_grads_into(f, c, xk, xr, tsc, sc):
     own = nn(xk[...], tsc[0]) + nn(xr[...], tsc[2])
     theirs = nn(xk[...], tsc[1]) + nn(xr[...], tsc[3])
     first = jnp.where(c == 0, own, theirs)
@@ -1236,21 +1189,121 @@
                     sc[pxx, pz] = both[b * ROWS : (b + 1) * ROWS, :]
 
 
+def start_outputs_grads(c, grads, dy, tsc, sem):
+    copies = []
+    for tok in range(2):
+        for k in range(2):
+            src = grads[tok * 2 + k]
+            for j in range(3):
+                part = src.at[:, pl.ds(j * HALF, HALF)]
+                at = sem.at[tok * 8 + k * 4 + j]
+                copies.append(pltpu.make_async_copy(part, dy.at[tok, 2 * j + (c ^ k)], at))
+            part = src.at[:, pl.ds(1152, 128)]
+            at = sem.at[tok * 8 + k * 4 + 3]
+            copies.append(pltpu.make_async_copy(part, tsc.at[tok * 2 + k], at))
+    for copy in copies:
+        copy.start()
+    return copies
+
+
+def wait_all(copies):
+    for copy in copies:
+        copy.wait()
+
+
+FFN_SHAPES = [(4 * HALF, TOK)] * 2 + [(TOK, D)] * 2 + [(HALF, TOK)] * 2 + [(TOK, FF)] * 2
+QKV_SHAPES = [(HALF, TOK)] * 4 + [(TOK, D)] * 2
+DY_SCRATCH = [pltpu.VMEM((2, 6, TOK, HALF), BF16), pltpu.VMEM((4, TOK, 128), BF16)]
+
+
+def ffn_grad_kernel(idx, *refs):
+    ins, outs, refs = refs[:8], refs[8:12], refs[12:]
+    held, (tmp, tmp2, sem) = refs[:8], refs[8:]
+    copies = load(list(zip(ins, held)), sem)
+    ak, ar, dk, dr, xk, xr, gk, gr = held
+    wait_all(copies[:4])
+    down_grads_into(idx[0], idx[1], ak, ar, dk, dr, outs, tmp2, 1)
+    wait_all(copies[4:])
+    up_grads_into(idx[0], idx[1], xk, xr, gk, gr, outs, tmp, 0)
+
+
+def ffn_grad_call(idx, xk, xr, gk, gr, ak, ar, dk, dr):
+    ins = [v.reshape(4 * HALF, TOK) for v in (ak, ar)] + [dk, dr]
+    ins += [v.reshape(HALF, TOK) for v in (xk, xr)] + [gk, gr]
+    return kernel_call(
+        ffn_grad_kernel,
+        [idx, *ins],
+        [SM] + [HB] * 8,
+        [sds((2, 4, 2, ROWS, D), BF16)] * 4,
+        [VM] * 4,
+        [pltpu.VMEM(shape, BF16) for shape in FFN_SHAPES]
+        + [pltpu.VMEM((4, HALF, D), BF16), pltpu.VMEM((2, 4 * HALF, HALF), BF16)]
+        + [pltpu.SemaphoreType.DMA((8,))],
+        "ffn_grad",
+    )
+
+
+def qkv_grad_kernel(idx, *refs):
+    ins, grads, outs, sc, refs = refs[:6], refs[6:10], refs[10:14], refs[14], refs[15:]
+    held, (dy, tsc, tmp, sem, isem) = refs[:6], refs[6:]
+    f, y, c = idx[0], idx[1], idx[2]
+    copies = start_outputs_grads(c, grads, dy, tsc, sem) + load(list(zip(ins, held)), isem)
+    xk, xr, mk, mr, gk, gr = held
+    wait_all(copies)
+    qkv_grads_into(y, xk, xr, mk, mr, dy, gk, gr, outs, tmp, f)
+    score_grads_into(f, c, xk, xr, tsc, sc)
+
+
 def qkv_grad_call(idx, xk, xr, mk, mr, d00, d01, d10, d11, gk, gr):
-    flat = [v.reshape(HALF, TOK) for v in (xk, xr, mk, mr)]
+    ins = [v.reshape(HALF, TOK) for v in (xk, xr, mk, mr)] + [gk, gr, d00, d01, d10, d11]
     return kernel_call(
         qkv_grad_kernel,
-        [idx, *flat, d00, d01, d10, d11, gk, gr],
-        [SM, VM, VM, VM, VM, HB, HB, HB, HB, VM, VM],
+        [idx, *ins],
+        [SM] + [HB] * 10,
         [sds((2, 4, 1, ROWS, D), BF16)] * 4 + [sds((2, 4, ROWS, 128), F32)],
         [VM] * 5,
-        [
-            pltpu.VMEM((2, 6, TOK, HALF), BF16),
-            pltpu.VMEM((4, HALF, D), BF16),
-            pltpu.VMEM((4, TOK, 128), BF16),
-            pltpu.SemaphoreType.DMA((16,)),
-        ],
+        [pltpu.VMEM(shape, BF16) for shape in QKV_SHAPES]
+        + DY_SCRATCH
+        + [pltpu.VMEM((4, HALF, D), BF16)]
+        + [pltpu.SemaphoreType.DMA((16,)), pltpu.SemaphoreType.DMA((6,))],
         "qkv_grad",
+    )
+
+
+def layer_grad_kernel(idx, *refs):
+    ins, grads, out, sc, refs = refs[:14], refs[14:18], refs[18], refs[19], refs[20:]
+    held, (dy, tsc, tmp, tmp2, sem, isem) = refs[:14], refs[14:]
+    f, c = idx[0], idx[2]
+    copies = load(list(zip(ins, held)), isem)
+    more = start_outputs_grads(c, grads, dy, tsc, sem)
+    ak, ar, dk, dr, xk, xr, gk, gr = held[:8]
+    wait_all(copies[:4])
+    down_grads_into(0, 0, ak, ar, dk, dr, [out], tmp2, 2)
+    wait_all(copies[4:8])
+    up_grads_into(0, 0, xk, xr, gk, gr, [out], tmp, 1)
+    wait_all(copies[8:] + more)
+    xk, xr, mk, mr, gk, gr = held[8:]
+    qkv_grads_into(0, xk, xr, mk, mr, dy, gk, gr, [out], tmp, 0)
+    score_grads_into(f, c, xk, xr, tsc, sc)
+
+
+def layer_grad_call(idx, ffn, qkv):
+    xk, xr, gk, gr, ak, ar, dk, dr = ffn
+    ins = [v.reshape(4 * HALF, TOK) for v in (ak, ar)] + [dk, dr]
+    ins += [v.reshape(HALF, TOK) for v in (xk, xr)] + [gk, gr]
+    xk, xr, mk, mr, d00, d01, d10, d11, gk, gr = qkv
+    ins += [v.reshape(HALF, TOK) for v in (xk, xr, mk, mr)] + [gk, gr, d00, d01, d10, d11]
+    return kernel_call(
+        layer_grad_kernel,
+        [idx, *ins],
+        [SM] + [HB] * 18,
+        [sds((16, 2, 3, ROWS, D), BF16), sds((2, 4, ROWS, 128), F32)],
+        [VM] * 2,
+        [pltpu.VMEM(shape, BF16) for shape in FFN_SHAPES + QKV_SHAPES]
+        + DY_SCRATCH
+        + [pltpu.VMEM((4, HALF, D), BF16), pltpu.VMEM((2, 4 * HALF, HALF), BF16)]
+        + [pltpu.SemaphoreType.DMA((16,)), pltpu.SemaphoreType.DMA((14,))],
+        "layer_grad",
     )
 
 
@@ -1511,23 +1564,21 @@
     low, low_r = cot, over_core(cot)
     gu, gu_r = down_back(1, low, out1)
     ga, nrm2, gm, gat = up_back(1, cot.astype(F32), gu, out1)
-    grads = ffn_grad_call(order.gate, *out1[2], gu, gu_r, *out1[3], low, low_r, False)
-    ffn1 = order.passed(grads[0])
-    ffn1 = lax.psum_scatter(ffn1, ("zx", "ctx"), scatter_dimension=0, tiled=False)
     d = attend_back(head1, lse1, gm)
-    grad, low, nrm1 = qkv_back(1, ga, d, res1, head1)
-    low_r = over_core(low)
-    *g, scores[1] = qkv_grads(head1, out1, d, gat)
+    grad, new_low, nrm1 = qkv_back(1, ga, d, res1, head1)
+    ffn = (*out1[2], gu, gu_r, *out1[3], low, low_r)
+    qkv_parts = (head1[2], head1[3], *out1[4], *d, *gat)
+    grads1, scores[1] = order.passed(layer_grad_call(order.gate, ffn, qkv_parts))
+    grads1 = lax.psum_scatter(grads1, ("zx", "ctx"), scatter_dimension=0, tiled=False)
+    low, low_r = new_low, over_core(new_low)
     norms[1] = jnp.concatenate([nrm1[0:1], nrm2[0:1], nrm1[1:2], nrm2[1:2]])
-    qo1 = Chain(reduce_stages(*g))
     gu, gu_r = down_back(0, low, out0)
+    gu_r = order.passed(gu_r)
+    grads = ffn_grad_call(order.gate, *out0[2], gu, gu_r, *out0[3], low, low_r)
+    ffn0 = Chain(reduce_stages(*order.passed(grads)))
     ga, nrm2, gm, gat = up_back(0, grad, gu, out0)
-    order.meet(qo1)
-    grads = ffn_grad_call(order.gate, *out0[2], gu, gu_r, *out0[3], low, low_r, True)
-    ffn0 = Chain(reduce_stages(*order.passed(grads)))
-    order.meet(qo1)
     d = attend_back(head0, lse0, gm)
-    order.meet(ffn0, qo1)
+    order.meet(ffn0)
     *g, scores[0] = qkv_grads(head0, out0, d, gat)
     qo0 = Chain(reduce_stages(*g))
     grad, low, nrm1 = qkv_back(0, ga, d, residual, head0)
@@ -1541,18 +1592,18 @@
     lanes = jnp.pad(jnp.concatenate(lanes, -1), ((0, 0), (0, 0), (0, 0), (0, 96)))
     lanes = Chain(small_stages(lanes))
     token_grad = turn(low)
-    order.meet(ffn0, qo0)
-    order.meet(qo0, lanes)
-    order.meet(ffn0, lanes)
+    order.meet(ffn0, qo0, lanes)
+    order.meet(ffn0, qo0, lanes)
     order.meet(qo0)
     token_grad = order.passed(token_grad).astype(F32)
     lanes = order.after(lanes.result)
     score_grad = jnp.stack([lanes[:, 0:12], lanes[:, 12:24]])
     nrm = lanes[:, 24:32].T.reshape(LAYERS, 2, 2, ROWS)
-    qo = [qo0.result[:, 0], qo1.result[:, 0]]
+    grads1 = grads1.astype(F32)
+    qo = [qo0.result[:, 0], grads1[:, 0]]
     qkv_grad = jnp.stack([jnp.concatenate([v[0], v[1, :, :HALF]], 1) for v in qo])
     out_grad = jnp.stack([v[1, :, HALF:] for v in qo])
-    ffn = [ffn0.result, ffn1.astype(F32)]
+    ffn = [ffn0.result, grads1[:, 1:]]
     up_grad = jnp.stack([jnp.concatenate([v[0, 0], v[1, 0]], 1) for v in ffn])
     down_grad = jnp.stack(
         [v[:, 1].reshape(2, ROWS, 2, HALF).swapaxes(1, 2).reshape(DROWS, HALF) for v in ffn]

time: 593 us -> 587 us (0.990)
  starting transfers between devices: 119 us -> 98.6 us
  waiting for transfers between devices: 160 us -> 179 us
  Pallas kernels: 244 us -> 230 us
  local copies, waits for them, and re-layouts: 30.8 us -> 41.1 us
    ppermute x16 -> x14, waiting for transfers between devices: 43.9 us -> 62.2 us  [over_ctx(): return lax.ppermute(v, 'ctx', [(0, 1), (1, 0)])]
    ppermute x41 -> x36, starting transfers between devices: 76.7 us -> 63.4 us  [pairwise(): return lax.ppermute(v, 'zx', [(i, i ^ bits) for i in range(8)])]
    ppermute x41 -> x36, waiting for transfers between devices: 104 us -> 92.2 us  [pairwise(): return lax.ppermute(v, 'zx', [(i, i ^ bits) for i in range(8)])]
    ppermute x53, waiting for transfers between devices: 12.1 us -> 24.3 us  [over_core(): return lax.ppermute(v, 'core', [(0, 1), (1, 0)])]
    pallas_call x18 -> x17, Pallas kernels: 222 us -> 215 us  [kernel_call(): pl.pallas_call(body, out_shape=tuple(outs), in_specs=in_specs, out_specs=...]
    optimization_barrier x0 -> x1, local copies, waits for them, and re-layouts: none -> 6.74 us  [passed(): self.gate, value = lax.optimization_barrier((self.gate, value))]
    ppermute x16 -> x14, starting transfers between devices: 21.6 us -> 16.7 us  [over_ctx(): return lax.ppermute(v, 'ctx', [(0, 1), (1, 0)])]
    unnamed x173 -> x189, local copies, waits for them, and re-layouts: 16.6 us -> 18.1 us
  transfers between devices with their start and end apart: 117 -> 110, of which waited for: 36 -> 35; matrix products, arithmetic and copies ran while one was open for 5% -> 5% of each run, Pallas kernels for 35% -> 33%
where the time goes in v3:
time: 587 us; the launch traced here: 581 us
  Pallas kernels  230 us (39%)
  waiting for transfers between devices  179 us (30%)
  starting transfers between devices  98.6 us (17%)
  local copies, waits for them, and re-layouts  41.1 us (7%)
  between operations  16.3 us (3%)
  other arithmetic  16.2 us (3%)
    pallas_call x17, Pallas kernels, kernel_call(): pl.pallas_call(body, out_shape=tuple(outs), in_specs=in_specs, out_specs=...  215 us
    ppermute x36, waiting for transfers between devices, pairwise(): return lax.ppermute(v, 'zx', [(i, i ^ bits) for i in range(8)])  92.2 us
    ppermute x36, starting transfers between devices, pairwise(): return lax.ppermute(v, 'zx', [(i, i ^ bits) for i in range(8)])  63.4 us
    ppermute x14, waiting for transfers between devices, over_ctx(): return lax.ppermute(v, 'ctx', [(0, 1), (1, 0)])  62.2 us
    ppermute x53, waiting for transfers between devices, over_core(): return lax.ppermute(v, 'core', [(0, 1), (1, 0)])  24.3 us
    unnamed x189, local copies, waits for them, and re-layouts  18.1 us
    ppermute x14, starting transfers between devices, over_ctx(): return lax.ppermute(v, 'ctx', [(0, 1), (1, 0)])  16.7 us
    ppermute x53, starting transfers between devices, over_core(): return lax.ppermute(v, 'core', [(0, 1), (1, 0)])  12 us
  transfers between devices with their start and end apart: 110, of which 35 were waited for; matrix products, arithmetic and copies ran while one was open for 5% of the time, Pallas kernels for 33%

profile of v3, /device:TPU:0, one launch (start us, length us, event | category | flops | bytes accessed | tf_op | source)
XLA Modules:
  0.0 580.7 jit_solution(69023897675065069)
XLA Ops:
  11.1 3.1 collective-permute-start.3
  15.7 3.0 collective-permute-start.1
  22.3 14.1 %collective-permute-done.4 = bf16[32,128]{1,0:T(8,128)(2,1)S(1)} collective-permute-done((bf16[32,128]{1,0:T(8,128)(2,1)S(1)}, bf16[32,128]{1,0:T(8,128)(2,1)S(1)}, u32[]{:S(2)}, u32[]{:S(2)}) %collective-permute-start.4) | collective-permute-done | bytes 8224 | tf_op jit(solution)/shard_map/ppermute | solution.py:1358
  36.5 5.2 collective-permute-start.5
  43.5 1.8 collective-permute-start.10
  45.3 2.5 collective-permute-start.8
  51.9 16.8 %collective-permute-done.11 = bf16[4,32,128]{2,1,0:T(8,128)(2,1)S(1)} collective-permute-done((bf16[4,32,128]{2,1,0:T(8,128)(2,1)S(1)}, bf16[4,32,128]{2,1,0:T(8,128)(2,1)S(1)}, u32[]{:S(2)}, u32[]{:S(2)}) %collective-permute-start.11) | collective-permute-done | bytes 32800 | tf_op jit(solution)/shard_map/ppermute | solution.py:1358
  73.3 6.1 %collective-permute-done.12.refs_3_ = bf16[4,1,48,768]{3,2,1,0:T(8,128)(2,1)S(1)} collective-permute-done((bf16[4,1,48,768]{3,2,1,0:T(8,128)(2,1)S(1)}, bf16[4,1,48,768]{3,2,1,0:T(8,128)(2,1)S(1)}, u32[]{:S(2)}, u32[]{:S(2)}) %collective-permute-start.12) | collective-permute-done | bytes 294944 | tf_op jit(solution)/shard_map/ppermute | solution.py:1362
  81.4 2.1 collective-permute-done.13.refs_11_
  91.8 4.9 collective-permute-start.24
  96.7 8.7 %qkv.2 = (bf16[512,1280]{1,0:T(8,128)(2,1)}, bf16[512,1280]{1,0:T(8,128)(2,1)}, bf16[8,48,512]{2,1,0:T(8,128)(2,1)}, bf16[8,48,512]{2,1,0:T(8,128)(2,1)}) custom-call(s32[3]{0:T(128)} %pad_add_fusion.idx, f32[512,768]{1,0:T(8,128)} %convert_element_type.52.res.res_in, f32[8,768]{1,0:T(8,128)} %pad_convert_fusion.1.gb, bf16[128,768]{1,0:T(8,128)(2,1)} %pad.35.sw0, ...), custom_call_target="tpu_custom_call" | custom-call | flops 2800000000 | bytes 1048576 | tf_op jit(solution)/shard_map/qkv/pallas_call | solution.py:407
  105.4 9.0 %collective-permute-done.24 = bf16[2,1,48,768]{3,2,1,0:T(8,128)(2,1)S(1)} collective-permute-done((bf16[2,1,48,768]{3,2,1,0:T(8,128)(2,1)S(1)}, bf16[2,1,48,768]{3,2,1,0:T(8,128)(2,1)S(1)}, u32[]{:S(2)}, u32[]{:S(2)}) %collective-permute-start.24) | collective-permute-done | bytes 147488 | tf_op jit(solution)/shard_map/ppermute | solution.py:1358
  115.3 2.7 collective-permute-start.30
  118.0 1.8 collective-permute-start.32
  122.0 3.5 collective-permute-done.30.refs_10_
  125.4 4.9 collective-permute-start.33
  130.4 1.9 collective-permute-start.34
  132.3 2.5 collective-permute-start.35
  134.8 11.8 %attend.2 = (bf16[512,384]{1,0:T(8,128)(2,1)}, bf16[512,384]{1,0:T(8,128)(2,1)}, f32[8,1024]{1,0:T(8,128)}) custom-call(s32[3]{0:T(128)} %pad_add_fusion.idx, s32[6,8]{1,0:T(8,128)} %dynamic-slice_select_fusion.kept, s32[2]{0:T(128)} %broadcast_select_fusion.1.pics, bf16[512,1280]{1,0:T(8,128)(2,1)} %get-tuple-element.297.own, bf16[512,1280]{1,0:T(8,128)(2,1)} %copy-done.73), custom_call_target="tpu_custom_call" | custom-call | flops 4800000000 | bytes 1048576 | tf_op jit(solution)/shard_map/attend/pallas_call | solution.py:407
  147.3 6.1 %collective-permute-done.34 = bf16[2,2,48,768]{3,2,1,0:T(8,128)(2,1)S(1)} collective-permute-done((bf16[2,2,48,768]{3,2,1,0:T(8,128)(2,1)S(1)}, bf16[2,2,48,768]{3,2,1,0:T(8,128)(2,1)S(1)}, u32[]{:S(2)}, u32[]{:S(2)}) %collective-permute-start.34) | collective-permute-done | bytes 294944 | tf_op jit(solution)/shard_map/ppermute | solution.py:1358
  156.7 3.4 collective-permute-done.36.refs_3_
  160.2 4.1 collective-permute-done.37.refs_11_
  171.6 2.5 collective-permute-done.44
  174.9 7.7 %collective-permute-done.49.refs_26_.refs_10_ = bf16[4,2,48,768]{3,2,1,0:T(8,128)(2,1)S(1)} collective-permute-done((bf16[4,2,48,768]{3,2,1,0:T(8,128)(2,1)S(1)}, bf16[4,2,48,768]{3,2,1,0:T(8,128)(2,1)S(1)}, u32[]{:S(2)}, u32[]{:S(2)}) %collective-permute-start.49) | collective-permute-done | bytes 589856 | tf_op jit(solution)/shard_map/ppermute | solution.py:1362
  182.6 17.4 %ffn.2 = (f32[512,768]{1,0:T(8,128)}, f32[512,768]{1,0:T(8,128)}, bf16[512,768]{1,0:T(8,128)(2,1)}, bf16[8,48,512]{2,1,0:T(8,128)(2,1)}, bf16[8,48,512]{2,1,0:T(...) custom-call(s32[3]{0:T(128)} %pad_add_fusion.idx, ...), custom_call_target="tpu_custom_call" | custom-call | flops 8000000000 | bytes 1048576 | tf_op jit(solution)/shard_map/ffn/pallas_call | solution.py:407
  201.9 8.4 %qkv.3 = (bf16[512,1280]{1,0:T(8,128)(2,1)}, bf16[512,1280]{1,0:T(8,128)(2,1)}, bf16[8,48,512]{2,1,0:T(8,128)(2,1)}, bf16[8,48,512]{2,1,0:T(8,128)(2,1)}) custom-call(s32[3]{0:T(128)} %pad_add_fusion.idx, f32[512,768]{1,0:T(8,128)} %get-tuple-element.336.res.res_in, f32[8,768]{1,0:T(8,128)} %pad_convert_fusion.gb, bf16[128,768]{1,0:T(8,128)(2,1)} %pad.39.sw0, ...), custom_call_target="tpu_custom_call" | custom-call | flops 2800000000 | bytes 1048576 | tf_op jit(solution)/shard_map/qkv/pallas_call | solution.py:407
  215.4 11.2 %collective-permute-done.52.refs_19_.refs_3_ = bf16[4,2,48,768]{3,2,1,0:T(8,128)(2,1)S(1)} collective-permute-done((bf16[4,2,48,768]{3,2,1,0:T(8,128)(2,1)S(1)}, bf16[4,2,48,768]{3,2,1,0:T(8,128)(2,1)S(1)}, u32[]{:S(2)}, u32[]{:S(2)}) %collective-permute-start.52) | collective-permute-done | bytes 589856 | tf_op jit(solution)/shard_map/ppermute | solution.py:1362
  230.3 11.9 %attend.3 = (bf16[512,384]{1,0:T(8,128)(2,1)}, bf16[512,384]{1,0:T(8,128)(2,1)}, f32[8,1024]{1,0:T(8,128)}) custom-call(s32[3]{0:T(128)} %pad_add_fusion.idx, s32[6,8]{1,0:T(8,128)} %dynamic-slice_select_fusion.kept, s32[2]{0:T(128)} %broadcast_select_fusion.1.pics, bf16[512,1280]{1,0:T(8,128)(2,1)} %get-tuple-element.355.own, ...), custom_call_target="tpu_custom_call" | custom-call | flops 4800000000 | bytes 1048576 | tf_op jit(solution)/shard_map/attend/pallas_call | solution.py:407
  242.5 1.8 collective-permute-start.65
  245.0 17.3 %ffn.3 = (f32[512,768]{1,0:T(8,128)}, f32[512,768]{1,0:T(8,128)}, bf16[512,768]{1,0:T(8,128)(2,1)}, bf16[8,48,512]{2,1,0:T(8,128)(2,1)}, bf16[8,48,512]{2,1,0:T(...) custom-call(s32[3]{0:T(128)} %pad_add_fusion.idx, ...), custom_call_target="tpu_custom_call" | custom-call | flops 8000000000 | bytes 1048576 | tf_op jit(solution)/shard_map/ffn/pallas_call | solution.py:407
  263.2 11.2 %down_back.2.gu.refs_6_ = bf16[512,3072]{1,0:T(8,128)(2,1)} custom-call(s32[3]{0:T(128)} %pad_add_fusion.idx, bf16[512,768]{1,0:T(8,128)(2,1)} %copy-done.2, bf16[512,3072]{1,0:T(8,128)(2,1)} %get-tuple-element.386.slope_in, bf16[4,2,48,768]{3,2,1,0:T(8,128)(2,1)} %copy-done.1, bf16[4,2,48,768]{3,2,1,0:T(8,128)(2,1)} %copy-done.6, ...), custom_call_target="tpu_custom_call" | custom-call | flops 2400000000 | bytes 1048576 | tf_op jit(solution)/shard_map/down_back/pallas_call | solution.py:407
  275.7 2.4 convert_element_type.55.grad_in
  278.1 10.8 %up_back.2 = (f32[512,768]{1,0:T(8,128)}, bf16[512,768]{1,0:T(8,128)(2,1)}, bf16[512,384]{1,0:T(8,128)(2,1)}, bf16[512,384]{1,0:T(8,128)(2,1)}, f32[8,768]{1,0:T(8,128)}) custom-call(s32[3]{0:T(128)} %pad_add_fusion.idx, f32[512,768]{1,0:T(8,128)} %convert_element_type.55.grad_in, bf16[512,3072]{1,0:T(8,128)(2,1)} %down_back.2.gu.refs_6_, ...), custom_call_target="tpu_custom_call" | custom-call | flops 4000000000 | bytes 1048576 | tf_op jit(solution)/shard_map/up_back/pallas_call | solution.py:407
  289.0 2.1 collective-permute-done.66.gother
  291.1 17.3 %attend_back.2 = (bf16[512,1280]{1,0:T(8,128)(2,1)}, bf16[512,1280]{1,0:T(8,128)(2,1)}) custom-call(s32[3]{0:T(128)} %pad_add_fusion.idx, s32[6,8]{1,0:T(8,128)} %dynamic-slice_select_fusion.kept, s32[2]{0:T(128)} %broadcast_select_fusion.1.pics, f32[8,1024]{1,0:T(8,128)} %get-tuple-element.396.lse, bf16[512,1280]{1,0:T(8,128)(2,1)} %get-tuple-element.355.own, ...), custom_call_target="tpu_custom_call" | custom-call | flops 6400000000 | bytes 1048576 | tf_op jit(solution)/shard_map/attend_back/pallas_call | solution.py:407
  309.5 3.5 collective-permute-done.72
  313.5 2.7 collective-permute-done.73
  316.8 10.0 %qkv_back.2 = (f32[512,768]{1,0:T(8,128)}, bf16[512,768]{1,0:T(8,128)(2,1)}, f32[8,768]{1,0:T(8,128)}) custom-call(s32[3]{0:T(128)} %pad_add_fusion.idx, f32[512,768]{1,0:T(8,128)} %get-tuple-element.402.ga_in, bf16[512,1280]{1,0:T(8,128)(2,1)} %get-tuple-element.403.down_.refs_14_, bf16[512,1280]{1,0:T(8,128)(2,1)} %collective-permute-done.67.dr.refs_15_, ...), custom_call_target="tpu_custom_call" | custom-call | flops 3600000000 | bytes 1048576 | tf_op jit(solution)/shard_map/qkv_back/pallas_call | solution.py:407
  326.9 1.7 copy-done.68
  328.6 18.4 %layer_grad.1 = (bf16[16,2,3,48,768]{4,3,2,1,0:T(8,128)(2,1)}, f32[2,4,48,128]{3,2,1,0:T(8,128)}) custom-call(s32[3]{0:T(128)} %pad_add_fusion.idx, bf16[1536,512]{1,0:T(8,128)(2,1)} %bitcast.206, bf16[1536,512]{1,0:T(8,128)(2,1)} %bitcast.40.refs_1_, bf16[512,768]{1,0:T(8,128)(2,1)} %copy-done.2, bf16[512,768]{1,0:T(8,128)(2,1)} %collective-permute-done.69.refs_3_, ...), custom_call_target="tpu_custom_call" | custom-call | flops 8000000000 | bytes 1048576 | tf_op jit(solution)/shard_map/layer_grad/pallas_call | solution.py:407
  347.0 6.7 %copy.98 = bf16[16,2,3,48,768]{4,3,1,2,0:T(8,128)(2,1)} copy(bf16[16,2,3,48,768]{4,3,2,1,0:T(8,128)(2,1)} %get-tuple-element.507) | data formatting | bytes 14155776 | tf_op jit(solution)/shard_map/optimization_barrier | solution.py:1401
  353.8 11.6 %down_back.3.refs_6_.gu = bf16[512,3072]{1,0:T(8,128)(2,1)} custom-call(s32[3]{0:T(128)} %pad_add_fusion.idx, bf16[512,768]{1,0:T(8,128)(2,1)} %get-tuple-element.421.grad.refs_2_, bf16[512,3072]{1,0:T(8,128)(2,1)} %get-tuple-element.422.slope_in, bf16[4,2,2,2,2,48,768]{6,5,4,3,2,1,0:T(8,128)(2,1)} %bitcast.175, ...), custom_call_target="tpu_custom_call" | custom-call | flops 2400000000 | bytes 1048576 | tf_op jit(solution)/shard_map/down_back/pallas_call | solution.py:407
  366.5 7.9 %collective-permute-done.76.refs_7_ = bf16[512,3072]{1,0:T(8,128)(2,1)S(1)} collective-permute-done((bf16[512,3072]{1,0:T(8,128)(2,1)}, bf16[512,3072]{1,0:T(8,128)(2,1)S(1)}, u32[]{:S(2)}, u32[]{:S(2)}) %collective-permute-start.76) | collective-permute-done | bytes 3145760 | tf_op jit(solution)/shard_map/ppermute | solution.py:1366
  377.5 11.8 %ffn_grad.1 = (bf16[2,4,2,48,768]{4,3,2,1,0:T(8,128)(2,1)}, bf16[2,4,2,48,768]{4,3,2,1,0:T(8,128)(2,1)}, bf16[2,4,2,48,768]{4,3,2,1,0:T(8,128)(2,1)}, bf16[2,4,2,48,768]{4,3,2,1,0:T(8,128)(2,1)}) custom-call(s32[3]{0:T(128)} %pad_add_fusion.idx, bf16[1536,512]{1,0:T(8,128)(2,1)} %bitcast.205, bf16[1536,512]{1,0:T(8,128)(2,1)} %bitcast.198, ...), custom_call_target="tpu_custom_call" | custom-call | flops 4400000000 | bytes 1048576 | tf_op jit(solution)/shard_map/ffn_grad/pallas_call | solution.py:407
  389.3 10.5 %up_back.3 = (f32[512,768]{1,0:T(8,128)}, bf16[512,768]{1,0:T(8,128)(2,1)}, bf16[512,384]{1,0:T(8,128)(2,1)}, bf16[512,384]{1,0:T(8,128)(2,1)}, f32[8,768]{1,0:T(8,128)}) custom-call(s32[3]{0:T(128)} %pad_add_fusion.idx, f32[512,768]{1,0:T(8,128)} %get-tuple-element.436.grad_in, bf16[512,3072]{1,0:T(8,128)(2,1)} %down_back.3.refs_6_.gu, ...), custom_call_target="tpu_custom_call" | custom-call | flops 4000000000 | bytes 1048576 | tf_op jit(solution)/shard_map/up_back/pallas_call | solution.py:407
  403.2 17.4 %attend_back.3 = (bf16[512,1280]{1,0:T(8,128)(2,1)}, bf16[512,1280]{1,0:T(8,128)(2,1)}) custom-call(s32[3]{0:T(128)} %pad_add_fusion.idx, s32[6,8]{1,0:T(8,128)} %dynamic-slice_select_fusion.kept, s32[2]{0:T(128)} %broadcast_select_fusion.1.pics, f32[8,1024]{1,0:T(8,128)} %get-tuple-element.444.lse, bf16[512,1280]{1,0:T(8,128)(2,1)} %get-tuple-element.297.own, ...), custom_call_target="tpu_custom_call" | custom-call | flops 6400000000 | bytes 1048576 | tf_op jit(solution)/shard_map/attend_back/pallas_call | solution.py:407
  423.1 15.0 %collective-permute-done.81.ra = bf16[2,4,2,48,768]{4,3,2,1,0:T(8,128)(2,1)} collective-permute-done((bf16[2,4,2,48,768]{4,3,2,1,0:T(8,128)(2,1)}, bf16[2,4,2,48,768]{4,3,2,1,0:T(8,128)(2,1)}, u32[]{:S(2)}, u32[]{:S(2)}) %collective-permute-start.81) | collective-permute-done | bytes 1179680 | tf_op jit(solution)/shard_map/ppermute | solution.py:1358
  439.9 3.7 cross.2
  447.2 10.1 %qkv_grad.1 = (bf16[2,4,1,48,768]{4,3,2,1,0:T(8,128)(2,1)}, bf16[2,4,1,48,768]{4,3,2,1,0:T(8,128)(2,1)}, bf16[2,4,1,48,768]{4,3,2,1,0:T(8,128)(2,1)}, bf16[2,4,1...) custom-call(s32[3]{0:T(128)} %pad_add_fusion.idx, bf16[384,512]{1,0:T(8,128)(2,1)} %bitcast.207, ...), custom_call_target="tpu_custom_call" | custom-call | flops 3200000000 | bytes 1048576 | tf_op jit(solution)/shard_map/qkv_grad/pallas_call | solution.py:407
  457.4 10.0 %qkv_back.3 = (f32[512,768]{1,0:T(8,128)}, bf16[512,768]{1,0:T(8,128)(2,1)}, f32[8,768]{1,0:T(8,128)}) custom-call(s32[3]{0:T(128)} %pad_add_fusion.idx, f32[512,768]{1,0:T(8,128)} %get-tuple-element.466.ga_in, bf16[512,1280]{1,0:T(8,128)(2,1)} %get-tuple-element.458.refs_6_.down_, bf16[512,1280]{1,0:T(8,128)(2,1)} %copy-done.74, ...), custom_call_target="tpu_custom_call" | custom-call | flops 3600000000 | bytes 1048576 | tf_op jit(solution)/shard_map/qkv_back/pallas_call | solution.py:407
  475.6 27.8 %collective-permute-done.94 = f32[4,48,128]{1,2,0:T(8,128)S(1)} collective-permute-done((f32[4,48,128]{1,2,0:T(8,128)S(1)}, f32[4,48,128]{1,2,0:T(8,128)S(1)}, u32[]{:S(2)}, u32[]{:S(2)}) %collective-permute-start.94) | collective-permute-done | bytes 98336 | tf_op jit(solution)/shard_map/ppermute | solution.py:1362
  504.1 1.8 collective-permute-start.88
  507.5 2.4 collective-permute-start.103
  510.4 4.6 own.2
  515.0 3.4 cross.3
  518.4 3.5 collective-permute-start.100
  521.8 1.7 collective-permute-start.101
  524.2 3.3 collective-permute-start.98
  530.5 1.9 collective-permute-done.100.ca
  532.4 4.1 collective-permute-done.97
  536.5 10.3 %collective-permute-done.98 = bf16[2,2,48,768]{3,2,1,0:T(8,128)(2,1)S(1)} collective-permute-done((bf16[2,2,48,768]{3,2,1,0:T(8,128)(2,1)}, bf16[2,2,48,768]{3,2,1,0:T(8,128)(2,1)S(1)}, u32[]{:S(2)}, u32[]{:S(2)}) %collective-permute-start.98) | collective-permute-done | bytes 294944 | tf_op jit(solution)/shard_map/ppermute | solution.py:1358
  547.2 3.4 own.3
  550.6 5.6 collective-permute-start.105
  560.8 7.8 %collective-permute-done.106 = bf16[2,1,48,768]{3,2,1,0:T(8,128)(2,1)S(1)} collective-permute-done((bf16[2,1,48,768]{3,2,1,0:T(8,128)(2,1)}, bf16[2,1,48,768]{3,2,1,0:T(8,128)(2,1)S(1)}, u32[]{:S(2)}, u32[]{:S(2)}) %collective-permute-start.106) | collective-permute-done | bytes 147488 | tf_op jit(solution)/shard_map/ppermute | solution.py:1358
  (492 shorter events, 99.7 us)
Async XLA Ops:
  7.2 158.7 %all-gather.3.cloned.1.call-start = ((), (), s32[]{:S(2)}) async-start(), calls=%async_computation.2 | async-start | bytes 5013504 | tf_op jit(solution)/shard_map/all_gather | solution.py:1485
  11.0 557.8 %reduce-scatter.2.cloned.1.call-start = ((), (), s32[]{:S(2)}) async-start(), calls=%async_computation.1 | async-start | bytes 7520256 | tf_op jit(solution)/shard_map/reduce_scatter | solution.py:1572
  14.2 29.1 %collective-permute-start.6 = (bf16[512,768]{1,0:T(8,128)(2,1)S(1)}, bf16[512,768]{1,0:T(8,128)(2,1)S(1)}, u32[]{:S(2)}, u32[]{:S(2)}) collective-permute-start(bf16[512,768]{1,0:T(8,128)(2,1)S(1)} %bitcast.199), channel_id=1, source_target_pairs={{0,0},{1,2},{2,1},{3,3},{4,4},{5,6},{6,5},{7,7},{8,8},{9,10},{10,9... | collective-permute-start | bytes 2359304 | tf_op jit(solution)/shard_map/ppermute | solution.py:1378
  15.6 27.6 %collective-permute-start = (bf16[2,1,48,768]{3,2,1,0:T(8,128)(2,1)S(1)}, bf16[2,1,48,768]{3,2,1,0:T(8,128)(2,1)S(1)}, u32[]{:S(2)}, u32[]{:S(2)}) collective-permute-start(bf16[2,1,48,768]{3,2,1,0:T(8,128)(2,1)S(1)} %maximum_bitcast_fusion.4), channel_id=1, source_target_pairs={{0,8},{4,12},{8,0},{12,4},{16,24},{20,28},{24,16},{28,20},{1,9},{5... | collective-permute-start | bytes 442376 | tf_op jit(solution)/shard_map/ppermute | solution.py:1358
  15.7 27.6 %collective-permute-start.1 = (bf16[2,1,48,768]{3,2,1,0:T(8,128)(2,1)S(1)}, bf16[2,1,48,768]{3,2,1,0:T(8,128)(2,1)S(1)}, u32[]{:S(2)}, u32[]{:S(2)}) collective-permute-start(bf16[2,1,48,768]{3,2,1,0:T(8,128)(2,1)S(1)} %maximum_bitcast_fusion.4), channel_id=1, source_target_pairs={{0,16},{4,20},{8,24},{12,28},{16,0},{20,4},{24,8},{28,12},{1,17},{... | collective-permute-start | bytes 442376 | tf_op jit(solution)/shard_map/ppermute | solution.py:1358
  18.7 24.6 %collective-permute-start.2 = (bf16[2,1,48,768]{3,2,1,0:T(8,128)(2,1)S(1)}, bf16[2,1,48,768]{3,2,1,0:T(8,128)(2,1)S(1)}, u32[]{:S(2)}, u32[]{:S(2)}) collective-permute-start(bf16[2,1,48,768]{3,2,1,0:T(8,128)(2,1)S(1)} %maximum_bitcast_fusion.4), channel_id=1, source_target_pairs={{0,24},{4,28},{8,16},{12,20},{16,8},{20,12},{24,0},{28,4},{1,25},{... | collective-permute-start | bytes 442376 | tf_op jit(solution)/shard_map/ppermute | solution.py:1358
  20.0 16.4 %collective-permute-start.4 = (bf16[32,128]{1,0:T(8,128)(2,1)S(1)}, bf16[32,128]{1,0:T(8,128)(2,1)S(1)}, u32[]{:S(2)}, u32[]{:S(2)}) collective-permute-start(bf16[32,128]{1,0:T(8,128)(2,1)S(1)} %get-tuple-element.643), channel_id=1, source_target_pairs={{0,16},{4,20},{8,24},{12,28},{16,0},{20,4},{24,8},{28,12},{1,17},{... | collective-permute-start | bytes 24584 | tf_op jit(solution)/shard_map/ppermute | solution.py:1358
  43.5 25.6 %collective-permute-start.10 = (bf16[4,1,48,768]{3,2,1,0:T(8,128)(2,1)S(1)}, bf16[4,1,48,768]{3,2,1,0:T(8,128)(2,1)S(1)}, u32[]{:S(2)}, u32[]{:S(2)}) collective-permute-start(bf16[4,1,48,768]{3,2,1,0:T(8,128)(2,1)S(1)} %pad_maximum_fusion.6.refs_8_), channel_id=1, source_target_pairs={{0,4},{4,0},{8,12},{12,8},{16,20},{20,16},{24,28},{28,24},{1,5},{5... | collective-permute-start | bytes 884744 | tf_op jit(solution)/shard_map/ppermute | solution.py:1358
  45.3 23.9 %collective-permute-start.8 = (bf16[4,1,48,768]{3,2,1,0:T(8,128)(2,1)S(1)}, bf16[4,1,48,768]{3,2,1,0:T(8,128)(2,1)S(1)}, u32[]{:S(2)}, u32[]{:S(2)}) collective-permute-start(bf16[4,1,48,768]{3,2,1,0:T(8,128)(2,1)S(1)} %pad_maximum_fusion.6.refs_8_), channel_id=1, source_target_pairs={{0,1},{1,0},{2,3},{3,2},{4,5},{5,4},{6,7},{7,6},{8,9},{9,8},{10,11... | collective-permute-start | bytes 884744 | tf_op jit(solution)/shard_map/ppermute | solution.py:1362
  47.9 21.4 %collective-permute-start.7 = (bf16[4,1,48,768]{3,2,1,0:T(8,128)(2,1)S(1)}, bf16[4,1,48,768]{3,2,1,0:T(8,128)(2,1)S(1)}, u32[]{:S(2)}, u32[]{:S(2)}) collective-permute-start(bf16[4,1,48,768]{3,2,1,0:T(8,128)(2,1)S(1)} %pad_maximum_fusion.5.refs_0_), channel_id=1, source_target_pairs={{0,4},{4,0},{8,12},{12,8},{16,20},{20,16},{24,28},{28,24},{1,5},{5... | collective-permute-start | bytes 884744 | tf_op jit(solution)/shard_map/ppermute | solution.py:1358
  48.5 20.7 %collective-permute-start.9 = (bf16[4,1,48,768]{3,2,1,0:T(8,128)(2,1)S(1)}, bf16[4,1,48,768]{3,2,1,0:T(8,128)(2,1)S(1)}, u32[]{:S(2)}, u32[]{:S(2)}) collective-permute-start(bf16[4,1,48,768]{3,2,1,0:T(8,128)(2,1)S(1)} %pad_maximum_fusion.5.refs_0_), channel_id=1, source_target_pairs={{0,1},{1,0},{2,3},{3,2},{4,5},{5,4},{6,7},{7,6},{8,9},{9,8},{10,11... | collective-permute-start | bytes 884744 | tf_op jit(solution)/shard_map/ppermute | solution.py:1362
  48.5 20.2 %collective-permute-start.11 = (bf16[4,32,128]{2,1,0:T(8,128)(2,1)S(1)}, bf16[4,32,128]{2,1,0:T(8,128)(2,1)S(1)}, u32[]{:S(2)}, u32[]{:S(2)}) collective-permute-start(bf16[4,32,128]{2,1,0:T(8,128)(2,1)S(1)} %pad_maximum_fusion.14), channel_id=1, source_target_pairs={{0,4},{4,0},{8,12},{12,8},{16,20},{20,16},{24,28},{28,24},{1,5},{5... | collective-permute-start | bytes 98312 | tf_op jit(solution)/shard_map/ppermute | solution.py:1358
  71.2 12.3 %collective-permute-start.15 = (bf16[4,1,48,768]{3,2,1,0:T(8,128)(2,1)S(1)}, bf16[4,1,48,768]{3,2,1,0:T(8,128)(2,1)S(1)}, u32[]{:S(2)}, u32[]{:S(2)}) collective-permute-start(bf16[4,1,48,768]{3,2,1,0:T(8,128)(2,1)S(1)} %collective-permute-done.7.refs_1_), channel_id=1, source_target_pairs={{0,2},{2,0},{1,3},{3,1},{4,6},{6,4},{5,7},{7,5},{8,10},{10,8},{9,1... | collective-permute-start | bytes 884744 | tf_op jit(solution)/shard_map/ppermute | solution.py:1366
  71.4 12.1 %collective-permute-start.13 = (bf16[4,1,48,768]{3,2,1,0:T(8,128)(2,1)S(1)}, bf16[4,1,48,768]{3,2,1,0:T(8,128)(2,1)S(1)}, u32[]{:S(2)}, u32[]{:S(2)}) collective-permute-start(bf16[4,1,48,768]{3,2,1,0:T(8,128)(2,1)S(1)} %collective-permute-done.8.refs_10_), channel_id=1, source_target_pairs={{0,4},{4,0},{8,12},{12,8},{16,20},{20,16},{24,28},{28,24},{1,5},{5... | collective-permute-start | bytes 884744 | tf_op jit(solution)/shard_map/ppermute | solution.py:1358
  83.5 37.4 %collective-permute-start.26 = (s32[12,8]{1,0:T(8,128)S(1)}, s32[12,8]{1,0:T(8,128)S(1)}, u32[]{:S(2)}, u32[]{:S(2)}) collective-permute-start(s32[12,8]{1,0:T(8,128)S(1)} %copy.85), channel_id=1, source_target_pairs={{0,2},{2,0},{1,3},{3,1},{4,6},{6,4},{5,7},{7,5},{8,10},{10,8},{9,1... | collective-permute-start | bytes 1160 | tf_op jit(solution)/shard_map/ppermute | solution.py:1366
  83.5 36.2 %collective-permute-start.27 = (s32[2]{0:T(128)}, s32[2]{0:T(128)S(1)}, u32[]{:S(2)}, u32[]{:S(2)}) collective-permute-start(s32[2]{0:T(128)} %bitcast.24), channel_id=1, source_target_pairs={{0,2},{2,0},{1,3},{3,1},{4,6},{6,4},{5,7},{7,5},{8,10},{10,8},{9,1... | collective-permute-start | bytes 32 | tf_op jit(solution)/shard_map/ppermute | solution.py:1366
  91.8 13.6 %collective-permute-start.23 = (bf16[2,1,48,768]{3,2,1,0:T(8,128)(2,1)S(1)}, bf16[2,1,48,768]{3,2,1,0:T(8,128)(2,1)S(1)}, u32[]{:S(2)}, u32[]{:S(2)}) collective-permute-start(bf16[2,1,48,768]{3,2,1,0:T(8,128)(2,1)S(1)} %maximum_bitcast_fusion.5), channel_id=1, source_target_pairs={{0,8},{4,12},{8,0},{12,4},{16,24},{20,28},{24,16},{28,20},{1,9},{5... | collective-permute-start | bytes 442376 | tf_op jit(solution)/shard_map/ppermute | solution.py:1358
  91.8 22.7 %collective-permute-start.24 = (bf16[2,1,48,768]{3,2,1,0:T(8,128)(2,1)S(1)}, bf16[2,1,48,768]{3,2,1,0:T(8,128)(2,1)S(1)}, u32[]{:S(2)}, u32[]{:S(2)}) collective-permute-start(bf16[2,1,48,768]{3,2,1,0:T(8,128)(2,1)S(1)} %maximum_bitcast_fusion.5), channel_id=1, source_target_pairs={{0,16},{4,20},{8,24},{12,28},{16,0},{20,4},{24,8},{28,12},{1,17},{... | collective-permute-start | bytes 442376 | tf_op jit(solution)/shard_map/ppermute | solution.py:1358
  96.6 18.4 %collective-permute-start.25 = (bf16[2,1,48,768]{3,2,1,0:T(8,128)(2,1)S(1)}, bf16[2,1,48,768]{3,2,1,0:T(8,128)(2,1)S(1)}, u32[]{:S(2)}, u32[]{:S(2)}) collective-permute-start(bf16[2,1,48,768]{3,2,1,0:T(8,128)(2,1)S(1)} %maximum_bitcast_fusion.5), channel_id=1, source_target_pairs={{0,24},{4,28},{8,16},{12,20},{16,8},{20,12},{24,0},{28,4},{1,25},{... | collective-permute-start | bytes 442376 | tf_op jit(solution)/shard_map/ppermute | solution.py:1358
  105.4 26.9 %collective-permute-start.28 = (bf16[512,1280]{1,0:T(8,128)(2,1)}, bf16[512,1280]{1,0:T(8,128)(2,1)S(1)}, u32[]{:S(2)}, u32[]{:S(2)}) collective-permute-start(bf16[512,1280]{1,0:T(8,128)(2,1)} %get-tuple-element.298), channel_id=1, source_target_pairs={{0,2},{2,0},{1,3},{3,1},{4,6},{6,4},{5,7},{7,5},{8,10},{10,8},{9,1... | collective-permute-start | bytes 3932168 | tf_op jit(solution)/shard_map/ppermute | solution.py:1366
  118.0 12.4 %collective-permute-start.32 = (bf16[4,1,48,768]{3,2,1,0:T(8,128)(2,1)S(1)}, bf16[4,1,48,768]{3,2,1,0:T(8,128)(2,1)S(1)}, u32[]{:S(2)}, u32[]{:S(2)}) collective-permute-start(bf16[4,1,48,768]{3,2,1,0:T(8,128)(2,1)S(1)} %pad_maximum_fusion.8.refs_8_), channel_id=1, source_target_pairs={{0,4},{4,0},{8,12},{12,8},{16,20},{20,16},{24,28},{28,24},{1,5},{5... | collective-permute-start | bytes 884744 | tf_op jit(solution)/shard_map/ppermute | solution.py:1358
  121.6 25.1 %collective-permute-start.29 = (bf16[4,1,48,768]{3,2,1,0:T(8,128)(2,1)S(1)}, bf16[4,1,48,768]{3,2,1,0:T(8,128)(2,1)S(1)}, u32[]{:S(2)}, u32[]{:S(2)}) collective-permute-start(bf16[4,1,48,768]{3,2,1,0:T(8,128)(2,1)S(1)} %pad_maximum_fusion.7.refs_0_), channel_id=1, source_target_pairs={{0,4},{4,0},{8,12},{12,8},{16,20},{20,16},{24,28},{28,24},{1,5},{5... | collective-permute-start | bytes 884744 | tf_op jit(solution)/shard_map/ppermute | solution.py:1358
  121.9 24.9 %collective-permute-start.31 = (bf16[4,1,48,768]{3,2,1,0:T(8,128)(2,1)S(1)}, bf16[4,1,48,768]{3,2,1,0:T(8,128)(2,1)S(1)}, u32[]{:S(2)}, u32[]{:S(2)}) collective-permute-start(bf16[4,1,48,768]{3,2,1,0:T(8,128)(2,1)S(1)} %pad_maximum_fusion.7.refs_0_), channel_id=1, source_target_pairs={{0,1},{1,0},{2,3},{3,2},{4,5},{5,4},{6,7},{7,6},{8,9},{9,8},{10,11... | collective-permute-start | bytes 884744 | tf_op jit(solution)/shard_map/ppermute | solution.py:1362
  125.4 21.9 %collective-permute-start.33 = (bf16[2,2,48,768]{3,2,1,0:T(8,128)(2,1)S(1)}, bf16[2,2,48,768]{3,2,1,0:T(8,128)(2,1)S(1)}, u32[]{:S(2)}, u32[]{:S(2)}) collective-permute-start(bf16[2,2,48,768]{3,2,1,0:T(8,128)(2,1)S(1)} %pad_maximum_fusion.9), channel_id=1, source_target_pairs={{0,8},{4,12},{8,0},{12,4},{16,24},{20,28},{24,16},{28,20},{1,9},{5... | collective-permute-start | bytes 884744 | tf_op jit(solution)/shard_map/ppermute | solution.py:1358
  130.4 23.0 %collective-permute-start.34 = (bf16[2,2,48,768]{3,2,1,0:T(8,128)(2,1)S(1)}, bf16[2,2,48,768]{3,2,1,0:T(8,128)(2,1)S(1)}, u32[]{:S(2)}, u32[]{:S(2)}) collective-permute-start(bf16[2,2,48,768]{3,2,1,0:T(8,128)(2,1)S(1)} %pad_maximum_fusion.9), channel_id=1, source_target_pairs={{0,16},{4,20},{8,24},{12,28},{16,0},{20,4},{24,8},{28,12},{1,17},{... | collective-permute-start | bytes 884744 | tf_op jit(solution)/shard_map/ppermute | solution.py:1358
  132.3 21.1 %collective-permute-start.35 = (bf16[2,2,48,768]{3,2,1,0:T(8,128)(2,1)S(1)}, bf16[2,2,48,768]{3,2,1,0:T(8,128)(2,1)S(1)}, u32[]{:S(2)}, u32[]{:S(2)}) collective-permute-start(bf16[2,2,48,768]{3,2,1,0:T(8,128)(2,1)S(1)} %pad_maximum_fusion.9), channel_id=1, source_target_pairs={{0,24},{4,28},{8,16},{12,20},{16,8},{20,12},{24,0},{28,4},{1,25},{... | collective-permute-start | bytes 884744 | tf_op jit(solution)/shard_map/ppermute | solution.py:1358
  166.4 16.2 %collective-permute-start.49 = (bf16[4,2,48,768]{3,2,1,0:T(8,128)(2,1)S(1)}, bf16[4,2,48,768]{3,2,1,0:T(8,128)(2,1)S(1)}, u32[]{:S(2)}, u32[]{:S(2)}) collective-permute-start(bf16[4,2,48,768]{3,2,1,0:T(8,128)(2,1)S(1)} %pad_maximum_fusion.1.refs_24_.refs_8_), channel_id=1, source_target_pairs={{0,1},{1,0},{2,3},{3,2},{4,5},{5,4},{6,7},{7,6},{8,9},{9,8},{10,11... | collective-permute-start | bytes 1769480 | tf_op jit(solution)/shard_map/ppermute | solution.py:1362
  169.5 30.5 %collective-permute-start.51 = (bf16[4,2,48,768]{3,2,1,0:T(8,128)(2,1)S(1)}, bf16[4,2,48,768]{3,2,1,0:T(8,128)(2,1)S(1)}, u32[]{:S(2)}, u32[]{:S(2)}) collective-permute-start(bf16[4,2,48,768]{3,2,1,0:T(8,128)(2,1)S(1)} %pad_maximum_fusion.1.refs_24_.refs_8_), channel_id=1, source_target_pairs={{0,4},{4,0},{8,12},{12,8},{16,20},{20,16},{24,28},{28,24},{1,5},{5... | collective-permute-start | bytes 1769480 | tf_op jit(solution)/shard_map/ppermute | solution.py:1358
  170.9 29.1 %collective-permute-start.48 = (bf16[4,2,48,768]{3,2,1,0:T(8,128)(2,1)S(1)}, bf16[4,2,48,768]{3,2,1,0:T(8,128)(2,1)S(1)}, u32[]{:S(2)}, u32[]{:S(2)}) collective-permute-start(bf16[4,2,48,768]{3,2,1,0:T(8,128)(2,1)S(1)} %pad_maximum_fusion.refs_16_.refs_0_), channel_id=1, source_target_pairs={{0,4},{4,0},{8,12},{12,8},{16,20},{20,16},{24,28},{28,24},{1,5},{5... | collective-permute-start | bytes 1769480 | tf_op jit(solution)/shard_map/ppermute | solution.py:1358
  174.2 25.8 %collective-permute-start.50 = (bf16[4,2,48,768]{3,2,1,0:T(8,128)(2,1)S(1)}, bf16[4,2,48,768]{3,2,1,0:T(8,128)(2,1)S(1)}, u32[]{:S(2)}, u32[]{:S(2)}) collective-permute-start(bf16[4,2,48,768]{3,2,1,0:T(8,128)(2,1)S(1)} %pad_maximum_fusion.refs_16_.refs_0_), channel_id=1, source_target_pairs={{0,1},{1,0},{2,3},{3,2},{4,5},{5,4},{6,7},{7,6},{8,9},{9,8},{10,11... | collective-permute-start | bytes 1769480 | tf_op jit(solution)/shard_map/ppermute | solution.py:1362
  174.8 25.3 %collective-permute-start.46 = (bf16[4,1,48,768]{3,2,1,0:T(8,128)(2,1)S(1)}, bf16[4,1,48,768]{3,2,1,0:T(8,128)(2,1)S(1)}, u32[]{:S(2)}, u32[]{:S(2)}) collective-permute-start(bf16[4,1,48,768]{3,2,1,0:T(8,128)(2,1)S(1)} %copy-done.50), channel_id=1, source_target_pairs={{0,2},{2,0},{1,3},{3,1},{4,6},{6,4},{5,7},{7,5},{8,10},{10,8},{9,1... | collective-permute-start | bytes 884744 | tf_op jit(solution)/shard_map/ppermute | solution.py:1366
  182.6 17.5 %collective-permute-start.47 = (bf16[4,1,48,768]{3,2,1,0:T(8,128)(2,1)S(1)}, bf16[4,1,48,768]{3,2,1,0:T(8,128)(2,1)S(1)}, u32[]{:S(2)}, u32[]{:S(2)}) collective-permute-start(bf16[4,1,48,768]{3,2,1,0:T(8,128)(2,1)S(1)} %copy-done.53), channel_id=1, source_target_pairs={{0,2},{2,0},{1,3},{3,1},{4,6},{6,4},{5,7},{7,5},{8,10},{10,8},{9,1... | collective-permute-start | bytes 884744 | tf_op jit(solution)/shard_map/ppermute | solution.py:1366
  210.3 20.0 %collective-permute-start.60 = (bf16[512,1280]{1,0:T(8,128)(2,1)}, bf16[512,1280]{1,0:T(8,128)(2,1)}, u32[]{:S(2)}, u32[]{:S(2)}) collective-permute-start(bf16[512,1280]{1,0:T(8,128)(2,1)} %get-tuple-element.356), channel_id=1, source_target_pairs={{0,2},{2,0},{1,3},{3,1},{4,6},{6,4},{5,7},{7,5},{8,10},{10,8},{9,1... | collective-permute-start | bytes 3932168 | tf_op jit(solution)/shard_map/ppermute | solution.py:1366
  211.2 15.5 %collective-permute-start.52 = (bf16[4,2,48,768]{3,2,1,0:T(8,128)(2,1)S(1)}, bf16[4,2,48,768]{3,2,1,0:T(8,128)(2,1)S(1)}, u32[]{:S(2)}, u32[]{:S(2)}) collective-permute-start(bf16[4,2,48,768]{3,2,1,0:T(8,128)(2,1)S(1)} %collective-permute-done.48.refs_17_.refs_1_), channel_id=1, source_target_pairs={{0,1},{1,0},{2,3},{3,2},{4,5},{5,4},{6,7},{7,6},{8,9},{9,8},{10,11... | collective-permute-start | bytes 1769480 | tf_op jit(solution)/shard_map/ppermute | solution.py:1362
  211.8 15.2 %collective-permute-start.53 = (bf16[4,2,48,768]{3,2,1,0:T(8,128)(2,1)S(1)}, bf16[4,2,48,768]{3,2,1,0:T(8,128)(2,1)S(1)}, u32[]{:S(2)}, u32[]{:S(2)}) collective-permute-start(bf16[4,2,48,768]{3,2,1,0:T(8,128)(2,1)S(1)} %collective-permute-done.49.refs_26_.refs_10_), channel_id=1, source_target_pairs={{0,4},{4,0},{8,12},{12,8},{16,20},{20,16},{24,28},{28,24},{1,5},{5... | collective-permute-start | bytes 1769480 | tf_op jit(solution)/shard_map/ppermute | solution.py:1358
  214.3 13.0 %collective-permute-start.55 = (bf16[4,2,48,768]{3,2,1,0:T(8,128)(2,1)S(1)}, bf16[4,2,48,768]{3,2,1,0:T(8,128)(2,1)S(1)}, u32[]{:S(2)}, u32[]{:S(2)}) collective-permute-start(bf16[4,2,48,768]{3,2,1,0:T(8,128)(2,1)S(1)} %collective-permute-done.48.refs_17_.refs_1_), channel_id=1, source_target_pairs={{0,2},{2,0},{1,3},{3,1},{4,6},{6,4},{5,7},{7,5},{8,10},{10,8},{9,1... | collective-permute-start | bytes 1769480 | tf_op jit(solution)/shard_map/ppermute | solution.py:1366
  229.5 12.9 %collective-permute-start.61 = (bf16[4,2,48,768]{3,2,1,0:T(8,128)(2,1)S(1)}, bf16[4,2,48,768]{3,2,1,0:T(8,128)(2,1)S(1)}, u32[]{:S(2)}, u32[]{:S(2)}) collective-permute-start(bf16[4,2,48,768]{3,2,1,0:T(8,128)(2,1)S(1)} %collective-permute-done.52.refs_19_.refs_3_), channel_id=1, source_target_pairs={{0,2},{2,0},{1,3},{3,1},{4,6},{6,4},{5,7},{7,5},{8,10},{10,8},{9,1... | collective-permute-start | bytes 1769480 | tf_op jit(solution)/shard_map/ppermute | solution.py:1366
  229.7 12.8 %collective-permute-start.62 = (bf16[4,2,48,768]{3,2,1,0:T(8,128)(2,1)S(1)}, bf16[4,2,48,768]{3,2,1,0:T(8,128)(2,1)S(1)}, u32[]{:S(2)}, u32[]{:S(2)}) collective-permute-start(bf16[4,2,48,768]{3,2,1,0:T(8,128)(2,1)S(1)} %collective-permute-done.53.refs_27_.refs_11_), channel_id=1, source_target_pairs={{0,2},{2,0},{1,3},{3,1},{4,6},{6,4},{5,7},{7,5},{8,10},{10,8},{9,1... | collective-permute-start | bytes 1769480 | tf_op jit(solution)/shard_map/ppermute | solution.py:1366
  242.5 19.9 %collective-permute-start.65 = (bf16[512,768]{1,0:T(8,128)(2,1)}, bf16[512,768]{1,0:T(8,128)(2,1)S(1)}, u32[]{:S(2)}, u32[]{:S(2)}) collective-permute-start(bf16[512,768]{1,0:T(8,128)(2,1)} %bitcast.200), channel_id=1, source_target_pairs={{0,0},{1,2},{2,1},{3,3},{4,4},{5,6},{6,5},{7,7},{8,8},{9,10},{10,9... | collective-permute-start | bytes 2359304 | tf_op jit(solution)/shard_map/ppermute | solution.py:1378
  274.4 52.4 %collective-permute-start.71 = (bf16[512,3072]{1,0:T(8,128)(2,1)}, bf16[512,3072]{1,0:T(8,128)(2,1)S(1)}, u32[]{:S(2)}, u32[]{:S(2)}) collective-permute-start(bf16[512,3072]{1,0:T(8,128)(2,1)} %down_back.2.gu.refs_6_), channel_id=1, source_target_pairs={{0,2},{2,0},{1,3},{3,1},{4,6},{6,4},{5,7},{7,5},{8,10},{10,8},{9,1... | collective-permute-start | bytes 9437192 | tf_op jit(solution)/shard_map/ppermute | solution.py:1366
  309.1 17.7 %collective-permute-start.68 = (bf16[8,192,512]{2,1,0:T(8,128)(2,1)S(1)}, bf16[8,192,512]{2,1,0:T(8,128)(2,1)}, u32[]{:S(2)}, u32[]{:S(2)}) collective-permute-start(bf16[8,192,512]{2,1,0:T(8,128)(2,1)S(1)} %copy-done.71), channel_id=1, source_target_pairs={{0,2},{2,0},{1,3},{3,1},{4,6},{6,4},{5,7},{7,5},{8,10},{10,8},{9,1... | collective-permute-start | bytes 4718600 | tf_op jit(solution)/shard_map/ppermute | solution.py:1366
  312.9 13.9 %collective-permute-start.75 = (bf16[512,1280]{1,0:T(8,128)(2,1)}, bf16[512,1280]{1,0:T(8,128)(2,1)}, u32[]{:S(2)}, u32[]{:S(2)}) collective-permute-start(bf16[512,1280]{1,0:T(8,128)(2,1)} %get-tuple-element.403.down_.refs_14_), channel_id=1, source_target_pairs={{0,2},{2,0},{1,3},{3,1},{4,6},{6,4},{5,7},{7,5},{8,10},{10,8},{9,1... | collective-permute-start | bytes 3932168 | tf_op jit(solution)/shard_map/ppermute | solution.py:1366
  400.0 38.1 %collective-permute-start.81 = (bf16[2,4,2,48,768]{4,3,2,1,0:T(8,128)(2,1)}, bf16[2,4,2,48,768]{4,3,2,1,0:T(8,128)(2,1)}, u32[]{:S(2)}, u32[]{:S(2)}) collective-permute-start(bf16[2,4,2,48,768]{4,3,2,1,0:T(8,128)(2,1)} %get-tuple-element.450), channel_id=1, source_target_pairs={{0,4},{4,0},{8,12},{12,8},{16,20},{20,16},{24,28},{28,24},{1,5},{5... | collective-permute-start | bytes 3538952 | tf_op jit(solution)/shard_map/ppermute | solution.py:1358
  401.3 37.4 %collective-permute-start.82 = (bf16[2,4,2,48,768]{4,3,2,1,0:T(8,128)(2,1)}, bf16[2,4,2,48,768]{4,3,2,1,0:T(8,128)(2,1)}, u32[]{:S(2)}, u32[]{:S(2)}) collective-permute-start(bf16[2,4,2,48,768]{4,3,2,1,0:T(8,128)(2,1)} %get-tuple-element.451), channel_id=1, source_target_pairs={{0,1},{1,0},{2,3},{3,2},{4,5},{5,4},{6,7},{7,6},{8,9},{9,8},{10,11... | collective-permute-start | bytes 3538952 | tf_op jit(solution)/shard_map/ppermute | solution.py:1362
  420.7 25.1 %collective-permute-start.86 = (bf16[512,1280]{1,0:T(8,128)(2,1)}, bf16[512,1280]{1,0:T(8,128)(2,1)S(1)}, u32[]{:S(2)}, u32[]{:S(2)}) collective-permute-start(bf16[512,1280]{1,0:T(8,128)(2,1)} %get-tuple-element.459.refs_8_), channel_id=1, source_target_pairs={{0,2},{2,0},{1,3},{3,1},{4,6},{6,4},{5,7},{7,5},{8,10},{10,8},{9,1... | collective-permute-start | bytes 3932168 | tf_op jit(solution)/shard_map/ppermute | solution.py:1366
  420.7 25.0 %collective-permute-start.87 = (bf16[512,1280]{1,0:T(8,128)(2,1)}, bf16[512,1280]{1,0:T(8,128)(2,1)S(1)}, u32[]{:S(2)}, u32[]{:S(2)}) collective-permute-start(bf16[512,1280]{1,0:T(8,128)(2,1)} %get-tuple-element.458.refs_6_.down_), channel_id=1, source_target_pairs={{0,2},{2,0},{1,3},{3,1},{4,6},{6,4},{5,7},{7,5},{8,10},{10,8},{9,1... | collective-permute-start | bytes 3932168 | tf_op jit(solution)/shard_map/ppermute | solution.py:1366
  422.2 23.6 %collective-permute-start.85 = (bf16[512,768]{1,0:T(8,128)(2,1)}, bf16[512,768]{1,0:T(8,128)(2,1)}, u32[]{:S(2)}, u32[]{:S(2)}) collective-permute-start(bf16[512,768]{1,0:T(8,128)(2,1)} %get-tuple-element.457.refs_4_), channel_id=1, source_target_pairs={{0,2},{2,0},{1,3},{3,1},{4,6},{6,4},{5,7},{7,5},{8,10},{10,8},{9,1... | collective-permute-start | bytes 2359304 | tf_op jit(solution)/shard_map/ppermute | solution.py:1366
  443.6 29.6 %collective-permute-start.89 = (bf16[4,2,48,768]{3,2,1,0:T(8,128)(2,1)}, bf16[4,2,48,768]{3,2,1,0:T(8,128)(2,1)}, u32[]{:S(2)}, u32[]{:S(2)}) collective-permute-start(bf16[4,2,48,768]{3,2,1,0:T(8,128)(2,1)} %get-tuple-element.475), channel_id=1, source_target_pairs={{0,1},{1,0},{2,3},{3,2},{4,5},{5,4},{6,7},{7,6},{8,9},{9,8},{10,11... | collective-permute-start | bytes 1769480 | tf_op jit(solution)/shard_map/ppermute | solution.py:1362
  444.9 29.2 %collective-permute-start.90 = (bf16[4,2,48,768]{3,2,1,0:T(8,128)(2,1)}, bf16[4,2,48,768]{3,2,1,0:T(8,128)(2,1)}, u32[]{:S(2)}, u32[]{:S(2)}) collective-permute-start(bf16[4,2,48,768]{3,2,1,0:T(8,128)(2,1)} %get-tuple-element.476), channel_id=1, source_target_pairs={{0,4},{4,0},{8,12},{12,8},{16,20},{20,16},{24,28},{28,24},{1,5},{5... | collective-permute-start | bytes 1769480 | tf_op jit(solution)/shard_map/ppermute | solution.py:1358
  469.0 36.9 %collective-permute-start.91 = (bf16[2,4,1,48,768]{4,3,2,1,0:T(8,128)(2,1)}, bf16[2,4,1,48,768]{4,3,2,1,0:T(8,128)(2,1)}, u32[]{:S(2)}, u32[]{:S(2)}) collective-permute-start(bf16[2,4,1,48,768]{4,3,2,1,0:T(8,128)(2,1)} %get-tuple-element.477), channel_id=1, source_target_pairs={{0,4},{4,0},{8,12},{12,8},{16,20},{20,16},{24,28},{28,24},{1,5},{5... | collective-permute-start | bytes 1769480 | tf_op jit(solution)/shard_map/ppermute | solution.py:1358
  470.3 35.6 %collective-permute-start.92 = (bf16[2,4,1,48,768]{4,3,2,1,0:T(8,128)(2,1)}, bf16[2,4,1,48,768]{4,3,2,1,0:T(8,128)(2,1)}, u32[]{:S(2)}, u32[]{:S(2)}) collective-permute-start(bf16[2,4,1,48,768]{4,3,2,1,0:T(8,128)(2,1)} %get-tuple-element.478), channel_id=1, source_target_pairs={{0,1},{1,0},{2,3},{3,2},{4,5},{5,4},{6,7},{7,6},{8,9},{9,8},{10,11... | collective-permute-start | bytes 1769480 | tf_op jit(solution)/shard_map/ppermute | solution.py:1362
  472.0 31.3 %collective-permute-start.94 = (f32[4,48,128]{1,2,0:T(8,128)S(1)}, f32[4,48,128]{1,2,0:T(8,128)S(1)}, u32[]{:S(2)}, u32[]{:S(2)}) collective-permute-start(f32[4,48,128]{1,2,0:T(8,128)S(1)} %get-tuple-element.605), channel_id=1, source_target_pairs={{0,1},{1,0},{2,3},{3,2},{4,5},{5,4},{6,7},{7,6},{8,9},{9,8},{10,11... | collective-permute-start | bytes 294920 | tf_op jit(solution)/shard_map/ppermute | solution.py:1362
  473.3 30.8 %collective-permute-start.95 = (f32[4,48,128]{1,2,0:T(8,128)S(1)}, f32[4,48,128]{1,2,0:T(8,128)S(1)}, u32[]{:S(2)}, u32[]{:S(2)}) collective-permute-start(f32[4,48,128]{1,2,0:T(8,128)S(1)} %get-tuple-element.604), channel_id=1, source_target_pairs={{0,4},{4,0},{8,12},{12,8},{16,20},{20,16},{24,28},{28,24},{1,5},{5... | collective-permute-start | bytes 294920 | tf_op jit(solution)/shard_map/ppermute | solution.py:1358
  474.1 31.8 %collective-permute-start.96 = (f32[4,48,128]{1,2,0:T(8,128)S(1)}, f32[4,48,128]{1,2,0:T(8,128)S(1)}, u32[]{:S(2)}, u32[]{:S(2)}) collective-permute-start(f32[4,48,128]{1,2,0:T(8,128)S(1)} %get-tuple-element.604), channel_id=1, source_target_pairs={{0,5},{1,4},{4,1},{5,0},{8,13},{9,12},{12,9},{13,8},{16,21},{17,20... | collective-permute-start | bytes 294920 | tf_op jit(solution)/shard_map/ppermute | solution.py:1374
  503.4 15.0 %collective-permute-start.64 = (bf16[512,768]{1,0:T(8,128)(2,1)S(1)}, bf16[512,768]{1,0:T(8,128)(2,1)S(1)}, u32[]{:S(2)}, u32[]{:S(2)}) collective-permute-start(bf16[512,768]{1,0:T(8,128)(2,1)S(1)} %copy-done.77), channel_id=1, source_target_pairs={{0,0},{1,2},{2,1},{3,3},{4,4},{5,6},{6,5},{7,7},{8,8},{9,10},{10,9... | collective-permute-start | bytes 2359304 | tf_op jit(solution)/shard_map/ppermute | solution.py:1378
  504.1 23.4 %collective-permute-start.88 = (bf16[512,768]{1,0:T(8,128)(2,1)}, bf16[512,768]{1,0:T(8,128)(2,1)S(1)}, u32[]{:S(2)}, u32[]{:S(2)}) collective-permute-start(bf16[512,768]{1,0:T(8,128)(2,1)} %get-tuple-element.469), channel_id=1, source_target_pairs={{0,0},{1,2},{2,1},{3,3},{4,4},{5,6},{6,5},{7,7},{8,8},{9,10},{10,9... | collective-permute-start | bytes 2359304 | tf_op jit(solution)/shard_map/ppermute | solution.py:1378
  506.0 15.9 %collective-permute-start.102 = (f32[48,128]{0,1:T(8,128)S(1)}, f32[48,128]{0,1:T(8,128)S(1)}, u32[]{:S(2)}, u32[]{:S(2)}) collective-permute-start(f32[48,128]{0,1:T(8,128)S(1)} %get-tuple-element.581), channel_id=1, source_target_pairs={{0,8},{4,12},{8,0},{12,4},{16,24},{20,28},{24,16},{28,20},{1,9},{5... | collective-permute-start | bytes 73736 | tf_op jit(solution)/shard_map/ppermute | solution.py:1358
  507.5 16.0 %collective-permute-start.103 = (f32[48,128]{0,1:T(8,128)S(1)}, f32[48,128]{0,1:T(8,128)S(1)}, u32[]{:S(2)}, u32[]{:S(2)}) collective-permute-start(f32[48,128]{0,1:T(8,128)S(1)} %get-tuple-element.580), channel_id=1, source_target_pairs={{0,16},{4,20},{8,24},{12,28},{16,0},{20,4},{24,8},{28,12},{1,17},{... | collective-permute-start | bytes 73736 | tf_op jit(solution)/shard_map/ppermute | solution.py:1358
  509.9 14.2 %collective-permute-start.104 = (f32[48,128]{0,1:T(8,128)S(1)}, f32[48,128]{0,1:T(8,128)S(1)}, u32[]{:S(2)}, u32[]{:S(2)}) collective-permute-start(f32[48,128]{0,1:T(8,128)S(1)} %get-tuple-element.579), channel_id=1, source_target_pairs={{0,24},{4,28},{8,16},{12,20},{16,8},{20,12},{24,0},{28,4},{1,25},{... | collective-permute-start | bytes 73736 | tf_op jit(solution)/shard_map/ppermute | solution.py:1358
  518.4 14.0 %collective-permute-start.100 = (bf16[4,1,48,768]{3,2,1,0:T(8,128)(2,1)}, bf16[4,1,48,768]{3,2,1,0:T(8,128)(2,1)S(1)}, u32[]{:S(2)}, u32[]{:S(2)}) collective-permute-start(bf16[4,1,48,768]{3,2,1,0:T(8,128)(2,1)} %get-tuple-element.493), channel_id=1, source_target_pairs={{0,1},{1,0},{2,3},{3,2},{4,5},{5,4},{6,7},{7,6},{8,9},{9,8},{10,11... | collective-permute-start | bytes 884744 | tf_op jit(solution)/shard_map/ppermute | solution.py:1362
  523.5 12.9 %collective-permute-start.97 = (bf16[2,2,48,768]{3,2,1,0:T(8,128)(2,1)}, bf16[2,2,48,768]{3,2,1,0:T(8,128)(2,1)S(1)}, u32[]{:S(2)}, u32[]{:S(2)}) collective-permute-start(bf16[2,2,48,768]{3,2,1,0:T(8,128)(2,1)} %get-tuple-element.488), channel_id=1, source_target_pairs={{0,8},{4,12},{8,0},{12,4},{16,24},{20,28},{24,16},{28,20},{1,9},{5... | collective-permute-start | bytes 884744 | tf_op jit(solution)/shard_map/ppermute | solution.py:1358
  524.2 22.7 %collective-permute-start.98 = (bf16[2,2,48,768]{3,2,1,0:T(8,128)(2,1)}, bf16[2,2,48,768]{3,2,1,0:T(8,128)(2,1)S(1)}, u32[]{:S(2)}, u32[]{:S(2)}) collective-permute-start(bf16[2,2,48,768]{3,2,1,0:T(8,128)(2,1)} %get-tuple-element.489), channel_id=1, source_target_pairs={{0,16},{4,20},{8,24},{12,28},{16,0},{20,4},{24,8},{28,12},{1,17},{... | collective-permute-start | bytes 884744 | tf_op jit(solution)/shard_map/ppermute | solution.py:1358
  527.5 19.4 %collective-permute-start.99 = (bf16[2,2,48,768]{3,2,1,0:T(8,128)(2,1)S(1)}, bf16[2,2,48,768]{3,2,1,0:T(8,128)(2,1)S(1)}, u32[]{:S(2)}, u32[]{:S(2)}) collective-permute-start(bf16[2,2,48,768]{3,2,1,0:T(8,128)(2,1)S(1)} %copy-done.89), channel_id=1, source_target_pairs={{0,24},{4,28},{8,16},{12,20},{16,8},{20,12},{24,0},{28,4},{1,25},{... | collective-permute-start | bytes 884744 | tf_op jit(solution)/shard_map/ppermute | solution.py:1358
  556.2 12.4 %collective-permute-start.106 = (bf16[2,1,48,768]{3,2,1,0:T(8,128)(2,1)}, bf16[2,1,48,768]{3,2,1,0:T(8,128)(2,1)S(1)}, u32[]{:S(2)}, u32[]{:S(2)}) collective-permute-start(bf16[2,1,48,768]{3,2,1,0:T(8,128)(2,1)} %get-tuple-element.502), channel_id=1, source_target_pairs={{0,16},{4,20},{8,24},{12,28},{16,0},{20,4},{24,8},{28,12},{1,17},{... | collective-permute-start | bytes 442376 | tf_op jit(solution)/shard_map/ppermute | solution.py:1358
  (137 other events, 1402.4 us)
Sparse Core Ops, SparseCore 0:
  11.4 107.8 all-gather.2
  353.9 170.3 reduce-scatter.1

commit v4 on v3

--- a/solution.py
+++ b/solution.py
@@ -769,7 +769,7 @@
     for g in range(4):
 
         def tile(t, carry):
-            rows = pl.ds(aligned(t * 256, 256), 256)
+            rows = pl.ds(0, TOK)
             u = nn(h[rows, :], wu[g].reshape(D, D))
             square = u * u
             th = jnp.tanh(u * (0.7978845608 + (0.7978845608 * 0.044715) * square))
@@ -784,7 +784,7 @@
             at[cols, rows] = a.T
             return carry
 
-        lax.fori_loop(0, 2, tile, 0)
+        tile(0, 0)
         cols = pl.ds(g * D, D)
         outs.append(pltpu.make_async_copy(slope.at[:, cols], slope_o.at[:, cols], osem.at[g]))
         outs[-1].start()
@@ -796,7 +796,7 @@
     arrived(wd, sem.at[2])
 
     def tile(t, carry):
-        rows = pl.ds(aligned(t * 256, 256), 256)
+        rows = pl.ds(0, TOK)
         for half in range(2):
             cols = pl.ds(half * HALF, HALF)
             total = aa[rows, cols] + nn(act[rows, :], wd[half].reshape(FF, HALF))
@@ -804,7 +804,7 @@
             low[rows, cols] = total.astype(BF16)
         return carry
 
-    lax.fori_loop(0, 2, tile, 0)
+    tile(0, 0)
     for copy in outs:
         copy.wait()
 

time: 587 us -> 597 us (1.017)
  Pallas kernels: 230 us -> 236 us
    pallas_call x17, Pallas kernels: 215 us -> 221 us  [kernel_call(): pl.pallas_call(body, out_shape=tuple(outs), in_specs=in_specs, out_specs=...]
  transfers between devices with their start and end apart: 110 -> 110, of which waited for: 35 -> 35; matrix products, arithmetic and copies ran while one was open for 5% -> 5% of each run, Pallas kernels for 33% -> 32%
where the time goes in v4:
time: 597 us; the launch traced here: 588 us
  Pallas kernels  236 us (40%)
  waiting for transfers between devices  179 us (30%)
  starting transfers between devices  98.6 us (17%)
  local copies, waits for them, and re-layouts  41.1 us (7%)
  between operations  16.3 us (3%)
  other arithmetic  16.2 us (3%)
    pallas_call x17, Pallas kernels, kernel_call(): pl.pallas_call(body, out_shape=tuple(outs), in_specs=in_specs, out_specs=...  221 us
    ppermute x36, waiting for transfers between devices, pairwise(): return lax.ppermute(v, 'zx', [(i, i ^ bits) for i in range(8)])  91.6 us
    ppermute x36, starting transfers between devices, pairwise(): return lax.ppermute(v, 'zx', [(i, i ^ bits) for i in range(8)])  64.1 us
    ppermute x14, waiting for transfers between devices, over_ctx(): return lax.ppermute(v, 'ctx', [(0, 1), (1, 0)])  63.6 us
    ppermute x53, waiting for transfers between devices, over_core(): return lax.ppermute(v, 'core', [(0, 1), (1, 0)])  24.2 us
    unnamed x189, local copies, waits for them, and re-layouts  18.1 us
    ppermute x14, starting transfers between devices, over_ctx(): return lax.ppermute(v, 'ctx', [(0, 1), (1, 0)])  16.6 us
  transfers between devices with their start and end apart: 110, of which 35 were waited for; matrix products, arithmetic and copies ran while one was open for 5% of the time, Pallas kernels for 32%

profile of v4, /device:TPU:0, one launch (start us, length us, event | category | flops | bytes accessed | tf_op | source)
XLA Modules:
  0.0 587.8 jit_solution(7705335761013339032)
XLA Ops:
  11.1 3.1 collective-permute-start.3
  15.7 3.0 collective-permute-start.1
  22.3 14.1 %collective-permute-done.4 = bf16[32,128]{1,0:T(8,128)(2,1)S(1)} collective-permute-done((bf16[32,128]{1,0:T(8,128)(2,1)S(1)}, bf16[32,128]{1,0:T(8,128)(2,1)S(1)}, u32[]{:S(2)}, u32[]{:S(2)}) %collective-permute-start.4) | collective-permute-done | bytes 8224 | tf_op jit(solution)/shard_map/ppermute | solution.py:1358
  36.5 5.2 collective-permute-start.5
  43.5 1.8 collective-permute-start.10
  45.3 2.5 collective-permute-start.8
  51.9 16.8 %collective-permute-done.11 = bf16[4,32,128]{2,1,0:T(8,128)(2,1)S(1)} collective-permute-done((bf16[4,32,128]{2,1,0:T(8,128)(2,1)S(1)}, bf16[4,32,128]{2,1,0:T(8,128)(2,1)S(1)}, u32[]{:S(2)}, u32[]{:S(2)}) %collective-permute-start.11) | collective-permute-done | bytes 32800 | tf_op jit(solution)/shard_map/ppermute | solution.py:1358
  73.3 6.1 %collective-permute-done.12.refs_3_ = bf16[4,1,48,768]{3,2,1,0:T(8,128)(2,1)S(1)} collective-permute-done((bf16[4,1,48,768]{3,2,1,0:T(8,128)(2,1)S(1)}, bf16[4,1,48,768]{3,2,1,0:T(8,128)(2,1)S(1)}, u32[]{:S(2)}, u32[]{:S(2)}) %collective-permute-start.12) | collective-permute-done | bytes 294944 | tf_op jit(solution)/shard_map/ppermute | solution.py:1362
  81.4 2.1 collective-permute-done.13.refs_11_
  91.7 4.9 collective-permute-start.24
  96.6 8.5 %qkv.2 = (bf16[512,1280]{1,0:T(8,128)(2,1)}, bf16[512,1280]{1,0:T(8,128)(2,1)}, bf16[8,48,512]{2,1,0:T(8,128)(2,1)}, bf16[8,48,512]{2,1,0:T(8,128)(2,1)}) custom-call(s32[3]{0:T(128)} %pad_add_fusion.idx, f32[512,768]{1,0:T(8,128)} %convert_element_type.52.res.res_in, f32[8,768]{1,0:T(8,128)} %pad_convert_fusion.1.gb, bf16[128,768]{1,0:T(8,128)(2,1)} %pad.35.sw0, ...), custom_call_target="tpu_custom_call" | custom-call | flops 2800000000 | bytes 1048576 | tf_op jit(solution)/shard_map/qkv/pallas_call | solution.py:407
  105.2 9.1 %collective-permute-done.24 = bf16[2,1,48,768]{3,2,1,0:T(8,128)(2,1)S(1)} collective-permute-done((bf16[2,1,48,768]{3,2,1,0:T(8,128)(2,1)S(1)}, bf16[2,1,48,768]{3,2,1,0:T(8,128)(2,1)S(1)}, u32[]{:S(2)}, u32[]{:S(2)}) %collective-permute-start.24) | collective-permute-done | bytes 147488 | tf_op jit(solution)/shard_map/ppermute | solution.py:1358
  115.3 2.7 collective-permute-start.30
  118.0 1.8 collective-permute-start.32
  122.0 3.5 collective-permute-done.30.refs_10_
  125.4 4.9 collective-permute-start.33
  130.4 1.9 collective-permute-start.34
  132.3 2.5 collective-permute-start.35
  134.8 12.1 %attend.2 = (bf16[512,384]{1,0:T(8,128)(2,1)}, bf16[512,384]{1,0:T(8,128)(2,1)}, f32[8,1024]{1,0:T(8,128)}) custom-call(s32[3]{0:T(128)} %pad_add_fusion.idx, s32[6,8]{1,0:T(8,128)} %dynamic-slice_select_fusion.kept, s32[2]{0:T(128)} %broadcast_select_fusion.1.pics, bf16[512,1280]{1,0:T(8,128)(2,1)} %get-tuple-element.297.own, bf16[512,1280]{1,0:T(8,128)(2,1)} %copy-done.73), custom_call_target="tpu_custom_call" | custom-call | flops 4800000000 | bytes 1048576 | tf_op jit(solution)/shard_map/attend/pallas_call | solution.py:407
  147.6 5.8 collective-permute-done.34
  156.7 3.4 collective-permute-done.36.refs_3_
  160.2 4.1 collective-permute-done.37.refs_11_
  171.6 2.5 collective-permute-done.44
  174.9 7.7 %collective-permute-done.49.refs_26_.refs_10_ = bf16[4,2,48,768]{3,2,1,0:T(8,128)(2,1)S(1)} collective-permute-done((bf16[4,2,48,768]{3,2,1,0:T(8,128)(2,1)S(1)}, bf16[4,2,48,768]{3,2,1,0:T(8,128)(2,1)S(1)}, u32[]{:S(2)}, u32[]{:S(2)}) %collective-permute-start.49) | collective-permute-done | bytes 589856 | tf_op jit(solution)/shard_map/ppermute | solution.py:1362
  182.6 15.5 %ffn.2 = (f32[512,768]{1,0:T(8,128)}, f32[512,768]{1,0:T(8,128)}, bf16[512,768]{1,0:T(8,128)(2,1)}, bf16[8,48,512]{2,1,0:T(8,128)(2,1)}, bf16[8,48,512]{2,1,0:T(...) custom-call(s32[3]{0:T(128)} %pad_add_fusion.idx, ...), custom_call_target="tpu_custom_call" | custom-call | flops 8000000000 | bytes 1048576 | tf_op jit(solution)/shard_map/ffn/pallas_call | solution.py:407
  200.1 18.5 %qkv.3 = (bf16[512,1280]{1,0:T(8,128)(2,1)}, bf16[512,1280]{1,0:T(8,128)(2,1)}, bf16[8,48,512]{2,1,0:T(8,128)(2,1)}, bf16[8,48,512]{2,1,0:T(8,128)(2,1)}) custom-call(s32[3]{0:T(128)} %pad_add_fusion.idx, f32[512,768]{1,0:T(8,128)} %get-tuple-element.336.res.res_in, f32[8,768]{1,0:T(8,128)} %pad_convert_fusion.gb, bf16[128,768]{1,0:T(8,128)(2,1)} %pad.39.sw0, ...), custom_call_target="tpu_custom_call" | custom-call | flops 2800000000 | bytes 1048576 | tf_op jit(solution)/shard_map/qkv/pallas_call | solution.py:407
  223.7 11.2 %collective-permute-done.52.refs_19_.refs_3_ = bf16[4,2,48,768]{3,2,1,0:T(8,128)(2,1)S(1)} collective-permute-done((bf16[4,2,48,768]{3,2,1,0:T(8,128)(2,1)S(1)}, bf16[4,2,48,768]{3,2,1,0:T(8,128)(2,1)S(1)}, u32[]{:S(2)}, u32[]{:S(2)}) %collective-permute-start.52) | collective-permute-done | bytes 589856 | tf_op jit(solution)/shard_map/ppermute | solution.py:1362
  238.6 11.9 %attend.3 = (bf16[512,384]{1,0:T(8,128)(2,1)}, bf16[512,384]{1,0:T(8,128)(2,1)}, f32[8,1024]{1,0:T(8,128)}) custom-call(s32[3]{0:T(128)} %pad_add_fusion.idx, s32[6,8]{1,0:T(8,128)} %dynamic-slice_select_fusion.kept, s32[2]{0:T(128)} %broadcast_select_fusion.1.pics, bf16[512,1280]{1,0:T(8,128)(2,1)} %get-tuple-element.355.own, ...), custom_call_target="tpu_custom_call" | custom-call | flops 4800000000 | bytes 1048576 | tf_op jit(solution)/shard_map/attend/pallas_call | solution.py:407
  250.7 1.8 collective-permute-start.65
  253.2 15.3 %ffn.3 = (f32[512,768]{1,0:T(8,128)}, f32[512,768]{1,0:T(8,128)}, bf16[512,768]{1,0:T(8,128)(2,1)}, bf16[8,48,512]{2,1,0:T(8,128)(2,1)}, bf16[8,48,512]{2,1,0:T(...) custom-call(s32[3]{0:T(128)} %pad_add_fusion.idx, ...), custom_call_target="tpu_custom_call" | custom-call | flops 8000000000 | bytes 1048576 | tf_op jit(solution)/shard_map/ffn/pallas_call | solution.py:407
  269.4 11.6 %down_back.2.gu.refs_6_ = bf16[512,3072]{1,0:T(8,128)(2,1)} custom-call(s32[3]{0:T(128)} %pad_add_fusion.idx, bf16[512,768]{1,0:T(8,128)(2,1)} %copy-done.2, bf16[512,3072]{1,0:T(8,128)(2,1)} %get-tuple-element.386.slope_in, bf16[4,2,48,768]{3,2,1,0:T(8,128)(2,1)} %copy-done.1, bf16[4,2,48,768]{3,2,1,0:T(8,128)(2,1)} %copy-done.6, ...), custom_call_target="tpu_custom_call" | custom-call | flops 2400000000 | bytes 1048576 | tf_op jit(solution)/shard_map/down_back/pallas_call | solution.py:407
  281.8 2.4 convert_element_type.55.grad_in
  284.2 10.8 %up_back.2 = (f32[512,768]{1,0:T(8,128)}, bf16[512,768]{1,0:T(8,128)(2,1)}, bf16[512,384]{1,0:T(8,128)(2,1)}, bf16[512,384]{1,0:T(8,128)(2,1)}, f32[8,768]{1,0:T(8,128)}) custom-call(s32[3]{0:T(128)} %pad_add_fusion.idx, f32[512,768]{1,0:T(8,128)} %convert_element_type.55.grad_in, bf16[512,3072]{1,0:T(8,128)(2,1)} %down_back.2.gu.refs_6_, ...), custom_call_target="tpu_custom_call" | custom-call | flops 4000000000 | bytes 1048576 | tf_op jit(solution)/shard_map/up_back/pallas_call | solution.py:407
  295.2 2.0 collective-permute-done.66.gother
  297.2 17.2 %attend_back.2 = (bf16[512,1280]{1,0:T(8,128)(2,1)}, bf16[512,1280]{1,0:T(8,128)(2,1)}) custom-call(s32[3]{0:T(128)} %pad_add_fusion.idx, s32[6,8]{1,0:T(8,128)} %dynamic-slice_select_fusion.kept, s32[2]{0:T(128)} %broadcast_select_fusion.1.pics, f32[8,1024]{1,0:T(8,128)} %get-tuple-element.396.lse, bf16[512,1280]{1,0:T(8,128)(2,1)} %get-tuple-element.355.own, ...), custom_call_target="tpu_custom_call" | custom-call | flops 6400000000 | bytes 1048576 | tf_op jit(solution)/shard_map/attend_back/pallas_call | solution.py:407
  315.5 3.5 collective-permute-done.72
  319.5 2.7 collective-permute-done.73
  322.8 10.0 %qkv_back.2 = (f32[512,768]{1,0:T(8,128)}, bf16[512,768]{1,0:T(8,128)(2,1)}, f32[8,768]{1,0:T(8,128)}) custom-call(s32[3]{0:T(128)} %pad_add_fusion.idx, f32[512,768]{1,0:T(8,128)} %get-tuple-element.402.ga_in, bf16[512,1280]{1,0:T(8,128)(2,1)} %get-tuple-element.403.down_.refs_14_, bf16[512,1280]{1,0:T(8,128)(2,1)} %collective-permute-done.67.dr.refs_15_, ...), custom_call_target="tpu_custom_call" | custom-call | flops 3600000000 | bytes 1048576 | tf_op jit(solution)/shard_map/qkv_back/pallas_call | solution.py:407
  332.8 1.7 copy-done.68
  334.5 18.6 %layer_grad.1 = (bf16[16,2,3,48,768]{4,3,2,1,0:T(8,128)(2,1)}, f32[2,4,48,128]{3,2,1,0:T(8,128)}) custom-call(s32[3]{0:T(128)} %pad_add_fusion.idx, bf16[1536,512]{1,0:T(8,128)(2,1)} %bitcast.206, bf16[1536,512]{1,0:T(8,128)(2,1)} %bitcast.40.refs_1_, bf16[512,768]{1,0:T(8,128)(2,1)} %copy-done.2, bf16[512,768]{1,0:T(8,128)(2,1)} %collective-permute-done.69.refs_3_, ...), custom_call_target="tpu_custom_call" | custom-call | flops 8000000000 | bytes 1048576 | tf_op jit(solution)/shard_map/layer_grad/pallas_call | solution.py:407
  353.1 6.7 %copy.98 = bf16[16,2,3,48,768]{4,3,1,2,0:T(8,128)(2,1)} copy(bf16[16,2,3,48,768]{4,3,2,1,0:T(8,128)(2,1)} %get-tuple-element.507) | data formatting | bytes 14155776 | tf_op jit(solution)/shard_map/optimization_barrier | solution.py:1401
  359.9 11.4 %down_back.3.refs_6_.gu = bf16[512,3072]{1,0:T(8,128)(2,1)} custom-call(s32[3]{0:T(128)} %pad_add_fusion.idx, bf16[512,768]{1,0:T(8,128)(2,1)} %get-tuple-element.421.grad.refs_2_, bf16[512,3072]{1,0:T(8,128)(2,1)} %get-tuple-element.422.slope_in, bf16[4,2,2,2,2,48,768]{6,5,4,3,2,1,0:T(8,128)(2,1)} %bitcast.175, ...), custom_call_target="tpu_custom_call" | custom-call | flops 2400000000 | bytes 1048576 | tf_op jit(solution)/shard_map/down_back/pallas_call | solution.py:407
  372.4 7.9 %collective-permute-done.76.refs_7_ = bf16[512,3072]{1,0:T(8,128)(2,1)S(1)} collective-permute-done((bf16[512,3072]{1,0:T(8,128)(2,1)}, bf16[512,3072]{1,0:T(8,128)(2,1)S(1)}, u32[]{:S(2)}, u32[]{:S(2)}) %collective-permute-start.76) | collective-permute-done | bytes 3145760 | tf_op jit(solution)/shard_map/ppermute | solution.py:1366
  383.4 11.8 %ffn_grad.1 = (bf16[2,4,2,48,768]{4,3,2,1,0:T(8,128)(2,1)}, bf16[2,4,2,48,768]{4,3,2,1,0:T(8,128)(2,1)}, bf16[2,4,2,48,768]{4,3,2,1,0:T(8,128)(2,1)}, bf16[2,4,2,48,768]{4,3,2,1,0:T(8,128)(2,1)}) custom-call(s32[3]{0:T(128)} %pad_add_fusion.idx, bf16[1536,512]{1,0:T(8,128)(2,1)} %bitcast.205, bf16[1536,512]{1,0:T(8,128)(2,1)} %bitcast.198, ...), custom_call_target="tpu_custom_call" | custom-call | flops 4400000000 | bytes 1048576 | tf_op jit(solution)/shard_map/ffn_grad/pallas_call | solution.py:407
  395.3 10.5 %up_back.3 = (f32[512,768]{1,0:T(8,128)}, bf16[512,768]{1,0:T(8,128)(2,1)}, bf16[512,384]{1,0:T(8,128)(2,1)}, bf16[512,384]{1,0:T(8,128)(2,1)}, f32[8,768]{1,0:T(8,128)}) custom-call(s32[3]{0:T(128)} %pad_add_fusion.idx, f32[512,768]{1,0:T(8,128)} %get-tuple-element.436.grad_in, bf16[512,3072]{1,0:T(8,128)(2,1)} %down_back.3.refs_6_.gu, ...), custom_call_target="tpu_custom_call" | custom-call | flops 4000000000 | bytes 1048576 | tf_op jit(solution)/shard_map/up_back/pallas_call | solution.py:407
  405.9 1.7 collective-permute-start.81
  409.5 17.4 %attend_back.3 = (bf16[512,1280]{1,0:T(8,128)(2,1)}, bf16[512,1280]{1,0:T(8,128)(2,1)}) custom-call(s32[3]{0:T(128)} %pad_add_fusion.idx, s32[6,8]{1,0:T(8,128)} %dynamic-slice_select_fusion.kept, s32[2]{0:T(128)} %broadcast_select_fusion.1.pics, f32[8,1024]{1,0:T(8,128)} %get-tuple-element.444.lse, bf16[512,1280]{1,0:T(8,128)(2,1)} %get-tuple-element.297.own, ...), custom_call_target="tpu_custom_call" | custom-call | flops 6400000000 | bytes 1048576 | tf_op jit(solution)/shard_map/attend_back/pallas_call | solution.py:407
  429.4 14.7 %collective-permute-done.81.ra = bf16[2,4,2,48,768]{4,3,2,1,0:T(8,128)(2,1)} collective-permute-done((bf16[2,4,2,48,768]{4,3,2,1,0:T(8,128)(2,1)}, bf16[2,4,2,48,768]{4,3,2,1,0:T(8,128)(2,1)}, u32[]{:S(2)}, u32[]{:S(2)}) %collective-permute-start.81) | collective-permute-done | bytes 1179680 | tf_op jit(solution)/shard_map/ppermute | solution.py:1358
  446.3 3.7 cross.2
  453.6 10.1 %qkv_grad.1 = (bf16[2,4,1,48,768]{4,3,2,1,0:T(8,128)(2,1)}, bf16[2,4,1,48,768]{4,3,2,1,0:T(8,128)(2,1)}, bf16[2,4,1,48,768]{4,3,2,1,0:T(8,128)(2,1)}, bf16[2,4,1...) custom-call(s32[3]{0:T(128)} %pad_add_fusion.idx, bf16[384,512]{1,0:T(8,128)(2,1)} %bitcast.207, ...), custom_call_target="tpu_custom_call" | custom-call | flops 3200000000 | bytes 1048576 | tf_op jit(solution)/shard_map/qkv_grad/pallas_call | solution.py:407
  463.7 10.0 %qkv_back.3 = (f32[512,768]{1,0:T(8,128)}, bf16[512,768]{1,0:T(8,128)(2,1)}, f32[8,768]{1,0:T(8,128)}) custom-call(s32[3]{0:T(128)} %pad_add_fusion.idx, f32[512,768]{1,0:T(8,128)} %get-tuple-element.466.ga_in, bf16[512,1280]{1,0:T(8,128)(2,1)} %get-tuple-element.458.refs_6_.down_, bf16[512,1280]{1,0:T(8,128)(2,1)} %copy-done.74, ...), custom_call_target="tpu_custom_call" | custom-call | flops 3600000000 | bytes 1048576 | tf_op jit(solution)/shard_map/qkv_back/pallas_call | solution.py:407
  482.1 28.2 %collective-permute-done.94 = f32[4,48,128]{1,2,0:T(8,128)S(1)} collective-permute-done((f32[4,48,128]{1,2,0:T(8,128)S(1)}, f32[4,48,128]{1,2,0:T(8,128)S(1)}, u32[]{:S(2)}, u32[]{:S(2)}) %collective-permute-start.94) | collective-permute-done | bytes 98336 | tf_op jit(solution)/shard_map/ppermute | solution.py:1362
  511.0 1.8 collective-permute-start.88
  514.5 2.4 collective-permute-start.103
  517.4 4.5 own.2
  521.8 3.4 cross.3
  525.3 3.5 collective-permute-start.100
  531.0 3.3 collective-permute-start.98
  537.3 2.4 collective-permute-done.100.ca
  539.8 3.8 collective-permute-done.97
  543.6 9.9 %collective-permute-done.98 = bf16[2,2,48,768]{3,2,1,0:T(8,128)(2,1)S(1)} collective-permute-done((bf16[2,2,48,768]{3,2,1,0:T(8,128)(2,1)}, bf16[2,2,48,768]{3,2,1,0:T(8,128)(2,1)S(1)}, u32[]{:S(2)}, u32[]{:S(2)}) %collective-permute-start.98) | collective-permute-done | bytes 294944 | tf_op jit(solution)/shard_map/ppermute | solution.py:1358
  553.9 3.4 own.3
  557.3 5.8 collective-permute-start.105
  567.8 8.0 %collective-permute-done.106 = bf16[2,1,48,768]{3,2,1,0:T(8,128)(2,1)S(1)} collective-permute-done((bf16[2,1,48,768]{3,2,1,0:T(8,128)(2,1)}, bf16[2,1,48,768]{3,2,1,0:T(8,128)(2,1)S(1)}, u32[]{:S(2)}, u32[]{:S(2)}) %collective-permute-start.106) | collective-permute-done | bytes 147488 | tf_op jit(solution)/shard_map/ppermute | solution.py:1358
  (492 shorter events, 100.2 us)
Async XLA Ops:
  7.2 158.7 %all-gather.3.cloned.1.call-start = ((), (), s32[]{:S(2)}) async-start(), calls=%async_computation.2 | async-start | bytes 5013504 | tf_op jit(solution)/shard_map/all_gather | solution.py:1485
  11.0 564.9 %reduce-scatter.2.cloned.1.call-start = ((), (), s32[]{:S(2)}) async-start(), calls=%async_computation.1 | async-start | bytes 7520256 | tf_op jit(solution)/shard_map/reduce_scatter | solution.py:1572
  14.2 29.1 %collective-permute-start.6 = (bf16[512,768]{1,0:T(8,128)(2,1)S(1)}, bf16[512,768]{1,0:T(8,128)(2,1)S(1)}, u32[]{:S(2)}, u32[]{:S(2)}) collective-permute-start(bf16[512,768]{1,0:T(8,128)(2,1)S(1)} %bitcast.199), channel_id=1, source_target_pairs={{0,0},{1,2},{2,1},{3,3},{4,4},{5,6},{6,5},{7,7},{8,8},{9,10},{10,9... | collective-permute-start | bytes 2359304 | tf_op jit(solution)/shard_map/ppermute | solution.py:1378
  15.6 27.6 %collective-permute-start = (bf16[2,1,48,768]{3,2,1,0:T(8,128)(2,1)S(1)}, bf16[2,1,48,768]{3,2,1,0:T(8,128)(2,1)S(1)}, u32[]{:S(2)}, u32[]{:S(2)}) collective-permute-start(bf16[2,1,48,768]{3,2,1,0:T(8,128)(2,1)S(1)} %maximum_bitcast_fusion.4), channel_id=1, source_target_pairs={{0,8},{4,12},{8,0},{12,4},{16,24},{20,28},{24,16},{28,20},{1,9},{5... | collective-permute-start | bytes 442376 | tf_op jit(solution)/shard_map/ppermute | solution.py:1358
  15.7 27.6 %collective-permute-start.1 = (bf16[2,1,48,768]{3,2,1,0:T(8,128)(2,1)S(1)}, bf16[2,1,48,768]{3,2,1,0:T(8,128)(2,1)S(1)}, u32[]{:S(2)}, u32[]{:S(2)}) collective-permute-start(bf16[2,1,48,768]{3,2,1,0:T(8,128)(2,1)S(1)} %maximum_bitcast_fusion.4), channel_id=1, source_target_pairs={{0,16},{4,20},{8,24},{12,28},{16,0},{20,4},{24,8},{28,12},{1,17},{... | collective-permute-start | bytes 442376 | tf_op jit(solution)/shard_map/ppermute | solution.py:1358
  18.7 24.6 %collective-permute-start.2 = (bf16[2,1,48,768]{3,2,1,0:T(8,128)(2,1)S(1)}, bf16[2,1,48,768]{3,2,1,0:T(8,128)(2,1)S(1)}, u32[]{:S(2)}, u32[]{:S(2)}) collective-permute-start(bf16[2,1,48,768]{3,2,1,0:T(8,128)(2,1)S(1)} %maximum_bitcast_fusion.4), channel_id=1, source_target_pairs={{0,24},{4,28},{8,16},{12,20},{16,8},{20,12},{24,0},{28,4},{1,25},{... | collective-permute-start | bytes 442376 | tf_op jit(solution)/shard_map/ppermute | solution.py:1358
  20.0 16.4 %collective-permute-start.4 = (bf16[32,128]{1,0:T(8,128)(2,1)S(1)}, bf16[32,128]{1,0:T(8,128)(2,1)S(1)}, u32[]{:S(2)}, u32[]{:S(2)}) collective-permute-start(bf16[32,128]{1,0:T(8,128)(2,1)S(1)} %get-tuple-element.643), channel_id=1, source_target_pairs={{0,16},{4,20},{8,24},{12,28},{16,0},{20,4},{24,8},{28,12},{1,17},{... | collective-permute-start | bytes 24584 | tf_op jit(solution)/shard_map/ppermute | solution.py:1358
  43.5 25.6 %collective-permute-start.10 = (bf16[4,1,48,768]{3,2,1,0:T(8,128)(2,1)S(1)}, bf16[4,1,48,768]{3,2,1,0:T(8,128)(2,1)S(1)}, u32[]{:S(2)}, u32[]{:S(2)}) collective-permute-start(bf16[4,1,48,768]{3,2,1,0:T(8,128)(2,1)S(1)} %pad_maximum_fusion.6.refs_8_), channel_id=1, source_target_pairs={{0,4},{4,0},{8,12},{12,8},{16,20},{20,16},{24,28},{28,24},{1,5},{5... | collective-permute-start | bytes 884744 | tf_op jit(solution)/shard_map/ppermute | solution.py:1358
  45.3 23.9 %collective-permute-start.8 = (bf16[4,1,48,768]{3,2,1,0:T(8,128)(2,1)S(1)}, bf16[4,1,48,768]{3,2,1,0:T(8,128)(2,1)S(1)}, u32[]{:S(2)}, u32[]{:S(2)}) collective-permute-start(bf16[4,1,48,768]{3,2,1,0:T(8,128)(2,1)S(1)} %pad_maximum_fusion.6.refs_8_), channel_id=1, source_target_pairs={{0,1},{1,0},{2,3},{3,2},{4,5},{5,4},{6,7},{7,6},{8,9},{9,8},{10,11... | collective-permute-start | bytes 884744 | tf_op jit(solution)/shard_map/ppermute | solution.py:1362
  47.9 21.4 %collective-permute-start.7 = (bf16[4,1,48,768]{3,2,1,0:T(8,128)(2,1)S(1)}, bf16[4,1,48,768]{3,2,1,0:T(8,128)(2,1)S(1)}, u32[]{:S(2)}, u32[]{:S(2)}) collective-permute-start(bf16[4,1,48,768]{3,2,1,0:T(8,128)(2,1)S(1)} %pad_maximum_fusion.5.refs_0_), channel_id=1, source_target_pairs={{0,4},{4,0},{8,12},{12,8},{16,20},{20,16},{24,28},{28,24},{1,5},{5... | collective-permute-start | bytes 884744 | tf_op jit(solution)/shard_map/ppermute | solution.py:1358
  48.5 20.7 %collective-permute-start.9 = (bf16[4,1,48,768]{3,2,1,0:T(8,128)(2,1)S(1)}, bf16[4,1,48,768]{3,2,1,0:T(8,128)(2,1)S(1)}, u32[]{:S(2)}, u32[]{:S(2)}) collective-permute-start(bf16[4,1,48,768]{3,2,1,0:T(8,128)(2,1)S(1)} %pad_maximum_fusion.5.refs_0_), channel_id=1, source_target_pairs={{0,1},{1,0},{2,3},{3,2},{4,5},{5,4},{6,7},{7,6},{8,9},{9,8},{10,11... | collective-permute-start | bytes 884744 | tf_op jit(solution)/shard_map/ppermute | solution.py:1362
  48.5 20.2 %collective-permute-start.11 = (bf16[4,32,128]{2,1,0:T(8,128)(2,1)S(1)}, bf16[4,32,128]{2,1,0:T(8,128)(2,1)S(1)}, u32[]{:S(2)}, u32[]{:S(2)}) collective-permute-start(bf16[4,32,128]{2,1,0:T(8,128)(2,1)S(1)} %pad_maximum_fusion.14), channel_id=1, source_target_pairs={{0,4},{4,0},{8,12},{12,8},{16,20},{20,16},{24,28},{28,24},{1,5},{5... | collective-permute-start | bytes 98312 | tf_op jit(solution)/shard_map/ppermute | solution.py:1358
  71.2 12.3 %collective-permute-start.15 = (bf16[4,1,48,768]{3,2,1,0:T(8,128)(2,1)S(1)}, bf16[4,1,48,768]{3,2,1,0:T(8,128)(2,1)S(1)}, u32[]{:S(2)}, u32[]{:S(2)}) collective-permute-start(bf16[4,1,48,768]{3,2,1,0:T(8,128)(2,1)S(1)} %collective-permute-done.7.refs_1_), channel_id=1, source_target_pairs={{0,2},{2,0},{1,3},{3,1},{4,6},{6,4},{5,7},{7,5},{8,10},{10,8},{9,1... | collective-permute-start | bytes 884744 | tf_op jit(solution)/shard_map/ppermute | solution.py:1366
  83.5 37.5 %collective-permute-start.26 = (s32[12,8]{1,0:T(8,128)S(1)}, s32[12,8]{1,0:T(8,128)S(1)}, u32[]{:S(2)}, u32[]{:S(2)}) collective-permute-start(s32[12,8]{1,0:T(8,128)S(1)} %copy.85), channel_id=1, source_target_pairs={{0,2},{2,0},{1,3},{3,1},{4,6},{6,4},{5,7},{7,5},{8,10},{10,8},{9,1... | collective-permute-start | bytes 1160 | tf_op jit(solution)/shard_map/ppermute | solution.py:1366
  83.5 36.3 %collective-permute-start.27 = (s32[2]{0:T(128)}, s32[2]{0:T(128)S(1)}, u32[]{:S(2)}, u32[]{:S(2)}) collective-permute-start(s32[2]{0:T(128)} %bitcast.24), channel_id=1, source_target_pairs={{0,2},{2,0},{1,3},{3,1},{4,6},{6,4},{5,7},{7,5},{8,10},{10,8},{9,1... | collective-permute-start | bytes 32 | tf_op jit(solution)/shard_map/ppermute | solution.py:1366
  91.7 13.4 %collective-permute-start.23 = (bf16[2,1,48,768]{3,2,1,0:T(8,128)(2,1)S(1)}, bf16[2,1,48,768]{3,2,1,0:T(8,128)(2,1)S(1)}, u32[]{:S(2)}, u32[]{:S(2)}) collective-permute-start(bf16[2,1,48,768]{3,2,1,0:T(8,128)(2,1)S(1)} %maximum_bitcast_fusion.5), channel_id=1, source_target_pairs={{0,8},{4,12},{8,0},{12,4},{16,24},{20,28},{24,16},{28,20},{1,9},{5... | collective-permute-start | bytes 442376 | tf_op jit(solution)/shard_map/ppermute | solution.py:1358
  91.7 22.6 %collective-permute-start.24 = (bf16[2,1,48,768]{3,2,1,0:T(8,128)(2,1)S(1)}, bf16[2,1,48,768]{3,2,1,0:T(8,128)(2,1)S(1)}, u32[]{:S(2)}, u32[]{:S(2)}) collective-permute-start(bf16[2,1,48,768]{3,2,1,0:T(8,128)(2,1)S(1)} %maximum_bitcast_fusion.5), channel_id=1, source_target_pairs={{0,16},{4,20},{8,24},{12,28},{16,0},{20,4},{24,8},{28,12},{1,17},{... | collective-permute-start | bytes 442376 | tf_op jit(solution)/shard_map/ppermute | solution.py:1358
  96.6 18.5 %collective-permute-start.25 = (bf16[2,1,48,768]{3,2,1,0:T(8,128)(2,1)S(1)}, bf16[2,1,48,768]{3,2,1,0:T(8,128)(2,1)S(1)}, u32[]{:S(2)}, u32[]{:S(2)}) collective-permute-start(bf16[2,1,48,768]{3,2,1,0:T(8,128)(2,1)S(1)} %maximum_bitcast_fusion.5), channel_id=1, source_target_pairs={{0,24},{4,28},{8,16},{12,20},{16,8},{20,12},{24,0},{28,4},{1,25},{... | collective-permute-start | bytes 442376 | tf_op jit(solution)/shard_map/ppermute | solution.py:1358
  105.2 27.1 %collective-permute-start.28 = (bf16[512,1280]{1,0:T(8,128)(2,1)}, bf16[512,1280]{1,0:T(8,128)(2,1)S(1)}, u32[]{:S(2)}, u32[]{:S(2)}) collective-permute-start(bf16[512,1280]{1,0:T(8,128)(2,1)} %get-tuple-element.298), channel_id=1, source_target_pairs={{0,2},{2,0},{1,3},{3,1},{4,6},{6,4},{5,7},{7,5},{8,10},{10,8},{9,1... | collective-permute-start | bytes 3932168 | tf_op jit(solution)/shard_map/ppermute | solution.py:1366
  118.0 12.4 %collective-permute-start.32 = (bf16[4,1,48,768]{3,2,1,0:T(8,128)(2,1)S(1)}, bf16[4,1,48,768]{3,2,1,0:T(8,128)(2,1)S(1)}, u32[]{:S(2)}, u32[]{:S(2)}) collective-permute-start(bf16[4,1,48,768]{3,2,1,0:T(8,128)(2,1)S(1)} %pad_maximum_fusion.8.refs_8_), channel_id=1, source_target_pairs={{0,4},{4,0},{8,12},{12,8},{16,20},{20,16},{24,28},{28,24},{1,5},{5... | collective-permute-start | bytes 884744 | tf_op jit(solution)/shard_map/ppermute | solution.py:1358
  121.6 25.3 %collective-permute-start.29 = (bf16[4,1,48,768]{3,2,1,0:T(8,128)(2,1)S(1)}, bf16[4,1,48,768]{3,2,1,0:T(8,128)(2,1)S(1)}, u32[]{:S(2)}, u32[]{:S(2)}) collective-permute-start(bf16[4,1,48,768]{3,2,1,0:T(8,128)(2,1)S(1)} %pad_maximum_fusion.7.refs_0_), channel_id=1, source_target_pairs={{0,4},{4,0},{8,12},{12,8},{16,20},{20,16},{24,28},{28,24},{1,5},{5... | collective-permute-start | bytes 884744 | tf_op jit(solution)/shard_map/ppermute | solution.py:1358
  121.9 25.1 %collective-permute-start.31 = (bf16[4,1,48,768]{3,2,1,0:T(8,128)(2,1)S(1)}, bf16[4,1,48,768]{3,2,1,0:T(8,128)(2,1)S(1)}, u32[]{:S(2)}, u32[]{:S(2)}) collective-permute-start(bf16[4,1,48,768]{3,2,1,0:T(8,128)(2,1)S(1)} %pad_maximum_fusion.7.refs_0_), channel_id=1, source_target_pairs={{0,1},{1,0},{2,3},{3,2},{4,5},{5,4},{6,7},{7,6},{8,9},{9,8},{10,11... | collective-permute-start | bytes 884744 | tf_op jit(solution)/shard_map/ppermute | solution.py:1362
  125.4 22.1 %collective-permute-start.33 = (bf16[2,2,48,768]{3,2,1,0:T(8,128)(2,1)S(1)}, bf16[2,2,48,768]{3,2,1,0:T(8,128)(2,1)S(1)}, u32[]{:S(2)}, u32[]{:S(2)}) collective-permute-start(bf16[2,2,48,768]{3,2,1,0:T(8,128)(2,1)S(1)} %pad_maximum_fusion.9), channel_id=1, source_target_pairs={{0,8},{4,12},{8,0},{12,4},{16,24},{20,28},{24,16},{28,20},{1,9},{5... | collective-permute-start | bytes 884744 | tf_op jit(solution)/shard_map/ppermute | solution.py:1358
  130.4 23.0 %collective-permute-start.34 = (bf16[2,2,48,768]{3,2,1,0:T(8,128)(2,1)S(1)}, bf16[2,2,48,768]{3,2,1,0:T(8,128)(2,1)S(1)}, u32[]{:S(2)}, u32[]{:S(2)}) collective-permute-start(bf16[2,2,48,768]{3,2,1,0:T(8,128)(2,1)S(1)} %pad_maximum_fusion.9), channel_id=1, source_target_pairs={{0,16},{4,20},{8,24},{12,28},{16,0},{20,4},{24,8},{28,12},{1,17},{... | collective-permute-start | bytes 884744 | tf_op jit(solution)/shard_map/ppermute | solution.py:1358
  132.3 21.1 %collective-permute-start.35 = (bf16[2,2,48,768]{3,2,1,0:T(8,128)(2,1)S(1)}, bf16[2,2,48,768]{3,2,1,0:T(8,128)(2,1)S(1)}, u32[]{:S(2)}, u32[]{:S(2)}) collective-permute-start(bf16[2,2,48,768]{3,2,1,0:T(8,128)(2,1)S(1)} %pad_maximum_fusion.9), channel_id=1, source_target_pairs={{0,24},{4,28},{8,16},{12,20},{16,8},{20,12},{24,0},{28,4},{1,25},{... | collective-permute-start | bytes 884744 | tf_op jit(solution)/shard_map/ppermute | solution.py:1358
  166.4 16.2 %collective-permute-start.49 = (bf16[4,2,48,768]{3,2,1,0:T(8,128)(2,1)S(1)}, bf16[4,2,48,768]{3,2,1,0:T(8,128)(2,1)S(1)}, u32[]{:S(2)}, u32[]{:S(2)}) collective-permute-start(bf16[4,2,48,768]{3,2,1,0:T(8,128)(2,1)S(1)} %pad_maximum_fusion.1.refs_24_.refs_8_), channel_id=1, source_target_pairs={{0,1},{1,0},{2,3},{3,2},{4,5},{5,4},{6,7},{7,6},{8,9},{9,8},{10,11... | collective-permute-start | bytes 1769480 | tf_op jit(solution)/shard_map/ppermute | solution.py:1362
  169.5 28.7 %collective-permute-start.51 = (bf16[4,2,48,768]{3,2,1,0:T(8,128)(2,1)S(1)}, bf16[4,2,48,768]{3,2,1,0:T(8,128)(2,1)S(1)}, u32[]{:S(2)}, u32[]{:S(2)}) collective-permute-start(bf16[4,2,48,768]{3,2,1,0:T(8,128)(2,1)S(1)} %pad_maximum_fusion.1.refs_24_.refs_8_), channel_id=1, source_target_pairs={{0,4},{4,0},{8,12},{12,8},{16,20},{20,16},{24,28},{28,24},{1,5},{5... | collective-permute-start | bytes 1769480 | tf_op jit(solution)/shard_map/ppermute | solution.py:1358
  170.8 27.3 %collective-permute-start.48 = (bf16[4,2,48,768]{3,2,1,0:T(8,128)(2,1)S(1)}, bf16[4,2,48,768]{3,2,1,0:T(8,128)(2,1)S(1)}, u32[]{:S(2)}, u32[]{:S(2)}) collective-permute-start(bf16[4,2,48,768]{3,2,1,0:T(8,128)(2,1)S(1)} %pad_maximum_fusion.refs_16_.refs_0_), channel_id=1, source_target_pairs={{0,4},{4,0},{8,12},{12,8},{16,20},{20,16},{24,28},{28,24},{1,5},{5... | collective-permute-start | bytes 1769480 | tf_op jit(solution)/shard_map/ppermute | solution.py:1358
  174.2 24.0 %collective-permute-start.50 = (bf16[4,2,48,768]{3,2,1,0:T(8,128)(2,1)S(1)}, bf16[4,2,48,768]{3,2,1,0:T(8,128)(2,1)S(1)}, u32[]{:S(2)}, u32[]{:S(2)}) collective-permute-start(bf16[4,2,48,768]{3,2,1,0:T(8,128)(2,1)S(1)} %pad_maximum_fusion.refs_16_.refs_0_), channel_id=1, source_target_pairs={{0,1},{1,0},{2,3},{3,2},{4,5},{5,4},{6,7},{7,6},{8,9},{9,8},{10,11... | collective-permute-start | bytes 1769480 | tf_op jit(solution)/shard_map/ppermute | solution.py:1362
  174.8 23.4 %collective-permute-start.46 = (bf16[4,1,48,768]{3,2,1,0:T(8,128)(2,1)S(1)}, bf16[4,1,48,768]{3,2,1,0:T(8,128)(2,1)S(1)}, u32[]{:S(2)}, u32[]{:S(2)}) collective-permute-start(bf16[4,1,48,768]{3,2,1,0:T(8,128)(2,1)S(1)} %copy-done.50), channel_id=1, source_target_pairs={{0,2},{2,0},{1,3},{3,1},{4,6},{6,4},{5,7},{7,5},{8,10},{10,8},{9,1... | collective-permute-start | bytes 884744 | tf_op jit(solution)/shard_map/ppermute | solution.py:1366
  182.6 15.6 %collective-permute-start.47 = (bf16[4,1,48,768]{3,2,1,0:T(8,128)(2,1)S(1)}, bf16[4,1,48,768]{3,2,1,0:T(8,128)(2,1)S(1)}, u32[]{:S(2)}, u32[]{:S(2)}) collective-permute-start(bf16[4,1,48,768]{3,2,1,0:T(8,128)(2,1)S(1)} %copy-done.53), channel_id=1, source_target_pairs={{0,2},{2,0},{1,3},{3,1},{4,6},{6,4},{5,7},{7,5},{8,10},{10,8},{9,1... | collective-permute-start | bytes 884744 | tf_op jit(solution)/shard_map/ppermute | solution.py:1366
  218.6 20.0 %collective-permute-start.60 = (bf16[512,1280]{1,0:T(8,128)(2,1)}, bf16[512,1280]{1,0:T(8,128)(2,1)}, u32[]{:S(2)}, u32[]{:S(2)}) collective-permute-start(bf16[512,1280]{1,0:T(8,128)(2,1)} %get-tuple-element.356), channel_id=1, source_target_pairs={{0,2},{2,0},{1,3},{3,1},{4,6},{6,4},{5,7},{7,5},{8,10},{10,8},{9,1... | collective-permute-start | bytes 3932168 | tf_op jit(solution)/shard_map/ppermute | solution.py:1366
  219.4 15.5 %collective-permute-start.52 = (bf16[4,2,48,768]{3,2,1,0:T(8,128)(2,1)S(1)}, bf16[4,2,48,768]{3,2,1,0:T(8,128)(2,1)S(1)}, u32[]{:S(2)}, u32[]{:S(2)}) collective-permute-start(bf16[4,2,48,768]{3,2,1,0:T(8,128)(2,1)S(1)} %collective-permute-done.48.refs_17_.refs_1_), channel_id=1, source_target_pairs={{0,1},{1,0},{2,3},{3,2},{4,5},{5,4},{6,7},{7,6},{8,9},{9,8},{10,11... | collective-permute-start | bytes 1769480 | tf_op jit(solution)/shard_map/ppermute | solution.py:1362
  220.1 15.4 %collective-permute-start.53 = (bf16[4,2,48,768]{3,2,1,0:T(8,128)(2,1)S(1)}, bf16[4,2,48,768]{3,2,1,0:T(8,128)(2,1)S(1)}, u32[]{:S(2)}, u32[]{:S(2)}) collective-permute-start(bf16[4,2,48,768]{3,2,1,0:T(8,128)(2,1)S(1)} %collective-permute-done.49.refs_26_.refs_10_), channel_id=1, source_target_pairs={{0,4},{4,0},{8,12},{12,8},{16,20},{20,16},{24,28},{28,24},{1,5},{5... | collective-permute-start | bytes 1769480 | tf_op jit(solution)/shard_map/ppermute | solution.py:1358
  222.5 13.0 %collective-permute-start.55 = (bf16[4,2,48,768]{3,2,1,0:T(8,128)(2,1)S(1)}, bf16[4,2,48,768]{3,2,1,0:T(8,128)(2,1)S(1)}, u32[]{:S(2)}, u32[]{:S(2)}) collective-permute-start(bf16[4,2,48,768]{3,2,1,0:T(8,128)(2,1)S(1)} %collective-permute-done.48.refs_17_.refs_1_), channel_id=1, source_target_pairs={{0,2},{2,0},{1,3},{3,1},{4,6},{6,4},{5,7},{7,5},{8,10},{10,8},{9,1... | collective-permute-start | bytes 1769480 | tf_op jit(solution)/shard_map/ppermute | solution.py:1366
  223.4 12.2 %collective-permute-start.56 = (bf16[4,2,48,768]{3,2,1,0:T(8,128)(2,1)S(1)}, bf16[4,2,48,768]{3,2,1,0:T(8,128)(2,1)S(1)}, u32[]{:S(2)}, u32[]{:S(2)}) collective-permute-start(bf16[4,2,48,768]{3,2,1,0:T(8,128)(2,1)S(1)} %collective-permute-done.50.refs_18_.refs_2_), channel_id=1, source_target_pairs={{0,2},{2,0},{1,3},{3,1},{4,6},{6,4},{5,7},{7,5},{8,10},{10,8},{9,1... | collective-permute-start | bytes 1769480 | tf_op jit(solution)/shard_map/ppermute | solution.py:1366
  237.8 12.9 %collective-permute-start.61 = (bf16[4,2,48,768]{3,2,1,0:T(8,128)(2,1)S(1)}, bf16[4,2,48,768]{3,2,1,0:T(8,128)(2,1)S(1)}, u32[]{:S(2)}, u32[]{:S(2)}) collective-permute-start(bf16[4,2,48,768]{3,2,1,0:T(8,128)(2,1)S(1)} %collective-permute-done.52.refs_19_.refs_3_), channel_id=1, source_target_pairs={{0,2},{2,0},{1,3},{3,1},{4,6},{6,4},{5,7},{7,5},{8,10},{10,8},{9,1... | collective-permute-start | bytes 1769480 | tf_op jit(solution)/shard_map/ppermute | solution.py:1366
  237.9 12.8 %collective-permute-start.62 = (bf16[4,2,48,768]{3,2,1,0:T(8,128)(2,1)S(1)}, bf16[4,2,48,768]{3,2,1,0:T(8,128)(2,1)S(1)}, u32[]{:S(2)}, u32[]{:S(2)}) collective-permute-start(bf16[4,2,48,768]{3,2,1,0:T(8,128)(2,1)S(1)} %collective-permute-done.53.refs_27_.refs_11_), channel_id=1, source_target_pairs={{0,2},{2,0},{1,3},{3,1},{4,6},{6,4},{5,7},{7,5},{8,10},{10,8},{9,1... | collective-permute-start | bytes 1769480 | tf_op jit(solution)/shard_map/ppermute | solution.py:1366
  250.7 17.8 %collective-permute-start.65 = (bf16[512,768]{1,0:T(8,128)(2,1)}, bf16[512,768]{1,0:T(8,128)(2,1)S(1)}, u32[]{:S(2)}, u32[]{:S(2)}) collective-permute-start(bf16[512,768]{1,0:T(8,128)(2,1)} %bitcast.200), channel_id=1, source_target_pairs={{0,0},{1,2},{2,1},{3,3},{4,4},{5,6},{6,5},{7,7},{8,8},{9,10},{10,9... | collective-permute-start | bytes 2359304 | tf_op jit(solution)/shard_map/ppermute | solution.py:1378
  281.0 51.8 %collective-permute-start.71 = (bf16[512,3072]{1,0:T(8,128)(2,1)}, bf16[512,3072]{1,0:T(8,128)(2,1)S(1)}, u32[]{:S(2)}, u32[]{:S(2)}) collective-permute-start(bf16[512,3072]{1,0:T(8,128)(2,1)} %down_back.2.gu.refs_6_), channel_id=1, source_target_pairs={{0,2},{2,0},{1,3},{3,1},{4,6},{6,4},{5,7},{7,5},{8,10},{10,8},{9,1... | collective-permute-start | bytes 9437192 | tf_op jit(solution)/shard_map/ppermute | solution.py:1366
  315.1 17.7 %collective-permute-start.68 = (bf16[8,192,512]{2,1,0:T(8,128)(2,1)S(1)}, bf16[8,192,512]{2,1,0:T(8,128)(2,1)}, u32[]{:S(2)}, u32[]{:S(2)}) collective-permute-start(bf16[8,192,512]{2,1,0:T(8,128)(2,1)S(1)} %copy-done.71), channel_id=1, source_target_pairs={{0,2},{2,0},{1,3},{3,1},{4,6},{6,4},{5,7},{7,5},{8,10},{10,8},{9,1... | collective-permute-start | bytes 4718600 | tf_op jit(solution)/shard_map/ppermute | solution.py:1366
  318.9 13.9 %collective-permute-start.75 = (bf16[512,1280]{1,0:T(8,128)(2,1)}, bf16[512,1280]{1,0:T(8,128)(2,1)}, u32[]{:S(2)}, u32[]{:S(2)}) collective-permute-start(bf16[512,1280]{1,0:T(8,128)(2,1)} %get-tuple-element.403.down_.refs_14_), channel_id=1, source_target_pairs={{0,2},{2,0},{1,3},{3,1},{4,6},{6,4},{5,7},{7,5},{8,10},{10,8},{9,1... | collective-permute-start | bytes 3932168 | tf_op jit(solution)/shard_map/ppermute | solution.py:1366
  405.9 38.2 %collective-permute-start.81 = (bf16[2,4,2,48,768]{4,3,2,1,0:T(8,128)(2,1)}, bf16[2,4,2,48,768]{4,3,2,1,0:T(8,128)(2,1)}, u32[]{:S(2)}, u32[]{:S(2)}) collective-permute-start(bf16[2,4,2,48,768]{4,3,2,1,0:T(8,128)(2,1)} %get-tuple-element.450), channel_id=1, source_target_pairs={{0,4},{4,0},{8,12},{12,8},{16,20},{20,16},{24,28},{28,24},{1,5},{5... | collective-permute-start | bytes 3538952 | tf_op jit(solution)/shard_map/ppermute | solution.py:1358
  407.7 37.4 %collective-permute-start.82 = (bf16[2,4,2,48,768]{4,3,2,1,0:T(8,128)(2,1)}, bf16[2,4,2,48,768]{4,3,2,1,0:T(8,128)(2,1)}, u32[]{:S(2)}, u32[]{:S(2)}) collective-permute-start(bf16[2,4,2,48,768]{4,3,2,1,0:T(8,128)(2,1)} %get-tuple-element.451), channel_id=1, source_target_pairs={{0,1},{1,0},{2,3},{3,2},{4,5},{5,4},{6,7},{7,6},{8,9},{9,8},{10,11... | collective-permute-start | bytes 3538952 | tf_op jit(solution)/shard_map/ppermute | solution.py:1362
  427.0 25.1 %collective-permute-start.86 = (bf16[512,1280]{1,0:T(8,128)(2,1)}, bf16[512,1280]{1,0:T(8,128)(2,1)S(1)}, u32[]{:S(2)}, u32[]{:S(2)}) collective-permute-start(bf16[512,1280]{1,0:T(8,128)(2,1)} %get-tuple-element.459.refs_8_), channel_id=1, source_target_pairs={{0,2},{2,0},{1,3},{3,1},{4,6},{6,4},{5,7},{7,5},{8,10},{10,8},{9,1... | collective-permute-start | bytes 3932168 | tf_op jit(solution)/shard_map/ppermute | solution.py:1366
  427.1 25.0 %collective-permute-start.87 = (bf16[512,1280]{1,0:T(8,128)(2,1)}, bf16[512,1280]{1,0:T(8,128)(2,1)S(1)}, u32[]{:S(2)}, u32[]{:S(2)}) collective-permute-start(bf16[512,1280]{1,0:T(8,128)(2,1)} %get-tuple-element.458.refs_6_.down_), channel_id=1, source_target_pairs={{0,2},{2,0},{1,3},{3,1},{4,6},{6,4},{5,7},{7,5},{8,10},{10,8},{9,1... | collective-permute-start | bytes 3932168 | tf_op jit(solution)/shard_map/ppermute | solution.py:1366
  428.5 23.6 %collective-permute-start.85 = (bf16[512,768]{1,0:T(8,128)(2,1)}, bf16[512,768]{1,0:T(8,128)(2,1)}, u32[]{:S(2)}, u32[]{:S(2)}) collective-permute-start(bf16[512,768]{1,0:T(8,128)(2,1)} %get-tuple-element.457.refs_4_), channel_id=1, source_target_pairs={{0,2},{2,0},{1,3},{3,1},{4,6},{6,4},{5,7},{7,5},{8,10},{10,8},{9,1... | collective-permute-start | bytes 2359304 | tf_op jit(solution)/shard_map/ppermute | solution.py:1366
  450.0 29.6 %collective-permute-start.89 = (bf16[4,2,48,768]{3,2,1,0:T(8,128)(2,1)}, bf16[4,2,48,768]{3,2,1,0:T(8,128)(2,1)}, u32[]{:S(2)}, u32[]{:S(2)}) collective-permute-start(bf16[4,2,48,768]{3,2,1,0:T(8,128)(2,1)} %get-tuple-element.475), channel_id=1, source_target_pairs={{0,1},{1,0},{2,3},{3,2},{4,5},{5,4},{6,7},{7,6},{8,9},{9,8},{10,11... | collective-permute-start | bytes 1769480 | tf_op jit(solution)/shard_map/ppermute | solution.py:1362
  451.3 29.3 %collective-permute-start.90 = (bf16[4,2,48,768]{3,2,1,0:T(8,128)(2,1)}, bf16[4,2,48,768]{3,2,1,0:T(8,128)(2,1)}, u32[]{:S(2)}, u32[]{:S(2)}) collective-permute-start(bf16[4,2,48,768]{3,2,1,0:T(8,128)(2,1)} %get-tuple-element.476), channel_id=1, source_target_pairs={{0,4},{4,0},{8,12},{12,8},{16,20},{20,16},{24,28},{28,24},{1,5},{5... | collective-permute-start | bytes 1769480 | tf_op jit(solution)/shard_map/ppermute | solution.py:1358
  475.4 37.4 %collective-permute-start.91 = (bf16[2,4,1,48,768]{4,3,2,1,0:T(8,128)(2,1)}, bf16[2,4,1,48,768]{4,3,2,1,0:T(8,128)(2,1)}, u32[]{:S(2)}, u32[]{:S(2)}) collective-permute-start(bf16[2,4,1,48,768]{4,3,2,1,0:T(8,128)(2,1)} %get-tuple-element.477), channel_id=1, source_target_pairs={{0,4},{4,0},{8,12},{12,8},{16,20},{20,16},{24,28},{28,24},{1,5},{5... | collective-permute-start | bytes 1769480 | tf_op jit(solution)/shard_map/ppermute | solution.py:1358
  476.6 36.2 %collective-permute-start.92 = (bf16[2,4,1,48,768]{4,3,2,1,0:T(8,128)(2,1)}, bf16[2,4,1,48,768]{4,3,2,1,0:T(8,128)(2,1)}, u32[]{:S(2)}, u32[]{:S(2)}) collective-permute-start(bf16[2,4,1,48,768]{4,3,2,1,0:T(8,128)(2,1)} %get-tuple-element.478), channel_id=1, source_target_pairs={{0,1},{1,0},{2,3},{3,2},{4,5},{5,4},{6,7},{7,6},{8,9},{9,8},{10,11... | collective-permute-start | bytes 1769480 | tf_op jit(solution)/shard_map/ppermute | solution.py:1362
  478.5 31.8 %collective-permute-start.94 = (f32[4,48,128]{1,2,0:T(8,128)S(1)}, f32[4,48,128]{1,2,0:T(8,128)S(1)}, u32[]{:S(2)}, u32[]{:S(2)}) collective-permute-start(f32[4,48,128]{1,2,0:T(8,128)S(1)} %get-tuple-element.605), channel_id=1, source_target_pairs={{0,1},{1,0},{2,3},{3,2},{4,5},{5,4},{6,7},{7,6},{8,9},{9,8},{10,11... | collective-permute-start | bytes 294920 | tf_op jit(solution)/shard_map/ppermute | solution.py:1362
  479.7 31.3 %collective-permute-start.95 = (f32[4,48,128]{1,2,0:T(8,128)S(1)}, f32[4,48,128]{1,2,0:T(8,128)S(1)}, u32[]{:S(2)}, u32[]{:S(2)}) collective-permute-start(f32[4,48,128]{1,2,0:T(8,128)S(1)} %get-tuple-element.604), channel_id=1, source_target_pairs={{0,4},{4,0},{8,12},{12,8},{16,20},{20,16},{24,28},{28,24},{1,5},{5... | collective-permute-start | bytes 294920 | tf_op jit(solution)/shard_map/ppermute | solution.py:1358
  480.5 32.3 %collective-permute-start.96 = (f32[4,48,128]{1,2,0:T(8,128)S(1)}, f32[4,48,128]{1,2,0:T(8,128)S(1)}, u32[]{:S(2)}, u32[]{:S(2)}) collective-permute-start(f32[4,48,128]{1,2,0:T(8,128)S(1)} %get-tuple-element.604), channel_id=1, source_target_pairs={{0,5},{1,4},{4,1},{5,0},{8,13},{9,12},{12,9},{13,8},{16,21},{17,20... | collective-permute-start | bytes 294920 | tf_op jit(solution)/shard_map/ppermute | solution.py:1374
  510.3 15.0 %collective-permute-start.64 = (bf16[512,768]{1,0:T(8,128)(2,1)S(1)}, bf16[512,768]{1,0:T(8,128)(2,1)S(1)}, u32[]{:S(2)}, u32[]{:S(2)}) collective-permute-start(bf16[512,768]{1,0:T(8,128)(2,1)S(1)} %copy-done.77), channel_id=1, source_target_pairs={{0,0},{1,2},{2,1},{3,3},{4,4},{5,6},{6,5},{7,7},{8,8},{9,10},{10,9... | collective-permute-start | bytes 2359304 | tf_op jit(solution)/shard_map/ppermute | solution.py:1378
  511.0 23.3 %collective-permute-start.88 = (bf16[512,768]{1,0:T(8,128)(2,1)}, bf16[512,768]{1,0:T(8,128)(2,1)S(1)}, u32[]{:S(2)}, u32[]{:S(2)}) collective-permute-start(bf16[512,768]{1,0:T(8,128)(2,1)} %get-tuple-element.469), channel_id=1, source_target_pairs={{0,0},{1,2},{2,1},{3,3},{4,4},{5,6},{6,5},{7,7},{8,8},{9,10},{10,9... | collective-permute-start | bytes 2359304 | tf_op jit(solution)/shard_map/ppermute | solution.py:1378
  512.9 15.8 %collective-permute-start.102 = (f32[48,128]{0,1:T(8,128)S(1)}, f32[48,128]{0,1:T(8,128)S(1)}, u32[]{:S(2)}, u32[]{:S(2)}) collective-permute-start(f32[48,128]{0,1:T(8,128)S(1)} %get-tuple-element.581), channel_id=1, source_target_pairs={{0,8},{4,12},{8,0},{12,4},{16,24},{20,28},{24,16},{28,20},{1,9},{5... | collective-permute-start | bytes 73736 | tf_op jit(solution)/shard_map/ppermute | solution.py:1358
  514.5 16.0 %collective-permute-start.103 = (f32[48,128]{0,1:T(8,128)S(1)}, f32[48,128]{0,1:T(8,128)S(1)}, u32[]{:S(2)}, u32[]{:S(2)}) collective-permute-start(f32[48,128]{0,1:T(8,128)S(1)} %get-tuple-element.580), channel_id=1, source_target_pairs={{0,16},{4,20},{8,24},{12,28},{16,0},{20,4},{24,8},{28,12},{1,17},{... | collective-permute-start | bytes 73736 | tf_op jit(solution)/shard_map/ppermute | solution.py:1358
  516.9 14.1 %collective-permute-start.104 = (f32[48,128]{0,1:T(8,128)S(1)}, f32[48,128]{0,1:T(8,128)S(1)}, u32[]{:S(2)}, u32[]{:S(2)}) collective-permute-start(f32[48,128]{0,1:T(8,128)S(1)} %get-tuple-element.579), channel_id=1, source_target_pairs={{0,24},{4,28},{8,16},{12,20},{16,8},{20,12},{24,0},{28,4},{1,25},{... | collective-permute-start | bytes 73736 | tf_op jit(solution)/shard_map/ppermute | solution.py:1358
  525.3 14.5 %collective-permute-start.100 = (bf16[4,1,48,768]{3,2,1,0:T(8,128)(2,1)}, bf16[4,1,48,768]{3,2,1,0:T(8,128)(2,1)S(1)}, u32[]{:S(2)}, u32[]{:S(2)}) collective-permute-start(bf16[4,1,48,768]{3,2,1,0:T(8,128)(2,1)} %get-tuple-element.493), channel_id=1, source_target_pairs={{0,1},{1,0},{2,3},{3,2},{4,5},{5,4},{6,7},{7,6},{8,9},{9,8},{10,11... | collective-permute-start | bytes 884744 | tf_op jit(solution)/shard_map/ppermute | solution.py:1362
  530.4 13.1 %collective-permute-start.97 = (bf16[2,2,48,768]{3,2,1,0:T(8,128)(2,1)}, bf16[2,2,48,768]{3,2,1,0:T(8,128)(2,1)S(1)}, u32[]{:S(2)}, u32[]{:S(2)}) collective-permute-start(bf16[2,2,48,768]{3,2,1,0:T(8,128)(2,1)} %get-tuple-element.488), channel_id=1, source_target_pairs={{0,8},{4,12},{8,0},{12,4},{16,24},{20,28},{24,16},{28,20},{1,9},{5... | collective-permute-start | bytes 884744 | tf_op jit(solution)/shard_map/ppermute | solution.py:1358
  531.0 22.5 %collective-permute-start.98 = (bf16[2,2,48,768]{3,2,1,0:T(8,128)(2,1)}, bf16[2,2,48,768]{3,2,1,0:T(8,128)(2,1)S(1)}, u32[]{:S(2)}, u32[]{:S(2)}) collective-permute-start(bf16[2,2,48,768]{3,2,1,0:T(8,128)(2,1)} %get-tuple-element.489), channel_id=1, source_target_pairs={{0,16},{4,20},{8,24},{12,28},{16,0},{20,4},{24,8},{28,12},{1,17},{... | collective-permute-start | bytes 884744 | tf_op jit(solution)/shard_map/ppermute | solution.py:1358
  534.3 19.2 %collective-permute-start.99 = (bf16[2,2,48,768]{3,2,1,0:T(8,128)(2,1)S(1)}, bf16[2,2,48,768]{3,2,1,0:T(8,128)(2,1)S(1)}, u32[]{:S(2)}, u32[]{:S(2)}) collective-permute-start(bf16[2,2,48,768]{3,2,1,0:T(8,128)(2,1)S(1)} %copy-done.89), channel_id=1, source_target_pairs={{0,24},{4,28},{8,16},{12,20},{16,8},{20,12},{24,0},{28,4},{1,25},{... | collective-permute-start | bytes 884744 | tf_op jit(solution)/shard_map/ppermute | solution.py:1358
  563.1 12.6 %collective-permute-start.106 = (bf16[2,1,48,768]{3,2,1,0:T(8,128)(2,1)}, bf16[2,1,48,768]{3,2,1,0:T(8,128)(2,1)S(1)}, u32[]{:S(2)}, u32[]{:S(2)}) collective-permute-start(bf16[2,1,48,768]{3,2,1,0:T(8,128)(2,1)} %get-tuple-element.502), channel_id=1, source_target_pairs={{0,16},{4,20},{8,24},{12,28},{16,0},{20,4},{24,8},{28,12},{1,17},{... | collective-permute-start | bytes 442376 | tf_op jit(solution)/shard_map/ppermute | solution.py:1358
  (137 other events, 1457.2 us)
Sparse Core Ops, SparseCore 0:
  11.4 107.8 all-gather.2
  360.0 171.8 reduce-scatter.1
